TPU v7x, 32 devices: a whole 2x2x4 slice. The times are simulated.
32 devices in a mesh: ctx: 16 (over z, x, core), head: 2 (over y).
Axes of the slice: x: 2, y: 2, z: 4, core: 2. Of those that a mesh axis runs over, the one named last changes fastest.
Arguments:
- queries: bfloat16 [4096, 4096], P('ctx', 'head')
- keys: bfloat16 [4096, 1024], P(('ctx', 'head'))
- values: bfloat16 [4096, 1024], P(('ctx', 'head')), may hold values from -6 to 6
- selected: int32 [32, 8, 3], P('ctx', 'head'), may hold values from 0 to 6, as said below
Outputs:
- attended: bfloat16 [4096, 4096], P('ctx', 'head')
Inputs may be any that keep to these rules, and one draw needn't show every extreme that they name: selected[t, g, :] names 3 different blocks of 512 positions that lie before the block of tile t; where fewer than 3 such blocks exist, the remaining entries equal the tile's own block and name nothing more.
All inputs are finite; a program needn't handle non-finite values.
Results may differ from a plain program's by a relative error of at most 0.0041.
Values may be sent and summed in bfloat16 or wider, within the bound.
No kernel may reach another device: no remote copies, remote signals or barrier semaphores. Data moves between devices by JAX's collectives and lax.ppermute only.
A program may use at most 64 MiB of HBM per device.

v0:
```python
import math

import jax
import jax.numpy as jnp
from jax import lax
from jax.sharding import PartitionSpec as P

HD = 128
QH = 32
KVH = 8
BLK = 512
TILE = 128


floor_value = -1e30


def body(queries, keys, values, selected):
    local_rows = queries.shape[0]
    group_count = KVH // lax.axis_size("head")
    per_group = QH // KVH
    score_scale = HD ** (-0.5)
    own_keys, own_values = (
        lax.all_to_all(keys, "head", split_axis=1, concat_axis=0, tiled=True),
        lax.all_to_all(values, "head", split_axis=1, concat_axis=0, tiled=True),
    )
    query_four = queries.reshape(local_rows, group_count, per_group, HD)
    offset = lax.axis_index("ctx") * local_rows
    query_pos = offset + jnp.arange(local_rows, dtype=jnp.int32)
    query_block = query_pos // BLK
    row_select = jnp.repeat(selected, TILE, axis=0)

    def attend(running, key_rows, value_rows, first_row):
        row_count = key_rows.shape[0]
        key_pos = first_row + jnp.arange(row_count, dtype=jnp.int32)
        key_block = key_pos // BLK
        own_part = (key_block[None, :] == query_block[:, None]) & (
            key_pos[None, :] <= query_pos[:, None]
        )
        picked = jnp.any(row_select[:, :, :, None] == key_block[None, None, None, :], axis=2)
        picked = picked & (key_block[None, None, :] != query_block[:, None, None])
        allowed = jnp.transpose(picked | own_part[:, None, :], (1, 0, 2))

        def compute(current):
            running_max, totals, accumulated = current
            scores = (
                jnp.einsum(
                    "qgjd,kgd->gjqk",
                    query_four,
                    key_rows.reshape(row_count, group_count, HD),
                    preferred_element_type=jnp.float32,
                )
                * score_scale
            )
            live_mask = allowed[:, None]
            row_top = jnp.max(jnp.where(live_mask, scores, floor_value), axis=-1)
            newest = jnp.maximum(running_max, row_top)
            weights = jnp.where(live_mask, jnp.exp(scores - newest[..., None]), 0.0)
            factor = jnp.exp(running_max - newest)
            totals = totals * factor + jnp.sum(weights, axis=-1)
            product = jnp.einsum(
                "gjqk,kgd->gjqd",
                weights.astype(jnp.bfloat16),
                value_rows.reshape(row_count, group_count, HD),
                preferred_element_type=jnp.float32,
            )
            accumulated = accumulated * factor[..., None] + product
            return (newest, totals, accumulated)

        def keep_running(current):
            return current

        needed = jnp.any(allowed)
        return lax.cond(needed, compute, keep_running, running)

    start_max = jnp.full((group_count, per_group, local_rows), floor_value, jnp.float32)
    start_totals = jnp.zeros((group_count, per_group, local_rows), jnp.float32)
    start_accumulated = jnp.zeros((group_count, per_group, local_rows, HD), jnp.float32)
    key_piece = lax.all_gather(own_keys, "ctx", axis=0, tiled=True)
    value_piece = lax.all_gather(own_values, "ctx", axis=0, tiled=True)
    row_count = key_piece.shape[0]
    step_rows = math.gcd(row_count, 512)

    def loop_body(block_index, current):
        key_part = lax.dynamic_slice_in_dim(key_piece, block_index * step_rows, step_rows, 0)
        value_part = lax.dynamic_slice_in_dim(value_piece, block_index * step_rows, step_rows, 0)
        return attend(current, key_part, value_part, block_index * step_rows)

    running_max, totals, accumulated = lax.fori_loop(
        0, row_count // step_rows, loop_body, (start_max, start_totals, start_accumulated)
    )
    mixed = accumulated / totals[..., None]
    return (
        jnp.transpose(mixed, (2, 0, 1, 3))
        .reshape(local_rows, group_count * per_group * HD)
        .astype(jnp.bfloat16)
    )


def solution(mesh):
    placed = (
        P("ctx", "head"),
        P(("ctx", "head"), None),
        P(("ctx", "head"), None),
        P("ctx", "head", None),
    )
    return jax.shard_map(
        body, mesh=mesh, in_specs=placed, out_specs=P("ctx", "head"), check_vma=False
    )
```

profile of v0, /device:TPU:27, one launch (start us, length us, event | category | flops | bytes accessed | tf_op | source)
XLA Modules:
  0.0 254.5 jit_solution(11256422979810992226)
XLA Ops:
  7.8 6.7 %all_to_all.38 = bf16[128,2,512]{0,2,1:T(8,128)(2,1)S(1)} all-to-all(bf16[128,2,512]{0,2,1:T(8,128)(2,1)S(1)} %bitcast.60), channel_id=1, replica_groups=mesh['ctx'=16,'head'=2] {'head'}, dimensions={1} | all-to-all | bytes 524288 | tf_op jit(solution)/shard_map/all_to_all | solution.py:24
  16.5 6.4 %all_to_all.39 = bf16[128,2,512]{0,2,1:T(8,128)(2,1)S(1)} all-to-all(bf16[128,2,512]{0,2,1:T(8,128)(2,1)S(1)} %bitcast.61), channel_id=1, replica_groups=mesh['ctx'=16,'head'=2] {'head'}, dimensions={1} | all-to-all | bytes 524288 | tf_op jit(solution)/shard_map/all_to_all | solution.py:25
  25.8 39.4 %all-gather.3.cloned.1.call-done = bf16[4096,512]{1,0:T(8,128)(2,1)} async-done(((bf16[256,512]{1,0:T(8,128)(2,1)}), bf16[4096,512]{1,0:T(8,128)(2,1)}) %all-gather.3.cloned.1.call-update) | async-done | bytes 4194320 | tf_op jit(solution)/shard_map/all_gather | solution.py:79
  65.2 6.4 %copy.69 = bf16[4096,512]{0,1:T(8,128)(2,1)} copy(bf16[4096,512]{1,0:T(8,128)(2,1)} %all-gather.3.cloned.1.call-done) | data formatting | bytes 8388608
  71.6 44.8 %all-gather.5.cloned.1.call-done = bf16[4096,512]{1,0:T(8,128)(2,1)} async-done(((bf16[256,512]{1,0:T(8,128)(2,1)}), bf16[4096,512]{1,0:T(8,128)(2,1)}) %all-gather.5.cloned.1.call-update) | async-done | bytes 4194320 | tf_op jit(solution)/shard_map/all_gather | solution.py:80
  116.4 6.5 %copy.71 = bf16[4096,512]{0,1:T(8,128)(2,1)} copy(bf16[4096,512]{1,0:T(8,128)(2,1)} %all-gather.5.cloned.1.call-done) | data formatting | bytes 8388608
  124.5 118.8 %while.21 = (s32[]{:T(128)}, f32[4,4,256]{2,1,0:T(4,128)S(1)}, f32[4,4,256]{2,1,0:T(4,128)S(1)}, f32[4,4,256,128]{3,2,1,0:T(8,128)}, bf16[4096,512]{0,1:T(8,128)...) while((s32[]{:T(128)}, f32[4,4,256]{2,1,0:T(4,128)S(1)}, ...), condition=%wide.region_7.8_spmd.clone.clone, body=%wide.region_0.7_spmd.clone.clone.sunk | while | flops 1103646720 | bytes 56711624 | solution.py:89
  128.2 11.1 %conditional.4 = ((f32[4,4,256]{2,1,0:T(4,128)S(1)}, f32[4,4,256]{2,1,0:T(4,128)S(1)}, f32[4,4,256,128]{3,2,1,0:T(8,128)})) conditional(s32[]{:T(128)} %convert_element_type.38, (f32[4,4,256]{2,1,0:T(4,128)S(1)}, f32[4,4,256]{2,1,0:T(4,128)S(1)}, f32[4,4,256,128]{3,2,1,0:T(8,128)}) %tuple.84, (pred[256,512]{0,1:T(8,128)(4,1)S(1)}, ...), branch_computations={%region_3.3_spmd, %region_4.6_spmd} | conditional | flops 1098915840 | bytes 54526076 | solution.py:74
  130.9 1.9 fusion.6
  134.6 3.3 %multiply_add_fusion = f32[4,4,256,128]{3,2,1,0:T(8,128)S(1)} fusion(f32[4,4,256,128]{3,2,1,0:T(8,128)S(1)} %copy-done, bf16[512,4,128,1]{0,2,3,1:T(8,128)(2,1)S(1)} %bitcast.53, f32[4,512,256,4]{2,1,3,0:T(8,128)S(1)} %get-tuple-element.534, f32[4,4,256]{2,1,0:T(4,128)S(1)} %max.5, pred[4,256,512]{1,2,0:T(8,128)(4,1)S(1)} %and_or_fusion, ...), kind=kOutput, calls=%fused_computation.15 | convolution fusion | flops 546308096 | bytes 13664256 | tf_op jit(solution)/shard_map/while/body/eval_jaxpr/cond/branch_1_fun/gjqk,kgd->gjqd/dot_general | solution.py:61
  143.0 11.1 %conditional.4 = ((f32[4,4,256]{2,1,0:T(4,128)S(1)}, f32[4,4,256]{2,1,0:T(4,128)S(1)}, f32[4,4,256,128]{3,2,1,0:T(8,128)})) conditional(s32[]{:T(128)} %convert_element_type.38, (f32[4,4,256]{2,1,0:T(4,128)S(1)}, f32[4,4,256]{2,1,0:T(4,128)S(1)}, f32[4,4,256,128]{3,2,1,0:T(8,128)}) %tuple.84, (pred[256,512]{0,1:T(8,128)(4,1)S(1)}, ...), branch_computations={%region_3.3_spmd, %region_4.6_spmd} | conditional | flops 1098915840 | bytes 54526076 | solution.py:74
  145.7 1.9 fusion.6
  149.5 3.3 %multiply_add_fusion = f32[4,4,256,128]{3,2,1,0:T(8,128)S(1)} fusion(f32[4,4,256,128]{3,2,1,0:T(8,128)S(1)} %copy-done, bf16[512,4,128,1]{0,2,3,1:T(8,128)(2,1)S(1)} %bitcast.53, f32[4,512,256,4]{2,1,3,0:T(8,128)S(1)} %get-tuple-element.534, f32[4,4,256]{2,1,0:T(4,128)S(1)} %max.5, pred[4,256,512]{1,2,0:T(8,128)(4,1)S(1)} %and_or_fusion, ...), kind=kOutput, calls=%fused_computation.15 | convolution fusion | flops 546308096 | bytes 13664256 | tf_op jit(solution)/shard_map/while/body/eval_jaxpr/cond/branch_1_fun/gjqk,kgd->gjqd/dot_general | solution.py:61
  157.9 11.1 %conditional.4 = ((f32[4,4,256]{2,1,0:T(4,128)S(1)}, f32[4,4,256]{2,1,0:T(4,128)S(1)}, f32[4,4,256,128]{3,2,1,0:T(8,128)})) conditional(s32[]{:T(128)} %convert_element_type.38, (f32[4,4,256]{2,1,0:T(4,128)S(1)}, f32[4,4,256]{2,1,0:T(4,128)S(1)}, f32[4,4,256,128]{3,2,1,0:T(8,128)}) %tuple.84, (pred[256,512]{0,1:T(8,128)(4,1)S(1)}, ...), branch_computations={%region_3.3_spmd, %region_4.6_spmd} | conditional | flops 1098915840 | bytes 54526076 | solution.py:74
  160.5 1.9 fusion.6
  164.3 3.3 %multiply_add_fusion = f32[4,4,256,128]{3,2,1,0:T(8,128)S(1)} fusion(f32[4,4,256,128]{3,2,1,0:T(8,128)S(1)} %copy-done, bf16[512,4,128,1]{0,2,3,1:T(8,128)(2,1)S(1)} %bitcast.53, f32[4,512,256,4]{2,1,3,0:T(8,128)S(1)} %get-tuple-element.534, f32[4,4,256]{2,1,0:T(4,128)S(1)} %max.5, pred[4,256,512]{1,2,0:T(8,128)(4,1)S(1)} %and_or_fusion, ...), kind=kOutput, calls=%fused_computation.15 | convolution fusion | flops 546308096 | bytes 13664256 | tf_op jit(solution)/shard_map/while/body/eval_jaxpr/cond/branch_1_fun/gjqk,kgd->gjqd/dot_general | solution.py:61
  172.7 11.1 %conditional.4 = ((f32[4,4,256]{2,1,0:T(4,128)S(1)}, f32[4,4,256]{2,1,0:T(4,128)S(1)}, f32[4,4,256,128]{3,2,1,0:T(8,128)})) conditional(s32[]{:T(128)} %convert_element_type.38, (f32[4,4,256]{2,1,0:T(4,128)S(1)}, f32[4,4,256]{2,1,0:T(4,128)S(1)}, f32[4,4,256,128]{3,2,1,0:T(8,128)}) %tuple.84, (pred[256,512]{0,1:T(8,128)(4,1)S(1)}, ...), branch_computations={%region_3.3_spmd, %region_4.6_spmd} | conditional | flops 1098915840 | bytes 54526076 | solution.py:74
  175.4 1.9 fusion.6
  179.2 3.3 %multiply_add_fusion = f32[4,4,256,128]{3,2,1,0:T(8,128)S(1)} fusion(f32[4,4,256,128]{3,2,1,0:T(8,128)S(1)} %copy-done, bf16[512,4,128,1]{0,2,3,1:T(8,128)(2,1)S(1)} %bitcast.53, f32[4,512,256,4]{2,1,3,0:T(8,128)S(1)} %get-tuple-element.534, f32[4,4,256]{2,1,0:T(4,128)S(1)} %max.5, pred[4,256,512]{1,2,0:T(8,128)(4,1)S(1)} %and_or_fusion, ...), kind=kOutput, calls=%fused_computation.15 | convolution fusion | flops 546308096 | bytes 13664256 | tf_op jit(solution)/shard_map/while/body/eval_jaxpr/cond/branch_1_fun/gjqk,kgd->gjqd/dot_general | solution.py:61
  187.6 11.1 %conditional.4 = ((f32[4,4,256]{2,1,0:T(4,128)S(1)}, f32[4,4,256]{2,1,0:T(4,128)S(1)}, f32[4,4,256,128]{3,2,1,0:T(8,128)})) conditional(s32[]{:T(128)} %convert_element_type.38, (f32[4,4,256]{2,1,0:T(4,128)S(1)}, f32[4,4,256]{2,1,0:T(4,128)S(1)}, f32[4,4,256,128]{3,2,1,0:T(8,128)}) %tuple.84, (pred[256,512]{0,1:T(8,128)(4,1)S(1)}, ...), branch_computations={%region_3.3_spmd, %region_4.6_spmd} | conditional | flops 1098915840 | bytes 54526076 | solution.py:74
  190.2 1.9 fusion.6
  194.0 3.3 %multiply_add_fusion = f32[4,4,256,128]{3,2,1,0:T(8,128)S(1)} fusion(f32[4,4,256,128]{3,2,1,0:T(8,128)S(1)} %copy-done, bf16[512,4,128,1]{0,2,3,1:T(8,128)(2,1)S(1)} %bitcast.53, f32[4,512,256,4]{2,1,3,0:T(8,128)S(1)} %get-tuple-element.534, f32[4,4,256]{2,1,0:T(4,128)S(1)} %max.5, pred[4,256,512]{1,2,0:T(8,128)(4,1)S(1)} %and_or_fusion, ...), kind=kOutput, calls=%fused_computation.15 | convolution fusion | flops 546308096 | bytes 13664256 | tf_op jit(solution)/shard_map/while/body/eval_jaxpr/cond/branch_1_fun/gjqk,kgd->gjqd/dot_general | solution.py:61
  202.4 11.1 %conditional.4 = ((f32[4,4,256]{2,1,0:T(4,128)S(1)}, f32[4,4,256]{2,1,0:T(4,128)S(1)}, f32[4,4,256,128]{3,2,1,0:T(8,128)})) conditional(s32[]{:T(128)} %convert_element_type.38, (f32[4,4,256]{2,1,0:T(4,128)S(1)}, f32[4,4,256]{2,1,0:T(4,128)S(1)}, f32[4,4,256,128]{3,2,1,0:T(8,128)}) %tuple.84, (pred[256,512]{0,1:T(8,128)(4,1)S(1)}, ...), branch_computations={%region_3.3_spmd, %region_4.6_spmd} | conditional | flops 1098915840 | bytes 54526076 | solution.py:74
  205.1 1.9 fusion.6
  208.9 3.3 %multiply_add_fusion = f32[4,4,256,128]{3,2,1,0:T(8,128)S(1)} fusion(f32[4,4,256,128]{3,2,1,0:T(8,128)S(1)} %copy-done, bf16[512,4,128,1]{0,2,3,1:T(8,128)(2,1)S(1)} %bitcast.53, f32[4,512,256,4]{2,1,3,0:T(8,128)S(1)} %get-tuple-element.534, f32[4,4,256]{2,1,0:T(4,128)S(1)} %max.5, pred[4,256,512]{1,2,0:T(8,128)(4,1)S(1)} %and_or_fusion, ...), kind=kOutput, calls=%fused_computation.15 | convolution fusion | flops 546308096 | bytes 13664256 | tf_op jit(solution)/shard_map/while/body/eval_jaxpr/cond/branch_1_fun/gjqk,kgd->gjqd/dot_general | solution.py:61
  217.3 11.1 %conditional.4 = ((f32[4,4,256]{2,1,0:T(4,128)S(1)}, f32[4,4,256]{2,1,0:T(4,128)S(1)}, f32[4,4,256,128]{3,2,1,0:T(8,128)})) conditional(s32[]{:T(128)} %convert_element_type.38, (f32[4,4,256]{2,1,0:T(4,128)S(1)}, f32[4,4,256]{2,1,0:T(4,128)S(1)}, f32[4,4,256,128]{3,2,1,0:T(8,128)}) %tuple.84, (pred[256,512]{0,1:T(8,128)(4,1)S(1)}, ...), branch_computations={%region_3.3_spmd, %region_4.6_spmd} | conditional | flops 1098915840 | bytes 54526076 | solution.py:74
  219.9 1.9 fusion.6
  223.7 3.3 %multiply_add_fusion = f32[4,4,256,128]{3,2,1,0:T(8,128)S(1)} fusion(f32[4,4,256,128]{3,2,1,0:T(8,128)S(1)} %copy-done, bf16[512,4,128,1]{0,2,3,1:T(8,128)(2,1)S(1)} %bitcast.53, f32[4,512,256,4]{2,1,3,0:T(8,128)S(1)} %get-tuple-element.534, f32[4,4,256]{2,1,0:T(4,128)S(1)} %max.5, pred[4,256,512]{1,2,0:T(8,128)(4,1)S(1)} %and_or_fusion, ...), kind=kOutput, calls=%fused_computation.15 | convolution fusion | flops 546308096 | bytes 13664256 | tf_op jit(solution)/shard_map/while/body/eval_jaxpr/cond/branch_1_fun/gjqk,kgd->gjqd/dot_general | solution.py:61
  232.1 11.1 %conditional.4 = ((f32[4,4,256]{2,1,0:T(4,128)S(1)}, f32[4,4,256]{2,1,0:T(4,128)S(1)}, f32[4,4,256,128]{3,2,1,0:T(8,128)})) conditional(s32[]{:T(128)} %convert_element_type.38, (f32[4,4,256]{2,1,0:T(4,128)S(1)}, f32[4,4,256]{2,1,0:T(4,128)S(1)}, f32[4,4,256,128]{3,2,1,0:T(8,128)}) %tuple.84, (pred[256,512]{0,1:T(8,128)(4,1)S(1)}, ...), branch_computations={%region_3.3_spmd, %region_4.6_spmd} | conditional | flops 1098915840 | bytes 54526076 | solution.py:74
  234.8 1.9 fusion.6
  238.6 3.3 %multiply_add_fusion = f32[4,4,256,128]{3,2,1,0:T(8,128)S(1)} fusion(f32[4,4,256,128]{3,2,1,0:T(8,128)S(1)} %copy-done, bf16[512,4,128,1]{0,2,3,1:T(8,128)(2,1)S(1)} %bitcast.53, f32[4,512,256,4]{2,1,3,0:T(8,128)S(1)} %get-tuple-element.534, f32[4,4,256]{2,1,0:T(4,128)S(1)} %max.5, pred[4,256,512]{1,2,0:T(8,128)(4,1)S(1)} %and_or_fusion, ...), kind=kOutput, calls=%fused_computation.15 | convolution fusion | flops 546308096 | bytes 13664256 | tf_op jit(solution)/shard_map/while/body/eval_jaxpr/cond/branch_1_fun/gjqk,kgd->gjqd/dot_general | solution.py:61
  243.3 1.9 fusion.24
  (186 shorter events, 81.1 us)
Async XLA Ops:
  6.5 18.1 %copy-start.2 = (bf16[256,2048]{1,0:T(8,128)(2,1)S(1)}, bf16[256,2048]{1,0:T(8,128)(2,1)}, u32[]{:S(2)}) copy-start(bf16[256,2048]{1,0:T(8,128)(2,1)} %param.8) | copy-start | bytes 3145732
  6.5 58.6 %all-gather.3.cloned.1.call-start = ((), (), s32[]{:S(2)}) async-start(), calls=%async_computation.2 | async-start | bytes 4456448 | tf_op jit(solution)/shard_map/all_gather | solution.py:79
  15.4 101.1 %all-gather.5.cloned.1.call-start = ((), (), s32[]{:S(2)}) async-start(), calls=%async_computation.3 | async-start | bytes 4456448 | tf_op jit(solution)/shard_map/all_gather | solution.py:80
  132.8 1.9 copy-start
  138.0 1.4 copy-start.1
  147.6 1.9 copy-start
  152.8 1.4 copy-start.1
  162.5 1.9 copy-start
  167.7 1.4 copy-start.1
  177.3 1.9 copy-start
  182.5 1.4 copy-start.1
  192.1 1.9 copy-start
  197.4 1.4 copy-start.1
  207.0 1.9 copy-start
  212.2 1.4 copy-start.1
  221.8 1.9 copy-start
  227.1 1.4 copy-start.1
  236.7 1.9 copy-start
  241.9 1.4 copy-start.1
Sparse Core Ops, SparseCore 0:
  15.5 49.6 all-gather.2
  67.3 49.0 all-gather.4
where the time goes:
time: 255 us; the launch traced here: 254 us
  waiting for transfers between devices  84.2 us (33%)
  local copies, waits for them, and re-layouts  56.3 us (22%)
  matrix products  41.6 us (16%)
  other arithmetic  39.5 us (15%)
  between operations  13.5 us (5%)
  blocking collectives  13.1 us (5%)
  loops' own time  6.12 us (2%)
    all_gather x1, waiting for transfers between devices, body(): value_piece = lax.all_gather(own_values, 'ctx', axis=0, tiled=True)  44.8 us
    all_gather x1, waiting for transfers between devices, body(): key_piece = lax.all_gather(own_keys, 'ctx', axis=0, tiled=True)  39.4 us
    dot_general x8, matrix products, compute(): jnp.einsum('gjqk,kgd->gjqd', weights.astype(jnp.bfloat16), value_rows.res...  26.6 us
    unnamed x9, local copies, waits for them, and re-layouts  17.2 us
    dot_general x8, matrix products, compute(): jnp.einsum('qgjd,kgd->gjqk', query_four, key_rows.reshape(row_count, grou...  15.1 us
    reduce_sum x8, other arithmetic, compute(): totals = totals * factor + jnp.sum(weights, axis=-1)  14.7 us
    cond x40, local copies, waits for them, and re-layouts  10.8 us
    dynamic_slice x8, local copies, waits for them, and re-layouts, loop_body(): lax.dynamic_slice_in_dim(value_piece, block_index * step_rows, step_rows, 0)  10.2 us
  transfers between devices with their start and end apart: 2, of which 2 were waited for; matrix products, arithmetic and copies ran while one was open for 4% of the time, Pallas kernels for 0%

commit v1 on v0

v1 whole, which is shorter than its diff:
```python
import functools
import math

import jax
import jax.numpy as jnp
from jax import lax
from jax.experimental import pallas as pl
from jax.experimental.pallas import tpu as pltpu
from jax.sharding import Mesh, PartitionSpec as P

HD = 128
QH = 32
KVH = 8
BLK = 512
TILE = 128
TOPK = 3
PER = QH // KVH
QW = PER * HD

FLOOR = -1e30
SCALE = HD ** -0.5 * math.log2(math.e)
NONE = -100000
F32 = jnp.float32
BF16 = jnp.bfloat16


def dot_nt(a, b):
    return lax.dot_general(a, b, (((1,), (1,)), ((), ())), preferred_element_type=F32)


def dot_nn(a, b):
    return lax.dot_general(a, b, (((1,), (0,)), ((), ())), preferred_element_type=F32)


def attention(levels, first, last, flipped, bases_of, queries, sel, sources, state):
    parts, rows = queries.shape[0], queries.shape[1] // TILE * TILE
    tiles = parts * rows // TILE
    tiles_in_part = rows // TILE
    chunk_rows = sources[0].shape[2]
    per_block = BLK // chunk_rows
    n_src = len(sources)

    def kernel(*refs):
        sel_ref, q_ref = refs[:2]
        src = refs[2 : 2 + n_src]
        rest = refs[2 + n_src :]
        if not first:
            m_in, l_in, acc_in = rest[:3]
            rest = rest[3:]
        if last:
            out_ref, m_ref, l_ref, acc_ref = rest
        else:
            m_ref, l_ref, acc_ref = rest
        level = lax.axis_index("lev")
        bases = bases_of(level)

        def key_rows(ref, block, count):
            part = ref[pl.ds(block * per_block, count // chunk_rows), 0]
            return part.reshape(count, HD)

        def value_columns(ref, block, count):
            n = count // chunk_rows
            if flipped:
                pieces = [ref[block * per_block + i, 1] for i in range(n)]
                return jnp.concatenate(pieces, axis=1) if n > 1 else pieces[0]
            part = ref[pl.ds(block * per_block, n), 1]
            return part.reshape(count, HD).T

        def one_tile(t, carry):
            slot = 0 if last else t
            part, at = t // tiles_in_part, lax.rem(t, tiles_in_part) * TILE
            tile = level * tiles + t
            own = tile * TILE // BLK
            rows4 = q_ref[part, pl.ds(pl.multiple_of(at, TILE), TILE), :]
            q = jnp.concatenate([rows4[:, j * HD : (j + 1) * HD] for j in range(PER)], axis=0)

            def own_part(pieces):
                count = pieces * TILE
                block = own - bases[0]
                s = dot_nt(key_rows(src[0], block, count), q)
                key_at = lax.broadcasted_iota(jnp.int32, s.shape, 0)
                query_at = lax.rem(lax.broadcasted_iota(jnp.int32, s.shape, 1), TILE)
                s = jnp.where(key_at <= query_at + (count - TILE), s, FLOOR)
                m = jnp.max(s, axis=0, keepdims=True)
                p = jnp.exp2((s - m) * SCALE)
                m_ref[slot] = m
                l_ref[slot] = jnp.sum(p, axis=0, keepdims=True)
                acc_ref[slot] = dot_nn(value_columns(src[0], block, count), p.astype(BF16))

            if first:
                for pieces in range(1, BLK // TILE + 1):
                    pl.when(lax.rem(tile, BLK // TILE) == pieces - 1)(
                        functools.partial(own_part, pieces)
                    )
            else:
                m_ref[slot] = m_in[t]
                l_ref[slot] = l_in[t]
                acc_ref[slot] = acc_in[t]

            def other(e, carry):
                block = sel_ref[t * TOPK + e]
                for ref, base in zip(src, bases):
                    blocks = ref.shape[0] // per_block

                    @pl.when((block != own) & (block >= base) & (block < base + blocks))
                    def _():
                        s = dot_nt(key_rows(ref, block - base, BLK), q)
                        old = m_ref[slot]
                        m = jnp.maximum(old, jnp.max(s, axis=0, keepdims=True))
                        p = jnp.exp2((s - m) * SCALE)
                        fade = jnp.exp2((old - m) * SCALE)
                        m_ref[slot] = m
                        l_ref[slot] = l_ref[slot] * fade + jnp.sum(p, axis=0, keepdims=True)
                        acc_ref[slot] = acc_ref[slot] * fade + dot_nn(
                            value_columns(ref, block - base, BLK), p.astype(BF16)
                        )

                return carry

            lax.fori_loop(0, TOPK, other, 0)
            if last:
                mixed = acc_ref[0] / l_ref[0]
                for j in range(PER):
                    out_ref[part, pl.ds(pl.multiple_of(at, TILE), TILE), j * HD : (j + 1) * HD] = (
                        mixed[:, j * HD : (j + 1) * HD].T.astype(BF16)
                    )
            return carry

        lax.fori_loop(0, tiles, one_tile, 0)

    kept = (
        jax.ShapeDtypeStruct((tiles, 1, QW), F32),
        jax.ShapeDtypeStruct((tiles, 1, QW), F32),
        jax.ShapeDtypeStruct((tiles, HD, QW), F32),
    )
    vmem = pl.BlockSpec(memory_space=pltpu.VMEM)
    return pl.pallas_call(
        kernel,
        in_specs=[pl.BlockSpec(memory_space=pltpu.SMEM)] + [vmem] * (1 + n_src + len(state)),
        out_shape=jax.ShapeDtypeStruct((parts, rows, QW), BF16) if last else kept,
        out_specs=vmem if last else (vmem,) * 3,
        scratch_shapes=[
            pltpu.VMEM((1, 1, QW), F32),
            pltpu.VMEM((1, 1, QW), F32),
            pltpu.VMEM((1, HD, QW), F32),
        ]
        if last
        else [],
        compiler_params=pltpu.CompilerParams(vmem_limit_bytes=50 * 1024 * 1024),
        cost_estimate=pl.CostEstimate(
            flops=4 * n_src * tiles * QW * BLK * HD,
            transcendentals=n_src * tiles * QW * BLK,
            bytes_accessed=8 * 1024 * 1024,
        ),
    )(sel, queries, *sources, *state)


def body(levels, subs, heads, queries, keys, values, selected):
    rows = queries.shape[0]
    r = keys.shape[0]
    tiles_here = selected.shape[0]
    flipped = r == HD

    def by_owner(a, flip):
        a = a.reshape(r, heads, subs, HD)
        a = jnp.transpose(a, (2, 1, 3, 0) if flip else (2, 1, 0, 3))
        return a.reshape(subs * heads, 1, r, HD)

    packed = jnp.concatenate([by_owner(keys, False), by_owner(values, flipped)], axis=1)
    own = lax.all_to_all(packed, ("sub", "head"), 0, 0, tiled=True)

    picks = jnp.transpose(selected, (1, 0, 2)).reshape(subs, 1, tiles_here * TOPK).astype(BF16)
    picks = jnp.pad(picks, ((0, 0), (0, 15), (0, QW - tiles_here * TOPK)))
    q = jnp.transpose(queries.reshape(rows, subs, QW), (1, 0, 2))
    q = jnp.concatenate([q, picks], axis=1)
    if subs > 1:
        q = lax.all_to_all(q, "sub", 0, 0, tiled=True)
    sel = q[:, rows, : tiles_here * TOPK].astype(jnp.int32).reshape(-1)

    level_blocks = subs * rows // BLK
    if levels == 4 and subs * rows % BLK == 0:
        level = lax.axis_index("lev")
        p1 = lax.ppermute(own, "lev", [(0, 2), (2, 3)])
        p2 = lax.ppermute(own, "lev", [(1, 3), (0, 1)])
        p3 = lax.ppermute(jnp.where(level == 2, p1, own), "lev", [(2, 3), (1, 2)])

        def at(level, *which):
            base = jnp.int32(NONE)
            for here, holds in which:
                base = jnp.where(level == here, holds * level_blocks, base)
            return base

        def early(level):
            return (level * level_blocks, at(level, (2, 0), (3, 2)), at(level, (1, 0), (3, 1)))

        def late(level):
            return (at(level, (2, 1), (3, 0)),)

        state = attention(levels, True, False, flipped, early, q, sel, (own, p1, p2), ())
        out = attention(levels, False, True, flipped, late, q, sel, (p3,), state)
    else:
        whole = lax.all_gather(own, "lev", axis=0, tiled=True)
        out = attention(
            levels, True, True, flipped, lambda level: (0,), q, sel, (whole,), ()
        )
    if subs > 1:
        out = lax.all_to_all(out, "sub", 0, 0, tiled=True)
    return jnp.transpose(out, (1, 0, 2)).reshape(rows, subs * QW)


def solution(mesh):
    ctx, heads = mesh.shape["ctx"], mesh.shape["head"]
    subs = math.gcd(KVH // heads, ctx)
    if subs * heads != KVH:
        raise ValueError("unsupported mesh")
    levels = ctx // subs
    split = Mesh(mesh.devices.reshape(levels, subs, heads), ("lev", "sub", "head"))
    placed = (
        P(("lev", "sub"), "head"),
        P(("lev", "sub", "head"), None),
        P(("lev", "sub", "head"), None),
        P(("lev", "sub"), "head", None),
    )
    return jax.shard_map(
        functools.partial(body, levels, subs, heads),
        mesh=split,
        in_specs=placed,
        out_specs=P(("lev", "sub"), "head"),
        check_vma=False,
    )
```

time: 255 us -> 88.7 us (0.35)
  the two profiles are of different devices: /device:TPU:27 before, /device:TPU:24 now
where the time goes in v1:
time: 88.7 us; the launch traced here: 88.2 us
  Pallas kernels  26.3 us (30%)
  waiting for transfers between devices  25.9 us (29%)
  blocking collectives  16.9 us (19%)
  starting transfers between devices  11.1 us (13%)
  local copies, waits for them, and re-layouts  5.03 us (6%)
  other arithmetic  2.82 us (3%)
    pallas_call x2, Pallas kernels, attention(): pl.pallas_call(kernel, in_specs=[pl.BlockSpec(memory_space=pltpu.SMEM)] +...  26.3 us
    all_to_all x1, blocking collectives, body(): out = lax.all_to_all(out, 'sub', 0, 0, tiled=True)  16.9 us
    ppermute x1, waiting for transfers between devices, body(): p1 = lax.ppermute(own, 'lev', [(0, 2), (2, 3)])  8.69 us
    all_to_all x1, waiting for transfers between devices, body(): own = lax.all_to_all(packed, ('sub', 'head'), 0, 0, tiled=True)  7.42 us
    ppermute x1, waiting for transfers between devices, body(): p2 = lax.ppermute(own, 'lev', [(1, 3), (0, 1)])  6.78 us
    all_to_all x1, starting transfers between devices, body(): own = lax.all_to_all(packed, ('sub', 'head'), 0, 0, tiled=True)  3.72 us
    all_to_all x1, starting transfers between devices, body(): q = lax.all_to_all(q, 'sub', 0, 0, tiled=True)  3.52 us
    all_to_all x1, waiting for transfers between devices, body(): q = lax.all_to_all(q, 'sub', 0, 0, tiled=True)  3 us
  transfers between devices with their start and end apart: 5, of which 4 were waited for; matrix products, arithmetic and copies ran while one was open for 4% of the time, Pallas kernels for 22%

profile of v1, /device:TPU:24, one launch (start us, length us, event | category | flops | bytes accessed | tf_op | source)
XLA Modules:
  0.0 88.2 jit_solution(15989724106188339279)
XLA Ops:
  0.0 0.0 copy-start.1
  0.0 1.2 %reshape.37 = bf16[128,2,4,128]{3,2,1,0:T(4,128)(2,1)S(1)} reshape(bf16[128,1024]{1,0:T(8,128)(2,1)} %param.5) | data formatting | bytes 524288 | tf_op jit(solution)/shard_map/reshape | solution.py:165
  1.2 0.0 copy-done.1
  1.2 0.2 reshape.39
  1.4 0.2 copy.14
  1.6 0.0 copy-start
  1.6 0.8 pad_maximum_fusion
  2.5 3.7 %all-to-all-start.1 = ((bf16[8,2,128,128]{3,2,1,0:T(8,128)(2,1)}), bf16[8,2,128,128]{3,2,1,0:T(8,128)(2,1)S(1)}, u32[]{:S(2)}, u32[]{:S(2)}) async-start(bf16[8,2,128,128]{3,2,1,0:T(8,128)(2,1)} %pad_maximum_fusion), calls=%async_computation.1 | async-start | bytes 1048576 | tf_op jit(solution)/shard_map/all_to_all | solution.py:170
  6.2 0.0 copy-done
  6.2 0.5 copy.9
  6.7 0.0 copy-start.2
  6.8 0.5 copy.10
  7.3 0.1 copy-done.2
  7.4 0.1 copy.11
  7.6 0.1 convert_element_type.32
  7.6 7.4 %all-to-all-done.1.refs_2_ = bf16[8,2,128,128]{3,2,1,0:T(8,128)(2,1)S(1)} async-done(((bf16[8,2,128,128]{3,2,1,0:T(8,128)(2,1)}), bf16[8,2,128,128]{3,2,1,0:T(8,128)(2,1)S(1)}, u32[]{:S(2)}, u32[]{:S(2)}) %all-to-all-start.1) | async-done | bytes 524320 | tf_op jit(solution)/shard_map/all_to_all | solution.py:170
  15.1 1.3 %collective-permute-start = (bf16[8,2,128,128]{3,2,1,0:T(8,128)(2,1)S(1)}, bf16[8,2,128,128]{3,2,1,0:T(8,128)(2,1)S(1)}, u32[]{:S(2)}, u32[]{:S(2)}) collective-permute-start(bf16[8,2,128,128]{3,2,1,0:T(8,128)(2,1)S(1)} %all-to-all-done.1.refs_2_), channel_id=1, source_target_pairs={{0,16},{16,24},{1,17},{17,25},{2,18},{18,26},{3,19},{19,27},{4,20}... | collective-permute-start | bytes 1572872 | tf_op jit(solution)/shard_map/ppermute | solution.py:183
  16.3 1.1 %fusion.1 = bf16[4,272,512]{2,1,0:T(8,128)(2,1)} fusion(bf16[4,1,6]{2,1,0:T(2,128)(2,1)S(1)} %convert_element_type.32, bf16[4,256,512]{2,1,0:T(8,128)(2,1)S(1)} %bitcast.12), kind=kLoop, calls=%fused_computation.2 | loop fusion | flops 3342336 | bytes 2162736 | tf_op jit(solution)/shard_map/concatenate | solution.py:175
  17.4 3.5 %all-to-all-start = ((bf16[4,272,512]{2,1,0:T(8,128)(2,1)}), bf16[4,272,512]{2,1,0:T(8,128)(2,1)S(1)}, u32[]{:S(2)}, u32[]{:S(2)}) async-start(bf16[4,272,512]{2,1,0:T(8,128)(2,1)} %fusion.1), calls=%async_computation | async-start | bytes 2228224 | tf_op jit(solution)/shard_map/all_to_all | solution.py:177
  21.0 1.3 %collective-permute-start.2 = (bf16[8,2,128,128]{3,2,1,0:T(8,128)(2,1)S(1)}, bf16[8,2,128,128]{3,2,1,0:T(8,128)(2,1)S(1)}, u32[]{:S(2)}, u32[]{:S(2)}) collective-permute-start(bf16[8,2,128,128]{3,2,1,0:T(8,128)(2,1)S(1)} %all-to-all-done.1.refs_2_), channel_id=1, source_target_pairs={{8,24},{0,8},{9,25},{1,9},{10,26},{2,10},{11,27},{3,11},{12,28},{4... | collective-permute-start | bytes 1572872 | tf_op jit(solution)/shard_map/ppermute | solution.py:184
  22.3 8.7 %collective-permute-done.refs_3_ = bf16[8,2,128,128]{3,2,1,0:T(8,128)(2,1)S(1)} collective-permute-done((bf16[8,2,128,128]{3,2,1,0:T(8,128)(2,1)S(1)}, bf16[8,2,128,128]{3,2,1,0:T(8,128)(2,1)S(1)}, u32[]{:S(2)}, u32[]{:S(2)}) %collective-permute-start) | collective-permute-done | bytes 524320 | tf_op jit(solution)/shard_map/ppermute | solution.py:183
  31.0 0.8 broadcast_select_fusion
  31.8 1.3 %collective-permute-start.1 = (bf16[8,2,128,128]{3,2,1,0:T(8,128)(2,1)}, bf16[8,2,128,128]{3,2,1,0:T(8,128)(2,1)S(1)}, u32[]{:S(2)}, u32[]{:S(2)}) collective-permute-start(bf16[8,2,128,128]{3,2,1,0:T(8,128)(2,1)} %broadcast_select_fusion), channel_id=1, source_target_pairs={{16,24},{8,16},{17,25},{9,17},{18,26},{10,18},{19,27},{11,19},{20,... | collective-permute-start | bytes 1572872 | tf_op jit(solution)/shard_map/ppermute | solution.py:185
  33.1 3.0 %all-to-all-done.refs_1_ = bf16[4,272,512]{2,1,0:T(8,128)(2,1)S(1)} async-done(((bf16[4,272,512]{2,1,0:T(8,128)(2,1)}), bf16[4,272,512]{2,1,0:T(8,128)(2,1)S(1)}, u32[]{:S(2)}, u32[]{:S(2)}) %all-to-all-start) | async-done | bytes 1114144 | tf_op jit(solution)/shard_map/all_to_all | solution.py:177
  36.1 0.1 reshape.42.refs_0_
  36.2 6.8 %collective-permute-done.2.refs_4_ = bf16[8,2,128,128]{3,2,1,0:T(8,128)(2,1)S(1)} collective-permute-done((bf16[8,2,128,128]{3,2,1,0:T(8,128)(2,1)S(1)}, bf16[8,2,128,128]{3,2,1,0:T(8,128)(2,1)S(1)}, u32[]{:S(2)}, u32[]{:S(2)}) %collective-permute-start.2) | collective-permute-done | bytes 524320 | tf_op jit(solution)/shard_map/ppermute | solution.py:184
  43.0 19.2 %shard_map.46 = (f32[8,1,512]{2,1,0:T(1,128)S(1)}, f32[8,1,512]{2,1,0:T(1,128)S(1)}, f32[8,128,512]{2,1,0:T(8,128)}) custom-call(s32[24]{0:T(128)S(1)} %reshape.42.refs_0_, bf16[4,272,512]{2,1,0:T(8,128)(2,1)S(1)} %all-to-all-done.refs_1_, bf16[8,2,128,128]{3,2,1,0:T(8,128)(2,1)S(1)} %all-to-all-done.1.refs_2_, ...), custom_call_target="tpu_custom_call" | custom-call | flops 3221225472 | bytes 8388608 | tf_op jit(solution)/shard_map/pallas_call | solution.py:137
  62.2 0.0 collective-permute-done.1.refs_2_
  62.2 7.1 %shard_map.47 = bf16[4,256,512]{2,1,0:T(8,128)(2,1)S(1)} custom-call(s32[24]{0:T(128)S(1)} %reshape.42.refs_0_, bf16[4,272,512]{2,1,0:T(8,128)(2,1)S(1)} %all-to-all-done.refs_1_, bf16[8,2,128,128]{3,2,1,0:T(8,128)(2,1)S(1)} %collective-permute-done.1.refs_2_, f32[8,1,512]{2,1,0:T(1,128)S(1)} %get-tuple-element.8.refs_3_, ...), custom_call_target="tpu_custom_call" | custom-call | flops 1073741824 | bytes 8388608 | tf_op jit(solution)/shard_map/pallas_call | solution.py:137
  69.4 16.9 %all_to_all.15 = bf16[4,256,512]{2,1,0:T(8,128)(2,1)S(1)} all-to-all(bf16[4,256,512]{2,1,0:T(8,128)(2,1)S(1)} %shard_map.47), channel_id=1, replica_groups=mesh['lev'=4,'sub'=4,'head'=2] {'sub'}, dimensions={0} | all-to-all | bytes 2097152 | tf_op jit(solution)/shard_map/all_to_all | solution.py:207
  86.3 0.5 copy.15
  86.8 1.4 %copy.16 = bf16[256,2048]{1,0:T(8,128)(2,1)} copy(bf16[256,2048]{0,1:T(8,128)(2,1)S(1)} %bitcast.14) | data formatting | bytes 2097152 | tf_op jit(solution)/shard_map/reshape | solution.py:208
  (3 shorter events, 0.1 us)
Async XLA Ops:
  0.0 1.2 %copy-start.1 = (bf16[128,1024]{1,0:T(8,128)(2,1)S(1)}, bf16[128,1024]{1,0:T(8,128)(2,1)}, u32[]{:S(2)}) copy-start(bf16[128,1024]{1,0:T(8,128)(2,1)} %param.6) | copy-start | bytes 786436
  1.6 4.6 %copy-start = (bf16[256,2048]{1,0:T(8,128)(2,1)S(1)}, bf16[256,2048]{1,0:T(8,128)(2,1)}, u32[]{:S(2)}) copy-start(bf16[256,2048]{1,0:T(8,128)(2,1)} %param.4) | copy-start | bytes 3145732
  2.5 12.6 %all-to-all-start.1 = ((bf16[8,2,128,128]{3,2,1,0:T(8,128)(2,1)}), bf16[8,2,128,128]{3,2,1,0:T(8,128)(2,1)S(1)}, u32[]{:S(2)}, u32[]{:S(2)}) async-start(bf16[8,2,128,128]{3,2,1,0:T(8,128)(2,1)} %pad_maximum_fusion), calls=%async_computation.1 | async-start | bytes 1048576 | tf_op jit(solution)/shard_map/all_to_all | solution.py:170
  6.7 0.7 copy-start.2
  15.1 15.9 %collective-permute-start = (bf16[8,2,128,128]{3,2,1,0:T(8,128)(2,1)S(1)}, bf16[8,2,128,128]{3,2,1,0:T(8,128)(2,1)S(1)}, u32[]{:S(2)}, u32[]{:S(2)}) collective-permute-start(bf16[8,2,128,128]{3,2,1,0:T(8,128)(2,1)S(1)} %all-to-all-done.1.refs_2_), channel_id=1, source_target_pairs={{0,16},{16,24},{1,17},{17,25},{2,18},{18,26},{3,19},{19,27},{4,20}... | collective-permute-start | bytes 1572872 | tf_op jit(solution)/shard_map/ppermute | solution.py:183
  17.4 18.7 %all-to-all-start = ((bf16[4,272,512]{2,1,0:T(8,128)(2,1)}), bf16[4,272,512]{2,1,0:T(8,128)(2,1)S(1)}, u32[]{:S(2)}, u32[]{:S(2)}) async-start(bf16[4,272,512]{2,1,0:T(8,128)(2,1)} %fusion.1), calls=%async_computation | async-start | bytes 2228224 | tf_op jit(solution)/shard_map/all_to_all | solution.py:177
  21.0 22.0 %collective-permute-start.2 = (bf16[8,2,128,128]{3,2,1,0:T(8,128)(2,1)S(1)}, bf16[8,2,128,128]{3,2,1,0:T(8,128)(2,1)S(1)}, u32[]{:S(2)}, u32[]{:S(2)}) collective-permute-start(bf16[8,2,128,128]{3,2,1,0:T(8,128)(2,1)S(1)} %all-to-all-done.1.refs_2_), channel_id=1, source_target_pairs={{8,24},{0,8},{9,25},{1,9},{10,26},{2,10},{11,27},{3,11},{12,28},{4... | collective-permute-start | bytes 1572872 | tf_op jit(solution)/shard_map/ppermute | solution.py:184
  31.8 30.4 %collective-permute-start.1 = (bf16[8,2,128,128]{3,2,1,0:T(8,128)(2,1)}, bf16[8,2,128,128]{3,2,1,0:T(8,128)(2,1)S(1)}, u32[]{:S(2)}, u32[]{:S(2)}) collective-permute-start(bf16[8,2,128,128]{3,2,1,0:T(8,128)(2,1)} %broadcast_select_fusion), channel_id=1, source_target_pairs={{16,24},{8,16},{17,25},{9,17},{18,26},{10,18},{19,27},{11,19},{20,... | collective-permute-start | bytes 1572872 | tf_op jit(solution)/shard_map/ppermute | solution.py:185

commit v2 on v1

v2 whole, which is shorter than its diff:
```python
import functools
import math

import jax
import jax.numpy as jnp
from jax import lax
from jax.experimental import pallas as pl
from jax.experimental.pallas import tpu as pltpu
from jax.sharding import Mesh, PartitionSpec as P

HD = 128
QH = 32
KVH = 8
BLK = 512
TILE = 128
TOPK = 3
PER = QH // KVH
QW = PER * HD
EXTRA = 16

FLOOR = -1e30
SCALE = HD ** -0.5 * math.log2(math.e)
NONE = -100000
F32 = jnp.float32
BF16 = jnp.bfloat16
VMEM = pl.BlockSpec(memory_space=pltpu.VMEM)
SMEM = pl.BlockSpec(memory_space=pltpu.SMEM)
MIB = 1024 * 1024


def dot_nt(a, b):
    return lax.dot_general(a, b, (((1,), (1,)), ((), ())), preferred_element_type=F32)


def dot_nn(a, b):
    return lax.dot_general(a, b, (((1,), (0,)), ((), ())), preferred_element_type=F32)


def copy_cost(bytes_moved):
    return pl.CostEstimate(flops=0, transcendentals=0, bytes_accessed=bytes_moved)


def pack_keys_values(subs, heads, keys, values):
    r = keys.shape[0]

    def kernel(k_ref, v_ref, out_ref):
        for sub in range(subs):
            for head in range(heads):
                at = (head * subs + sub) * HD
                out_ref[sub * heads + head, 0] = k_ref[:, at : at + HD]
                out_ref[sub * heads + head, 1] = v_ref[:, at : at + HD]

    return pl.pallas_call(
        kernel,
        in_specs=[VMEM, VMEM],
        out_specs=VMEM,
        out_shape=jax.ShapeDtypeStruct((subs * heads, 2, r, HD), BF16),
        cost_estimate=copy_cost(4 * keys.size * 2),
        compiler_params=pltpu.CompilerParams(vmem_limit_bytes=8 * MIB),
        name="pack_kv",
    )(keys, values)


def pack_queries(subs, queries, selected):
    rows = queries.shape[0]
    tiles_here = selected.shape[0]

    def kernel(sel_ref, q_ref, *outs):
        sub = lax.axis_index("sub") if subs > 1 else 0
        lane = lax.broadcasted_iota(jnp.int32, (EXTRA, QW), 1)
        for k, out_ref in enumerate(outs):
            head = sub ^ k
            out_ref[:rows] = q_ref[:, pl.ds(pl.multiple_of(head * QW, QW), QW)]
            row = jnp.zeros((EXTRA, QW), jnp.int32)
            for t in range(tiles_here):
                for e in range(TOPK):
                    row = jnp.where(lane == t * TOPK + e, sel_ref[t, head, e], row)
            out_ref[rows:] = row.astype(F32).astype(BF16)

    return pl.pallas_call(
        kernel,
        in_specs=[SMEM, VMEM],
        out_specs=(VMEM,) * subs,
        out_shape=(jax.ShapeDtypeStruct((rows + EXTRA, QW), BF16),) * subs,
        cost_estimate=copy_cost(2 * queries.size * 2),
        compiler_params=pltpu.CompilerParams(vmem_limit_bytes=8 * MIB),
        name="pack_q",
    )(selected, queries)


def unpack_output(subs, pieces):
    rows = pieces[0].shape[0]

    def kernel(*refs):
        sub = lax.axis_index("sub")
        for k in range(subs):
            at = pl.multiple_of((sub ^ k) * QW, QW)
            refs[subs][:, pl.ds(at, QW)] = refs[k][...]

    return pl.pallas_call(
        kernel,
        in_specs=[VMEM] * subs,
        out_specs=VMEM,
        out_shape=jax.ShapeDtypeStruct((rows, subs * QW), BF16),
        cost_estimate=copy_cost(4 * subs * rows * QW),
        compiler_params=pltpu.CompilerParams(vmem_limit_bytes=8 * MIB),
        name="unpack",
    )(*pieces)


def attention(name, first, last, partners, bases_of, queries, sel, sources, state):
    parts, rows = len(queries), queries[0].shape[0] - EXTRA
    tiles_in_part = rows // TILE
    tiles = parts * tiles_in_part
    r = sources[0].shape[2]
    per_block = BLK // r
    n_src = len(sources)
    slots = [src.shape[0] // per_block for src in sources]
    most = min(TOPK, sum(slots))
    n_q = len(partners)
    n_out = len(partners) if last else 2

    def kernel(*refs):
        sel_ref, q_refs = refs[0], refs[1 : 1 + n_q]
        src = refs[1 + n_q : 1 + n_q + n_src]
        rest = refs[1 + n_q + n_src :]
        m_in, acc_in = (None, None) if first else rest[:2]
        rest = rest if first else rest[2:]
        outs, k_buf, v_buf, m_tmp, acc_tmp, q_buf = rest[:n_out], *rest[n_out:]
        level = lax.axis_index("lev")
        sub = lax.axis_index("sub") if parts > 1 else 0
        for i, q_ref in enumerate(q_refs):
            q_buf[i] = q_ref[:rows]
        bases = bases_of(level)

        v_buf[:, HD:] = jnp.ones((sum(slots) * BLK, HD), BF16)
        start = 0
        for ref, base, n in zip(src, bases, slots):

            def fill(ref=ref, start=start, n=n):
                if n * per_block <= 8:
                    k_buf[start * BLK : (start + n) * BLK] = ref[:, 0].reshape(n * BLK, HD)
                    v_buf[start * BLK : (start + n) * BLK, :HD] = ref[:, 1].reshape(n * BLK, HD)
                else:

                    def chunk(i, carry):
                        at = pl.ds(pl.multiple_of(start * BLK + i * r, r), r)
                        k_buf[at] = ref[i, 0]
                        v_buf[at, :HD] = ref[i, 1]
                        return carry

                    lax.fori_loop(0, n * per_block, chunk, 0)

            if isinstance(base, int):
                fill()
            else:
                pl.when(base >= 0)(fill)
            start += n

        def one_tile(k, part, i, out_ref, out_at):
            t = k * tiles_in_part + i
            tile = level * tiles + (sub ^ k) * tiles_in_part + i
            own = tile * TILE // BLK
            q_rows = pl.ds(pl.multiple_of(i * TILE, TILE), TILE)
            m_old, acc_old, at_old = (m_tmp, acc_tmp, 0) if first else (m_in, acc_in, t)

            def finish(j, acc):
                out_ref[out_at, j * HD : (j + 1) * HD] = (acc[:, :HD] / acc[:, HD:]).astype(BF16)

            def keep(j, m, acc):
                outs[0][t, j * TILE : (j + 1) * TILE] = m
                outs[1][t, j * TILE : (j + 1) * TILE] = acc

            def own_part(pieces):
                count = pieces * TILE
                at = pl.ds(pl.multiple_of((own - bases[0]) * BLK, BLK), count)
                key_at = lax.broadcasted_iota(jnp.int32, (TILE, TILE), 1)
                query_at = lax.broadcasted_iota(jnp.int32, (TILE, TILE), 0)
                for j in range(PER):
                    s = dot_nt(q_buf[part, q_rows, j * HD : (j + 1) * HD], k_buf[at])
                    edge = jnp.where(key_at <= query_at, s[:, count - TILE :], FLOOR)
                    s = jnp.concatenate([s[:, : count - TILE], edge], axis=1) if pieces > 1 else edge
                    m = jnp.max(s, axis=1, keepdims=True)
                    p = jnp.exp2((s - m) * SCALE).astype(BF16)
                    m_tmp[0, j * TILE : (j + 1) * TILE] = jnp.broadcast_to(m, (TILE, HD))
                    acc_tmp[0, j * TILE : (j + 1) * TILE] = dot_nn(p, v_buf[at])

            if first:
                for pieces in range(1, BLK // TILE + 1):
                    pl.when(lax.rem(tile, BLK // TILE) == pieces - 1)(
                        functools.partial(own_part, pieces)
                    )

            found = jnp.int32(0)
            where = [jnp.int32(0)] * most
            for e in range(TOPK):
                block = sel_ref[t * TOPK + e]
                start = 0
                for base, n in zip(bases, slots):
                    hit = (block != own) & (block >= base) & (block < base + n)
                    where = [
                        jnp.where(hit & (found == i), start + block - base, w)
                        for i, w in enumerate(where)
                    ]
                    found = found + hit.astype(jnp.int32)
                    start += n

            def others(n):
                at = [pl.ds(pl.multiple_of(w * BLK, BLK), BLK) for w in where[:n]]
                for j in range(PER):
                    here = slice(j * TILE, (j + 1) * TILE)
                    old = m_old[at_old, here]
                    acc = acc_old[at_old, here]
                    if n:
                        q = q_buf[part, q_rows, j * HD : (j + 1) * HD]
                        s = [dot_nt(q, k_buf[a]) for a in at]
                        s = jnp.concatenate(s, axis=1) if n > 1 else s[0]
                        m = jnp.maximum(old, jnp.max(s, axis=1, keepdims=True))
                        p = jnp.exp2((s - jnp.tile(m, (1, n * BLK // HD))) * SCALE).astype(BF16)
                        fade = jnp.exp2((old - m) * SCALE)
                        acc = acc * jnp.tile(fade, (1, 2))
                        for i, a in enumerate(at):
                            acc = acc + dot_nn(p[:, i * BLK : (i + 1) * BLK], v_buf[a])
                        old = m
                    if last:
                        finish(j, acc)
                    else:
                        keep(j, old, acc)

            for n in range(most + 1):
                pl.when(found == n)(functools.partial(others, n))

        if last:
            for part, (out_ref, k) in enumerate(zip(outs, partners)):

                def step(i, carry, out_ref=out_ref, k=k, part=part):
                    out_at = pl.ds(pl.multiple_of(i * TILE, TILE), TILE)
                    one_tile(k, part, i, out_ref, out_at)
                    return carry

                lax.fori_loop(0, tiles_in_part, step, 0)
        else:

            def step(t, carry):
                k = t // tiles_in_part
                one_tile(k, k, lax.rem(t, tiles_in_part), None, None)
                return carry

            lax.fori_loop(0, tiles, step, 0)

    if last:
        out_shape = tuple(jax.ShapeDtypeStruct((rows, QW), BF16) for _ in partners)
    else:
        out_shape = (
            jax.ShapeDtypeStruct((tiles, QW, HD), F32),
            jax.ShapeDtypeStruct((tiles, QW, 2 * HD), F32),
        )
    work = (tiles if not last else len(partners) * tiles_in_part) * QW * BLK * (1 + n_src) // 2
    return pl.pallas_call(
        kernel,
        in_specs=[SMEM] + [VMEM] * (n_q + n_src + len(state)),
        out_shape=out_shape,
        out_specs=(VMEM,) * n_out,
        scratch_shapes=[
            pltpu.VMEM((sum(slots) * BLK, HD), BF16),
            pltpu.VMEM((sum(slots) * BLK, 2 * HD), BF16),
            pltpu.VMEM((1, QW, HD), F32),
            pltpu.VMEM((1, QW, 2 * HD), F32),
            pltpu.VMEM((n_q, rows, QW), BF16),
        ],
        compiler_params=pltpu.CompilerParams(
            vmem_limit_bytes=(24 if sum(slots) <= 16 else 56) * MIB
        ),
        cost_estimate=pl.CostEstimate(
            flops=8 * work * HD, transcendentals=work, bytes_accessed=4 * MIB
        ),
        name=name,
    )(sel, *[queries[k] for k in partners], *sources, *state)


def body(levels, subs, heads, queries, keys, values, selected):
    rows = queries.shape[0]
    tiles_here = selected.shape[0]
    level_blocks = subs * rows // BLK
    by_levels = levels == 4 and subs * rows % BLK == 0

    def exchange(pieces):
        return tuple(
            lax.ppermute(piece, "sub", [(i, i ^ k) for i in range(subs)]) if k else piece
            for k, piece in enumerate(pieces)
        )

    packed = pack_keys_values(subs, heads, keys, values)
    if by_levels:
        p1 = lax.ppermute(packed, "lev", [(0, 2), (2, 3)])
    own = lax.all_to_all(packed, ("sub", "head"), 0, 0, tiled=True)
    q = pack_queries(subs, queries, selected)
    q = exchange(q)
    sel = jnp.concatenate([piece[rows, : tiles_here * TOPK] for piece in q]).astype(jnp.int32)

    everyone = tuple(range(subs))
    if by_levels:
        p1 = lax.all_to_all(p1, ("sub", "head"), 0, 0, tiled=True)
        p2 = lax.ppermute(own, "lev", [(1, 3), (0, 1)])
        later, p1 = lax.optimization_barrier((own, p1))
        p3 = lax.ppermute(p1, "lev", [(2, 3)])
        p4 = lax.ppermute(later, "lev", [(1, 2)])

        def at(level, *which):
            base = jnp.int32(NONE)
            for here, holds in which:
                base = jnp.where(level == here, holds * level_blocks, base)
            return base

        def early(level):
            return (level * level_blocks, at(level, (2, 0), (3, 2)), at(level, (1, 0), (3, 1)))

        def late(level):
            return (at(level, (3, 0)), at(level, (2, 1)))

        state = attention(
            "early", True, False, everyone, early, q, sel, (own, p1, p2), ()
        )
        far, near = everyone[subs // 2 :], everyone[: subs // 2]
        out_far = attention("late_far", False, True, far, late, q, sel, (p3, p4), state)
        out_near = attention("late_near", False, True, near, late, q, sel, (p3, p4), state)
        out = out_near + out_far
    else:
        whole = lax.all_gather(own, "lev", axis=0, tiled=True)
        out = attention(
            "all", True, True, everyone, lambda level: (0,), q, sel, (whole,), ()
        )
    out = exchange(out)
    return unpack_output(subs, out) if subs > 1 else out[0]


def solution(mesh):
    ctx, heads = mesh.shape["ctx"], mesh.shape["head"]
    subs = math.gcd(KVH // heads, ctx)
    if subs * heads != KVH:
        raise ValueError("unsupported mesh")
    levels = ctx // subs
    split = Mesh(mesh.devices.reshape(levels, subs, heads), ("lev", "sub", "head"))
    placed = (
        P(("lev", "sub"), "head"),
        P(("lev", "sub", "head"), None),
        P(("lev", "sub", "head"), None),
        P(("lev", "sub"), "head", None),
    )
    return jax.shard_map(
        functools.partial(body, levels, subs, heads),
        mesh=split,
        in_specs=placed,
        out_specs=P(("lev", "sub"), "head"),
        check_vma=False,
    )
```

time: 88.7 us -> 75.2 us (0.85)
  the two profiles are of different devices: /device:TPU:24 before, /device:TPU:9 now
where the time goes in v2:
time: 75.2 us; the launch traced here: 74.5 us
  starting transfers between devices  25.7 us (34%)
  Pallas kernels  22.3 us (30%)
  waiting for transfers between devices  22.3 us (30%)
  local copies, waits for them, and re-layouts  3.91 us (5%)
    pallas_call x3, Pallas kernels, attention(): pl.pallas_call(kernel, in_specs=[SMEM] + [VMEM] * (n_q + n_src + len(stat...  19.7 us
    ppermute x6, waiting for transfers between devices, exchange(): lax.ppermute(piece, 'sub', [(i, i ^ k) for i in range(subs)])  13 us
    ppermute x1, starting transfers between devices, body(): p4 = lax.ppermute(later, 'lev', [(1, 2)])  5.92 us
    all_to_all x1, waiting for transfers between devices, body(): p1 = lax.all_to_all(p1, ('sub', 'head'), 0, 0, tiled=True)  5.77 us
    ppermute x6, starting transfers between devices, exchange(): lax.ppermute(piece, 'sub', [(i, i ^ k) for i in range(subs)])  4.96 us
    all_to_all x1, starting transfers between devices, body(): own = lax.all_to_all(packed, ('sub', 'head'), 0, 0, tiled=True)  4.39 us
    all_to_all x1, starting transfers between devices, body(): p1 = lax.all_to_all(p1, ('sub', 'head'), 0, 0, tiled=True)  4.28 us
    ppermute x1, starting transfers between devices, body(): p2 = lax.ppermute(own, 'lev', [(1, 3), (0, 1)])  4.06 us
  transfers between devices with their start and end apart: 12, of which 6 were waited for; matrix products, arithmetic and copies ran while one was open for 1% of the time, Pallas kernels for 26%

profile of v2, /device:TPU:9, one launch (start us, length us, event | category | flops | bytes accessed | tf_op | source)
XLA Modules:
  0.0 74.5 jit_solution(7234281739974790941)
XLA Ops:
  0.0 0.9 %copy-done.1 = bf16[128,1024]{1,0:T(8,128)(2,1)S(1)} copy-done((bf16[128,1024]{1,0:T(8,128)(2,1)S(1)}, bf16[128,1024]{1,0:T(8,128)(2,1)}, u32[]{:S(2)}) %copy-start.1) | copy-done | bytes 262168
  1.0 0.9 %copy-done.2 = bf16[128,1024]{1,0:T(8,128)(2,1)S(1)} copy-done((bf16[128,1024]{1,0:T(8,128)(2,1)S(1)}, bf16[128,1024]{1,0:T(8,128)(2,1)}, u32[]{:S(2)}) %copy-start.2) | copy-done | bytes 262168
  1.9 0.9 %pack_kv.1 = bf16[8,2,128,128]{3,2,1,0:T(8,128)(2,1)} custom-call(bf16[128,1024]{1,0:T(8,128)(2,1)S(1)} %copy-done.1, bf16[128,1024]{1,0:T(8,128)(2,1)S(1)} %copy-done.2), custom_call_target="tpu_custom_call" | custom-call | bytes 1048576 | tf_op jit(solution)/shard_map/pack_kv/pallas_call | solution.py:53
  2.8 1.4 %collective-permute-start.3 = (bf16[8,2,128,128]{3,2,1,0:T(8,128)(2,1)}, bf16[8,2,128,128]{3,2,1,0:T(8,128)(2,1)}, u32[]{:S(2)}, u32[]{:S(2)}) collective-permute-start(bf16[8,2,128,128]{3,2,1,0:T(8,128)(2,1)} %pack_kv.1), channel_id=1, source_target_pairs={{0,16},{16,24},{1,17},{17,25},{2,18},{18,26},{3,19},{19,27},{4,20}... | collective-permute-start | bytes 1572872 | tf_op jit(solution)/shard_map/ppermute | solution.py:295
  4.2 4.4 %all-to-all-start = ((bf16[8,2,128,128]{3,2,1,0:T(8,128)(2,1)}), bf16[8,2,128,128]{3,2,1,0:T(8,128)(2,1)S(1)}, u32[]{:S(2)}, u32[]{:S(2)}) async-start(bf16[8,2,128,128]{3,2,1,0:T(8,128)(2,1)} %pack_kv.1), calls=%async_computation | async-start | bytes 1048576 | tf_op jit(solution)/shard_map/all_to_all | solution.py:296
  8.6 0.8 %copy.5.sel_ref = s32[2,4,3]{2,1,0:T(4,128)S(1)} copy(s32[2,4,3]{1,0,2:T(2,128)} %param.7) | data formatting | bytes 192 | tf_op args[3]
  9.4 1.2 %copy-done = bf16[256,2048]{1,0:T(8,128)(2,1)S(1)} copy-done((bf16[256,2048]{1,0:T(8,128)(2,1)S(1)}, bf16[256,2048]{1,0:T(8,128)(2,1)}, u32[]{:S(2)}) %copy-start) | copy-done | bytes 1048600
  10.6 0.7 pack_q.1
  11.3 1.7 %collective-permute-start.2 = (bf16[272,512]{1,0:T(8,128)(2,1)S(1)}, bf16[272,512]{1,0:T(8,128)(2,1)S(1)}, u32[]{:S(2)}, u32[]{:S(2)}) collective-permute-start(bf16[272,512]{1,0:T(8,128)(2,1)S(1)} %get-tuple-element.20), channel_id=1, source_target_pairs={{0,6},{2,4},{4,2},{6,0},{1,7},{3,5},{5,3},{7,1},{8,14},{10,12},{12... | collective-permute-start | bytes 835592 | tf_op jit(solution)/shard_map/ppermute | solution.py:289
  13.0 0.0 collective-permute-start.1
  13.0 0.5 collective-permute-start
  13.5 3.6 %all-to-all-done.refs_5_ = bf16[8,2,128,128]{3,2,1,0:T(8,128)(2,1)S(1)} async-done(((bf16[8,2,128,128]{3,2,1,0:T(8,128)(2,1)}), bf16[8,2,128,128]{3,2,1,0:T(8,128)(2,1)S(1)}, u32[]{:S(2)}, u32[]{:S(2)}) %all-to-all-start) | async-done | bytes 524320 | tf_op jit(solution)/shard_map/all_to_all | solution.py:296
  17.1 0.0 collective-permute-done.3
  17.1 4.3 %all-to-all-start.1 = ((bf16[8,2,128,128]{3,2,1,0:T(8,128)(2,1)}), bf16[8,2,128,128]{3,2,1,0:T(8,128)(2,1)S(1)}, u32[]{:S(2)}, u32[]{:S(2)}) async-start(bf16[8,2,128,128]{3,2,1,0:T(8,128)(2,1)} %collective-permute-done.3), calls=%async_computation.1 | async-start | bytes 1048576 | tf_op jit(solution)/shard_map/all_to_all | solution.py:303
  21.4 1.9 %collective-permute-done.2.refs_4_.refs_2_ = bf16[272,512]{1,0:T(8,128)(2,1)S(1)} collective-permute-done((bf16[272,512]{1,0:T(8,128)(2,1)S(1)}, bf16[272,512]{1,0:T(8,128)(2,1)S(1)}, u32[]{:S(2)}, u32[]{:S(2)}) %collective-permute-start.2) | collective-permute-done | bytes 278560 | tf_op jit(solution)/shard_map/ppermute | solution.py:289
  23.2 4.1 %collective-permute-start.6 = (bf16[8,2,128,128]{3,2,1,0:T(8,128)(2,1)S(1)}, bf16[8,2,128,128]{3,2,1,0:T(8,128)(2,1)S(1)}, u32[]{:S(2)}, u32[]{:S(2)}) collective-permute-start(bf16[8,2,128,128]{3,2,1,0:T(8,128)(2,1)S(1)} %all-to-all-done.refs_5_), channel_id=1, source_target_pairs={{8,24},{0,8},{9,25},{1,9},{10,26},{2,10},{11,27},{3,11},{12,28},{4... | collective-permute-start | bytes 1572872 | tf_op jit(solution)/shard_map/ppermute | solution.py:304
  27.3 1.2 %collective-permute-done.1.refs_3_.refs_1_ = bf16[272,512]{1,0:T(8,128)(2,1)S(1)} collective-permute-done((bf16[272,512]{1,0:T(8,128)(2,1)S(1)}, bf16[272,512]{1,0:T(8,128)(2,1)S(1)}, u32[]{:S(2)}, u32[]{:S(2)}) %collective-permute-start.1) | collective-permute-done | bytes 278560 | tf_op jit(solution)/shard_map/ppermute | solution.py:289
  28.6 5.8 %all-to-all-done.1.refs_6_ = bf16[8,2,128,128]{3,2,1,0:T(8,128)(2,1)S(1)} async-done(((bf16[8,2,128,128]{3,2,1,0:T(8,128)(2,1)}), bf16[8,2,128,128]{3,2,1,0:T(8,128)(2,1)S(1)}, u32[]{:S(2)}, u32[]{:S(2)}) %all-to-all-start.1) | async-done | bytes 524320 | tf_op jit(solution)/shard_map/all_to_all | solution.py:303
  34.3 0.7 collective-permute-start.4
  35.0 5.9 %collective-permute-start.5 = (bf16[8,2,128,128]{3,2,1,0:T(8,128)(2,1)S(1)}, bf16[8,2,128,128]{3,2,1,0:T(8,128)(2,1)S(1)}, u32[]{:S(2)}, u32[]{:S(2)}) collective-permute-start(bf16[8,2,128,128]{3,2,1,0:T(8,128)(2,1)S(1)} %all-to-all-done.refs_5_), channel_id=1, source_target_pairs={{8,16},{9,17},{10,18},{11,19},{12,20},{13,21},{14,22},{15,23}} | collective-permute-start | bytes 1572872 | tf_op jit(solution)/shard_map/ppermute | solution.py:307
  40.9 0.0 collective-permute-done.refs_2_
  41.0 0.1 maximum_convert_fusion.refs_0_
  41.0 17.4 %early.1 = (f32[8,512,128]{2,1,0:T(8,128)S(1)}, f32[8,512,256]{2,1,0:T(8,128)S(1)}) custom-call(s32[24]{0:T(128)S(1)} %maximum_convert_fusion.refs_0_, bf16[272,512]{1,0:T(8,128)(2,1)S(1)} %get-tuple-element.17.refs_1_, bf16[272,512]{1,0:T(8,128)(2,1)S(1)} %collective-permute-done.refs_2_, bf16[272,512]{1,0:T(8,128)(2,1)S(1)} %collective-permute-done.1.refs_3_.refs_1_, ...), custom_call_target="tpu_custom_call" | custom-call | flops 4294967296 | bytes 4194304 | tf_op jit(solution)/shard_map/early/pallas_call | solution.py:259
  58.5 0.0 collective-permute-done.4.refs_3_
  58.5 1.2 %late_far.1 = (bf16[256,512]{1,0:T(8,128)(2,1)S(1)}, bf16[256,512]{1,0:T(8,128)(2,1)S(1)}) custom-call(s32[24]{0:T(128)S(1)} %maximum_convert_fusion.refs_0_, bf16[272,512]{1,0:T(8,128)(2,1)S(1)} %collective-permute-done.1.refs_3_.refs_1_, bf16[272,512]{1,0:T(8,128)(2,1)S(1)} %collective-permute-done.2.refs_4_.refs_2_, ...), custom_call_target="tpu_custom_call" | custom-call | flops 1610612736 | bytes 4194304 | tf_op jit(solution)/shard_map/late_far/pallas_call | solution.py:259
  59.7 0.3 collective-permute-start.8
  60.1 2.3 %collective-permute-start.9 = (bf16[256,512]{1,0:T(8,128)(2,1)S(1)}, bf16[256,512]{1,0:T(8,128)(2,1)S(1)}, u32[]{:S(2)}, u32[]{:S(2)}) collective-permute-start(bf16[256,512]{1,0:T(8,128)(2,1)S(1)} %get-tuple-element.28), channel_id=1, source_target_pairs={{0,6},{2,4},{4,2},{6,0},{1,7},{3,5},{5,3},{7,1},{8,14},{10,12},{12... | collective-permute-start | bytes 786440 | tf_op jit(solution)/shard_map/ppermute | solution.py:289
  62.4 1.1 %late_near.1 = (bf16[256,512]{1,0:T(8,128)(2,1)S(1)}, bf16[256,512]{1,0:T(8,128)(2,1)S(1)}) custom-call(s32[24]{0:T(128)S(1)} %maximum_convert_fusion.refs_0_, bf16[272,512]{1,0:T(8,128)(2,1)S(1)} %get-tuple-element.17.refs_1_, bf16[272,512]{1,0:T(8,128)(2,1)S(1)} %collective-permute-done.refs_2_, ...), custom_call_target="tpu_custom_call" | custom-call | flops 1610612736 | bytes 4194304 | tf_op jit(solution)/shard_map/late_near/pallas_call | solution.py:259
  63.5 0.1 collective-permute-start.7
  63.6 3.1 %collective-permute-done.8.refs_2_ = bf16[256,512]{1,0:T(8,128)(2,1)S(1)} collective-permute-done((bf16[256,512]{1,0:T(8,128)(2,1)S(1)}, bf16[256,512]{1,0:T(8,128)(2,1)S(1)}, u32[]{:S(2)}, u32[]{:S(2)}) %collective-permute-start.8) | collective-permute-done | bytes 262176 | tf_op jit(solution)/shard_map/ppermute | solution.py:289
  66.6 6.8 %collective-permute-done.9.refs_3_ = bf16[256,512]{1,0:T(8,128)(2,1)S(1)} collective-permute-done((bf16[256,512]{1,0:T(8,128)(2,1)S(1)}, bf16[256,512]{1,0:T(8,128)(2,1)S(1)}, u32[]{:S(2)}, u32[]{:S(2)}) %collective-permute-start.9) | collective-permute-done | bytes 262176 | tf_op jit(solution)/shard_map/ppermute | solution.py:289
  73.5 1.1 %unpack.1 = bf16[256,2048]{1,0:T(8,128)(2,1)} custom-call(bf16[256,512]{1,0:T(8,128)(2,1)S(1)} %get-tuple-element.25.refs_0_, bf16[256,512]{1,0:T(8,128)(2,1)S(1)} %collective-permute-done.7.refs_1_, bf16[256,512]{1,0:T(8,128)(2,1)S(1)} %collective-permute-done.8.refs_2_, bf16[256,512]{1,0:T(8,128)(2,1)S(1)} %collective-permute-done.9.refs_3_), custom_call_target="tpu_custom_call" | custom-call | bytes 2097152 | tf_op jit(solution)/shard_map/unpack/pallas_call | solution.py:100
  (10 shorter events, 0.0 us)
Async XLA Ops:
  0.0 0.9 %copy-start.1 = (bf16[128,1024]{1,0:T(8,128)(2,1)S(1)}, bf16[128,1024]{1,0:T(8,128)(2,1)}, u32[]{:S(2)}) copy-start(bf16[128,1024]{1,0:T(8,128)(2,1)} %k_ref.1) | copy-start | bytes 786436
  1.0 0.9 %copy-start.2 = (bf16[128,1024]{1,0:T(8,128)(2,1)S(1)}, bf16[128,1024]{1,0:T(8,128)(2,1)}, u32[]{:S(2)}) copy-start(bf16[128,1024]{1,0:T(8,128)(2,1)} %v_ref.1) | copy-start | bytes 786436
  2.8 14.3 %collective-permute-start.3 = (bf16[8,2,128,128]{3,2,1,0:T(8,128)(2,1)}, bf16[8,2,128,128]{3,2,1,0:T(8,128)(2,1)}, u32[]{:S(2)}, u32[]{:S(2)}) collective-permute-start(bf16[8,2,128,128]{3,2,1,0:T(8,128)(2,1)} %pack_kv.1), channel_id=1, source_target_pairs={{0,16},{16,24},{1,17},{17,25},{2,18},{18,26},{3,19},{19,27},{4,20}... | collective-permute-start | bytes 1572872 | tf_op jit(solution)/shard_map/ppermute | solution.py:295
  4.2 12.8 %all-to-all-start = ((bf16[8,2,128,128]{3,2,1,0:T(8,128)(2,1)}), bf16[8,2,128,128]{3,2,1,0:T(8,128)(2,1)S(1)}, u32[]{:S(2)}, u32[]{:S(2)}) async-start(bf16[8,2,128,128]{3,2,1,0:T(8,128)(2,1)} %pack_kv.1), calls=%async_computation | async-start | bytes 1048576 | tf_op jit(solution)/shard_map/all_to_all | solution.py:296
  9.4 1.2 %copy-start = (bf16[256,2048]{1,0:T(8,128)(2,1)S(1)}, bf16[256,2048]{1,0:T(8,128)(2,1)}, u32[]{:S(2)}) copy-start(bf16[256,2048]{1,0:T(8,128)(2,1)} %q_ref.1) | copy-start | bytes 3145732
  11.3 11.9 %collective-permute-start.2 = (bf16[272,512]{1,0:T(8,128)(2,1)S(1)}, bf16[272,512]{1,0:T(8,128)(2,1)S(1)}, u32[]{:S(2)}, u32[]{:S(2)}) collective-permute-start(bf16[272,512]{1,0:T(8,128)(2,1)S(1)} %get-tuple-element.20), channel_id=1, source_target_pairs={{0,6},{2,4},{4,2},{6,0},{1,7},{3,5},{5,3},{7,1},{8,14},{10,12},{12... | collective-permute-start | bytes 835592 | tf_op jit(solution)/shard_map/ppermute | solution.py:289
  13.0 15.5 %collective-permute-start.1 = (bf16[272,512]{1,0:T(8,128)(2,1)S(1)}, bf16[272,512]{1,0:T(8,128)(2,1)S(1)}, u32[]{:S(2)}, u32[]{:S(2)}) collective-permute-start(bf16[272,512]{1,0:T(8,128)(2,1)S(1)} %get-tuple-element.19), channel_id=1, source_target_pairs={{0,4},{2,6},{4,0},{6,2},{1,5},{3,7},{5,1},{7,3},{8,12},{10,14},{12... | collective-permute-start | bytes 835592 | tf_op jit(solution)/shard_map/ppermute | solution.py:289
  13.0 27.9 %collective-permute-start = (bf16[272,512]{1,0:T(8,128)(2,1)S(1)}, bf16[272,512]{1,0:T(8,128)(2,1)S(1)}, u32[]{:S(2)}, u32[]{:S(2)}) collective-permute-start(bf16[272,512]{1,0:T(8,128)(2,1)S(1)} %get-tuple-element.18), channel_id=1, source_target_pairs={{0,2},{2,0},{4,6},{6,4},{1,3},{3,1},{5,7},{7,5},{8,10},{10,8},{12,... | collective-permute-start | bytes 835592 | tf_op jit(solution)/shard_map/ppermute | solution.py:289
  17.1 17.2 %all-to-all-start.1 = ((bf16[8,2,128,128]{3,2,1,0:T(8,128)(2,1)}), bf16[8,2,128,128]{3,2,1,0:T(8,128)(2,1)S(1)}, u32[]{:S(2)}, u32[]{:S(2)}) async-start(bf16[8,2,128,128]{3,2,1,0:T(8,128)(2,1)} %collective-permute-done.3), calls=%async_computation.1 | async-start | bytes 1048576 | tf_op jit(solution)/shard_map/all_to_all | solution.py:303
  23.2 17.8 %collective-permute-start.6 = (bf16[8,2,128,128]{3,2,1,0:T(8,128)(2,1)S(1)}, bf16[8,2,128,128]{3,2,1,0:T(8,128)(2,1)S(1)}, u32[]{:S(2)}, u32[]{:S(2)}) collective-permute-start(bf16[8,2,128,128]{3,2,1,0:T(8,128)(2,1)S(1)} %all-to-all-done.refs_5_), channel_id=1, source_target_pairs={{8,24},{0,8},{9,25},{1,9},{10,26},{2,10},{11,27},{3,11},{12,28},{4... | collective-permute-start | bytes 1572872 | tf_op jit(solution)/shard_map/ppermute | solution.py:304
  34.3 24.2 %collective-permute-start.4 = (bf16[8,2,128,128]{3,2,1,0:T(8,128)(2,1)S(1)}, bf16[8,2,128,128]{3,2,1,0:T(8,128)(2,1)S(1)}, u32[]{:S(2)}, u32[]{:S(2)}) collective-permute-start(bf16[8,2,128,128]{3,2,1,0:T(8,128)(2,1)S(1)} %all-to-all-done.1.refs_6_), channel_id=1, source_target_pairs={{16,24},{17,25},{18,26},{19,27},{20,28},{21,29},{22,30},{23,31}} | collective-permute-start | bytes 1572872 | tf_op jit(solution)/shard_map/ppermute | solution.py:306
  35.0 23.5 %collective-permute-start.5 = (bf16[8,2,128,128]{3,2,1,0:T(8,128)(2,1)S(1)}, bf16[8,2,128,128]{3,2,1,0:T(8,128)(2,1)S(1)}, u32[]{:S(2)}, u32[]{:S(2)}) collective-permute-start(bf16[8,2,128,128]{3,2,1,0:T(8,128)(2,1)S(1)} %all-to-all-done.refs_5_), channel_id=1, source_target_pairs={{8,16},{9,17},{10,18},{11,19},{12,20},{13,21},{14,22},{15,23}} | collective-permute-start | bytes 1572872 | tf_op jit(solution)/shard_map/ppermute | solution.py:307
  59.7 6.9 %collective-permute-start.8 = (bf16[256,512]{1,0:T(8,128)(2,1)S(1)}, bf16[256,512]{1,0:T(8,128)(2,1)S(1)}, u32[]{:S(2)}, u32[]{:S(2)}) collective-permute-start(bf16[256,512]{1,0:T(8,128)(2,1)S(1)} %get-tuple-element.27), channel_id=1, source_target_pairs={{0,4},{2,6},{4,0},{6,2},{1,5},{3,7},{5,1},{7,3},{8,12},{10,14},{12... | collective-permute-start | bytes 786440 | tf_op jit(solution)/shard_map/ppermute | solution.py:289
  60.1 13.4 %collective-permute-start.9 = (bf16[256,512]{1,0:T(8,128)(2,1)S(1)}, bf16[256,512]{1,0:T(8,128)(2,1)S(1)}, u32[]{:S(2)}, u32[]{:S(2)}) collective-permute-start(bf16[256,512]{1,0:T(8,128)(2,1)S(1)} %get-tuple-element.28), channel_id=1, source_target_pairs={{0,6},{2,4},{4,2},{6,0},{1,7},{3,5},{5,3},{7,1},{8,14},{10,12},{12... | collective-permute-start | bytes 786440 | tf_op jit(solution)/shard_map/ppermute | solution.py:289
  63.5 10.0 %collective-permute-start.7 = (bf16[256,512]{1,0:T(8,128)(2,1)S(1)}, bf16[256,512]{1,0:T(8,128)(2,1)S(1)}, u32[]{:S(2)}, u32[]{:S(2)}) collective-permute-start(bf16[256,512]{1,0:T(8,128)(2,1)S(1)} %get-tuple-element.26), channel_id=1, source_target_pairs={{0,2},{2,0},{4,6},{6,4},{1,3},{3,1},{5,7},{7,5},{8,10},{10,8},{12,... | collective-permute-start | bytes 786440 | tf_op jit(solution)/shard_map/ppermute | solution.py:289

commit v3 on v2

--- a/solution.py
+++ b/solution.py
@@ -25,6 +25,7 @@
 BF16 = jnp.bfloat16
 VMEM = pl.BlockSpec(memory_space=pltpu.VMEM)
 SMEM = pl.BlockSpec(memory_space=pltpu.SMEM)
+HBM = pl.BlockSpec(memory_space=pltpu.HBM)
 MIB = 1024 * 1024
 
 
@@ -43,20 +44,30 @@
 def pack_keys_values(subs, heads, keys, values):
     r = keys.shape[0]
 
-    def kernel(k_ref, v_ref, out_ref):
+    def kernel(k_ref, v_ref, out_ref, sems):
+        copies = []
         for sub in range(subs):
             for head in range(heads):
-                at = (head * subs + sub) * HD
-                out_ref[sub * heads + head, 0] = k_ref[:, at : at + HD]
-                out_ref[sub * heads + head, 1] = v_ref[:, at : at + HD]
+                at = pl.ds((head * subs + sub) * HD, HD)
+                chunk = sub * heads + head
+                for i, ref in enumerate((k_ref, v_ref)):
+                    copies.append(
+                        pltpu.make_async_copy(
+                            ref.at[:, at], out_ref.at[chunk, i], sems.at[2 * chunk + i]
+                        )
+                    )
+        for copy in copies:
+            copy.start()
+        for copy in copies:
+            copy.wait()
 
     return pl.pallas_call(
         kernel,
-        in_specs=[VMEM, VMEM],
-        out_specs=VMEM,
+        in_specs=[HBM, HBM],
+        out_specs=HBM,
         out_shape=jax.ShapeDtypeStruct((subs * heads, 2, r, HD), BF16),
+        scratch_shapes=[pltpu.SemaphoreType.DMA((2 * subs * heads,))],
         cost_estimate=copy_cost(4 * keys.size * 2),
-        compiler_params=pltpu.CompilerParams(vmem_limit_bytes=8 * MIB),
         name="pack_kv",
     )(keys, values)
 
@@ -292,7 +303,7 @@
 
     packed = pack_keys_values(subs, heads, keys, values)
     if by_levels:
-        p1 = lax.ppermute(packed, "lev", [(0, 2), (2, 3)])
+        raw = lax.ppermute(packed, "lev", [(1, 3), (0, 1)])
     own = lax.all_to_all(packed, ("sub", "head"), 0, 0, tiled=True)
     q = pack_queries(subs, queries, selected)
     q = exchange(q)
@@ -300,11 +311,12 @@
 
     everyone = tuple(range(subs))
     if by_levels:
-        p1 = lax.all_to_all(p1, ("sub", "head"), 0, 0, tiled=True)
-        p2 = lax.ppermute(own, "lev", [(1, 3), (0, 1)])
-        later, p1 = lax.optimization_barrier((own, p1))
-        p3 = lax.ppermute(p1, "lev", [(2, 3)])
-        p4 = lax.ppermute(later, "lev", [(1, 2)])
+        own, raw = lax.optimization_barrier((own, raw))
+        pa = lax.ppermute(own, "lev", [(0, 2), (2, 3)])
+        p2 = lax.all_to_all(raw, ("sub", "head"), 0, 0, tiled=True)
+        pf = lax.ppermute(pa, "lev", [(2, 3)])
+        later, pa = lax.optimization_barrier((own, pa))
+        po = lax.ppermute(later, "lev", [(1, 2)])
 
         def at(level, *which):
             base = jnp.int32(NONE)
@@ -319,11 +331,11 @@
             return (at(level, (3, 0)), at(level, (2, 1)))
 
         state = attention(
-            "early", True, False, everyone, early, q, sel, (own, p1, p2), ()
+            "early", True, False, everyone, early, q, sel, (own, pa, p2), ()
         )
         far, near = everyone[subs // 2 :], everyone[: subs // 2]
-        out_far = attention("late_far", False, True, far, late, q, sel, (p3, p4), state)
-        out_near = attention("late_near", False, True, near, late, q, sel, (p3, p4), state)
+        out_far = attention("late_far", False, True, far, late, q, sel, (pf, po), state)
+        out_near = attention("late_near", False, True, near, late, q, sel, (pf, po), state)
         out = out_near + out_far
     else:
         whole = lax.all_gather(own, "lev", axis=0, tiled=True)

time: 75.2 us -> 86.5 us (1.15)
  the two profiles are of different devices: /device:TPU:9 before, /device:TPU:23 now
where the time goes in v3:
time: 86.5 us; the launch traced here: 85.6 us
  Pallas kernels  42.4 us (49%)
  starting transfers between devices  28.8 us (33%)
  waiting for transfers between devices  12 us (14%)
  local copies, waits for them, and re-layouts  2.01 us (2%)
    pallas_call x3, Pallas kernels, attention(): pl.pallas_call(kernel, in_specs=[SMEM] + [VMEM] * (n_q + n_src + len(stat...  23.6 us
    pallas_call x1, Pallas kernels, pack_keys_values(): pl.pallas_call(kernel, in_specs=[HBM, HBM], out_specs=HBM, out_shape=jax....  17.1 us
    ppermute x1, starting transfers between devices, body(): pa = lax.ppermute(own, 'lev', [(0, 2), (2, 3)])  6.66 us
    ppermute x6, starting transfers between devices, exchange(): lax.ppermute(piece, 'sub', [(i, i ^ k) for i in range(subs)])  6.35 us
    ppermute x6, waiting for transfers between devices, exchange(): lax.ppermute(piece, 'sub', [(i, i ^ k) for i in range(subs)])  5.92 us
    all_to_all x1, starting transfers between devices, body(): p2 = lax.all_to_all(raw, ('sub', 'head'), 0, 0, tiled=True)  5.68 us
    all_to_all x1, starting transfers between devices, body(): own = lax.all_to_all(packed, ('sub', 'head'), 0, 0, tiled=True)  4.52 us
    ppermute x1, waiting for transfers between devices, body(): pa = lax.ppermute(own, 'lev', [(0, 2), (2, 3)])  3.92 us
  transfers between devices with their start and end apart: 12, of which 3 were waited for; matrix products, arithmetic and copies ran while one was open for 1% of the time, Pallas kernels for 23%

profile of v3, /device:TPU:23, one launch (start us, length us, event | category | flops | bytes accessed | tf_op | source)
XLA Modules:
  0.0 85.6 jit_solution(17644651877509417414)
XLA Ops:
  0.0 17.1 %pack_kv.1 = bf16[8,2,128,128]{3,2,1,0:T(8,128)(2,1)} custom-call(bf16[128,1024]{1,0:T(8,128)(2,1)} %k_ref.1, bf16[128,1024]{1,0:T(8,128)(2,1)} %v_ref.1), custom_call_target="tpu_custom_call" | custom-call | bytes 1048576 | tf_op jit(solution)/shard_map/pack_kv/pallas_call | solution.py:64
  17.1 0.7 collective-permute-start.3
  17.8 4.5 %all-to-all-start = ((bf16[8,2,128,128]{3,2,1,0:T(8,128)(2,1)}), bf16[8,2,128,128]{3,2,1,0:T(8,128)(2,1)S(1)}, u32[]{:S(2)}, u32[]{:S(2)}) async-start(bf16[8,2,128,128]{3,2,1,0:T(8,128)(2,1)} %pack_kv.1), calls=%async_computation | async-start | bytes 1048576 | tf_op jit(solution)/shard_map/all_to_all | solution.py:307
  22.4 0.8 copy.5.sel_ref
  23.1 1.2 %copy-done = bf16[256,2048]{1,0:T(8,128)(2,1)S(1)} copy-done((bf16[256,2048]{1,0:T(8,128)(2,1)S(1)}, bf16[256,2048]{1,0:T(8,128)(2,1)}, u32[]{:S(2)}) %copy-start) | copy-done | bytes 1048600
  24.4 0.7 pack_q.1
  25.1 0.6 collective-permute-start.2
  25.6 1.2 %collective-permute-start.1 = (bf16[272,512]{1,0:T(8,128)(2,1)S(1)}, bf16[272,512]{1,0:T(8,128)(2,1)S(1)}, u32[]{:S(2)}, u32[]{:S(2)}) collective-permute-start(bf16[272,512]{1,0:T(8,128)(2,1)S(1)} %get-tuple-element.21), channel_id=1, source_target_pairs={{0,4},{2,6},{4,0},{6,2},{1,5},{3,7},{5,1},{7,3},{8,12},{10,14},{12... | collective-permute-start | bytes 835592 | tf_op jit(solution)/shard_map/ppermute | solution.py:300
  26.8 0.4 collective-permute-start
  27.3 2.2 %all-to-all-done.refs_5_ = bf16[8,2,128,128]{3,2,1,0:T(8,128)(2,1)S(1)} async-done(((bf16[8,2,128,128]{3,2,1,0:T(8,128)(2,1)}), bf16[8,2,128,128]{3,2,1,0:T(8,128)(2,1)S(1)}, u32[]{:S(2)}, u32[]{:S(2)}) %all-to-all-start) | async-done | bytes 524320 | tf_op jit(solution)/shard_map/all_to_all | solution.py:307
  29.5 0.0 collective-permute-done.3
  29.5 6.7 %collective-permute-start.4 = (bf16[8,2,128,128]{3,2,1,0:T(8,128)(2,1)S(1)}, bf16[8,2,128,128]{3,2,1,0:T(8,128)(2,1)}, u32[]{:S(2)}, u32[]{:S(2)}) collective-permute-start(bf16[8,2,128,128]{3,2,1,0:T(8,128)(2,1)S(1)} %all-to-all-done.refs_5_), channel_id=1, source_target_pairs={{0,16},{16,24},{1,17},{17,25},{2,18},{18,26},{3,19},{19,27},{4,20}... | collective-permute-start | bytes 1572872 | tf_op jit(solution)/shard_map/ppermute | solution.py:315
  36.1 0.0 collective-permute-done.2.refs_4_.refs_2_
  36.2 5.7 %all-to-all-start.1 = ((bf16[8,2,128,128]{3,2,1,0:T(8,128)(2,1)}), bf16[8,2,128,128]{3,2,1,0:T(8,128)(2,1)S(1)}, u32[]{:S(2)}, u32[]{:S(2)}) async-start(bf16[8,2,128,128]{3,2,1,0:T(8,128)(2,1)} %copy-done.1), calls=%async_computation.1 | async-start | bytes 1048576 | tf_op jit(solution)/shard_map/all_to_all | solution.py:316
  41.9 0.0 collective-permute-done.1.refs_3_.refs_1_
  41.9 3.9 %collective-permute-done.4.refs_6_ = bf16[8,2,128,128]{3,2,1,0:T(8,128)(2,1)} collective-permute-done((bf16[8,2,128,128]{3,2,1,0:T(8,128)(2,1)S(1)}, bf16[8,2,128,128]{3,2,1,0:T(8,128)(2,1)}, u32[]{:S(2)}, u32[]{:S(2)}) %collective-permute-start.4) | collective-permute-done | bytes 524320 | tf_op jit(solution)/shard_map/ppermute | solution.py:315
  45.8 1.3 %collective-permute-start.6 = (bf16[8,2,128,128]{3,2,1,0:T(8,128)(2,1)S(1)}, bf16[8,2,128,128]{3,2,1,0:T(8,128)(2,1)S(1)}, u32[]{:S(2)}, u32[]{:S(2)}) collective-permute-start(bf16[8,2,128,128]{3,2,1,0:T(8,128)(2,1)S(1)} %all-to-all-done.refs_5_), channel_id=1, source_target_pairs={{8,16},{9,17},{10,18},{11,19},{12,20},{13,21},{14,22},{15,23}} | collective-permute-start | bytes 1572872 | tf_op jit(solution)/shard_map/ppermute | solution.py:319
  47.1 3.6 %collective-permute-start.5 = (bf16[8,2,128,128]{3,2,1,0:T(8,128)(2,1)}, bf16[8,2,128,128]{3,2,1,0:T(8,128)(2,1)S(1)}, u32[]{:S(2)}, u32[]{:S(2)}) collective-permute-start(bf16[8,2,128,128]{3,2,1,0:T(8,128)(2,1)} %collective-permute-done.4.refs_6_), channel_id=1, source_target_pairs={{16,24},{17,25},{18,26},{19,27},{20,28},{21,29},{22,30},{23,31}} | collective-permute-start | bytes 1572872 | tf_op jit(solution)/shard_map/ppermute | solution.py:317
  50.7 0.0 collective-permute-done.refs_2_
  50.7 0.1 maximum_convert_fusion.refs_0_
  50.8 0.0 all-to-all-done.1.refs_7_
  50.8 15.7 %early.1 = (f32[8,512,128]{2,1,0:T(8,128)S(1)}, f32[8,512,256]{2,1,0:T(8,128)S(1)}) custom-call(s32[24]{0:T(128)S(1)} %maximum_convert_fusion.refs_0_, bf16[272,512]{1,0:T(8,128)(2,1)S(1)} %get-tuple-element.19.refs_1_, bf16[272,512]{1,0:T(8,128)(2,1)S(1)} %collective-permute-done.refs_2_, bf16[272,512]{1,0:T(8,128)(2,1)S(1)} %collective-permute-done.1.refs_3_.refs_1_, ...), custom_call_target="tpu_custom_call" | custom-call | flops 4294967296 | bytes 4194304 | tf_op jit(solution)/shard_map/early/pallas_call | solution.py:270
  66.5 0.0 collective-permute-done.6.refs_4_
  66.5 4.2 %late_far.1 = (bf16[256,512]{1,0:T(8,128)(2,1)S(1)}, bf16[256,512]{1,0:T(8,128)(2,1)S(1)}) custom-call(s32[24]{0:T(128)S(1)} %maximum_convert_fusion.refs_0_, bf16[272,512]{1,0:T(8,128)(2,1)S(1)} %collective-permute-done.1.refs_3_.refs_1_, bf16[272,512]{1,0:T(8,128)(2,1)S(1)} %collective-permute-done.2.refs_4_.refs_2_, ...), custom_call_target="tpu_custom_call" | custom-call | flops 1610612736 | bytes 4194304 | tf_op jit(solution)/shard_map/late_far/pallas_call | solution.py:270
  70.8 0.1 collective-permute-start.8
  70.8 4.0 %collective-permute-start.9 = (bf16[256,512]{1,0:T(8,128)(2,1)S(1)}, bf16[256,512]{1,0:T(8,128)(2,1)S(1)}, u32[]{:S(2)}, u32[]{:S(2)}) collective-permute-start(bf16[256,512]{1,0:T(8,128)(2,1)S(1)} %get-tuple-element.32), channel_id=1, source_target_pairs={{0,6},{2,4},{4,2},{6,0},{1,7},{3,5},{5,3},{7,1},{8,14},{10,12},{12... | collective-permute-start | bytes 786440 | tf_op jit(solution)/shard_map/ppermute | solution.py:300
  74.8 3.7 %late_near.1 = (bf16[256,512]{1,0:T(8,128)(2,1)S(1)}, bf16[256,512]{1,0:T(8,128)(2,1)S(1)}) custom-call(s32[24]{0:T(128)S(1)} %maximum_convert_fusion.refs_0_, bf16[272,512]{1,0:T(8,128)(2,1)S(1)} %get-tuple-element.19.refs_1_, bf16[272,512]{1,0:T(8,128)(2,1)S(1)} %collective-permute-done.refs_2_, ...), custom_call_target="tpu_custom_call" | custom-call | flops 1610612736 | bytes 4194304 | tf_op jit(solution)/shard_map/late_near/pallas_call | solution.py:270
  78.5 0.1 collective-permute-start.7
  78.6 0.0 collective-permute-done.8.refs_2_
  78.6 5.9 %collective-permute-done.9.refs_3_ = bf16[256,512]{1,0:T(8,128)(2,1)S(1)} collective-permute-done((bf16[256,512]{1,0:T(8,128)(2,1)S(1)}, bf16[256,512]{1,0:T(8,128)(2,1)S(1)}, u32[]{:S(2)}, u32[]{:S(2)}) %collective-permute-start.9) | collective-permute-done | bytes 262176 | tf_op jit(solution)/shard_map/ppermute | solution.py:300
  84.5 0.0 collective-permute-done.7.refs_1_
  84.5 1.1 %unpack.1 = bf16[256,2048]{1,0:T(8,128)(2,1)} custom-call(bf16[256,512]{1,0:T(8,128)(2,1)S(1)} %get-tuple-element.29.refs_0_, bf16[256,512]{1,0:T(8,128)(2,1)S(1)} %collective-permute-done.7.refs_1_, bf16[256,512]{1,0:T(8,128)(2,1)S(1)} %collective-permute-done.8.refs_2_, bf16[256,512]{1,0:T(8,128)(2,1)S(1)} %collective-permute-done.9.refs_3_), custom_call_target="tpu_custom_call" | custom-call | bytes 2097152 | tf_op jit(solution)/shard_map/unpack/pallas_call | solution.py:111
  (8 shorter events, 0.0 us)
Async XLA Ops:
  17.1 12.3 %collective-permute-start.3 = (bf16[8,2,128,128]{3,2,1,0:T(8,128)(2,1)}, bf16[8,2,128,128]{3,2,1,0:T(8,128)(2,1)S(1)}, u32[]{:S(2)}, u32[]{:S(2)}) collective-permute-start(bf16[8,2,128,128]{3,2,1,0:T(8,128)(2,1)} %pack_kv.1), channel_id=1, source_target_pairs={{8,24},{0,8},{9,25},{1,9},{10,26},{2,10},{11,27},{3,11},{12,28},{4... | collective-permute-start | bytes 1572872 | tf_op jit(solution)/shard_map/ppermute | solution.py:306
  17.8 11.6 %all-to-all-start = ((bf16[8,2,128,128]{3,2,1,0:T(8,128)(2,1)}), bf16[8,2,128,128]{3,2,1,0:T(8,128)(2,1)S(1)}, u32[]{:S(2)}, u32[]{:S(2)}) async-start(bf16[8,2,128,128]{3,2,1,0:T(8,128)(2,1)} %pack_kv.1), calls=%async_computation | async-start | bytes 1048576 | tf_op jit(solution)/shard_map/all_to_all | solution.py:307
  23.1 1.2 %copy-start = (bf16[256,2048]{1,0:T(8,128)(2,1)S(1)}, bf16[256,2048]{1,0:T(8,128)(2,1)}, u32[]{:S(2)}) copy-start(bf16[256,2048]{1,0:T(8,128)(2,1)} %q_ref.1) | copy-start | bytes 3145732
  25.1 11.1 %collective-permute-start.2 = (bf16[272,512]{1,0:T(8,128)(2,1)S(1)}, bf16[272,512]{1,0:T(8,128)(2,1)S(1)}, u32[]{:S(2)}, u32[]{:S(2)}) collective-permute-start(bf16[272,512]{1,0:T(8,128)(2,1)S(1)} %get-tuple-element.22), channel_id=1, source_target_pairs={{0,6},{2,4},{4,2},{6,0},{1,7},{3,5},{5,3},{7,1},{8,14},{10,12},{12... | collective-permute-start | bytes 835592 | tf_op jit(solution)/shard_map/ppermute | solution.py:300
  25.6 16.2 %collective-permute-start.1 = (bf16[272,512]{1,0:T(8,128)(2,1)S(1)}, bf16[272,512]{1,0:T(8,128)(2,1)S(1)}, u32[]{:S(2)}, u32[]{:S(2)}) collective-permute-start(bf16[272,512]{1,0:T(8,128)(2,1)S(1)} %get-tuple-element.21), channel_id=1, source_target_pairs={{0,4},{2,6},{4,0},{6,2},{1,5},{3,7},{5,1},{7,3},{8,12},{10,14},{12... | collective-permute-start | bytes 835592 | tf_op jit(solution)/shard_map/ppermute | solution.py:300
  26.8 23.9 %collective-permute-start = (bf16[272,512]{1,0:T(8,128)(2,1)S(1)}, bf16[272,512]{1,0:T(8,128)(2,1)S(1)}, u32[]{:S(2)}, u32[]{:S(2)}) collective-permute-start(bf16[272,512]{1,0:T(8,128)(2,1)S(1)} %get-tuple-element.20), channel_id=1, source_target_pairs={{0,2},{2,0},{4,6},{6,4},{1,3},{3,1},{5,7},{7,5},{8,10},{10,8},{12,... | collective-permute-start | bytes 835592 | tf_op jit(solution)/shard_map/ppermute | solution.py:300
  29.5 6.7 %copy-start.1 = (bf16[8,2,128,128]{3,2,1,0:T(8,128)(2,1)}, bf16[8,2,128,128]{3,2,1,0:T(8,128)(2,1)S(1)}, u32[]{:S(2)}) copy-start(bf16[8,2,128,128]{3,2,1,0:T(8,128)(2,1)S(1)} %collective-permute-done.3) | copy-start | bytes 1572868
  29.5 16.3 %collective-permute-start.4 = (bf16[8,2,128,128]{3,2,1,0:T(8,128)(2,1)S(1)}, bf16[8,2,128,128]{3,2,1,0:T(8,128)(2,1)}, u32[]{:S(2)}, u32[]{:S(2)}) collective-permute-start(bf16[8,2,128,128]{3,2,1,0:T(8,128)(2,1)S(1)} %all-to-all-done.refs_5_), channel_id=1, source_target_pairs={{0,16},{16,24},{1,17},{17,25},{2,18},{18,26},{3,19},{19,27},{4,20}... | collective-permute-start | bytes 1572872 | tf_op jit(solution)/shard_map/ppermute | solution.py:315
  36.2 14.7 %all-to-all-start.1 = ((bf16[8,2,128,128]{3,2,1,0:T(8,128)(2,1)}), bf16[8,2,128,128]{3,2,1,0:T(8,128)(2,1)S(1)}, u32[]{:S(2)}, u32[]{:S(2)}) async-start(bf16[8,2,128,128]{3,2,1,0:T(8,128)(2,1)} %copy-done.1), calls=%async_computation.1 | async-start | bytes 1048576 | tf_op jit(solution)/shard_map/all_to_all | solution.py:316
  45.8 20.7 %collective-permute-start.6 = (bf16[8,2,128,128]{3,2,1,0:T(8,128)(2,1)S(1)}, bf16[8,2,128,128]{3,2,1,0:T(8,128)(2,1)S(1)}, u32[]{:S(2)}, u32[]{:S(2)}) collective-permute-start(bf16[8,2,128,128]{3,2,1,0:T(8,128)(2,1)S(1)} %all-to-all-done.refs_5_), channel_id=1, source_target_pairs={{8,16},{9,17},{10,18},{11,19},{12,20},{13,21},{14,22},{15,23}} | collective-permute-start | bytes 1572872 | tf_op jit(solution)/shard_map/ppermute | solution.py:319
  47.1 19.5 %collective-permute-start.5 = (bf16[8,2,128,128]{3,2,1,0:T(8,128)(2,1)}, bf16[8,2,128,128]{3,2,1,0:T(8,128)(2,1)S(1)}, u32[]{:S(2)}, u32[]{:S(2)}) collective-permute-start(bf16[8,2,128,128]{3,2,1,0:T(8,128)(2,1)} %collective-permute-done.4.refs_6_), channel_id=1, source_target_pairs={{16,24},{17,25},{18,26},{19,27},{20,28},{21,29},{22,30},{23,31}} | collective-permute-start | bytes 1572872 | tf_op jit(solution)/shard_map/ppermute | solution.py:317
  70.8 7.8 %collective-permute-start.8 = (bf16[256,512]{1,0:T(8,128)(2,1)S(1)}, bf16[256,512]{1,0:T(8,128)(2,1)S(1)}, u32[]{:S(2)}, u32[]{:S(2)}) collective-permute-start(bf16[256,512]{1,0:T(8,128)(2,1)S(1)} %get-tuple-element.31), channel_id=1, source_target_pairs={{0,4},{2,6},{4,0},{6,2},{1,5},{3,7},{5,1},{7,3},{8,12},{10,14},{12... | collective-permute-start | bytes 786440 | tf_op jit(solution)/shard_map/ppermute | solution.py:300
  70.8 13.7 %collective-permute-start.9 = (bf16[256,512]{1,0:T(8,128)(2,1)S(1)}, bf16[256,512]{1,0:T(8,128)(2,1)S(1)}, u32[]{:S(2)}, u32[]{:S(2)}) collective-permute-start(bf16[256,512]{1,0:T(8,128)(2,1)S(1)} %get-tuple-element.32), channel_id=1, source_target_pairs={{0,6},{2,4},{4,2},{6,0},{1,7},{3,5},{5,3},{7,1},{8,14},{10,12},{12... | collective-permute-start | bytes 786440 | tf_op jit(solution)/shard_map/ppermute | solution.py:300
  78.5 6.0 %collective-permute-start.7 = (bf16[256,512]{1,0:T(8,128)(2,1)S(1)}, bf16[256,512]{1,0:T(8,128)(2,1)S(1)}, u32[]{:S(2)}, u32[]{:S(2)}) collective-permute-start(bf16[256,512]{1,0:T(8,128)(2,1)S(1)} %get-tuple-element.30), channel_id=1, source_target_pairs={{0,2},{2,0},{4,6},{6,4},{1,3},{3,1},{5,7},{7,5},{8,10},{10,8},{12,... | collective-permute-start | bytes 786440 | tf_op jit(solution)/shard_map/ppermute | solution.py:300

commit v4 on v2

--- a/solution.py
+++ b/solution.py
@@ -56,7 +56,6 @@
         out_specs=VMEM,
         out_shape=jax.ShapeDtypeStruct((subs * heads, 2, r, HD), BF16),
         cost_estimate=copy_cost(4 * keys.size * 2),
-        compiler_params=pltpu.CompilerParams(vmem_limit_bytes=8 * MIB),
         name="pack_kv",
     )(keys, values)
 
@@ -292,7 +291,7 @@
 
     packed = pack_keys_values(subs, heads, keys, values)
     if by_levels:
-        p1 = lax.ppermute(packed, "lev", [(0, 2), (2, 3)])
+        raw = lax.ppermute(packed, "lev", [(1, 3), (0, 1)])
     own = lax.all_to_all(packed, ("sub", "head"), 0, 0, tiled=True)
     q = pack_queries(subs, queries, selected)
     q = exchange(q)
@@ -300,11 +299,12 @@
 
     everyone = tuple(range(subs))
     if by_levels:
-        p1 = lax.all_to_all(p1, ("sub", "head"), 0, 0, tiled=True)
-        p2 = lax.ppermute(own, "lev", [(1, 3), (0, 1)])
-        later, p1 = lax.optimization_barrier((own, p1))
-        p3 = lax.ppermute(p1, "lev", [(2, 3)])
-        p4 = lax.ppermute(later, "lev", [(1, 2)])
+        own, raw = lax.optimization_barrier((own, raw))
+        pa = lax.ppermute(own, "lev", [(0, 2), (2, 3)])
+        p2 = lax.all_to_all(raw, ("sub", "head"), 0, 0, tiled=True)
+        pf = lax.ppermute(pa, "lev", [(2, 3)])
+        later, pa = lax.optimization_barrier((own, pa))
+        po = lax.ppermute(later, "lev", [(1, 2)])
 
         def at(level, *which):
             base = jnp.int32(NONE)
@@ -319,11 +319,11 @@
             return (at(level, (3, 0)), at(level, (2, 1)))
 
         state = attention(
-            "early", True, False, everyone, early, q, sel, (own, p1, p2), ()
+            "early", True, False, everyone, early, q, sel, (own, pa, p2), ()
         )
         far, near = everyone[subs // 2 :], everyone[: subs // 2]
-        out_far = attention("late_far", False, True, far, late, q, sel, (p3, p4), state)
-        out_near = attention("late_near", False, True, near, late, q, sel, (p3, p4), state)
+        out_far = attention("late_far", False, True, far, late, q, sel, (pf, po), state)
+        out_near = attention("late_near", False, True, near, late, q, sel, (pf, po), state)
         out = out_near + out_far
     else:
         whole = lax.all_gather(own, "lev", axis=0, tiled=True)

time: 75.2 us -> 71.2 us (0.947)
  the two profiles are of different devices: /device:TPU:9 before, /device:TPU:23 now
where the time goes in v4:
time: 71.2 us; the launch traced here: 70 us
  starting transfers between devices  28.8 us (40%)
  Pallas kernels  27.2 us (38%)
  waiting for transfers between devices  11.7 us (16%)
  local copies, waits for them, and re-layouts  2.01 us (3%)
    pallas_call x3, Pallas kernels, attention(): pl.pallas_call(kernel, in_specs=[SMEM] + [VMEM] * (n_q + n_src + len(stat...  23.5 us
    ppermute x1, starting transfers between devices, body(): pa = lax.ppermute(own, 'lev', [(0, 2), (2, 3)])  6.66 us
    ppermute x6, starting transfers between devices, exchange(): lax.ppermute(piece, 'sub', [(i, i ^ k) for i in range(subs)])  6.38 us
    all_to_all x1, starting transfers between devices, body(): p2 = lax.all_to_all(raw, ('sub', 'head'), 0, 0, tiled=True)  5.68 us
    ppermute x6, waiting for transfers between devices, exchange(): lax.ppermute(piece, 'sub', [(i, i ^ k) for i in range(subs)])  5.57 us
    all_to_all x1, starting transfers between devices, body(): own = lax.all_to_all(packed, ('sub', 'head'), 0, 0, tiled=True)  4.52 us
    ppermute x1, waiting for transfers between devices, body(): pa = lax.ppermute(own, 'lev', [(0, 2), (2, 3)])  3.92 us
    ppermute x1, starting transfers between devices, body(): pf = lax.ppermute(pa, 'lev', [(2, 3)])  3.64 us
  transfers between devices with their start and end apart: 12, of which 3 were waited for; matrix products, arithmetic and copies ran while one was open for 1% of the time, Pallas kernels for 28%

profile of v4, /device:TPU:23, one launch (start us, length us, event | category | flops | bytes accessed | tf_op | source)
XLA Modules:
  0.0 70.0 jit_solution(14049469028320860558)
XLA Ops:
  0.0 1.9 %pack_kv.1 = bf16[8,2,128,128]{3,2,1,0:T(8,128)(2,1)} custom-call(bf16[128,1024]{1,0:T(8,128)(2,1)} %k_ref.1, bf16[128,1024]{1,0:T(8,128)(2,1)} %v_ref.1), custom_call_target="tpu_custom_call" | custom-call | bytes 1048576 | tf_op jit(solution)/shard_map/pack_kv/pallas_call | solution.py:53
  1.9 0.7 collective-permute-start.3
  2.6 4.5 %all-to-all-start = ((bf16[8,2,128,128]{3,2,1,0:T(8,128)(2,1)}), bf16[8,2,128,128]{3,2,1,0:T(8,128)(2,1)S(1)}, u32[]{:S(2)}, u32[]{:S(2)}) async-start(bf16[8,2,128,128]{3,2,1,0:T(8,128)(2,1)} %pack_kv.1), calls=%async_computation | async-start | bytes 1048576 | tf_op jit(solution)/shard_map/all_to_all | solution.py:295
  7.1 0.8 %copy.5.sel_ref = s32[2,4,3]{2,1,0:T(4,128)S(1)} copy(s32[2,4,3]{1,0,2:T(2,128)} %param.7) | data formatting | bytes 192 | tf_op args[3]
  7.9 1.2 %copy-done = bf16[256,2048]{1,0:T(8,128)(2,1)S(1)} copy-done((bf16[256,2048]{1,0:T(8,128)(2,1)S(1)}, bf16[256,2048]{1,0:T(8,128)(2,1)}, u32[]{:S(2)}) %copy-start) | copy-done | bytes 1048600
  9.1 0.7 pack_q.1
  9.8 0.6 collective-permute-start.2
  10.4 1.2 %collective-permute-start.1 = (bf16[272,512]{1,0:T(8,128)(2,1)S(1)}, bf16[272,512]{1,0:T(8,128)(2,1)S(1)}, u32[]{:S(2)}, u32[]{:S(2)}) collective-permute-start(bf16[272,512]{1,0:T(8,128)(2,1)S(1)} %get-tuple-element.21), channel_id=1, source_target_pairs={{0,4},{2,6},{4,0},{6,2},{1,5},{3,7},{5,1},{7,3},{8,12},{10,14},{12... | collective-permute-start | bytes 835592 | tf_op jit(solution)/shard_map/ppermute | solution.py:288
  11.6 0.4 collective-permute-start
  12.0 2.2 %all-to-all-done.refs_5_ = bf16[8,2,128,128]{3,2,1,0:T(8,128)(2,1)S(1)} async-done(((bf16[8,2,128,128]{3,2,1,0:T(8,128)(2,1)}), bf16[8,2,128,128]{3,2,1,0:T(8,128)(2,1)S(1)}, u32[]{:S(2)}, u32[]{:S(2)}) %all-to-all-start) | async-done | bytes 524320 | tf_op jit(solution)/shard_map/all_to_all | solution.py:295
  14.2 0.0 collective-permute-done.3
  14.2 6.7 %collective-permute-start.4 = (bf16[8,2,128,128]{3,2,1,0:T(8,128)(2,1)S(1)}, bf16[8,2,128,128]{3,2,1,0:T(8,128)(2,1)}, u32[]{:S(2)}, u32[]{:S(2)}) collective-permute-start(bf16[8,2,128,128]{3,2,1,0:T(8,128)(2,1)S(1)} %all-to-all-done.refs_5_), channel_id=1, source_target_pairs={{0,16},{16,24},{1,17},{17,25},{2,18},{18,26},{3,19},{19,27},{4,20}... | collective-permute-start | bytes 1572872 | tf_op jit(solution)/shard_map/ppermute | solution.py:303
  20.9 0.0 collective-permute-done.2.refs_4_.refs_2_
  20.9 5.7 %all-to-all-start.1 = ((bf16[8,2,128,128]{3,2,1,0:T(8,128)(2,1)}), bf16[8,2,128,128]{3,2,1,0:T(8,128)(2,1)S(1)}, u32[]{:S(2)}, u32[]{:S(2)}) async-start(bf16[8,2,128,128]{3,2,1,0:T(8,128)(2,1)} %copy-done.1), calls=%async_computation.1 | async-start | bytes 1048576 | tf_op jit(solution)/shard_map/all_to_all | solution.py:304
  26.6 0.0 collective-permute-done.1.refs_3_.refs_1_
  26.6 3.9 %collective-permute-done.4.refs_6_ = bf16[8,2,128,128]{3,2,1,0:T(8,128)(2,1)} collective-permute-done((bf16[8,2,128,128]{3,2,1,0:T(8,128)(2,1)S(1)}, bf16[8,2,128,128]{3,2,1,0:T(8,128)(2,1)}, u32[]{:S(2)}, u32[]{:S(2)}) %collective-permute-start.4) | collective-permute-done | bytes 524320 | tf_op jit(solution)/shard_map/ppermute | solution.py:303
  30.6 1.3 %collective-permute-start.6 = (bf16[8,2,128,128]{3,2,1,0:T(8,128)(2,1)S(1)}, bf16[8,2,128,128]{3,2,1,0:T(8,128)(2,1)S(1)}, u32[]{:S(2)}, u32[]{:S(2)}) collective-permute-start(bf16[8,2,128,128]{3,2,1,0:T(8,128)(2,1)S(1)} %all-to-all-done.refs_5_), channel_id=1, source_target_pairs={{8,16},{9,17},{10,18},{11,19},{12,20},{13,21},{14,22},{15,23}} | collective-permute-start | bytes 1572872 | tf_op jit(solution)/shard_map/ppermute | solution.py:307
  31.8 3.6 %collective-permute-start.5 = (bf16[8,2,128,128]{3,2,1,0:T(8,128)(2,1)}, bf16[8,2,128,128]{3,2,1,0:T(8,128)(2,1)S(1)}, u32[]{:S(2)}, u32[]{:S(2)}) collective-permute-start(bf16[8,2,128,128]{3,2,1,0:T(8,128)(2,1)} %collective-permute-done.4.refs_6_), channel_id=1, source_target_pairs={{16,24},{17,25},{18,26},{19,27},{20,28},{21,29},{22,30},{23,31}} | collective-permute-start | bytes 1572872 | tf_op jit(solution)/shard_map/ppermute | solution.py:305
  35.5 0.0 collective-permute-done.refs_2_
  35.5 0.1 maximum_convert_fusion.refs_0_
  35.6 0.0 all-to-all-done.1.refs_7_
  35.6 15.0 %early.1 = (f32[8,512,128]{2,1,0:T(8,128)S(1)}, f32[8,512,256]{2,1,0:T(8,128)S(1)}) custom-call(s32[24]{0:T(128)S(1)} %maximum_convert_fusion.refs_0_, bf16[272,512]{1,0:T(8,128)(2,1)S(1)} %get-tuple-element.19.refs_1_, bf16[272,512]{1,0:T(8,128)(2,1)S(1)} %collective-permute-done.refs_2_, bf16[272,512]{1,0:T(8,128)(2,1)S(1)} %collective-permute-done.1.refs_3_.refs_1_, ...), custom_call_target="tpu_custom_call" | custom-call | flops 4294967296 | bytes 4194304 | tf_op jit(solution)/shard_map/early/pallas_call | solution.py:258
  50.6 0.0 collective-permute-done.6.refs_4_
  50.6 0.0 collective-permute-done.5.refs_3_
  50.6 4.5 %late_far.1 = (bf16[256,512]{1,0:T(8,128)(2,1)S(1)}, bf16[256,512]{1,0:T(8,128)(2,1)S(1)}) custom-call(s32[24]{0:T(128)S(1)} %maximum_convert_fusion.refs_0_, bf16[272,512]{1,0:T(8,128)(2,1)S(1)} %collective-permute-done.1.refs_3_.refs_1_, bf16[272,512]{1,0:T(8,128)(2,1)S(1)} %collective-permute-done.2.refs_4_.refs_2_, ...), custom_call_target="tpu_custom_call" | custom-call | flops 1610612736 | bytes 4194304 | tf_op jit(solution)/shard_map/late_far/pallas_call | solution.py:258
  55.2 0.1 collective-permute-start.8
  55.2 4.0 %collective-permute-start.9 = (bf16[256,512]{1,0:T(8,128)(2,1)S(1)}, bf16[256,512]{1,0:T(8,128)(2,1)S(1)}, u32[]{:S(2)}, u32[]{:S(2)}) collective-permute-start(bf16[256,512]{1,0:T(8,128)(2,1)S(1)} %get-tuple-element.32), channel_id=1, source_target_pairs={{0,6},{2,4},{4,2},{6,0},{1,7},{3,5},{5,3},{7,1},{8,14},{10,12},{12... | collective-permute-start | bytes 786440 | tf_op jit(solution)/shard_map/ppermute | solution.py:288
  59.3 4.0 %late_near.1 = (bf16[256,512]{1,0:T(8,128)(2,1)S(1)}, bf16[256,512]{1,0:T(8,128)(2,1)S(1)}) custom-call(s32[24]{0:T(128)S(1)} %maximum_convert_fusion.refs_0_, bf16[272,512]{1,0:T(8,128)(2,1)S(1)} %get-tuple-element.19.refs_1_, bf16[272,512]{1,0:T(8,128)(2,1)S(1)} %collective-permute-done.refs_2_, ...), custom_call_target="tpu_custom_call" | custom-call | flops 1610612736 | bytes 4194304 | tf_op jit(solution)/shard_map/late_near/pallas_call | solution.py:258
  63.3 0.1 collective-permute-start.7
  63.4 0.0 collective-permute-done.8.refs_2_
  63.4 5.6 %collective-permute-done.9.refs_3_ = bf16[256,512]{1,0:T(8,128)(2,1)S(1)} collective-permute-done((bf16[256,512]{1,0:T(8,128)(2,1)S(1)}, bf16[256,512]{1,0:T(8,128)(2,1)S(1)}, u32[]{:S(2)}, u32[]{:S(2)}) %collective-permute-start.9) | collective-permute-done | bytes 262176 | tf_op jit(solution)/shard_map/ppermute | solution.py:288
  68.9 1.1 %unpack.1 = bf16[256,2048]{1,0:T(8,128)(2,1)} custom-call(bf16[256,512]{1,0:T(8,128)(2,1)S(1)} %get-tuple-element.29.refs_0_, bf16[256,512]{1,0:T(8,128)(2,1)S(1)} %collective-permute-done.7.refs_1_, bf16[256,512]{1,0:T(8,128)(2,1)S(1)} %collective-permute-done.8.refs_2_, bf16[256,512]{1,0:T(8,128)(2,1)S(1)} %collective-permute-done.9.refs_3_), custom_call_target="tpu_custom_call" | custom-call | bytes 2097152 | tf_op jit(solution)/shard_map/unpack/pallas_call | solution.py:99
  (8 shorter events, 0.0 us)
Async XLA Ops:
  1.9 12.3 %collective-permute-start.3 = (bf16[8,2,128,128]{3,2,1,0:T(8,128)(2,1)}, bf16[8,2,128,128]{3,2,1,0:T(8,128)(2,1)S(1)}, u32[]{:S(2)}, u32[]{:S(2)}) collective-permute-start(bf16[8,2,128,128]{3,2,1,0:T(8,128)(2,1)} %pack_kv.1), channel_id=1, source_target_pairs={{8,24},{0,8},{9,25},{1,9},{10,26},{2,10},{11,27},{3,11},{12,28},{4... | collective-permute-start | bytes 1572872 | tf_op jit(solution)/shard_map/ppermute | solution.py:294
  2.6 11.6 %all-to-all-start = ((bf16[8,2,128,128]{3,2,1,0:T(8,128)(2,1)}), bf16[8,2,128,128]{3,2,1,0:T(8,128)(2,1)S(1)}, u32[]{:S(2)}, u32[]{:S(2)}) async-start(bf16[8,2,128,128]{3,2,1,0:T(8,128)(2,1)} %pack_kv.1), calls=%async_computation | async-start | bytes 1048576 | tf_op jit(solution)/shard_map/all_to_all | solution.py:295
  7.9 1.2 %copy-start = (bf16[256,2048]{1,0:T(8,128)(2,1)S(1)}, bf16[256,2048]{1,0:T(8,128)(2,1)}, u32[]{:S(2)}) copy-start(bf16[256,2048]{1,0:T(8,128)(2,1)} %q_ref.1) | copy-start | bytes 3145732
  9.8 11.1 %collective-permute-start.2 = (bf16[272,512]{1,0:T(8,128)(2,1)S(1)}, bf16[272,512]{1,0:T(8,128)(2,1)S(1)}, u32[]{:S(2)}, u32[]{:S(2)}) collective-permute-start(bf16[272,512]{1,0:T(8,128)(2,1)S(1)} %get-tuple-element.22), channel_id=1, source_target_pairs={{0,6},{2,4},{4,2},{6,0},{1,7},{3,5},{5,3},{7,1},{8,14},{10,12},{12... | collective-permute-start | bytes 835592 | tf_op jit(solution)/shard_map/ppermute | solution.py:288
  10.4 16.2 %collective-permute-start.1 = (bf16[272,512]{1,0:T(8,128)(2,1)S(1)}, bf16[272,512]{1,0:T(8,128)(2,1)S(1)}, u32[]{:S(2)}, u32[]{:S(2)}) collective-permute-start(bf16[272,512]{1,0:T(8,128)(2,1)S(1)} %get-tuple-element.21), channel_id=1, source_target_pairs={{0,4},{2,6},{4,0},{6,2},{1,5},{3,7},{5,1},{7,3},{8,12},{10,14},{12... | collective-permute-start | bytes 835592 | tf_op jit(solution)/shard_map/ppermute | solution.py:288
  11.6 23.9 %collective-permute-start = (bf16[272,512]{1,0:T(8,128)(2,1)S(1)}, bf16[272,512]{1,0:T(8,128)(2,1)S(1)}, u32[]{:S(2)}, u32[]{:S(2)}) collective-permute-start(bf16[272,512]{1,0:T(8,128)(2,1)S(1)} %get-tuple-element.20), channel_id=1, source_target_pairs={{0,2},{2,0},{4,6},{6,4},{1,3},{3,1},{5,7},{7,5},{8,10},{10,8},{12,... | collective-permute-start | bytes 835592 | tf_op jit(solution)/shard_map/ppermute | solution.py:288
  14.2 6.7 %copy-start.1 = (bf16[8,2,128,128]{3,2,1,0:T(8,128)(2,1)}, bf16[8,2,128,128]{3,2,1,0:T(8,128)(2,1)S(1)}, u32[]{:S(2)}) copy-start(bf16[8,2,128,128]{3,2,1,0:T(8,128)(2,1)S(1)} %collective-permute-done.3) | copy-start | bytes 1572868
  14.2 16.3 %collective-permute-start.4 = (bf16[8,2,128,128]{3,2,1,0:T(8,128)(2,1)S(1)}, bf16[8,2,128,128]{3,2,1,0:T(8,128)(2,1)}, u32[]{:S(2)}, u32[]{:S(2)}) collective-permute-start(bf16[8,2,128,128]{3,2,1,0:T(8,128)(2,1)S(1)} %all-to-all-done.refs_5_), channel_id=1, source_target_pairs={{0,16},{16,24},{1,17},{17,25},{2,18},{18,26},{3,19},{19,27},{4,20}... | collective-permute-start | bytes 1572872 | tf_op jit(solution)/shard_map/ppermute | solution.py:303
  20.9 14.7 %all-to-all-start.1 = ((bf16[8,2,128,128]{3,2,1,0:T(8,128)(2,1)}), bf16[8,2,128,128]{3,2,1,0:T(8,128)(2,1)S(1)}, u32[]{:S(2)}, u32[]{:S(2)}) async-start(bf16[8,2,128,128]{3,2,1,0:T(8,128)(2,1)} %copy-done.1), calls=%async_computation.1 | async-start | bytes 1048576 | tf_op jit(solution)/shard_map/all_to_all | solution.py:304
  30.6 20.0 %collective-permute-start.6 = (bf16[8,2,128,128]{3,2,1,0:T(8,128)(2,1)S(1)}, bf16[8,2,128,128]{3,2,1,0:T(8,128)(2,1)S(1)}, u32[]{:S(2)}, u32[]{:S(2)}) collective-permute-start(bf16[8,2,128,128]{3,2,1,0:T(8,128)(2,1)S(1)} %all-to-all-done.refs_5_), channel_id=1, source_target_pairs={{8,16},{9,17},{10,18},{11,19},{12,20},{13,21},{14,22},{15,23}} | collective-permute-start | bytes 1572872 | tf_op jit(solution)/shard_map/ppermute | solution.py:307
  31.8 18.7 %collective-permute-start.5 = (bf16[8,2,128,128]{3,2,1,0:T(8,128)(2,1)}, bf16[8,2,128,128]{3,2,1,0:T(8,128)(2,1)S(1)}, u32[]{:S(2)}, u32[]{:S(2)}) collective-permute-start(bf16[8,2,128,128]{3,2,1,0:T(8,128)(2,1)} %collective-permute-done.4.refs_6_), channel_id=1, source_target_pairs={{16,24},{17,25},{18,26},{19,27},{20,28},{21,29},{22,30},{23,31}} | collective-permute-start | bytes 1572872 | tf_op jit(solution)/shard_map/ppermute | solution.py:305
  55.2 8.2 %collective-permute-start.8 = (bf16[256,512]{1,0:T(8,128)(2,1)S(1)}, bf16[256,512]{1,0:T(8,128)(2,1)S(1)}, u32[]{:S(2)}, u32[]{:S(2)}) collective-permute-start(bf16[256,512]{1,0:T(8,128)(2,1)S(1)} %get-tuple-element.31), channel_id=1, source_target_pairs={{0,4},{2,6},{4,0},{6,2},{1,5},{3,7},{5,1},{7,3},{8,12},{10,14},{12... | collective-permute-start | bytes 786440 | tf_op jit(solution)/shard_map/ppermute | solution.py:288
  55.2 13.7 %collective-permute-start.9 = (bf16[256,512]{1,0:T(8,128)(2,1)S(1)}, bf16[256,512]{1,0:T(8,128)(2,1)S(1)}, u32[]{:S(2)}, u32[]{:S(2)}) collective-permute-start(bf16[256,512]{1,0:T(8,128)(2,1)S(1)} %get-tuple-element.32), channel_id=1, source_target_pairs={{0,6},{2,4},{4,2},{6,0},{1,7},{3,5},{5,3},{7,1},{8,14},{10,12},{12... | collective-permute-start | bytes 786440 | tf_op jit(solution)/shard_map/ppermute | solution.py:288
  63.3 5.7 %collective-permute-start.7 = (bf16[256,512]{1,0:T(8,128)(2,1)S(1)}, bf16[256,512]{1,0:T(8,128)(2,1)S(1)}, u32[]{:S(2)}, u32[]{:S(2)}) collective-permute-start(bf16[256,512]{1,0:T(8,128)(2,1)S(1)} %get-tuple-element.30), channel_id=1, source_target_pairs={{0,2},{2,0},{4,6},{6,4},{1,3},{3,1},{5,7},{7,5},{8,10},{10,8},{12,... | collective-permute-start | bytes 786440 | tf_op jit(solution)/shard_map/ppermute | solution.py:288

commit v5 on v4

--- a/solution.py
+++ b/solution.py
@@ -25,6 +25,7 @@
 BF16 = jnp.bfloat16
 VMEM = pl.BlockSpec(memory_space=pltpu.VMEM)
 SMEM = pl.BlockSpec(memory_space=pltpu.SMEM)
+ANY = pl.BlockSpec(memory_space=pl.ANY)
 MIB = 1024 * 1024
 
 
@@ -87,30 +88,39 @@
     )(selected, queries)
 
 
-def unpack_output(subs, pieces):
+def unpack_output(name, subs, pieces, ks, begun):
     rows = pieces[0].shape[0]
+    n = len(pieces)
 
     def kernel(*refs):
+        out_ref, sems = refs[-2:]
         sub = lax.axis_index("sub")
-        for k in range(subs):
-            at = pl.multiple_of((sub ^ k) * QW, QW)
-            refs[subs][:, pl.ds(at, QW)] = refs[k][...]
+        copies = []
+        for i, k in enumerate(ks):
+            at = pl.ds(pl.multiple_of((sub ^ k) * QW, QW), QW)
+            copies.append(pltpu.make_async_copy(refs[i], out_ref.at[:, at], sems.at[i]))
+        for copy in copies:
+            copy.start()
+        for copy in copies:
+            copy.wait()
 
     return pl.pallas_call(
         kernel,
-        in_specs=[VMEM] * subs,
-        out_specs=VMEM,
+        in_specs=[VMEM] * n + [ANY] * len(begun),
+        out_specs=ANY,
         out_shape=jax.ShapeDtypeStruct((rows, subs * QW), BF16),
-        cost_estimate=copy_cost(4 * subs * rows * QW),
+        scratch_shapes=[pltpu.SemaphoreType.DMA((n,))],
+        input_output_aliases={n: 0} if begun else {},
+        cost_estimate=copy_cost(4 * n * rows * QW),
         compiler_params=pltpu.CompilerParams(vmem_limit_bytes=8 * MIB),
-        name="unpack",
-    )(*pieces)
+        name=name,
+    )(*pieces, *begun)
 
 
 def attention(name, first, last, partners, bases_of, queries, sel, sources, state):
     parts, rows = len(queries), queries[0].shape[0] - EXTRA
     tiles_in_part = rows // TILE
-    tiles = parts * tiles_in_part
+    tiles_here = len(partners) * tiles_in_part
     r = sources[0].shape[2]
     per_block = BLK // r
     n_src = len(sources)
@@ -157,8 +167,8 @@
             start += n
 
         def one_tile(k, part, i, out_ref, out_at):
-            t = k * tiles_in_part + i
-            tile = level * tiles + (sub ^ k) * tiles_in_part + i
+            t = part * tiles_in_part + i
+            tile = (level * parts + (sub ^ k)) * tiles_in_part + i
             own = tile * TILE // BLK
             q_rows = pl.ds(pl.multiple_of(i * TILE, TILE), TILE)
             m_old, acc_old, at_old = (m_tmp, acc_tmp, 0) if first else (m_in, acc_in, t)
@@ -193,7 +203,7 @@
             found = jnp.int32(0)
             where = [jnp.int32(0)] * most
             for e in range(TOPK):
-                block = sel_ref[t * TOPK + e]
+                block = sel_ref[(k * tiles_in_part + i) * TOPK + e]
                 start = 0
                 for base, n in zip(bases, slots):
                     hit = (block != own) & (block >= base) & (block < base + n)
@@ -241,20 +251,20 @@
         else:
 
             def step(t, carry):
-                k = t // tiles_in_part
-                one_tile(k, k, lax.rem(t, tiles_in_part), None, None)
+                part = t // tiles_in_part
+                one_tile(partners[0] + part, part, lax.rem(t, tiles_in_part), None, None)
                 return carry
 
-            lax.fori_loop(0, tiles, step, 0)
+            lax.fori_loop(0, tiles_here, step, 0)
 
     if last:
         out_shape = tuple(jax.ShapeDtypeStruct((rows, QW), BF16) for _ in partners)
     else:
         out_shape = (
-            jax.ShapeDtypeStruct((tiles, QW, HD), F32),
-            jax.ShapeDtypeStruct((tiles, QW, 2 * HD), F32),
+            jax.ShapeDtypeStruct((tiles_here, QW, HD), F32),
+            jax.ShapeDtypeStruct((tiles_here, QW, 2 * HD), F32),
         )
-    work = (tiles if not last else len(partners) * tiles_in_part) * QW * BLK * (1 + n_src) // 2
+    work = tiles_here * QW * BLK * 3 // 2
     return pl.pallas_call(
         kernel,
         in_specs=[SMEM] + [VMEM] * (n_q + n_src + len(state)),
@@ -283,23 +293,24 @@
     level_blocks = subs * rows // BLK
     by_levels = levels == 4 and subs * rows % BLK == 0
 
-    def exchange(pieces):
+    def exchange(pieces, ks):
         return tuple(
             lax.ppermute(piece, "sub", [(i, i ^ k) for i in range(subs)]) if k else piece
-            for k, piece in enumerate(pieces)
+            for k, piece in zip(ks, pieces)
         )
 
+    everyone = tuple(range(subs))
     packed = pack_keys_values(subs, heads, keys, values)
     if by_levels:
         raw = lax.ppermute(packed, "lev", [(1, 3), (0, 1)])
     own = lax.all_to_all(packed, ("sub", "head"), 0, 0, tiled=True)
     q = pack_queries(subs, queries, selected)
-    q = exchange(q)
+    q = exchange(q, everyone)
     sel = jnp.concatenate([piece[rows, : tiles_here * TOPK] for piece in q]).astype(jnp.int32)
 
-    everyone = tuple(range(subs))
     if by_levels:
-        own, raw = lax.optimization_barrier((own, raw))
+        own, raw, first_piece = lax.optimization_barrier((own, raw, q[1]))
+        q = (q[0], first_piece, *q[2:])
         pa = lax.ppermute(own, "lev", [(0, 2), (2, 3)])
         p2 = lax.all_to_all(raw, ("sub", "head"), 0, 0, tiled=True)
         pf = lax.ppermute(pa, "lev", [(2, 3)])
@@ -318,20 +329,26 @@
         def late(level):
             return (at(level, (3, 0)), at(level, (2, 1)))
 
+        def whole_range(level):
+            return early(level) + late(level)
+
+        far, near = everyone[subs // 2 :], everyone[: subs // 2]
         state = attention(
-            "early", True, False, everyone, early, q, sel, (own, pa, p2), ()
+            "far_early", True, False, far, early, q, sel, (own, pa, p2), ()
         )
-        far, near = everyone[subs // 2 :], everyone[: subs // 2]
-        out_far = attention("late_far", False, True, far, late, q, sel, (pf, po), state)
-        out_near = attention("late_near", False, True, near, late, q, sel, (pf, po), state)
-        out = out_near + out_far
-    else:
-        whole = lax.all_gather(own, "lev", axis=0, tiled=True)
-        out = attention(
-            "all", True, True, everyone, lambda level: (0,), q, sel, (whole,), ()
+        out_far = attention("far_late", False, True, far, late, q, sel, (pf, po), state)
+        q_near, _ = lax.optimization_barrier((q[: subs // 2], out_far))
+        q = tuple(q_near) + q[subs // 2 :]
+        out_near = attention(
+            "near", True, True, near, whole_range, q, sel, (own, pa, p2, pf, po), ()
         )
-    out = exchange(out)
-    return unpack_output(subs, out) if subs > 1 else out[0]
+        begun = unpack_output("unpack_far", subs, exchange(out_far, far), far, ())
+        return unpack_output("unpack_near", subs, exchange(out_near, near), near, (begun,))
+    whole = lax.all_gather(own, "lev", axis=0, tiled=True)
+    out = attention("all", True, True, everyone, lambda level: (0,), q, sel, (whole,), ())
+    if subs == 1:
+        return out[0]
+    return unpack_output("unpack", subs, exchange(out, everyone), everyone, ())
 
 
 def solution(mesh):

time: 71.2 us -> 70.6 us (level)
  Pallas kernels: 27.2 us -> 28.4 us
    unnamed x5, local copies, waits for them, and re-layouts: 2 us -> 0.11 us
    ppermute x1, waiting for transfers between devices: 3.92 us -> 2.17 us  [body(): pa = lax.ppermute(own, 'lev', [(0, 2), (2, 3)])]
    all_to_all x1, waiting for transfers between devices: 2.18 us -> 3.92 us  [body(): own = lax.all_to_all(packed, ('sub', 'head'), 0, 0, tiled=True)]
    all_to_all x1, starting transfers between devices: 5.68 us -> 3.95 us  [body(): p2 = lax.all_to_all(raw, ('sub', 'head'), 0, 0, tiled=True)]
    ppermute x6, waiting for transfers between devices: 5.57 us -> 3.88 us  [exchange(): lax.ppermute(piece, 'sub', [(i, i ^ k) for i in range(subs)])]
    squeeze x4, local copies, waits for them, and re-layouts: 0.01 us -> 1.35 us  [body(): piece[rows, :tiles_here * TOPK]]
    all_to_all x1, waiting for transfers between devices: 0.01 us -> 1.11 us  [body(): p2 = lax.all_to_all(raw, ('sub', 'head'), 0, 0, tiled=True)]
    ppermute x6, starting transfers between devices: 6.38 us -> 7.47 us  [exchange(): lax.ppermute(piece, 'sub', [(i, i ^ k) for i in range(subs)])]
  transfers between devices with their start and end apart: 12 -> 12, of which waited for: 3 -> 6; matrix products, arithmetic and copies ran while one was open for 1% -> 2% of each run, Pallas kernels for 28% -> 29%
where the time goes in v5:
time: 70.6 us; the launch traced here: 69.6 us
  Pallas kernels  28.4 us (40%)
  starting transfers between devices  28.3 us (40%)
  waiting for transfers between devices  11.1 us (16%)
  local copies, waits for them, and re-layouts  1.45 us (2%)
    pallas_call x3, Pallas kernels, attention(): pl.pallas_call(kernel, in_specs=[SMEM] + [VMEM] * (n_q + n_src + len(stat...  23.2 us
    ppermute x6, starting transfers between devices, exchange(): lax.ppermute(piece, 'sub', [(i, i ^ k) for i in range(subs)])  7.47 us
    ppermute x1, starting transfers between devices, body(): pa = lax.ppermute(own, 'lev', [(0, 2), (2, 3)])  6.01 us
    all_to_all x1, starting transfers between devices, body(): own = lax.all_to_all(packed, ('sub', 'head'), 0, 0, tiled=True)  4.51 us
    all_to_all x1, starting transfers between devices, body(): p2 = lax.all_to_all(raw, ('sub', 'head'), 0, 0, tiled=True)  3.95 us
    all_to_all x1, waiting for transfers between devices, body(): own = lax.all_to_all(packed, ('sub', 'head'), 0, 0, tiled=True)  3.92 us
    ppermute x6, waiting for transfers between devices, exchange(): lax.ppermute(piece, 'sub', [(i, i ^ k) for i in range(subs)])  3.88 us
    ppermute x1, starting transfers between devices, body(): pf = lax.ppermute(pa, 'lev', [(2, 3)])  3.64 us
  transfers between devices with their start and end apart: 12, of which 6 were waited for; matrix products, arithmetic and copies ran while one was open for 2% of the time, Pallas kernels for 29%

profile of v5, /device:TPU:23, one launch (start us, length us, event | category | flops | bytes accessed | tf_op | source)
XLA Modules:
  0.0 69.6 jit_solution(16663846913472885037)
XLA Ops:
  0.0 2.0 %pack_kv.1 = bf16[8,2,128,128]{3,2,1,0:T(8,128)(2,1)} custom-call(bf16[128,1024]{1,0:T(8,128)(2,1)} %k_ref.1, bf16[128,1024]{1,0:T(8,128)(2,1)} %v_ref.1), custom_call_target="tpu_custom_call" | custom-call | bytes 1048576 | tf_op jit(solution)/shard_map/pack_kv/pallas_call | solution.py:54
  2.0 1.5 %collective-permute-start.3 = (bf16[8,2,128,128]{3,2,1,0:T(8,128)(2,1)}, bf16[8,2,128,128]{3,2,1,0:T(8,128)(2,1)}, u32[]{:S(2)}, u32[]{:S(2)}) collective-permute-start(bf16[8,2,128,128]{3,2,1,0:T(8,128)(2,1)} %pack_kv.1), channel_id=1, source_target_pairs={{8,24},{0,8},{9,25},{1,9},{10,26},{2,10},{11,27},{3,11},{12,28},{4... | collective-permute-start | bytes 1572872 | tf_op jit(solution)/shard_map/ppermute | solution.py:305
  3.5 4.5 %all-to-all-start = ((bf16[8,2,128,128]{3,2,1,0:T(8,128)(2,1)}), bf16[8,2,128,128]{3,2,1,0:T(8,128)(2,1)S(1)}, u32[]{:S(2)}, u32[]{:S(2)}) async-start(bf16[8,2,128,128]{3,2,1,0:T(8,128)(2,1)} %pack_kv.1), calls=%async_computation | async-start | bytes 1048576 | tf_op jit(solution)/shard_map/all_to_all | solution.py:306
  8.0 0.1 copy.6.sel_ref
  8.1 1.5 %pack_q.1 = (bf16[272,512]{1,0:T(8,128)(2,1)S(1)}, bf16[272,512]{1,0:T(8,128)(2,1)S(1)}, bf16[272,512]{1,0:T(8,128)(2,1)}, bf16[272,512]{1,0:T(8,128)(2,1)}) custom-call(s32[2,4,3]{2,1,0:T(4,128)S(1)} %copy.6.sel_ref, bf16[256,2048]{1,0:T(8,128)(2,1)S(1)} %copy-done), custom_call_target="tpu_custom_call" | custom-call | bytes 2097152 | tf_op jit(solution)/shard_map/pack_q/pallas_call | solution.py:80
  9.6 0.4 collective-permute-start
  10.0 1.2 %collective-permute-done.refs_2_ = bf16[272,512]{1,0:T(8,128)(2,1)S(1)} collective-permute-done((bf16[272,512]{1,0:T(8,128)(2,1)S(1)}, bf16[272,512]{1,0:T(8,128)(2,1)S(1)}, u32[]{:S(2)}, u32[]{:S(2)}) %collective-permute-start) | collective-permute-done | bytes 278560 | tf_op jit(solution)/shard_map/ppermute | solution.py:298
  11.2 3.9 %all-to-all-done.refs_3_ = bf16[8,2,128,128]{3,2,1,0:T(8,128)(2,1)S(1)} async-done(((bf16[8,2,128,128]{3,2,1,0:T(8,128)(2,1)}), bf16[8,2,128,128]{3,2,1,0:T(8,128)(2,1)S(1)}, u32[]{:S(2)}, u32[]{:S(2)}) %all-to-all-start) | async-done | bytes 524320 | tf_op jit(solution)/shard_map/all_to_all | solution.py:306
  15.1 0.0 collective-permute-done.3
  15.1 6.0 %collective-permute-start.4 = (bf16[8,2,128,128]{3,2,1,0:T(8,128)(2,1)S(1)}, bf16[8,2,128,128]{3,2,1,0:T(8,128)(2,1)S(1)}, u32[]{:S(2)}, u32[]{:S(2)}) collective-permute-start(bf16[8,2,128,128]{3,2,1,0:T(8,128)(2,1)S(1)} %all-to-all-done.refs_3_), channel_id=1, source_target_pairs={{0,16},{16,24},{1,17},{17,25},{2,18},{18,26},{3,19},{19,27},{4,20}... | collective-permute-start | bytes 1572872 | tf_op jit(solution)/shard_map/ppermute | solution.py:314
  21.1 0.3 collective-permute-start.1
  21.4 3.2 %collective-permute-start.2 = (bf16[272,512]{1,0:T(8,128)(2,1)}, bf16[272,512]{1,0:T(8,128)(2,1)}, u32[]{:S(2)}, u32[]{:S(2)}) collective-permute-start(bf16[272,512]{1,0:T(8,128)(2,1)} %get-tuple-element.25), channel_id=1, source_target_pairs={{0,6},{2,4},{4,2},{6,0},{1,7},{3,5},{5,3},{7,1},{8,14},{10,12},{12... | collective-permute-start | bytes 835592 | tf_op jit(solution)/shard_map/ppermute | solution.py:298
  24.6 4.0 %all-to-all-start.1 = ((bf16[8,2,128,128]{3,2,1,0:T(8,128)(2,1)}), bf16[8,2,128,128]{3,2,1,0:T(8,128)(2,1)S(1)}, u32[]{:S(2)}, u32[]{:S(2)}) async-start(bf16[8,2,128,128]{3,2,1,0:T(8,128)(2,1)} %collective-permute-done.3), calls=%async_computation.1 | async-start | bytes 1048576 | tf_op jit(solution)/shard_map/all_to_all | solution.py:315
  28.6 2.2 %collective-permute-done.4.refs_4_ = bf16[8,2,128,128]{3,2,1,0:T(8,128)(2,1)S(1)} collective-permute-done((bf16[8,2,128,128]{3,2,1,0:T(8,128)(2,1)S(1)}, bf16[8,2,128,128]{3,2,1,0:T(8,128)(2,1)S(1)}, u32[]{:S(2)}, u32[]{:S(2)}) %collective-permute-start.4) | collective-permute-done | bytes 524320 | tf_op jit(solution)/shard_map/ppermute | solution.py:314
  30.8 1.3 %collective-permute-start.6 = (bf16[8,2,128,128]{3,2,1,0:T(8,128)(2,1)S(1)}, bf16[8,2,128,128]{3,2,1,0:T(8,128)(2,1)S(1)}, u32[]{:S(2)}, u32[]{:S(2)}) collective-permute-start(bf16[8,2,128,128]{3,2,1,0:T(8,128)(2,1)S(1)} %all-to-all-done.refs_3_), channel_id=1, source_target_pairs={{8,16},{9,17},{10,18},{11,19},{12,20},{13,21},{14,22},{15,23}} | collective-permute-start | bytes 1572872 | tf_op jit(solution)/shard_map/ppermute | solution.py:318
  32.0 3.6 %collective-permute-start.5 = (bf16[8,2,128,128]{3,2,1,0:T(8,128)(2,1)S(1)}, bf16[8,2,128,128]{3,2,1,0:T(8,128)(2,1)S(1)}, u32[]{:S(2)}, u32[]{:S(2)}) collective-permute-start(bf16[8,2,128,128]{3,2,1,0:T(8,128)(2,1)S(1)} %collective-permute-done.4.refs_4_), channel_id=1, source_target_pairs={{16,24},{17,25},{18,26},{19,27},{20,28},{21,29},{22,30},{23,31}} | collective-permute-start | bytes 1572872 | tf_op jit(solution)/shard_map/ppermute | solution.py:316
  35.7 0.7 slice_bitcast_fusion.1
  36.4 2.0 %collective-permute-done.2.refs_2_ = bf16[272,512]{1,0:T(8,128)(2,1)} collective-permute-done((bf16[272,512]{1,0:T(8,128)(2,1)}, bf16[272,512]{1,0:T(8,128)(2,1)}, u32[]{:S(2)}, u32[]{:S(2)}) %collective-permute-start.2) | collective-permute-done | bytes 278560 | tf_op jit(solution)/shard_map/ppermute | solution.py:298
  38.4 0.7 slice_bitcast_fusion
  39.0 0.1 maximum_convert_fusion.refs_0_
  39.1 1.1 %all-to-all-done.1.refs_5_ = bf16[8,2,128,128]{3,2,1,0:T(8,128)(2,1)S(1)} async-done(((bf16[8,2,128,128]{3,2,1,0:T(8,128)(2,1)}), bf16[8,2,128,128]{3,2,1,0:T(8,128)(2,1)S(1)}, u32[]{:S(2)}, u32[]{:S(2)}) %all-to-all-start.1) | async-done | bytes 524320 | tf_op jit(solution)/shard_map/all_to_all | solution.py:315
  40.2 7.9 %far_early.1 = (f32[4,512,128]{2,1,0:T(8,128)S(1)}, f32[4,512,256]{2,1,0:T(8,128)S(1)}) custom-call(s32[24]{0:T(128)S(1)} %maximum_convert_fusion.refs_0_, bf16[272,512]{1,0:T(8,128)(2,1)} %collective-permute-done.1.refs_1_, bf16[272,512]{1,0:T(8,128)(2,1)} %collective-permute-done.2.refs_2_, bf16[8,2,128,128]{3,2,1,0:T(8,128)(2,1)S(1)} %all-to-all-done.refs_3_, ...), custom_call_target="tpu_custom_call" | custom-call | flops 1610612736 | bytes 4194304 | tf_op jit(solution)/shard_map/far_early/pallas_call | solution.py:268
  48.2 0.0 collective-permute-done.5.refs_3_.refs_6_
  48.2 5.1 %far_late.1 = (bf16[256,512]{1,0:T(8,128)(2,1)S(1)}, bf16[256,512]{1,0:T(8,128)(2,1)S(1)}) custom-call(s32[24]{0:T(128)S(1)} %maximum_convert_fusion.refs_0_, bf16[272,512]{1,0:T(8,128)(2,1)} %collective-permute-done.1.refs_1_, bf16[272,512]{1,0:T(8,128)(2,1)} %collective-permute-done.2.refs_2_, ...), custom_call_target="tpu_custom_call" | custom-call | flops 1610612736 | bytes 4194304 | tf_op jit(solution)/shard_map/far_late/pallas_call | solution.py:268
  53.3 0.3 collective-permute-start.8
  53.6 3.2 %collective-permute-start.9 = (bf16[256,512]{1,0:T(8,128)(2,1)S(1)}, bf16[256,512]{1,0:T(8,128)(2,1)S(1)}, u32[]{:S(2)}, u32[]{:S(2)}) collective-permute-start(bf16[256,512]{1,0:T(8,128)(2,1)S(1)} %get-tuple-element.34), channel_id=1, source_target_pairs={{0,6},{2,4},{4,2},{6,0},{1,7},{3,5},{5,3},{7,1},{8,14},{10,12},{12... | collective-permute-start | bytes 786440 | tf_op jit(solution)/shard_map/ppermute | solution.py:298
  56.8 10.2 %near.1 = (bf16[256,512]{1,0:T(8,128)(2,1)S(1)}, bf16[256,512]{1,0:T(8,128)(2,1)S(1)}) custom-call(s32[24]{0:T(128)S(1)} %maximum_convert_fusion.refs_0_, bf16[272,512]{1,0:T(8,128)(2,1)S(1)} %get-tuple-element.35.refs_1_, bf16[272,512]{1,0:T(8,128)(2,1)S(1)} %collective-permute-done.refs_2_, bf16[8,2,128,128]{3,2,1,0:T(8,128)(2,1)S(1)} %all-to-all-done.refs_3_, ...), custom_call_target="tpu_custom_call" | custom-call | flops 1610612736 | bytes 4194304 | tf_op jit(solution)/shard_map/near/pallas_call | solution.py:268
  67.0 0.1 collective-permute-start.7
  67.1 0.0 collective-permute-done.8.refs_0_
  67.1 0.8 %unpack_far.1.refs_2_ = bf16[256,2048]{1,0:T(8,128)(2,1)} custom-call(bf16[256,512]{1,0:T(8,128)(2,1)S(1)} %collective-permute-done.8.refs_0_, bf16[256,512]{1,0:T(8,128)(2,1)S(1)} %collective-permute-done.9.refs_1_), custom_call_target="tpu_custom_call" | custom-call | bytes 1048576 | tf_op jit(solution)/shard_map/unpack_far/pallas_call | solution.py:107
  68.0 0.7 collective-permute-done.7.refs_1_
  68.6 0.8 %unpack_near.1 = bf16[256,2048]{1,0:T(8,128)(2,1)} custom-call(bf16[256,512]{1,0:T(8,128)(2,1)S(1)} %get-tuple-element.37.refs_0_, bf16[256,512]{1,0:T(8,128)(2,1)S(1)} %collective-permute-done.7.refs_1_, bf16[256,2048]{1,0:T(8,128)(2,1)} %unpack_far.1.refs_2_), custom_call_target="tpu_custom_call", output_to_operand_aliasing={{}: (2, {})} | custom-call | bytes 1048576 | tf_op jit(solution)/shard_map/unpack_near/pallas_call | solution.py:107
  (9 shorter events, 0.0 us)
Async XLA Ops:
  0.0 8.0 %copy-start.1 = (s32[2,4,3]{1,0,2:T(2,128)S(1)}, s32[2,4,3]{1,0,2:T(2,128)}, u32[]{:S(2)}) copy-start(s32[2,4,3]{1,0,2:T(2,128)} %param.7) | copy-start | bytes 292
  0.0 8.1 %copy-start = (bf16[256,2048]{1,0:T(8,128)(2,1)S(1)}, bf16[256,2048]{1,0:T(8,128)(2,1)}, u32[]{:S(2)}) copy-start(bf16[256,2048]{1,0:T(8,128)(2,1)} %q_ref.1) | copy-start | bytes 3145732
  2.0 13.1 %collective-permute-start.3 = (bf16[8,2,128,128]{3,2,1,0:T(8,128)(2,1)}, bf16[8,2,128,128]{3,2,1,0:T(8,128)(2,1)}, u32[]{:S(2)}, u32[]{:S(2)}) collective-permute-start(bf16[8,2,128,128]{3,2,1,0:T(8,128)(2,1)} %pack_kv.1), channel_id=1, source_target_pairs={{8,24},{0,8},{9,25},{1,9},{10,26},{2,10},{11,27},{3,11},{12,28},{4... | collective-permute-start | bytes 1572872 | tf_op jit(solution)/shard_map/ppermute | solution.py:305
  3.5 11.6 %all-to-all-start = ((bf16[8,2,128,128]{3,2,1,0:T(8,128)(2,1)}), bf16[8,2,128,128]{3,2,1,0:T(8,128)(2,1)S(1)}, u32[]{:S(2)}, u32[]{:S(2)}) async-start(bf16[8,2,128,128]{3,2,1,0:T(8,128)(2,1)} %pack_kv.1), calls=%async_computation | async-start | bytes 1048576 | tf_op jit(solution)/shard_map/all_to_all | solution.py:306
  9.6 1.6 %collective-permute-start = (bf16[272,512]{1,0:T(8,128)(2,1)S(1)}, bf16[272,512]{1,0:T(8,128)(2,1)S(1)}, u32[]{:S(2)}, u32[]{:S(2)}) collective-permute-start(bf16[272,512]{1,0:T(8,128)(2,1)S(1)} %get-tuple-element.23), channel_id=1, source_target_pairs={{0,2},{2,0},{4,6},{6,4},{1,3},{3,1},{5,7},{7,5},{8,10},{10,8},{12,... | collective-permute-start | bytes 835592 | tf_op jit(solution)/shard_map/ppermute | solution.py:298
  15.1 15.7 %collective-permute-start.4 = (bf16[8,2,128,128]{3,2,1,0:T(8,128)(2,1)S(1)}, bf16[8,2,128,128]{3,2,1,0:T(8,128)(2,1)S(1)}, u32[]{:S(2)}, u32[]{:S(2)}) collective-permute-start(bf16[8,2,128,128]{3,2,1,0:T(8,128)(2,1)S(1)} %all-to-all-done.refs_3_), channel_id=1, source_target_pairs={{0,16},{16,24},{1,17},{17,25},{2,18},{18,26},{3,19},{19,27},{4,20}... | collective-permute-start | bytes 1572872 | tf_op jit(solution)/shard_map/ppermute | solution.py:314
  21.1 14.6 %collective-permute-start.1 = (bf16[272,512]{1,0:T(8,128)(2,1)}, bf16[272,512]{1,0:T(8,128)(2,1)}, u32[]{:S(2)}, u32[]{:S(2)}) collective-permute-start(bf16[272,512]{1,0:T(8,128)(2,1)} %get-tuple-element.24), channel_id=1, source_target_pairs={{0,4},{2,6},{4,0},{6,2},{1,5},{3,7},{5,1},{7,3},{8,12},{10,14},{12... | collective-permute-start | bytes 835592 | tf_op jit(solution)/shard_map/ppermute | solution.py:298
  21.4 16.9 %collective-permute-start.2 = (bf16[272,512]{1,0:T(8,128)(2,1)}, bf16[272,512]{1,0:T(8,128)(2,1)}, u32[]{:S(2)}, u32[]{:S(2)}) collective-permute-start(bf16[272,512]{1,0:T(8,128)(2,1)} %get-tuple-element.25), channel_id=1, source_target_pairs={{0,6},{2,4},{4,2},{6,0},{1,7},{3,5},{5,3},{7,1},{8,14},{10,12},{12... | collective-permute-start | bytes 835592 | tf_op jit(solution)/shard_map/ppermute | solution.py:298
  24.6 15.6 %all-to-all-start.1 = ((bf16[8,2,128,128]{3,2,1,0:T(8,128)(2,1)}), bf16[8,2,128,128]{3,2,1,0:T(8,128)(2,1)S(1)}, u32[]{:S(2)}, u32[]{:S(2)}) async-start(bf16[8,2,128,128]{3,2,1,0:T(8,128)(2,1)} %collective-permute-done.3), calls=%async_computation.1 | async-start | bytes 1048576 | tf_op jit(solution)/shard_map/all_to_all | solution.py:315
  30.8 17.4 %collective-permute-start.6 = (bf16[8,2,128,128]{3,2,1,0:T(8,128)(2,1)S(1)}, bf16[8,2,128,128]{3,2,1,0:T(8,128)(2,1)S(1)}, u32[]{:S(2)}, u32[]{:S(2)}) collective-permute-start(bf16[8,2,128,128]{3,2,1,0:T(8,128)(2,1)S(1)} %all-to-all-done.refs_3_), channel_id=1, source_target_pairs={{8,16},{9,17},{10,18},{11,19},{12,20},{13,21},{14,22},{15,23}} | collective-permute-start | bytes 1572872 | tf_op jit(solution)/shard_map/ppermute | solution.py:318
  32.0 16.2 %collective-permute-start.5 = (bf16[8,2,128,128]{3,2,1,0:T(8,128)(2,1)S(1)}, bf16[8,2,128,128]{3,2,1,0:T(8,128)(2,1)S(1)}, u32[]{:S(2)}, u32[]{:S(2)}) collective-permute-start(bf16[8,2,128,128]{3,2,1,0:T(8,128)(2,1)S(1)} %collective-permute-done.4.refs_4_), channel_id=1, source_target_pairs={{16,24},{17,25},{18,26},{19,27},{20,28},{21,29},{22,30},{23,31}} | collective-permute-start | bytes 1572872 | tf_op jit(solution)/shard_map/ppermute | solution.py:316
  53.3 13.8 %collective-permute-start.8 = (bf16[256,512]{1,0:T(8,128)(2,1)S(1)}, bf16[256,512]{1,0:T(8,128)(2,1)S(1)}, u32[]{:S(2)}, u32[]{:S(2)}) collective-permute-start(bf16[256,512]{1,0:T(8,128)(2,1)S(1)} %get-tuple-element.33), channel_id=1, source_target_pairs={{0,4},{2,6},{4,0},{6,2},{1,5},{3,7},{5,1},{7,3},{8,12},{10,14},{12... | collective-permute-start | bytes 786440 | tf_op jit(solution)/shard_map/ppermute | solution.py:298
  53.6 13.5 %collective-permute-start.9 = (bf16[256,512]{1,0:T(8,128)(2,1)S(1)}, bf16[256,512]{1,0:T(8,128)(2,1)S(1)}, u32[]{:S(2)}, u32[]{:S(2)}) collective-permute-start(bf16[256,512]{1,0:T(8,128)(2,1)S(1)} %get-tuple-element.34), channel_id=1, source_target_pairs={{0,6},{2,4},{4,2},{6,0},{1,7},{3,5},{5,3},{7,1},{8,14},{10,12},{12... | collective-permute-start | bytes 786440 | tf_op jit(solution)/shard_map/ppermute | solution.py:298
  67.0 1.6 %collective-permute-start.7 = (bf16[256,512]{1,0:T(8,128)(2,1)S(1)}, bf16[256,512]{1,0:T(8,128)(2,1)S(1)}, u32[]{:S(2)}, u32[]{:S(2)}) collective-permute-start(bf16[256,512]{1,0:T(8,128)(2,1)S(1)} %get-tuple-element.38), channel_id=1, source_target_pairs={{0,2},{2,0},{4,6},{6,4},{1,3},{3,1},{5,7},{7,5},{8,10},{10,8},{12,... | collective-permute-start | bytes 786440 | tf_op jit(solution)/shard_map/ppermute | solution.py:298

commit v6 on v5

--- a/solution.py
+++ b/solution.py
@@ -291,7 +291,7 @@
     rows = queries.shape[0]
     tiles_here = selected.shape[0]
     level_blocks = subs * rows // BLK
-    by_levels = levels == 4 and subs * rows % BLK == 0
+    by_levels = levels == 4 and subs * rows % (2 * BLK) == 0
 
     def exchange(pieces, ks):
         return tuple(
@@ -305,17 +305,25 @@
         raw = lax.ppermute(packed, "lev", [(1, 3), (0, 1)])
     own = lax.all_to_all(packed, ("sub", "head"), 0, 0, tiled=True)
     q = pack_queries(subs, queries, selected)
-    q = exchange(q, everyone)
-    sel = jnp.concatenate([piece[rows, : tiles_here * TOPK] for piece in q]).astype(jnp.int32)
-
+    hop = subs // 2
+    if hop > 1:
+        over = exchange(q[hop:], [hop] * hop)
+        q = exchange(q[:hop], range(hop)) + exchange(over, range(hop))
+    else:
+        q = exchange(q, everyone)
     if by_levels:
-        own, raw, first_piece = lax.optimization_barrier((own, raw, q[1]))
-        q = (q[0], first_piece, *q[2:])
-        pa = lax.ppermute(own, "lev", [(0, 2), (2, 3)])
+        own, raw = lax.optimization_barrier((own, raw))
+        half = own.shape[0] // 2
+        halves = lax.optimization_barrier((own[:half], own[half:]))
+        up = [lax.ppermute(piece, "lev", [(0, 2), (2, 3)]) for piece in halves]
         p2 = lax.all_to_all(raw, ("sub", "head"), 0, 0, tiled=True)
-        pf = lax.ppermute(pa, "lev", [(2, 3)])
-        later, pa = lax.optimization_barrier((own, pa))
-        po = lax.ppermute(later, "lev", [(1, 2)])
+        q, _ = lax.optimization_barrier((q, up))
+        sel = jnp.concatenate([piece[rows, : tiles_here * TOPK] for piece in q]).astype(jnp.int32)
+        forwards = lax.axis_index("lev") == 2
+        last_up = [
+            lax.ppermute(jnp.where(forwards, a, b), "lev", [(2, 3), (1, 2)])
+            for a, b in zip(up, halves)
+        ]
 
         def at(level, *which):
             base = jnp.int32(NONE)
@@ -323,27 +331,35 @@
                 base = jnp.where(level == here, holds * level_blocks, base)
             return base
 
+        def in_halves(base):
+            return (base, base + level_blocks // 2)
+
         def early(level):
-            return (level * level_blocks, at(level, (2, 0), (3, 2)), at(level, (1, 0), (3, 1)))
+            return (
+                level * level_blocks,
+                *in_halves(at(level, (2, 0), (3, 2))),
+                at(level, (1, 0), (3, 1)),
+            )
 
         def late(level):
-            return (at(level, (3, 0)), at(level, (2, 1)))
+            return in_halves(at(level, (2, 1), (3, 0)))
 
         def whole_range(level):
             return early(level) + late(level)
 
         far, near = everyone[subs // 2 :], everyone[: subs // 2]
         state = attention(
-            "far_early", True, False, far, early, q, sel, (own, pa, p2), ()
+            "far_early", True, False, far, early, q, sel, (own, *up, p2), ()
         )
-        out_far = attention("far_late", False, True, far, late, q, sel, (pf, po), state)
+        out_far = attention("far_late", False, True, far, late, q, sel, tuple(last_up), state)
         q_near, _ = lax.optimization_barrier((q[: subs // 2], out_far))
-        q = tuple(q_near) + q[subs // 2 :]
+        q = tuple(q_near) + tuple(q[subs // 2 :])
         out_near = attention(
-            "near", True, True, near, whole_range, q, sel, (own, pa, p2, pf, po), ()
+            "near", True, True, near, whole_range, q, sel, (own, *up, p2, *last_up), ()
         )
         begun = unpack_output("unpack_far", subs, exchange(out_far, far), far, ())
         return unpack_output("unpack_near", subs, exchange(out_near, near), near, (begun,))
+    sel = jnp.concatenate([piece[rows, : tiles_here * TOPK] for piece in q]).astype(jnp.int32)
     whole = lax.all_gather(own, "lev", axis=0, tiled=True)
     out = attention("all", True, True, everyone, lambda level: (0,), q, sel, (whole,), ())
     if subs == 1:

time: 70.6 us -> 68.7 us (0.973); the launches traced: 69.6 us -> 68.6 us
  waiting for transfers between devices: 11.1 us -> 8.78 us
  other arithmetic: 0.08 us -> 1.55 us
  starting transfers between devices: 28.3 us -> 29.7 us
  Pallas kernels: 28.4 us -> 27.4 us
    ppermute x6 -> x7, waiting for transfers between devices: 3.88 us -> 0.69 us  [exchange(): lax.ppermute(piece, 'sub', [(i, i ^ k) for i in range(subs)])]
    ppermute x3 -> x4, starting transfers between devices: 10.9 us -> 13.4 us  [the longest x2 8.58 us: body(): up = [lax.ppermute(piece, 'lev', [(0, 2), (2, 3)]) for piece in halves]]
    ppermute x3 -> x4, waiting for transfers between devices: 2.17 us -> 0.01 us  [the longest x2 0.01 us: body(): lax.ppermute(jnp.where(forwards, a, b), 'lev', [(2, 3), (1, 2)])]
    all_to_all x1, waiting for transfers between devices: 3.92 us -> 5.96 us  [body(): own = lax.all_to_all(packed, ('sub', 'head'), 0, 0, tiled=True)]
    select_n x0 -> x2, other arithmetic: none -> 1.47 us  [body(): jnp.where(forwards, a, b)]
    squeeze x4 -> x2, local copies, waits for them, and re-layouts: 1.35 us -> 0.01 us  [body(): piece[rows, :tiles_here * TOPK]]
    ppermute x6 -> x7, starting transfers between devices: 7.47 us -> 6.39 us  [exchange(): lax.ppermute(piece, 'sub', [(i, i ^ k) for i in range(subs)])]
    all_to_all x1, waiting for transfers between devices: 1.11 us -> 2.12 us  [body(): p2 = lax.all_to_all(raw, ('sub', 'head'), 0, 0, tiled=True)]
  transfers between devices with their start and end apart: 12 -> 14, of which waited for: 6 -> 3; matrix products, arithmetic and copies ran while one was open for 2% -> 4% of each run, Pallas kernels for 29% -> 29%
where the time goes in v6:
time: 68.7 us; the launch traced here: 68.6 us
  starting transfers between devices  29.7 us (43%)
  Pallas kernels  27.4 us (40%)
  waiting for transfers between devices  8.78 us (13%)
  other arithmetic  1.55 us (2%)
  local copies, waits for them, and re-layouts  0.95 us (1%)
    pallas_call x3, Pallas kernels, attention(): pl.pallas_call(kernel, in_specs=[SMEM] + [VMEM] * (n_q + n_src + len(stat...  23 us
    ppermute x2, starting transfers between devices, body(): up = [lax.ppermute(piece, 'lev', [(0, 2), (2, 3)]) for piece in halves]  8.58 us
    ppermute x7, starting transfers between devices, exchange(): lax.ppermute(piece, 'sub', [(i, i ^ k) for i in range(subs)])  6.39 us
    all_to_all x1, waiting for transfers between devices, body(): own = lax.all_to_all(packed, ('sub', 'head'), 0, 0, tiled=True)  5.96 us
    ppermute x2, starting transfers between devices, body(): lax.ppermute(jnp.where(forwards, a, b), 'lev', [(2, 3), (1, 2)])  4.82 us
    all_to_all x1, starting transfers between devices, body(): p2 = lax.all_to_all(raw, ('sub', 'head'), 0, 0, tiled=True)  4.66 us
    all_to_all x1, starting transfers between devices, body(): own = lax.all_to_all(packed, ('sub', 'head'), 0, 0, tiled=True)  4.52 us
    all_to_all x1, waiting for transfers between devices, body(): p2 = lax.all_to_all(raw, ('sub', 'head'), 0, 0, tiled=True)  2.12 us
  transfers between devices with their start and end apart: 14, of which 3 were waited for; matrix products, arithmetic and copies ran while one was open for 4% of the time, Pallas kernels for 29%

profile of v6, /device:TPU:23, one launch (start us, length us, event | category | flops | bytes accessed | tf_op | source)
XLA Modules:
  0.0 68.6 jit_solution(8458169614676649198)
XLA Ops:
  0.0 2.0 %pack_kv.1 = bf16[8,2,128,128]{3,2,1,0:T(8,128)(2,1)} custom-call(bf16[128,1024]{1,0:T(8,128)(2,1)} %k_ref.1, bf16[128,1024]{1,0:T(8,128)(2,1)} %v_ref.1), custom_call_target="tpu_custom_call" | custom-call | bytes 1048576 | tf_op jit(solution)/shard_map/pack_kv/pallas_call | solution.py:54
  2.0 0.7 collective-permute-start.4
  2.7 4.5 %all-to-all-start = ((bf16[8,2,128,128]{3,2,1,0:T(8,128)(2,1)}), bf16[8,2,128,128]{3,2,1,0:T(8,128)(2,1)S(1)}, u32[]{:S(2)}, u32[]{:S(2)}) async-start(bf16[8,2,128,128]{3,2,1,0:T(8,128)(2,1)} %pack_kv.1), calls=%async_computation | async-start | bytes 1048576 | tf_op jit(solution)/shard_map/all_to_all | solution.py:306
  7.2 0.1 copy.6.sel_ref
  7.3 0.7 pack_q.1
  8.0 0.3 collective-permute-start.2
  8.4 6.0 %all-to-all-done.refs_3_ = bf16[8,2,128,128]{3,2,1,0:T(8,128)(2,1)S(1)} async-done(((bf16[8,2,128,128]{3,2,1,0:T(8,128)(2,1)}), bf16[8,2,128,128]{3,2,1,0:T(8,128)(2,1)S(1)}, u32[]{:S(2)}, u32[]{:S(2)}) %all-to-all-start) | async-done | bytes 524320 | tf_op jit(solution)/shard_map/all_to_all | solution.py:306
  14.3 0.0 collective-permute-done.4
  14.3 0.8 %fusion = (bf16[4,2,128,128]{3,2,1,0:T(8,128)(2,1)}, bf16[4,2,128,128]{3,2,1,0:T(8,128)(2,1)S(1)}) fusion(bf16[8,2,128,128]{3,2,1,0:T(8,128)(2,1)S(1)} %all-to-all-done.refs_3_), kind=kLoop, calls=%fused_computation.7 | loop fusion | bytes 1048576 | tf_op jit(solution)/shard_map/slice | solution.py:317
  15.2 6.7 %collective-permute-start.5 = (bf16[4,2,128,128]{3,2,1,0:T(8,128)(2,1)S(1)}, bf16[4,2,128,128]{3,2,1,0:T(8,128)(2,1)S(1)}, u32[]{:S(2)}, u32[]{:S(2)}) collective-permute-start(bf16[4,2,128,128]{3,2,1,0:T(8,128)(2,1)S(1)} %get-tuple-element.30), channel_id=1, source_target_pairs={{0,16},{16,24},{1,17},{17,25},{2,18},{18,26},{3,19},{19,27},{4,20}... | collective-permute-start | bytes 786440 | tf_op jit(solution)/shard_map/ppermute | solution.py:318
  21.8 1.9 %collective-permute-start.6 = (bf16[4,2,128,128]{3,2,1,0:T(8,128)(2,1)}, bf16[4,2,128,128]{3,2,1,0:T(8,128)(2,1)S(1)}, u32[]{:S(2)}, u32[]{:S(2)}) collective-permute-start(bf16[4,2,128,128]{3,2,1,0:T(8,128)(2,1)} %get-tuple-element.31), channel_id=1, source_target_pairs={{0,16},{16,24},{1,17},{17,25},{2,18},{18,26},{3,19},{19,27},{4,20}... | collective-permute-start | bytes 786440 | tf_op jit(solution)/shard_map/ppermute | solution.py:318
  23.8 1.9 %collective-permute-start = (bf16[272,512]{1,0:T(8,128)(2,1)S(1)}, bf16[272,512]{1,0:T(8,128)(2,1)S(1)}, u32[]{:S(2)}, u32[]{:S(2)}) collective-permute-start(bf16[272,512]{1,0:T(8,128)(2,1)S(1)} %get-tuple-element.26), channel_id=1, source_target_pairs={{0,2},{2,0},{4,6},{6,4},{1,3},{3,1},{5,7},{7,5},{8,10},{10,8},{12,... | collective-permute-start | bytes 835592 | tf_op jit(solution)/shard_map/ppermute | solution.py:298
  25.7 0.3 collective-permute-start.1
  25.9 0.0 collective-permute-done.2
  25.9 0.3 collective-permute-start.3
  26.3 4.7 %all-to-all-start.1 = ((bf16[8,2,128,128]{3,2,1,0:T(8,128)(2,1)}), bf16[8,2,128,128]{3,2,1,0:T(8,128)(2,1)S(1)}, u32[]{:S(2)}, u32[]{:S(2)}) async-start(bf16[8,2,128,128]{3,2,1,0:T(8,128)(2,1)} %copy-done.1), calls=%async_computation.1 | async-start | bytes 1048576 | tf_op jit(solution)/shard_map/all_to_all | solution.py:319
  30.9 0.7 %broadcast_select_fusion.1 = bf16[4,2,128,128]{3,2,1,0:T(8,128)(2,1)} fusion(bf16[4,2,128,128]{3,2,1,0:T(8,128)(2,1)S(1)} %collective-permute-done.5.refs_4_, bf16[4,2,128,128]{3,2,1,0:T(8,128)(2,1)S(1)} %get-tuple-element.30, pred[]{:T(512)S(6)} %eq.3), kind=kLoop, calls=%fused_computation.1 | loop fusion | flops 131072 | bytes 786433 | tf_op jit(solution)/shard_map/jit(_where)/select_n | solution.py:324
  31.7 1.9 %collective-permute-start.7 = (bf16[4,2,128,128]{3,2,1,0:T(8,128)(2,1)}, bf16[4,2,128,128]{3,2,1,0:T(8,128)(2,1)S(1)}, u32[]{:S(2)}, u32[]{:S(2)}) collective-permute-start(bf16[4,2,128,128]{3,2,1,0:T(8,128)(2,1)} %broadcast_select_fusion.1), channel_id=1, source_target_pairs={{16,24},{8,16},{17,25},{9,17},{18,26},{10,18},{19,27},{11,19},{20,... | collective-permute-start | bytes 786440 | tf_op jit(solution)/shard_map/ppermute | solution.py:324
  33.6 0.0 collective-permute-done.6.refs_5_
  33.6 0.7 %broadcast_select_fusion = bf16[4,2,128,128]{3,2,1,0:T(8,128)(2,1)} fusion(bf16[4,2,128,128]{3,2,1,0:T(8,128)(2,1)S(1)} %collective-permute-done.6.refs_5_, bf16[4,2,128,128]{3,2,1,0:T(8,128)(2,1)} %get-tuple-element.31, pred[]{:T(512)S(6)} %eq.3), kind=kLoop, calls=%fused_computation | loop fusion | flops 131072 | bytes 786433 | tf_op jit(solution)/shard_map/jit(_where)/select_n | solution.py:324
  34.3 2.9 %collective-permute-start.8 = (bf16[4,2,128,128]{3,2,1,0:T(8,128)(2,1)}, bf16[4,2,128,128]{3,2,1,0:T(8,128)(2,1)}, u32[]{:S(2)}, u32[]{:S(2)}) collective-permute-start(bf16[4,2,128,128]{3,2,1,0:T(8,128)(2,1)} %broadcast_select_fusion), channel_id=1, source_target_pairs={{16,24},{8,16},{17,25},{9,17},{18,26},{10,18},{19,27},{11,19},{20,... | collective-permute-start | bytes 786440 | tf_op jit(solution)/shard_map/ppermute | solution.py:324
  37.3 0.1 maximum_convert_fusion.refs_0_
  37.4 2.1 %all-to-all-done.1.refs_6_ = bf16[8,2,128,128]{3,2,1,0:T(8,128)(2,1)S(1)} async-done(((bf16[8,2,128,128]{3,2,1,0:T(8,128)(2,1)}), bf16[8,2,128,128]{3,2,1,0:T(8,128)(2,1)S(1)}, u32[]{:S(2)}, u32[]{:S(2)}) %all-to-all-start.1) | async-done | bytes 524320 | tf_op jit(solution)/shard_map/all_to_all | solution.py:319
  39.5 8.0 %far_early.1 = (f32[4,512,128]{2,1,0:T(8,128)S(1)}, f32[4,512,256]{2,1,0:T(8,128)S(1)}) custom-call(s32[24]{0:T(128)S(1)} %maximum_convert_fusion.refs_0_, bf16[272,512]{1,0:T(8,128)(2,1)S(1)} %collective-permute-done.1.refs_1_, bf16[272,512]{1,0:T(8,128)(2,1)S(1)} %collective-permute-done.3.refs_2_, bf16[8,2,128,128]{3,2,1,0:T(8,128)(2,1)S(1)} %all-to-all-done.refs_3_, ...), custom_call_target="tpu_custom_call" | custom-call | flops 1610612736 | bytes 4194304 | tf_op jit(solution)/shard_map/far_early/pallas_call | solution.py:268
  47.5 4.4 %far_late.1 = (bf16[256,512]{1,0:T(8,128)(2,1)S(1)}, bf16[256,512]{1,0:T(8,128)(2,1)S(1)}) custom-call(s32[24]{0:T(128)S(1)} %maximum_convert_fusion.refs_0_, bf16[272,512]{1,0:T(8,128)(2,1)S(1)} %collective-permute-done.1.refs_1_, bf16[272,512]{1,0:T(8,128)(2,1)S(1)} %collective-permute-done.3.refs_2_, ...), custom_call_target="tpu_custom_call" | custom-call | flops 1610612736 | bytes 4194304 | tf_op jit(solution)/shard_map/far_late/pallas_call | solution.py:268
  51.9 0.3 collective-permute-start.10
  52.2 3.2 %collective-permute-start.11 = (bf16[256,512]{1,0:T(8,128)(2,1)S(1)}, bf16[256,512]{1,0:T(8,128)(2,1)S(1)}, u32[]{:S(2)}, u32[]{:S(2)}) collective-permute-start(bf16[256,512]{1,0:T(8,128)(2,1)S(1)} %get-tuple-element.40), channel_id=1, source_target_pairs={{0,6},{2,4},{4,2},{6,0},{1,7},{3,5},{5,3},{7,1},{8,14},{10,12},{12... | collective-permute-start | bytes 786440 | tf_op jit(solution)/shard_map/ppermute | solution.py:298
  55.4 10.6 %near.1 = (bf16[256,512]{1,0:T(8,128)(2,1)S(1)}, bf16[256,512]{1,0:T(8,128)(2,1)S(1)}) custom-call(s32[24]{0:T(128)S(1)} %maximum_convert_fusion.refs_0_, bf16[272,512]{1,0:T(8,128)(2,1)S(1)} %get-tuple-element.41.refs_1_, bf16[272,512]{1,0:T(8,128)(2,1)S(1)} %collective-permute-done.refs_2_, bf16[8,2,128,128]{3,2,1,0:T(8,128)(2,1)S(1)} %all-to-all-done.refs_3_, ...), custom_call_target="tpu_custom_call" | custom-call | flops 1610612736 | bytes 4194304 | tf_op jit(solution)/shard_map/near/pallas_call | solution.py:268
  66.1 0.1 collective-permute-start.9
  66.2 0.8 %unpack_far.1.refs_2_ = bf16[256,2048]{1,0:T(8,128)(2,1)} custom-call(bf16[256,512]{1,0:T(8,128)(2,1)S(1)} %collective-permute-done.10.refs_0_, bf16[256,512]{1,0:T(8,128)(2,1)S(1)} %collective-permute-done.11.refs_1_), custom_call_target="tpu_custom_call" | custom-call | bytes 1048576 | tf_op jit(solution)/shard_map/unpack_far/pallas_call | solution.py:107
  67.0 0.7 collective-permute-done.9.refs_1_
  67.7 0.8 %unpack_near.1 = bf16[256,2048]{1,0:T(8,128)(2,1)} custom-call(bf16[256,512]{1,0:T(8,128)(2,1)S(1)} %get-tuple-element.43.refs_0_, bf16[256,512]{1,0:T(8,128)(2,1)S(1)} %collective-permute-done.9.refs_1_, bf16[256,2048]{1,0:T(8,128)(2,1)} %unpack_far.1.refs_2_), custom_call_target="tpu_custom_call", output_to_operand_aliasing={{}: (2, {})} | custom-call | bytes 1048576 | tf_op jit(solution)/shard_map/unpack_near/pallas_call | solution.py:107
  (16 shorter events, 0.0 us)
Async XLA Ops:
  0.0 7.2 %copy-start.2 = (s32[2,4,3]{1,0,2:T(2,128)S(1)}, s32[2,4,3]{1,0,2:T(2,128)}, u32[]{:S(2)}) copy-start(s32[2,4,3]{1,0,2:T(2,128)} %param.7) | copy-start | bytes 292
  0.0 7.3 %copy-start = (bf16[256,2048]{1,0:T(8,128)(2,1)S(1)}, bf16[256,2048]{1,0:T(8,128)(2,1)}, u32[]{:S(2)}) copy-start(bf16[256,2048]{1,0:T(8,128)(2,1)} %q_ref.1) | copy-start | bytes 3145732
  2.0 12.3 %collective-permute-start.4 = (bf16[8,2,128,128]{3,2,1,0:T(8,128)(2,1)}, bf16[8,2,128,128]{3,2,1,0:T(8,128)(2,1)S(1)}, u32[]{:S(2)}, u32[]{:S(2)}) collective-permute-start(bf16[8,2,128,128]{3,2,1,0:T(8,128)(2,1)} %pack_kv.1), channel_id=1, source_target_pairs={{8,24},{0,8},{9,25},{1,9},{10,26},{2,10},{11,27},{3,11},{12,28},{4... | collective-permute-start | bytes 1572872 | tf_op jit(solution)/shard_map/ppermute | solution.py:305
  2.7 11.6 %all-to-all-start = ((bf16[8,2,128,128]{3,2,1,0:T(8,128)(2,1)}), bf16[8,2,128,128]{3,2,1,0:T(8,128)(2,1)S(1)}, u32[]{:S(2)}, u32[]{:S(2)}) async-start(bf16[8,2,128,128]{3,2,1,0:T(8,128)(2,1)} %pack_kv.1), calls=%async_computation | async-start | bytes 1048576 | tf_op jit(solution)/shard_map/all_to_all | solution.py:306
  8.0 17.9 %collective-permute-start.2 = (bf16[272,512]{1,0:T(8,128)(2,1)S(1)}, bf16[272,512]{1,0:T(8,128)(2,1)}, u32[]{:S(2)}, u32[]{:S(2)}) collective-permute-start(bf16[272,512]{1,0:T(8,128)(2,1)S(1)} %get-tuple-element.28), channel_id=1, source_target_pairs={{0,4},{2,6},{4,0},{6,2},{1,5},{3,7},{5,1},{7,3},{8,12},{10,14},{12... | collective-permute-start | bytes 835592 | tf_op jit(solution)/shard_map/ppermute | solution.py:298
  14.3 9.4 %copy-start.1 = (bf16[8,2,128,128]{3,2,1,0:T(8,128)(2,1)}, bf16[8,2,128,128]{3,2,1,0:T(8,128)(2,1)S(1)}, u32[]{:S(2)}) copy-start(bf16[8,2,128,128]{3,2,1,0:T(8,128)(2,1)S(1)} %collective-permute-done.4) | copy-start | bytes 1572868
  15.2 15.8 %collective-permute-start.5 = (bf16[4,2,128,128]{3,2,1,0:T(8,128)(2,1)S(1)}, bf16[4,2,128,128]{3,2,1,0:T(8,128)(2,1)S(1)}, u32[]{:S(2)}, u32[]{:S(2)}) collective-permute-start(bf16[4,2,128,128]{3,2,1,0:T(8,128)(2,1)S(1)} %get-tuple-element.30), channel_id=1, source_target_pairs={{0,16},{16,24},{1,17},{17,25},{2,18},{18,26},{3,19},{19,27},{4,20}... | collective-permute-start | bytes 786440 | tf_op jit(solution)/shard_map/ppermute | solution.py:318
  21.8 11.8 %collective-permute-start.6 = (bf16[4,2,128,128]{3,2,1,0:T(8,128)(2,1)}, bf16[4,2,128,128]{3,2,1,0:T(8,128)(2,1)S(1)}, u32[]{:S(2)}, u32[]{:S(2)}) collective-permute-start(bf16[4,2,128,128]{3,2,1,0:T(8,128)(2,1)} %get-tuple-element.31), channel_id=1, source_target_pairs={{0,16},{16,24},{1,17},{17,25},{2,18},{18,26},{3,19},{19,27},{4,20}... | collective-permute-start | bytes 786440 | tf_op jit(solution)/shard_map/ppermute | solution.py:318
  23.8 13.5 %collective-permute-start = (bf16[272,512]{1,0:T(8,128)(2,1)S(1)}, bf16[272,512]{1,0:T(8,128)(2,1)S(1)}, u32[]{:S(2)}, u32[]{:S(2)}) collective-permute-start(bf16[272,512]{1,0:T(8,128)(2,1)S(1)} %get-tuple-element.26), channel_id=1, source_target_pairs={{0,2},{2,0},{4,6},{6,4},{1,3},{3,1},{5,7},{7,5},{8,10},{10,8},{12,... | collective-permute-start | bytes 835592 | tf_op jit(solution)/shard_map/ppermute | solution.py:298
  25.7 11.6 %collective-permute-start.1 = (bf16[272,512]{1,0:T(8,128)(2,1)S(1)}, bf16[272,512]{1,0:T(8,128)(2,1)S(1)}, u32[]{:S(2)}, u32[]{:S(2)}) collective-permute-start(bf16[272,512]{1,0:T(8,128)(2,1)S(1)} %get-tuple-element.27), channel_id=1, source_target_pairs={{0,4},{2,6},{4,0},{6,2},{1,5},{3,7},{5,1},{7,3},{8,12},{10,14},{12... | collective-permute-start | bytes 835592 | tf_op jit(solution)/shard_map/ppermute | solution.py:298
  25.9 11.3 %collective-permute-start.3 = (bf16[272,512]{1,0:T(8,128)(2,1)}, bf16[272,512]{1,0:T(8,128)(2,1)S(1)}, u32[]{:S(2)}, u32[]{:S(2)}) collective-permute-start(bf16[272,512]{1,0:T(8,128)(2,1)} %collective-permute-done.2), channel_id=1, source_target_pairs={{0,2},{2,0},{4,6},{6,4},{1,3},{3,1},{5,7},{7,5},{8,10},{10,8},{12,... | collective-permute-start | bytes 835592 | tf_op jit(solution)/shard_map/ppermute | solution.py:298
  26.3 13.2 %all-to-all-start.1 = ((bf16[8,2,128,128]{3,2,1,0:T(8,128)(2,1)}), bf16[8,2,128,128]{3,2,1,0:T(8,128)(2,1)S(1)}, u32[]{:S(2)}, u32[]{:S(2)}) async-start(bf16[8,2,128,128]{3,2,1,0:T(8,128)(2,1)} %copy-done.1), calls=%async_computation.1 | async-start | bytes 1048576 | tf_op jit(solution)/shard_map/all_to_all | solution.py:319
  31.7 15.8 %collective-permute-start.7 = (bf16[4,2,128,128]{3,2,1,0:T(8,128)(2,1)}, bf16[4,2,128,128]{3,2,1,0:T(8,128)(2,1)S(1)}, u32[]{:S(2)}, u32[]{:S(2)}) collective-permute-start(bf16[4,2,128,128]{3,2,1,0:T(8,128)(2,1)} %broadcast_select_fusion.1), channel_id=1, source_target_pairs={{16,24},{8,16},{17,25},{9,17},{18,26},{10,18},{19,27},{11,19},{20,... | collective-permute-start | bytes 786440 | tf_op jit(solution)/shard_map/ppermute | solution.py:324
  34.3 13.2 %collective-permute-start.8 = (bf16[4,2,128,128]{3,2,1,0:T(8,128)(2,1)}, bf16[4,2,128,128]{3,2,1,0:T(8,128)(2,1)}, u32[]{:S(2)}, u32[]{:S(2)}) collective-permute-start(bf16[4,2,128,128]{3,2,1,0:T(8,128)(2,1)} %broadcast_select_fusion), channel_id=1, source_target_pairs={{16,24},{8,16},{17,25},{9,17},{18,26},{10,18},{19,27},{11,19},{20,... | collective-permute-start | bytes 786440 | tf_op jit(solution)/shard_map/ppermute | solution.py:324
  51.9 14.2 %collective-permute-start.10 = (bf16[256,512]{1,0:T(8,128)(2,1)S(1)}, bf16[256,512]{1,0:T(8,128)(2,1)S(1)}, u32[]{:S(2)}, u32[]{:S(2)}) collective-permute-start(bf16[256,512]{1,0:T(8,128)(2,1)S(1)} %get-tuple-element.39), channel_id=1, source_target_pairs={{0,4},{2,6},{4,0},{6,2},{1,5},{3,7},{5,1},{7,3},{8,12},{10,14},{12... | collective-permute-start | bytes 786440 | tf_op jit(solution)/shard_map/ppermute | solution.py:298
  52.2 13.9 %collective-permute-start.11 = (bf16[256,512]{1,0:T(8,128)(2,1)S(1)}, bf16[256,512]{1,0:T(8,128)(2,1)S(1)}, u32[]{:S(2)}, u32[]{:S(2)}) collective-permute-start(bf16[256,512]{1,0:T(8,128)(2,1)S(1)} %get-tuple-element.40), channel_id=1, source_target_pairs={{0,6},{2,4},{4,2},{6,0},{1,7},{3,5},{5,3},{7,1},{8,14},{10,12},{12... | collective-permute-start | bytes 786440 | tf_op jit(solution)/shard_map/ppermute | solution.py:298
  66.1 1.6 %collective-permute-start.9 = (bf16[256,512]{1,0:T(8,128)(2,1)S(1)}, bf16[256,512]{1,0:T(8,128)(2,1)S(1)}, u32[]{:S(2)}, u32[]{:S(2)}) collective-permute-start(bf16[256,512]{1,0:T(8,128)(2,1)S(1)} %get-tuple-element.44), channel_id=1, source_target_pairs={{0,2},{2,0},{4,6},{6,4},{1,3},{3,1},{5,7},{7,5},{8,10},{10,8},{12,... | collective-permute-start | bytes 786440 | tf_op jit(solution)/shard_map/ppermute | solution.py:298

commit v7 on v6

--- a/solution.py
+++ b/solution.py
@@ -121,13 +121,15 @@
     parts, rows = len(queries), queries[0].shape[0] - EXTRA
     tiles_in_part = rows // TILE
     tiles_here = len(partners) * tiles_in_part
+    in_block = BLK // TILE
     r = sources[0].shape[2]
     per_block = BLK // r
     n_src = len(sources)
     slots = [src.shape[0] // per_block for src in sources]
-    most = min(TOPK, sum(slots))
+    n_slots = sum(slots)
     n_q = len(partners)
-    n_out = len(partners) if last else 2
+    n_out = n_q if last else 2
+    one_block = parts > 1 and len(partners) * rows == BLK
 
     def kernel(*refs):
         sel_ref, q_refs = refs[0], refs[1 : 1 + n_q]
@@ -135,14 +137,18 @@
         rest = refs[1 + n_q + n_src :]
         m_in, acc_in = (None, None) if first else rest[:2]
         rest = rest if first else rest[2:]
-        outs, k_buf, v_buf, m_tmp, acc_tmp, q_buf = rest[:n_out], *rest[n_out:]
+        outs, k_buf, v_buf, q_buf, item_tile, item_slot = rest[:n_out], *rest[n_out : n_out + 5]
+        m_ref, acc_ref = rest[n_out + 5 :] if last else outs
         level = lax.axis_index("lev")
         sub = lax.axis_index("sub") if parts > 1 else 0
         for i, q_ref in enumerate(q_refs):
             q_buf[i] = q_ref[:rows]
+        if not first:
+            m_ref[:tiles_here] = m_in[:tiles_here]
+            acc_ref[:tiles_here] = acc_in[:tiles_here]
         bases = bases_of(level)
 
-        v_buf[:, HD:] = jnp.ones((sum(slots) * BLK, HD), BF16)
+        v_buf[:, HD:] = jnp.ones((n_slots * BLK, HD), BF16)
         start = 0
         for ref, base, n in zip(src, bases, slots):
 
@@ -166,104 +172,124 @@
                 pl.when(base >= 0)(fill)
             start += n
 
-        def one_tile(k, part, i, out_ref, out_at):
-            t = part * tiles_in_part + i
-            tile = (level * parts + (sub ^ k)) * tiles_in_part + i
-            own = tile * TILE // BLK
-            q_rows = pl.ds(pl.multiple_of(i * TILE, TILE), TILE)
-            m_old, acc_old, at_old = (m_tmp, acc_tmp, 0) if first else (m_in, acc_in, t)
-
-            def finish(j, acc):
-                out_ref[out_at, j * HD : (j + 1) * HD] = (acc[:, :HD] / acc[:, HD:]).astype(BF16)
-
-            def keep(j, m, acc):
-                outs[0][t, j * TILE : (j + 1) * TILE] = m
-                outs[1][t, j * TILE : (j + 1) * TILE] = acc
-
-            def own_part(pieces):
-                count = pieces * TILE
-                at = pl.ds(pl.multiple_of((own - bases[0]) * BLK, BLK), count)
-                key_at = lax.broadcasted_iota(jnp.int32, (TILE, TILE), 1)
-                query_at = lax.broadcasted_iota(jnp.int32, (TILE, TILE), 0)
+        def tile_of(t):
+            k = partners[0] + t // tiles_in_part
+            return (level * parts + (sub ^ k)) * tiles_in_part + lax.rem(t, tiles_in_part)
+
+        def q_of(t, j):
+            at = pl.ds(pl.multiple_of(lax.rem(t, tiles_in_part) * TILE, TILE), TILE)
+            return q_buf[t // tiles_in_part, at, j * HD : (j + 1) * HD]
+
+        def heads_rows(j):
+            return slice(j * TILE, (j + 1) * TILE)
+
+        def slot_rows(slot, count=BLK):
+            return pl.ds(pl.multiple_of(slot * BLK, BLK), count)
+
+        def own_part(t, slot, pieces):
+            count = pieces * TILE
+            at = slot_rows(slot, count)
+            key_at = lax.broadcasted_iota(jnp.int32, (TILE, TILE), 1)
+            query_at = lax.broadcasted_iota(jnp.int32, (TILE, TILE), 0)
+            for j in range(PER):
+                s = dot_nt(q_of(t, j), k_buf[at])
+                edge = jnp.where(key_at <= query_at, s[:, count - TILE :], FLOOR)
+                s = jnp.concatenate([s[:, : count - TILE], edge], axis=1) if pieces > 1 else edge
+                m = jnp.max(s, axis=1, keepdims=True)
+                p = jnp.exp2((s - m) * SCALE).astype(BF16)
+                m_ref[t, heads_rows(j)] = jnp.broadcast_to(m, (TILE, HD))
+                acc_ref[t, heads_rows(j)] = dot_nn(p, v_buf[at])
+
+        if first and one_block:
+            own = tile_of(0) // in_block
+            for i in range(in_block):
+                part = own * (in_block // tiles_in_part) + i // tiles_in_part - level * parts
+                t = ((part ^ sub) - partners[0]) * tiles_in_part + i % tiles_in_part
+                own_part(t, own - bases[0], i + 1)
+        elif first:
+
+            def own_tile(t, carry):
+                tile = tile_of(t)
+                for pieces in range(1, in_block + 1):
+                    pl.when(lax.rem(tile, in_block) == pieces - 1)(
+                        functools.partial(own_part, t, tile // in_block - bases[0], pieces)
+                    )
+                return carry
+
+            lax.fori_loop(0, tiles_here, own_tile, 0)
+
+        picks = [
+            [sel_ref[(partners[0] * tiles_in_part + t) * TOPK + e] for e in range(TOPK)]
+            for t in range(tiles_here)
+        ]
+        owns = [tile_of(jnp.int32(t)) // in_block for t in range(tiles_here)]
+
+        def list_slot(slot, block, carry):
+            count, before = carry
+            for t in range(tiles_here):
+                hit = functools.reduce(jnp.logical_or, [pick == block for pick in picks[t]])
+                hit = hit & (block != owns[t]) & (block >= 0)
+                clash = hit & (before == t) & (lax.rem(count, 2) == 1)
+                item_tile[count] = tiles_here
+                item_slot[count] = slot
+                put = jnp.where(clash, count + 1, count)
+                item_tile[put] = t
+                item_slot[put] = slot
+                count = jnp.where(hit, put + 1, count)
+                before = jnp.where(hit, t, before)
+            return count, before
+
+        carry = (jnp.int32(0), jnp.int32(-1))
+        start = 0
+        for base, n in zip(bases, slots):
+            if n <= 2:
+                for i in range(n):
+                    carry = list_slot(start + i, base + i, carry)
+            else:
+                carry = lax.fori_loop(
+                    0,
+                    n,
+                    lambda i, c, start=start, base=base: list_slot(start + i, base + i, c),
+                    carry,
+                )
+            start += n
+        count = carry[0]
+        item_tile[count] = tiles_here
+        item_slot[count] = 0
+
+        def two_items(i, carry):
+            pair = [(item_tile[2 * i + x], item_slot[2 * i + x]) for x in range(2)]
+            olds = [[m_ref[t, heads_rows(j)] for j in range(PER)] for t, _ in pair]
+            for j in range(PER):
+                for (t, slot), old in zip(pair, olds):
+                    at = slot_rows(slot)
+                    s = dot_nt(q_of(jnp.minimum(t, tiles_here - 1), j), k_buf[at])
+                    m = jnp.maximum(old[j], jnp.max(s, axis=1, keepdims=True))
+                    p = jnp.exp2((s - jnp.tile(m, (1, BLK // HD))) * SCALE).astype(BF16)
+                    fade = jnp.exp2((old[j] - m) * SCALE)
+                    m_ref[t, heads_rows(j)] = m
+                    acc_ref[t, heads_rows(j)] = acc_ref[t, heads_rows(j)] * jnp.tile(
+                        fade, (1, 2)
+                    ) + dot_nn(p, v_buf[at])
+            return carry
+
+        lax.fori_loop(0, (count + 1) // 2, two_items, 0)
+
+        if last:
+            for t in range(tiles_here):
+                at = slice(t % tiles_in_part * TILE, (t % tiles_in_part + 1) * TILE)
                 for j in range(PER):
-                    s = dot_nt(q_buf[part, q_rows, j * HD : (j + 1) * HD], k_buf[at])
-                    edge = jnp.where(key_at <= query_at, s[:, count - TILE :], FLOOR)
-                    s = jnp.concatenate([s[:, : count - TILE], edge], axis=1) if pieces > 1 else edge
-                    m = jnp.max(s, axis=1, keepdims=True)
-                    p = jnp.exp2((s - m) * SCALE).astype(BF16)
-                    m_tmp[0, j * TILE : (j + 1) * TILE] = jnp.broadcast_to(m, (TILE, HD))
-                    acc_tmp[0, j * TILE : (j + 1) * TILE] = dot_nn(p, v_buf[at])
-
-            if first:
-                for pieces in range(1, BLK // TILE + 1):
-                    pl.when(lax.rem(tile, BLK // TILE) == pieces - 1)(
-                        functools.partial(own_part, pieces)
-                    )
-
-            found = jnp.int32(0)
-            where = [jnp.int32(0)] * most
-            for e in range(TOPK):
-                block = sel_ref[(k * tiles_in_part + i) * TOPK + e]
-                start = 0
-                for base, n in zip(bases, slots):
-                    hit = (block != own) & (block >= base) & (block < base + n)
-                    where = [
-                        jnp.where(hit & (found == i), start + block - base, w)
-                        for i, w in enumerate(where)
-                    ]
-                    found = found + hit.astype(jnp.int32)
-                    start += n
-
-            def others(n):
-                at = [pl.ds(pl.multiple_of(w * BLK, BLK), BLK) for w in where[:n]]
-                for j in range(PER):
-                    here = slice(j * TILE, (j + 1) * TILE)
-                    old = m_old[at_old, here]
-                    acc = acc_old[at_old, here]
-                    if n:
-                        q = q_buf[part, q_rows, j * HD : (j + 1) * HD]
-                        s = [dot_nt(q, k_buf[a]) for a in at]
-                        s = jnp.concatenate(s, axis=1) if n > 1 else s[0]
-                        m = jnp.maximum(old, jnp.max(s, axis=1, keepdims=True))
-                        p = jnp.exp2((s - jnp.tile(m, (1, n * BLK // HD))) * SCALE).astype(BF16)
-                        fade = jnp.exp2((old - m) * SCALE)
-                        acc = acc * jnp.tile(fade, (1, 2))
-                        for i, a in enumerate(at):
-                            acc = acc + dot_nn(p[:, i * BLK : (i + 1) * BLK], v_buf[a])
-                        old = m
-                    if last:
-                        finish(j, acc)
-                    else:
-                        keep(j, old, acc)
-
-            for n in range(most + 1):
-                pl.when(found == n)(functools.partial(others, n))
-
-        if last:
-            for part, (out_ref, k) in enumerate(zip(outs, partners)):
-
-                def step(i, carry, out_ref=out_ref, k=k, part=part):
-                    out_at = pl.ds(pl.multiple_of(i * TILE, TILE), TILE)
-                    one_tile(k, part, i, out_ref, out_at)
-                    return carry
-
-                lax.fori_loop(0, tiles_in_part, step, 0)
-        else:
-
-            def step(t, carry):
-                part = t // tiles_in_part
-                one_tile(partners[0] + part, part, lax.rem(t, tiles_in_part), None, None)
-                return carry
-
-            lax.fori_loop(0, tiles_here, step, 0)
-
+                    acc = acc_ref[t, heads_rows(j)]
+                    outs[t // tiles_in_part][at, j * HD : (j + 1) * HD] = (
+                        acc[:, :HD] / acc[:, HD:]
+                    ).astype(BF16)
+
+    kept = [(tiles_here + 1, QW, HD), (tiles_here + 1, QW, 2 * HD)]
     if last:
         out_shape = tuple(jax.ShapeDtypeStruct((rows, QW), BF16) for _ in partners)
     else:
-        out_shape = (
-            jax.ShapeDtypeStruct((tiles_here, QW, HD), F32),
-            jax.ShapeDtypeStruct((tiles_here, QW, 2 * HD), F32),
-        )
+        out_shape = tuple(jax.ShapeDtypeStruct(shape, F32) for shape in kept)
+    items = 2 * tiles_here * TOPK + 4
     work = tiles_here * QW * BLK * 3 // 2
     return pl.pallas_call(
         kernel,
@@ -271,14 +297,15 @@
         out_shape=out_shape,
         out_specs=(VMEM,) * n_out,
         scratch_shapes=[
-            pltpu.VMEM((sum(slots) * BLK, HD), BF16),
-            pltpu.VMEM((sum(slots) * BLK, 2 * HD), BF16),
-            pltpu.VMEM((1, QW, HD), F32),
-            pltpu.VMEM((1, QW, 2 * HD), F32),
+            pltpu.VMEM((n_slots * BLK, HD), BF16),
+            pltpu.VMEM((n_slots * BLK, 2 * HD), BF16),
             pltpu.VMEM((n_q, rows, QW), BF16),
-        ],
+            pltpu.SMEM((items,), jnp.int32),
+            pltpu.SMEM((items,), jnp.int32),
+        ]
+        + ([pltpu.VMEM(shape, F32) for shape in kept] if last else []),
         compiler_params=pltpu.CompilerParams(
-            vmem_limit_bytes=(24 if sum(slots) <= 16 else 56) * MIB
+            vmem_limit_bytes=(24 if n_slots <= 16 else 56) * MIB
         ),
         cost_estimate=pl.CostEstimate(
             flops=8 * work * HD, transcendentals=work, bytes_accessed=4 * MIB

time: 68.7 us -> 68.4 us (level)
  Pallas kernels: 27.4 us -> 26.2 us
    pallas_call x3, Pallas kernels: 23 us -> 21.9 us  [attention(): pl.pallas_call(kernel, in_specs=[SMEM] + [VMEM] * (n_q + n_src + len(stat...]
  transfers between devices with their start and end apart: 14 -> 14, of which waited for: 3 -> 4; matrix products, arithmetic and copies ran while one was open for 4% -> 5% of each run, Pallas kernels for 29% -> 28%
where the time goes in v7:
time: 68.4 us; the launch traced here: 67.8 us
  starting transfers between devices  30.1 us (44%)
  Pallas kernels  26.2 us (38%)
  waiting for transfers between devices  8.2 us (12%)
  local copies, waits for them, and re-layouts  1.6 us (2%)
  other arithmetic  1.56 us (2%)
    pallas_call x3, Pallas kernels, attention(): pl.pallas_call(kernel, in_specs=[SMEM] + [VMEM] * (n_q + n_src + len(stat...  21.9 us
    ppermute x2, starting transfers between devices, body(): up = [lax.ppermute(piece, 'lev', [(0, 2), (2, 3)]) for piece in halves]  8.58 us
    ppermute x7, starting transfers between devices, exchange(): lax.ppermute(piece, 'sub', [(i, i ^ k) for i in range(subs)])  6.8 us
    all_to_all x1, waiting for transfers between devices, body(): own = lax.all_to_all(packed, ('sub', 'head'), 0, 0, tiled=True)  5.28 us
    ppermute x2, starting transfers between devices, body(): lax.ppermute(jnp.where(forwards, a, b), 'lev', [(2, 3), (1, 2)])  4.81 us
    all_to_all x1, starting transfers between devices, body(): p2 = lax.all_to_all(raw, ('sub', 'head'), 0, 0, tiled=True)  4.66 us
    all_to_all x1, starting transfers between devices, body(): own = lax.all_to_all(packed, ('sub', 'head'), 0, 0, tiled=True)  4.52 us
    all_to_all x1, waiting for transfers between devices, body(): p2 = lax.all_to_all(raw, ('sub', 'head'), 0, 0, tiled=True)  2.12 us
  transfers between devices with their start and end apart: 14, of which 4 were waited for; matrix products, arithmetic and copies ran while one was open for 5% of the time, Pallas kernels for 28%

profile of v7, /device:TPU:23, one launch (start us, length us, event | category | flops | bytes accessed | tf_op | source)
XLA Modules:
  0.0 67.8 jit_solution(9388563609153114745)
XLA Ops:
  0.0 2.0 %pack_kv.1 = bf16[8,2,128,128]{3,2,1,0:T(8,128)(2,1)} custom-call(bf16[128,1024]{1,0:T(8,128)(2,1)} %k_ref.1, bf16[128,1024]{1,0:T(8,128)(2,1)} %v_ref.1), custom_call_target="tpu_custom_call" | custom-call | bytes 1048576 | tf_op jit(solution)/shard_map/pack_kv/pallas_call | solution.py:54
  2.0 0.7 %collective-permute-start.4 = (bf16[8,2,128,128]{3,2,1,0:T(8,128)(2,1)}, bf16[8,2,128,128]{3,2,1,0:T(8,128)(2,1)S(1)}, u32[]{:S(2)}, u32[]{:S(2)}) collective-permute-start(bf16[8,2,128,128]{3,2,1,0:T(8,128)(2,1)} %pack_kv.1), channel_id=1, source_target_pairs={{8,24},{0,8},{9,25},{1,9},{10,26},{2,10},{11,27},{3,11},{12,28},{4... | collective-permute-start | bytes 1572872 | tf_op jit(solution)/shard_map/ppermute | solution.py:332
  2.7 4.5 %all-to-all-start = ((bf16[8,2,128,128]{3,2,1,0:T(8,128)(2,1)}), bf16[8,2,128,128]{3,2,1,0:T(8,128)(2,1)S(1)}, u32[]{:S(2)}, u32[]{:S(2)}) async-start(bf16[8,2,128,128]{3,2,1,0:T(8,128)(2,1)} %pack_kv.1), calls=%async_computation | async-start | bytes 1048576 | tf_op jit(solution)/shard_map/all_to_all | solution.py:333
  7.2 0.8 %copy.6.sel_ref = s32[2,4,3]{2,1,0:T(4,128)S(1)} copy(s32[2,4,3]{1,0,2:T(2,128)} %param.7) | data formatting | bytes 192 | tf_op args[3]
  8.0 0.7 %pack_q.1 = (bf16[272,512]{1,0:T(8,128)(2,1)S(1)}, bf16[272,512]{1,0:T(8,128)(2,1)S(1)}, bf16[272,512]{1,0:T(8,128)(2,1)S(1)}, bf16[272,512]{1,0:T(8,128)(2,1)S(1)}) custom-call(s32[2,4,3]{2,1,0:T(4,128)S(1)} %copy.6.sel_ref, bf16[256,2048]{1,0:T(8,128)(2,1)S(1)} %copy-done), custom_call_target="tpu_custom_call" | custom-call | bytes 2097152 | tf_op jit(solution)/shard_map/pack_q/pallas_call | solution.py:80
  8.7 0.3 collective-permute-start.2
  9.0 5.3 %all-to-all-done.refs_3_ = bf16[8,2,128,128]{3,2,1,0:T(8,128)(2,1)S(1)} async-done(((bf16[8,2,128,128]{3,2,1,0:T(8,128)(2,1)}), bf16[8,2,128,128]{3,2,1,0:T(8,128)(2,1)S(1)}, u32[]{:S(2)}, u32[]{:S(2)}) %all-to-all-start) | async-done | bytes 524320 | tf_op jit(solution)/shard_map/all_to_all | solution.py:333
  14.3 0.8 %fusion = (bf16[4,2,128,128]{3,2,1,0:T(8,128)(2,1)}, bf16[4,2,128,128]{3,2,1,0:T(8,128)(2,1)S(1)}) fusion(bf16[8,2,128,128]{3,2,1,0:T(8,128)(2,1)S(1)} %all-to-all-done.refs_3_), kind=kLoop, calls=%fused_computation.7 | loop fusion | bytes 1048576 | tf_op jit(solution)/shard_map/slice | solution.py:344
  15.1 6.7 %collective-permute-start.5 = (bf16[4,2,128,128]{3,2,1,0:T(8,128)(2,1)S(1)}, bf16[4,2,128,128]{3,2,1,0:T(8,128)(2,1)S(1)}, u32[]{:S(2)}, u32[]{:S(2)}) collective-permute-start(bf16[4,2,128,128]{3,2,1,0:T(8,128)(2,1)S(1)} %get-tuple-element.30), channel_id=1, source_target_pairs={{0,16},{16,24},{1,17},{17,25},{2,18},{18,26},{3,19},{19,27},{4,20}... | collective-permute-start | bytes 786440 | tf_op jit(solution)/shard_map/ppermute | solution.py:345
  21.8 1.9 %collective-permute-start.6 = (bf16[4,2,128,128]{3,2,1,0:T(8,128)(2,1)}, bf16[4,2,128,128]{3,2,1,0:T(8,128)(2,1)S(1)}, u32[]{:S(2)}, u32[]{:S(2)}) collective-permute-start(bf16[4,2,128,128]{3,2,1,0:T(8,128)(2,1)} %get-tuple-element.31), channel_id=1, source_target_pairs={{0,16},{16,24},{1,17},{17,25},{2,18},{18,26},{3,19},{19,27},{4,20}... | collective-permute-start | bytes 786440 | tf_op jit(solution)/shard_map/ppermute | solution.py:345
  23.7 1.9 %collective-permute-start = (bf16[272,512]{1,0:T(8,128)(2,1)S(1)}, bf16[272,512]{1,0:T(8,128)(2,1)S(1)}, u32[]{:S(2)}, u32[]{:S(2)}) collective-permute-start(bf16[272,512]{1,0:T(8,128)(2,1)S(1)} %get-tuple-element.26), channel_id=1, source_target_pairs={{0,2},{2,0},{4,6},{6,4},{1,3},{3,1},{5,7},{7,5},{8,10},{10,8},{12,... | collective-permute-start | bytes 835592 | tf_op jit(solution)/shard_map/ppermute | solution.py:325
  25.6 0.3 collective-permute-start.1
  25.9 0.0 collective-permute-done.2
  25.9 0.3 collective-permute-start.3
  26.2 4.7 %all-to-all-start.1 = ((bf16[8,2,128,128]{3,2,1,0:T(8,128)(2,1)}), bf16[8,2,128,128]{3,2,1,0:T(8,128)(2,1)S(1)}, u32[]{:S(2)}, u32[]{:S(2)}) async-start(bf16[8,2,128,128]{3,2,1,0:T(8,128)(2,1)} %copy-done.1), calls=%async_computation.1 | async-start | bytes 1048576 | tf_op jit(solution)/shard_map/all_to_all | solution.py:346
  30.9 0.7 %broadcast_select_fusion.1 = bf16[4,2,128,128]{3,2,1,0:T(8,128)(2,1)} fusion(bf16[4,2,128,128]{3,2,1,0:T(8,128)(2,1)S(1)} %collective-permute-done.5.refs_4_, bf16[4,2,128,128]{3,2,1,0:T(8,128)(2,1)S(1)} %get-tuple-element.30, pred[]{:T(512)S(6)} %eq.3), kind=kLoop, calls=%fused_computation.1 | loop fusion | flops 131072 | bytes 786433 | tf_op jit(solution)/shard_map/jit(_where)/select_n | solution.py:351
  31.7 1.9 %collective-permute-start.7 = (bf16[4,2,128,128]{3,2,1,0:T(8,128)(2,1)}, bf16[4,2,128,128]{3,2,1,0:T(8,128)(2,1)S(1)}, u32[]{:S(2)}, u32[]{:S(2)}) collective-permute-start(bf16[4,2,128,128]{3,2,1,0:T(8,128)(2,1)} %broadcast_select_fusion.1), channel_id=1, source_target_pairs={{16,24},{8,16},{17,25},{9,17},{18,26},{10,18},{19,27},{11,19},{20,... | collective-permute-start | bytes 786440 | tf_op jit(solution)/shard_map/ppermute | solution.py:351
  33.6 0.7 %broadcast_select_fusion = bf16[4,2,128,128]{3,2,1,0:T(8,128)(2,1)} fusion(bf16[4,2,128,128]{3,2,1,0:T(8,128)(2,1)S(1)} %collective-permute-done.6.refs_5_, bf16[4,2,128,128]{3,2,1,0:T(8,128)(2,1)} %get-tuple-element.31, pred[]{:T(512)S(6)} %eq.3), kind=kLoop, calls=%fused_computation | loop fusion | flops 131072 | bytes 786433 | tf_op jit(solution)/shard_map/jit(_where)/select_n | solution.py:351
  34.3 2.9 %collective-permute-start.8 = (bf16[4,2,128,128]{3,2,1,0:T(8,128)(2,1)}, bf16[4,2,128,128]{3,2,1,0:T(8,128)(2,1)}, u32[]{:S(2)}, u32[]{:S(2)}) collective-permute-start(bf16[4,2,128,128]{3,2,1,0:T(8,128)(2,1)} %broadcast_select_fusion), channel_id=1, source_target_pairs={{16,24},{8,16},{17,25},{9,17},{18,26},{10,18},{19,27},{11,19},{20,... | collective-permute-start | bytes 786440 | tf_op jit(solution)/shard_map/ppermute | solution.py:351
  37.2 0.0 collective-permute-done.refs_2_
  37.3 0.1 maximum_convert_fusion.refs_0_
  37.4 2.1 %all-to-all-done.1.refs_6_ = bf16[8,2,128,128]{3,2,1,0:T(8,128)(2,1)S(1)} async-done(((bf16[8,2,128,128]{3,2,1,0:T(8,128)(2,1)}), bf16[8,2,128,128]{3,2,1,0:T(8,128)(2,1)S(1)}, u32[]{:S(2)}, u32[]{:S(2)}) %all-to-all-start.1) | async-done | bytes 524320 | tf_op jit(solution)/shard_map/all_to_all | solution.py:346
  39.5 7.4 %far_early.1 = (f32[5,512,128]{2,1,0:T(8,128)S(1)}, f32[5,512,256]{2,1,0:T(8,128)S(1)}) custom-call(s32[24]{0:T(128)S(1)} %maximum_convert_fusion.refs_0_, bf16[272,512]{1,0:T(8,128)(2,1)S(1)} %collective-permute-done.1.refs_1_, bf16[272,512]{1,0:T(8,128)(2,1)S(1)} %collective-permute-done.3.refs_2_, bf16[8,2,128,128]{3,2,1,0:T(8,128)(2,1)S(1)} %all-to-all-done.refs_3_, ...), custom_call_target="tpu_custom_call" | custom-call | flops 1610612736 | bytes 4194304 | tf_op jit(solution)/shard_map/far_early/pallas_call | solution.py:294
  46.9 0.1 collective-permute-done.8.refs_4_.refs_8_
  47.0 4.5 %far_late.1 = (bf16[256,512]{1,0:T(8,128)(2,1)S(1)}, bf16[256,512]{1,0:T(8,128)(2,1)S(1)}) custom-call(s32[24]{0:T(128)S(1)} %maximum_convert_fusion.refs_0_, bf16[272,512]{1,0:T(8,128)(2,1)S(1)} %collective-permute-done.1.refs_1_, bf16[272,512]{1,0:T(8,128)(2,1)S(1)} %collective-permute-done.3.refs_2_, ...), custom_call_target="tpu_custom_call" | custom-call | flops 1610612736 | bytes 4194304 | tf_op jit(solution)/shard_map/far_late/pallas_call | solution.py:294
  51.5 0.3 collective-permute-start.10
  51.8 3.6 %collective-permute-start.11 = (bf16[256,512]{1,0:T(8,128)(2,1)S(1)}, bf16[256,512]{1,0:T(8,128)(2,1)S(1)}, u32[]{:S(2)}, u32[]{:S(2)}) collective-permute-start(bf16[256,512]{1,0:T(8,128)(2,1)S(1)} %get-tuple-element.40), channel_id=1, source_target_pairs={{0,6},{2,4},{4,2},{6,0},{1,7},{3,5},{5,3},{7,1},{8,14},{10,12},{12... | collective-permute-start | bytes 786440 | tf_op jit(solution)/shard_map/ppermute | solution.py:325
  55.4 10.0 %near.1 = (bf16[256,512]{1,0:T(8,128)(2,1)S(1)}, bf16[256,512]{1,0:T(8,128)(2,1)S(1)}) custom-call(s32[24]{0:T(128)S(1)} %maximum_convert_fusion.refs_0_, bf16[272,512]{1,0:T(8,128)(2,1)S(1)} %get-tuple-element.41.refs_1_, bf16[272,512]{1,0:T(8,128)(2,1)S(1)} %collective-permute-done.refs_2_, bf16[8,2,128,128]{3,2,1,0:T(8,128)(2,1)S(1)} %all-to-all-done.refs_3_, ...), custom_call_target="tpu_custom_call" | custom-call | flops 1610612736 | bytes 4194304 | tf_op jit(solution)/shard_map/near/pallas_call | solution.py:294
  65.4 0.1 collective-permute-start.9
  65.5 0.8 %unpack_far.1.refs_2_ = bf16[256,2048]{1,0:T(8,128)(2,1)} custom-call(bf16[256,512]{1,0:T(8,128)(2,1)S(1)} %collective-permute-done.10.refs_0_, bf16[256,512]{1,0:T(8,128)(2,1)S(1)} %collective-permute-done.11.refs_1_), custom_call_target="tpu_custom_call" | custom-call | bytes 1048576 | tf_op jit(solution)/shard_map/unpack_far/pallas_call | solution.py:107
  66.3 0.7 collective-permute-done.9.refs_1_
  67.0 0.8 %unpack_near.1 = bf16[256,2048]{1,0:T(8,128)(2,1)} custom-call(bf16[256,512]{1,0:T(8,128)(2,1)S(1)} %get-tuple-element.43.refs_0_, bf16[256,512]{1,0:T(8,128)(2,1)S(1)} %collective-permute-done.9.refs_1_, bf16[256,2048]{1,0:T(8,128)(2,1)} %unpack_far.1.refs_2_), custom_call_target="tpu_custom_call", output_to_operand_aliasing={{}: (2, {})} | custom-call | bytes 1048576 | tf_op jit(solution)/shard_map/unpack_near/pallas_call | solution.py:107
  (14 shorter events, 0.0 us)
Async XLA Ops:
  0.0 8.0 %copy-start = (bf16[256,2048]{1,0:T(8,128)(2,1)S(1)}, bf16[256,2048]{1,0:T(8,128)(2,1)}, u32[]{:S(2)}) copy-start(bf16[256,2048]{1,0:T(8,128)(2,1)} %q_ref.1) | copy-start | bytes 3145732
  2.0 12.3 %collective-permute-start.4 = (bf16[8,2,128,128]{3,2,1,0:T(8,128)(2,1)}, bf16[8,2,128,128]{3,2,1,0:T(8,128)(2,1)S(1)}, u32[]{:S(2)}, u32[]{:S(2)}) collective-permute-start(bf16[8,2,128,128]{3,2,1,0:T(8,128)(2,1)} %pack_kv.1), channel_id=1, source_target_pairs={{8,24},{0,8},{9,25},{1,9},{10,26},{2,10},{11,27},{3,11},{12,28},{4... | collective-permute-start | bytes 1572872 | tf_op jit(solution)/shard_map/ppermute | solution.py:332
  2.7 11.6 %all-to-all-start = ((bf16[8,2,128,128]{3,2,1,0:T(8,128)(2,1)}), bf16[8,2,128,128]{3,2,1,0:T(8,128)(2,1)S(1)}, u32[]{:S(2)}, u32[]{:S(2)}) async-start(bf16[8,2,128,128]{3,2,1,0:T(8,128)(2,1)} %pack_kv.1), calls=%async_computation | async-start | bytes 1048576 | tf_op jit(solution)/shard_map/all_to_all | solution.py:333
  8.7 17.2 %collective-permute-start.2 = (bf16[272,512]{1,0:T(8,128)(2,1)S(1)}, bf16[272,512]{1,0:T(8,128)(2,1)}, u32[]{:S(2)}, u32[]{:S(2)}) collective-permute-start(bf16[272,512]{1,0:T(8,128)(2,1)S(1)} %get-tuple-element.28), channel_id=1, source_target_pairs={{0,4},{2,6},{4,0},{6,2},{1,5},{3,7},{5,1},{7,3},{8,12},{10,14},{12... | collective-permute-start | bytes 835592 | tf_op jit(solution)/shard_map/ppermute | solution.py:325
  14.3 9.4 %copy-start.1 = (bf16[8,2,128,128]{3,2,1,0:T(8,128)(2,1)}, bf16[8,2,128,128]{3,2,1,0:T(8,128)(2,1)S(1)}, u32[]{:S(2)}) copy-start(bf16[8,2,128,128]{3,2,1,0:T(8,128)(2,1)S(1)} %collective-permute-done.4) | copy-start | bytes 1572868
  15.1 15.8 %collective-permute-start.5 = (bf16[4,2,128,128]{3,2,1,0:T(8,128)(2,1)S(1)}, bf16[4,2,128,128]{3,2,1,0:T(8,128)(2,1)S(1)}, u32[]{:S(2)}, u32[]{:S(2)}) collective-permute-start(bf16[4,2,128,128]{3,2,1,0:T(8,128)(2,1)S(1)} %get-tuple-element.30), channel_id=1, source_target_pairs={{0,16},{16,24},{1,17},{17,25},{2,18},{18,26},{3,19},{19,27},{4,20}... | collective-permute-start | bytes 786440 | tf_op jit(solution)/shard_map/ppermute | solution.py:345
  21.8 11.8 %collective-permute-start.6 = (bf16[4,2,128,128]{3,2,1,0:T(8,128)(2,1)}, bf16[4,2,128,128]{3,2,1,0:T(8,128)(2,1)S(1)}, u32[]{:S(2)}, u32[]{:S(2)}) collective-permute-start(bf16[4,2,128,128]{3,2,1,0:T(8,128)(2,1)} %get-tuple-element.31), channel_id=1, source_target_pairs={{0,16},{16,24},{1,17},{17,25},{2,18},{18,26},{3,19},{19,27},{4,20}... | collective-permute-start | bytes 786440 | tf_op jit(solution)/shard_map/ppermute | solution.py:345
  23.7 13.5 %collective-permute-start = (bf16[272,512]{1,0:T(8,128)(2,1)S(1)}, bf16[272,512]{1,0:T(8,128)(2,1)S(1)}, u32[]{:S(2)}, u32[]{:S(2)}) collective-permute-start(bf16[272,512]{1,0:T(8,128)(2,1)S(1)} %get-tuple-element.26), channel_id=1, source_target_pairs={{0,2},{2,0},{4,6},{6,4},{1,3},{3,1},{5,7},{7,5},{8,10},{10,8},{12,... | collective-permute-start | bytes 835592 | tf_op jit(solution)/shard_map/ppermute | solution.py:325
  25.6 11.6 %collective-permute-start.1 = (bf16[272,512]{1,0:T(8,128)(2,1)S(1)}, bf16[272,512]{1,0:T(8,128)(2,1)S(1)}, u32[]{:S(2)}, u32[]{:S(2)}) collective-permute-start(bf16[272,512]{1,0:T(8,128)(2,1)S(1)} %get-tuple-element.27), channel_id=1, source_target_pairs={{0,4},{2,6},{4,0},{6,2},{1,5},{3,7},{5,1},{7,3},{8,12},{10,14},{12... | collective-permute-start | bytes 835592 | tf_op jit(solution)/shard_map/ppermute | solution.py:325
  25.9 11.3 %collective-permute-start.3 = (bf16[272,512]{1,0:T(8,128)(2,1)}, bf16[272,512]{1,0:T(8,128)(2,1)S(1)}, u32[]{:S(2)}, u32[]{:S(2)}) collective-permute-start(bf16[272,512]{1,0:T(8,128)(2,1)} %collective-permute-done.2), channel_id=1, source_target_pairs={{0,2},{2,0},{4,6},{6,4},{1,3},{3,1},{5,7},{7,5},{8,10},{10,8},{12,... | collective-permute-start | bytes 835592 | tf_op jit(solution)/shard_map/ppermute | solution.py:325
  26.2 13.2 %all-to-all-start.1 = ((bf16[8,2,128,128]{3,2,1,0:T(8,128)(2,1)}), bf16[8,2,128,128]{3,2,1,0:T(8,128)(2,1)S(1)}, u32[]{:S(2)}, u32[]{:S(2)}) async-start(bf16[8,2,128,128]{3,2,1,0:T(8,128)(2,1)} %copy-done.1), calls=%async_computation.1 | async-start | bytes 1048576 | tf_op jit(solution)/shard_map/all_to_all | solution.py:346
  31.7 15.2 %collective-permute-start.7 = (bf16[4,2,128,128]{3,2,1,0:T(8,128)(2,1)}, bf16[4,2,128,128]{3,2,1,0:T(8,128)(2,1)S(1)}, u32[]{:S(2)}, u32[]{:S(2)}) collective-permute-start(bf16[4,2,128,128]{3,2,1,0:T(8,128)(2,1)} %broadcast_select_fusion.1), channel_id=1, source_target_pairs={{16,24},{8,16},{17,25},{9,17},{18,26},{10,18},{19,27},{11,19},{20,... | collective-permute-start | bytes 786440 | tf_op jit(solution)/shard_map/ppermute | solution.py:351
  34.3 12.7 %collective-permute-start.8 = (bf16[4,2,128,128]{3,2,1,0:T(8,128)(2,1)}, bf16[4,2,128,128]{3,2,1,0:T(8,128)(2,1)}, u32[]{:S(2)}, u32[]{:S(2)}) collective-permute-start(bf16[4,2,128,128]{3,2,1,0:T(8,128)(2,1)} %broadcast_select_fusion), channel_id=1, source_target_pairs={{16,24},{8,16},{17,25},{9,17},{18,26},{10,18},{19,27},{11,19},{20,... | collective-permute-start | bytes 786440 | tf_op jit(solution)/shard_map/ppermute | solution.py:351
  51.5 13.9 %collective-permute-start.10 = (bf16[256,512]{1,0:T(8,128)(2,1)S(1)}, bf16[256,512]{1,0:T(8,128)(2,1)S(1)}, u32[]{:S(2)}, u32[]{:S(2)}) collective-permute-start(bf16[256,512]{1,0:T(8,128)(2,1)S(1)} %get-tuple-element.39), channel_id=1, source_target_pairs={{0,4},{2,6},{4,0},{6,2},{1,5},{3,7},{5,1},{7,3},{8,12},{10,14},{12... | collective-permute-start | bytes 786440 | tf_op jit(solution)/shard_map/ppermute | solution.py:325
  51.8 13.7 %collective-permute-start.11 = (bf16[256,512]{1,0:T(8,128)(2,1)S(1)}, bf16[256,512]{1,0:T(8,128)(2,1)S(1)}, u32[]{:S(2)}, u32[]{:S(2)}) collective-permute-start(bf16[256,512]{1,0:T(8,128)(2,1)S(1)} %get-tuple-element.40), channel_id=1, source_target_pairs={{0,6},{2,4},{4,2},{6,0},{1,7},{3,5},{5,3},{7,1},{8,14},{10,12},{12... | collective-permute-start | bytes 786440 | tf_op jit(solution)/shard_map/ppermute | solution.py:325
  65.4 1.6 %collective-permute-start.9 = (bf16[256,512]{1,0:T(8,128)(2,1)S(1)}, bf16[256,512]{1,0:T(8,128)(2,1)S(1)}, u32[]{:S(2)}, u32[]{:S(2)}) collective-permute-start(bf16[256,512]{1,0:T(8,128)(2,1)S(1)} %get-tuple-element.44), channel_id=1, source_target_pairs={{0,2},{2,0},{4,6},{6,4},{1,3},{3,1},{5,7},{7,5},{8,10},{10,8},{12,... | collective-permute-start | bytes 786440 | tf_op jit(solution)/shard_map/ppermute | solution.py:325

commit v8 on v6

--- a/solution.py
+++ b/solution.py
@@ -117,7 +117,9 @@
     )(*pieces, *begun)
 
 
-def attention(name, first, last, partners, bases_of, queries, sel, sources, state):
+def attention(
+    name, first, last, partners, bases_of, queries, sel, sources, state, state_from=0
+):
     parts, rows = len(queries), queries[0].shape[0] - EXTRA
     tiles_in_part = rows // TILE
     tiles_here = len(partners) * tiles_in_part
@@ -128,6 +130,8 @@
     most = min(TOPK, sum(slots))
     n_q = len(partners)
     n_out = len(partners) if last else 2
+    in_block = BLK // TILE
+    one_block = parts > 1 and len(partners) * rows == BLK
 
     def kernel(*refs):
         sel_ref, q_refs = refs[0], refs[1 : 1 + n_q]
@@ -166,12 +170,40 @@
                 pl.when(base >= 0)(fill)
             start += n
 
+        def own_part(t, part, at, slot, own, pieces):
+            count = pieces * TILE
+            keys_at = pl.ds(pl.multiple_of((own - bases[0]) * BLK, BLK), count)
+            q_rows = pl.ds(pl.multiple_of(at, TILE), TILE)
+            key_at = lax.broadcasted_iota(jnp.int32, (TILE, TILE), 1)
+            query_at = lax.broadcasted_iota(jnp.int32, (TILE, TILE), 0)
+            for j in range(PER):
+                here = slice(j * TILE, (j + 1) * TILE)
+                s = dot_nt(q_buf[part, q_rows, j * HD : (j + 1) * HD], k_buf[keys_at])
+                edge = jnp.where(key_at <= query_at, s[:, count - TILE :], FLOOR)
+                s = jnp.concatenate([s[:, : count - TILE], edge], axis=1) if pieces > 1 else edge
+                m = jnp.max(s, axis=1, keepdims=True)
+                p = jnp.exp2((s - m) * SCALE).astype(BF16)
+                m_tmp[slot, here] = jnp.broadcast_to(m, (TILE, HD))
+                acc_tmp[slot, here] = dot_nn(p, v_buf[keys_at])
+
+        if first and one_block:
+            first_part = level * parts
+            own = (first_part + (sub ^ partners[0])) * tiles_in_part // in_block
+            for i in range(in_block):
+                part = own * (in_block // tiles_in_part) + i // tiles_in_part - first_part
+                local = (part ^ sub) - partners[0]
+                t = local * tiles_in_part + i % tiles_in_part
+                own_part(t, local, i % tiles_in_part * TILE, t, own, i + 1)
+
         def one_tile(k, part, i, out_ref, out_at):
             t = part * tiles_in_part + i
             tile = (level * parts + (sub ^ k)) * tiles_in_part + i
-            own = tile * TILE // BLK
+            own = tile // in_block
             q_rows = pl.ds(pl.multiple_of(i * TILE, TILE), TILE)
-            m_old, acc_old, at_old = (m_tmp, acc_tmp, 0) if first else (m_in, acc_in, t)
+            if first:
+                m_old, acc_old, at_old = m_tmp, acc_tmp, t if one_block else 0
+            else:
+                m_old, acc_old, at_old = m_in, acc_in, t + (partners[0] - state_from) * tiles_in_part
 
             def finish(j, acc):
                 out_ref[out_at, j * HD : (j + 1) * HD] = (acc[:, :HD] / acc[:, HD:]).astype(BF16)
@@ -180,24 +212,10 @@
                 outs[0][t, j * TILE : (j + 1) * TILE] = m
                 outs[1][t, j * TILE : (j + 1) * TILE] = acc
 
-            def own_part(pieces):
-                count = pieces * TILE
-                at = pl.ds(pl.multiple_of((own - bases[0]) * BLK, BLK), count)
-                key_at = lax.broadcasted_iota(jnp.int32, (TILE, TILE), 1)
-                query_at = lax.broadcasted_iota(jnp.int32, (TILE, TILE), 0)
-                for j in range(PER):
-                    s = dot_nt(q_buf[part, q_rows, j * HD : (j + 1) * HD], k_buf[at])
-                    edge = jnp.where(key_at <= query_at, s[:, count - TILE :], FLOOR)
-                    s = jnp.concatenate([s[:, : count - TILE], edge], axis=1) if pieces > 1 else edge
-                    m = jnp.max(s, axis=1, keepdims=True)
-                    p = jnp.exp2((s - m) * SCALE).astype(BF16)
-                    m_tmp[0, j * TILE : (j + 1) * TILE] = jnp.broadcast_to(m, (TILE, HD))
-                    acc_tmp[0, j * TILE : (j + 1) * TILE] = dot_nn(p, v_buf[at])
-
-            if first:
-                for pieces in range(1, BLK // TILE + 1):
-                    pl.when(lax.rem(tile, BLK // TILE) == pieces - 1)(
-                        functools.partial(own_part, pieces)
+            if first and not one_block:
+                for pieces in range(1, in_block + 1):
+                    pl.when(lax.rem(tile, in_block) == pieces - 1)(
+                        functools.partial(own_part, t, part, i * TILE, 0, own, pieces)
                     )
 
             found = jnp.int32(0)
@@ -273,8 +291,8 @@
         scratch_shapes=[
             pltpu.VMEM((sum(slots) * BLK, HD), BF16),
             pltpu.VMEM((sum(slots) * BLK, 2 * HD), BF16),
-            pltpu.VMEM((1, QW, HD), F32),
-            pltpu.VMEM((1, QW, 2 * HD), F32),
+            pltpu.VMEM((tiles_here if one_block else 1, QW, HD), F32),
+            pltpu.VMEM((tiles_here if one_block else 1, QW, 2 * HD), F32),
             pltpu.VMEM((n_q, rows, QW), BF16),
         ],
         compiler_params=pltpu.CompilerParams(
@@ -351,7 +369,11 @@
         state = attention(
             "far_early", True, False, far, early, q, sel, (own, *up, p2), ()
         )
-        out_far = attention("far_late", False, True, far, late, q, sel, tuple(last_up), state)
+        out_far = ()
+        for k in far:
+            out_far += attention(
+                "far_late", False, True, (k,), late, q, sel, tuple(last_up), state, far[0]
+            )
         q_near, _ = lax.optimization_barrier((q[: subs // 2], out_far))
         q = tuple(q_near) + tuple(q[subs // 2 :])
         out_near = attention(

time: 68.7 us -> 67.2 us (0.978)
  starting transfers between devices: 29.7 us -> 28.1 us
  Pallas kernels: 27.4 us -> 26.2 us
  waiting for transfers between devices: 8.78 us -> 9.64 us
    pallas_call x3 -> x4, Pallas kernels: 23 us -> 21.2 us  [attention(): pl.pallas_call(kernel, in_specs=[SMEM] + [VMEM] * (n_q + n_src + len(stat...]
    all_to_all x1, waiting for transfers between devices: 2.12 us -> 3.05 us  [body(): p2 = lax.all_to_all(raw, ('sub', 'head'), 0, 0, tiled=True)]
    ppermute x2, starting transfers between devices: 4.82 us -> 3.89 us  [body(): lax.ppermute(jnp.where(forwards, a, b), 'lev', [(2, 3), (1, 2)])]
    slice x1, local copies, waits for them, and re-layouts: 0.83 us -> 0.04 us  [body(): halves = lax.optimization_barrier((own[:half], own[half:]))]
    unnamed x7, local copies, waits for them, and re-layouts: 0.11 us -> 0.85 us
    pallas_call x1, Pallas kernels: 0.68 us -> 1.4 us  [pack_queries(): pl.pallas_call(kernel, in_specs=[SMEM, VMEM], out_specs=(VMEM,) * subs, o...]
  transfers between devices with their start and end apart: 14 -> 14, of which waited for: 3 -> 4; matrix products, arithmetic and copies ran while one was open for 4% -> 3% of each run, Pallas kernels for 29% -> 31%
where the time goes in v8:
time: 67.2 us; the launch traced here: 66.8 us
  starting transfers between devices  28.1 us (42%)
  Pallas kernels  26.2 us (39%)
  waiting for transfers between devices  9.64 us (14%)
  other arithmetic  1.54 us (2%)
  local copies, waits for them, and re-layouts  0.9 us (1%)
    pallas_call x4, Pallas kernels, attention(): pl.pallas_call(kernel, in_specs=[SMEM] + [VMEM] * (n_q + n_src + len(stat...  21.2 us
    ppermute x2, starting transfers between devices, body(): up = [lax.ppermute(piece, 'lev', [(0, 2), (2, 3)]) for piece in halves]  8.58 us
    ppermute x7, starting transfers between devices, exchange(): lax.ppermute(piece, 'sub', [(i, i ^ k) for i in range(subs)])  5.81 us
    all_to_all x1, waiting for transfers between devices, body(): own = lax.all_to_all(packed, ('sub', 'head'), 0, 0, tiled=True)  5.31 us
    all_to_all x1, starting transfers between devices, body(): p2 = lax.all_to_all(raw, ('sub', 'head'), 0, 0, tiled=True)  4.66 us
    all_to_all x1, starting transfers between devices, body(): own = lax.all_to_all(packed, ('sub', 'head'), 0, 0, tiled=True)  4.52 us
    ppermute x2, starting transfers between devices, body(): lax.ppermute(jnp.where(forwards, a, b), 'lev', [(2, 3), (1, 2)])  3.89 us
    all_to_all x1, waiting for transfers between devices, body(): p2 = lax.all_to_all(raw, ('sub', 'head'), 0, 0, tiled=True)  3.05 us
  transfers between devices with their start and end apart: 14, of which 4 were waited for; matrix products, arithmetic and copies ran while one was open for 3% of the time, Pallas kernels for 31%

profile of v8, /device:TPU:23, one launch (start us, length us, event | category | flops | bytes accessed | tf_op | source)
XLA Modules:
  0.0 66.8 jit_solution(2201538553779425021)
XLA Ops:
  0.0 2.0 %pack_kv.1 = bf16[8,2,128,128]{3,2,1,0:T(8,128)(2,1)} custom-call(bf16[128,1024]{1,0:T(8,128)(2,1)} %k_ref.1, bf16[128,1024]{1,0:T(8,128)(2,1)} %v_ref.1), custom_call_target="tpu_custom_call" | custom-call | bytes 1048576 | tf_op jit(solution)/shard_map/pack_kv/pallas_call | solution.py:54
  2.0 0.7 %collective-permute-start.4 = (bf16[8,2,128,128]{3,2,1,0:T(8,128)(2,1)}, bf16[8,2,128,128]{3,2,1,0:T(8,128)(2,1)S(1)}, u32[]{:S(2)}, u32[]{:S(2)}) collective-permute-start(bf16[8,2,128,128]{3,2,1,0:T(8,128)(2,1)} %pack_kv.1), channel_id=1, source_target_pairs={{8,24},{0,8},{9,25},{1,9},{10,26},{2,10},{11,27},{3,11},{12,28},{4... | collective-permute-start | bytes 1572872 | tf_op jit(solution)/shard_map/ppermute | solution.py:323
  2.7 4.5 %all-to-all-start = ((bf16[8,2,128,128]{3,2,1,0:T(8,128)(2,1)}), bf16[8,2,128,128]{3,2,1,0:T(8,128)(2,1)S(1)}, u32[]{:S(2)}, u32[]{:S(2)}) async-start(bf16[8,2,128,128]{3,2,1,0:T(8,128)(2,1)} %pack_kv.1), calls=%async_computation | async-start | bytes 1048576 | tf_op jit(solution)/shard_map/all_to_all | solution.py:324
  7.2 0.1 copy.6.sel_ref
  7.3 1.4 %pack_q.1 = (bf16[272,512]{1,0:T(8,128)(2,1)S(1)}, bf16[272,512]{1,0:T(8,128)(2,1)}, bf16[272,512]{1,0:T(8,128)(2,1)S(1)}, bf16[272,512]{1,0:T(8,128)(2,1)S(1)}) custom-call(s32[2,4,3]{2,1,0:T(4,128)S(1)} %copy.6.sel_ref, bf16[256,2048]{1,0:T(8,128)(2,1)S(1)} %copy-done), custom_call_target="tpu_custom_call" | custom-call | bytes 2097152 | tf_op jit(solution)/shard_map/pack_q/pallas_call | solution.py:80
  8.7 0.3 collective-permute-start.2
  9.0 5.3 %all-to-all-done.refs_3_ = bf16[8,2,128,128]{3,2,1,0:T(8,128)(2,1)S(1)} async-done(((bf16[8,2,128,128]{3,2,1,0:T(8,128)(2,1)}), bf16[8,2,128,128]{3,2,1,0:T(8,128)(2,1)S(1)}, u32[]{:S(2)}, u32[]{:S(2)}) %all-to-all-start) | async-done | bytes 524320 | tf_op jit(solution)/shard_map/all_to_all | solution.py:324
  14.3 0.0 collective-permute-done.4
  14.4 0.7 %copy-done.1 = bf16[8,2,128,128]{3,2,1,0:T(8,128)(2,1)} copy-done((bf16[8,2,128,128]{3,2,1,0:T(8,128)(2,1)}, bf16[8,2,128,128]{3,2,1,0:T(8,128)(2,1)S(1)}, u32[]{:S(2)}) %copy-start.1) | copy-done | bytes 524312
  15.1 6.7 %collective-permute-start.5 = (bf16[4,2,128,128]{3,2,1,0:T(8,128)(2,1)S(1)}, bf16[4,2,128,128]{3,2,1,0:T(8,128)(2,1)S(1)}, u32[]{:S(2)}, u32[]{:S(2)}) collective-permute-start(bf16[4,2,128,128]{3,2,1,0:T(8,128)(2,1)S(1)} %get-tuple-element.28), channel_id=1, source_target_pairs={{0,16},{16,24},{1,17},{17,25},{2,18},{18,26},{3,19},{19,27},{4,20}... | collective-permute-start | bytes 786440 | tf_op jit(solution)/shard_map/ppermute | solution.py:336
  21.8 1.9 %collective-permute-start.6 = (bf16[4,2,128,128]{3,2,1,0:T(8,128)(2,1)S(1)}, bf16[4,2,128,128]{3,2,1,0:T(8,128)(2,1)S(1)}, u32[]{:S(2)}, u32[]{:S(2)}) collective-permute-start(bf16[4,2,128,128]{3,2,1,0:T(8,128)(2,1)S(1)} %get-tuple-element.29), channel_id=1, source_target_pairs={{0,16},{16,24},{1,17},{17,25},{2,18},{18,26},{3,19},{19,27},{4,20}... | collective-permute-start | bytes 786440 | tf_op jit(solution)/shard_map/ppermute | solution.py:336
  23.7 1.9 %collective-permute-start = (bf16[272,512]{1,0:T(8,128)(2,1)}, bf16[272,512]{1,0:T(8,128)(2,1)S(1)}, u32[]{:S(2)}, u32[]{:S(2)}) collective-permute-start(bf16[272,512]{1,0:T(8,128)(2,1)} %get-tuple-element.24), channel_id=1, source_target_pairs={{0,2},{2,0},{4,6},{6,4},{1,3},{3,1},{5,7},{7,5},{8,10},{10,8},{12,... | collective-permute-start | bytes 835592 | tf_op jit(solution)/shard_map/ppermute | solution.py:316
  25.6 0.3 collective-permute-start.1
  25.9 0.3 collective-permute-start.3
  26.2 4.7 %all-to-all-start.1 = ((bf16[8,2,128,128]{3,2,1,0:T(8,128)(2,1)}), bf16[8,2,128,128]{3,2,1,0:T(8,128)(2,1)S(1)}, u32[]{:S(2)}, u32[]{:S(2)}) async-start(bf16[8,2,128,128]{3,2,1,0:T(8,128)(2,1)} %copy-done.1), calls=%async_computation.1 | async-start | bytes 1048576 | tf_op jit(solution)/shard_map/all_to_all | solution.py:337
  30.9 0.7 %broadcast_select_fusion.1 = bf16[4,2,128,128]{3,2,1,0:T(8,128)(2,1)} fusion(bf16[4,2,128,128]{3,2,1,0:T(8,128)(2,1)S(1)} %collective-permute-done.5.refs_4_, bf16[4,2,128,128]{3,2,1,0:T(8,128)(2,1)S(1)} %get-tuple-element.28, pred[]{:T(512)S(6)} %eq.3), kind=kLoop, calls=%fused_computation.1 | loop fusion | flops 131072 | bytes 786433 | tf_op jit(solution)/shard_map/jit(_where)/select_n | solution.py:342
  31.6 1.9 %collective-permute-start.7 = (bf16[4,2,128,128]{3,2,1,0:T(8,128)(2,1)}, bf16[4,2,128,128]{3,2,1,0:T(8,128)(2,1)S(1)}, u32[]{:S(2)}, u32[]{:S(2)}) collective-permute-start(bf16[4,2,128,128]{3,2,1,0:T(8,128)(2,1)} %broadcast_select_fusion.1), channel_id=1, source_target_pairs={{16,24},{8,16},{17,25},{9,17},{18,26},{10,18},{19,27},{11,19},{20,... | collective-permute-start | bytes 786440 | tf_op jit(solution)/shard_map/ppermute | solution.py:342
  33.5 0.7 %broadcast_select_fusion = bf16[4,2,128,128]{3,2,1,0:T(8,128)(2,1)} fusion(bf16[4,2,128,128]{3,2,1,0:T(8,128)(2,1)S(1)} %collective-permute-done.6.refs_5_, bf16[4,2,128,128]{3,2,1,0:T(8,128)(2,1)S(1)} %get-tuple-element.29, pred[]{:T(512)S(6)} %eq.3), kind=kLoop, calls=%fused_computation | loop fusion | flops 131072 | bytes 786433 | tf_op jit(solution)/shard_map/jit(_where)/select_n | solution.py:342
  34.3 2.0 %collective-permute-start.8 = (bf16[4,2,128,128]{3,2,1,0:T(8,128)(2,1)}, bf16[4,2,128,128]{3,2,1,0:T(8,128)(2,1)S(1)}, u32[]{:S(2)}, u32[]{:S(2)}) collective-permute-start(bf16[4,2,128,128]{3,2,1,0:T(8,128)(2,1)} %broadcast_select_fusion), channel_id=1, source_target_pairs={{16,24},{8,16},{17,25},{9,17},{18,26},{10,18},{19,27},{11,19},{20,... | collective-permute-start | bytes 786440 | tf_op jit(solution)/shard_map/ppermute | solution.py:342
  36.3 0.1 maximum_convert_fusion.refs_0_
  36.4 3.0 %all-to-all-done.1.refs_6_ = bf16[8,2,128,128]{3,2,1,0:T(8,128)(2,1)S(1)} async-done(((bf16[8,2,128,128]{3,2,1,0:T(8,128)(2,1)}), bf16[8,2,128,128]{3,2,1,0:T(8,128)(2,1)S(1)}, u32[]{:S(2)}, u32[]{:S(2)}) %all-to-all-start.1) | async-done | bytes 524320 | tf_op jit(solution)/shard_map/all_to_all | solution.py:337
  39.5 6.8 %far_early.1 = (f32[4,512,128]{2,1,0:T(8,128)S(1)}, f32[4,512,256]{2,1,0:T(8,128)S(1)}) custom-call(s32[24]{0:T(128)S(1)} %maximum_convert_fusion.refs_0_, bf16[272,512]{1,0:T(8,128)(2,1)S(1)} %collective-permute-done.1.refs_1_, bf16[272,512]{1,0:T(8,128)(2,1)S(1)} %collective-permute-done.3.refs_2_.refs_1_, ...), custom_call_target="tpu_custom_call" | custom-call | flops 1610612736 | bytes 4194304 | tf_op jit(solution)/shard_map/far_early/pallas_call | solution.py:286
  46.3 0.6 collective-permute-done.8.refs_3_.refs_8_
  46.9 2.5 %far_late.2 = bf16[256,512]{1,0:T(8,128)(2,1)S(1)} custom-call(s32[24]{0:T(128)S(1)} %maximum_convert_fusion.refs_0_, bf16[272,512]{1,0:T(8,128)(2,1)S(1)} %collective-permute-done.1.refs_1_, bf16[4,2,128,128]{3,2,1,0:T(8,128)(2,1)S(1)} %collective-permute-done.7.refs_2_.refs_7_, bf16[4,2,128,128]{3,2,1,0:T(8,128)(2,1)S(1)} %collective-permute-done.8.refs_3_.refs_8_, ...), custom_call_target="tpu_custom_call" | custom-call | flops 805306368 | bytes 4194304 | tf_op jit(solution)/shard_map/far_late/pallas_call | solution.py:286
  49.3 0.3 collective-permute-start.10
  49.6 2.5 %far_late.3 = bf16[256,512]{1,0:T(8,128)(2,1)S(1)} custom-call(s32[24]{0:T(128)S(1)} %maximum_convert_fusion.refs_0_, bf16[272,512]{1,0:T(8,128)(2,1)S(1)} %collective-permute-done.3.refs_2_.refs_1_, bf16[4,2,128,128]{3,2,1,0:T(8,128)(2,1)S(1)} %collective-permute-done.7.refs_2_.refs_7_, bf16[4,2,128,128]{3,2,1,0:T(8,128)(2,1)S(1)} %collective-permute-done.8.refs_3_.refs_8_, ...), custom_call_target="tpu_custom_call" | custom-call | flops 805306368 | bytes 4194304 | tf_op jit(solution)/shard_map/far_late/pallas_call | solution.py:286
  52.1 2.6 %collective-permute-start.11 = (bf16[256,512]{1,0:T(8,128)(2,1)S(1)}, bf16[256,512]{1,0:T(8,128)(2,1)S(1)}, u32[]{:S(2)}, u32[]{:S(2)}) collective-permute-start(bf16[256,512]{1,0:T(8,128)(2,1)S(1)} %far_late.3), channel_id=1, source_target_pairs={{0,6},{2,4},{4,2},{6,0},{1,7},{3,5},{5,3},{7,1},{8,14},{10,12},{12... | collective-permute-start | bytes 786440 | tf_op jit(solution)/shard_map/ppermute | solution.py:316
  54.7 9.5 %near.1 = (bf16[256,512]{1,0:T(8,128)(2,1)S(1)}, bf16[256,512]{1,0:T(8,128)(2,1)S(1)}) custom-call(s32[24]{0:T(128)S(1)} %maximum_convert_fusion.refs_0_, bf16[272,512]{1,0:T(8,128)(2,1)S(1)} %get-tuple-element.37.refs_1_, bf16[272,512]{1,0:T(8,128)(2,1)S(1)} %collective-permute-done.refs_2_, bf16[8,2,128,128]{3,2,1,0:T(8,128)(2,1)S(1)} %all-to-all-done.refs_3_, ...), custom_call_target="tpu_custom_call" | custom-call | flops 1610612736 | bytes 4194304 | tf_op jit(solution)/shard_map/near/pallas_call | solution.py:286
  64.3 0.1 collective-permute-start.9
  64.4 0.8 %unpack_far.1.refs_2_ = bf16[256,2048]{1,0:T(8,128)(2,1)} custom-call(bf16[256,512]{1,0:T(8,128)(2,1)S(1)} %collective-permute-done.10.refs_0_, bf16[256,512]{1,0:T(8,128)(2,1)S(1)} %collective-permute-done.11.refs_1_), custom_call_target="tpu_custom_call" | custom-call | bytes 1048576 | tf_op jit(solution)/shard_map/unpack_far/pallas_call | solution.py:107
  65.2 0.7 %collective-permute-done.9.refs_1_ = bf16[256,512]{1,0:T(8,128)(2,1)S(1)} collective-permute-done((bf16[256,512]{1,0:T(8,128)(2,1)S(1)}, bf16[256,512]{1,0:T(8,128)(2,1)S(1)}, u32[]{:S(2)}, u32[]{:S(2)}) %collective-permute-start.9) | collective-permute-done | bytes 262176 | tf_op jit(solution)/shard_map/ppermute | solution.py:316
  65.9 0.8 %unpack_near.1 = bf16[256,2048]{1,0:T(8,128)(2,1)} custom-call(bf16[256,512]{1,0:T(8,128)(2,1)S(1)} %get-tuple-element.39.refs_0_, bf16[256,512]{1,0:T(8,128)(2,1)S(1)} %collective-permute-done.9.refs_1_, bf16[256,2048]{1,0:T(8,128)(2,1)} %unpack_far.1.refs_2_), custom_call_target="tpu_custom_call", output_to_operand_aliasing={{}: (2, {})} | custom-call | bytes 1048576 | tf_op jit(solution)/shard_map/unpack_near/pallas_call | solution.py:107
  (17 shorter events, 0.1 us)
Async XLA Ops:
  0.0 7.2 %copy-start.2 = (s32[2,4,3]{1,0,2:T(2,128)S(1)}, s32[2,4,3]{1,0,2:T(2,128)}, u32[]{:S(2)}) copy-start(s32[2,4,3]{1,0,2:T(2,128)} %param.7) | copy-start | bytes 292
  0.0 7.3 %copy-start = (bf16[256,2048]{1,0:T(8,128)(2,1)S(1)}, bf16[256,2048]{1,0:T(8,128)(2,1)}, u32[]{:S(2)}) copy-start(bf16[256,2048]{1,0:T(8,128)(2,1)} %q_ref.1) | copy-start | bytes 3145732
  2.0 12.3 %collective-permute-start.4 = (bf16[8,2,128,128]{3,2,1,0:T(8,128)(2,1)}, bf16[8,2,128,128]{3,2,1,0:T(8,128)(2,1)S(1)}, u32[]{:S(2)}, u32[]{:S(2)}) collective-permute-start(bf16[8,2,128,128]{3,2,1,0:T(8,128)(2,1)} %pack_kv.1), channel_id=1, source_target_pairs={{8,24},{0,8},{9,25},{1,9},{10,26},{2,10},{11,27},{3,11},{12,28},{4... | collective-permute-start | bytes 1572872 | tf_op jit(solution)/shard_map/ppermute | solution.py:323
  2.7 11.6 %all-to-all-start = ((bf16[8,2,128,128]{3,2,1,0:T(8,128)(2,1)}), bf16[8,2,128,128]{3,2,1,0:T(8,128)(2,1)S(1)}, u32[]{:S(2)}, u32[]{:S(2)}) async-start(bf16[8,2,128,128]{3,2,1,0:T(8,128)(2,1)} %pack_kv.1), calls=%async_computation | async-start | bytes 1048576 | tf_op jit(solution)/shard_map/all_to_all | solution.py:324
  8.7 17.1 %collective-permute-start.2 = (bf16[272,512]{1,0:T(8,128)(2,1)S(1)}, bf16[272,512]{1,0:T(8,128)(2,1)}, u32[]{:S(2)}, u32[]{:S(2)}) collective-permute-start(bf16[272,512]{1,0:T(8,128)(2,1)S(1)} %get-tuple-element.26), channel_id=1, source_target_pairs={{0,4},{2,6},{4,0},{6,2},{1,5},{3,7},{5,1},{7,3},{8,12},{10,14},{12... | collective-permute-start | bytes 835592 | tf_op jit(solution)/shard_map/ppermute | solution.py:316
  14.3 0.8 %copy-start.1 = (bf16[8,2,128,128]{3,2,1,0:T(8,128)(2,1)}, bf16[8,2,128,128]{3,2,1,0:T(8,128)(2,1)S(1)}, u32[]{:S(2)}) copy-start(bf16[8,2,128,128]{3,2,1,0:T(8,128)(2,1)S(1)} %collective-permute-done.4) | copy-start | bytes 1572868
  15.1 15.8 %collective-permute-start.5 = (bf16[4,2,128,128]{3,2,1,0:T(8,128)(2,1)S(1)}, bf16[4,2,128,128]{3,2,1,0:T(8,128)(2,1)S(1)}, u32[]{:S(2)}, u32[]{:S(2)}) collective-permute-start(bf16[4,2,128,128]{3,2,1,0:T(8,128)(2,1)S(1)} %get-tuple-element.28), channel_id=1, source_target_pairs={{0,16},{16,24},{1,17},{17,25},{2,18},{18,26},{3,19},{19,27},{4,20}... | collective-permute-start | bytes 786440 | tf_op jit(solution)/shard_map/ppermute | solution.py:336
  21.8 11.7 %collective-permute-start.6 = (bf16[4,2,128,128]{3,2,1,0:T(8,128)(2,1)S(1)}, bf16[4,2,128,128]{3,2,1,0:T(8,128)(2,1)S(1)}, u32[]{:S(2)}, u32[]{:S(2)}) collective-permute-start(bf16[4,2,128,128]{3,2,1,0:T(8,128)(2,1)S(1)} %get-tuple-element.29), channel_id=1, source_target_pairs={{0,16},{16,24},{1,17},{17,25},{2,18},{18,26},{3,19},{19,27},{4,20}... | collective-permute-start | bytes 786440 | tf_op jit(solution)/shard_map/ppermute | solution.py:336
  23.7 12.6 %collective-permute-start = (bf16[272,512]{1,0:T(8,128)(2,1)}, bf16[272,512]{1,0:T(8,128)(2,1)S(1)}, u32[]{:S(2)}, u32[]{:S(2)}) collective-permute-start(bf16[272,512]{1,0:T(8,128)(2,1)} %get-tuple-element.24), channel_id=1, source_target_pairs={{0,2},{2,0},{4,6},{6,4},{1,3},{3,1},{5,7},{7,5},{8,10},{10,8},{12,... | collective-permute-start | bytes 835592 | tf_op jit(solution)/shard_map/ppermute | solution.py:316
  25.6 10.7 %collective-permute-start.1 = (bf16[272,512]{1,0:T(8,128)(2,1)S(1)}, bf16[272,512]{1,0:T(8,128)(2,1)S(1)}, u32[]{:S(2)}, u32[]{:S(2)}) collective-permute-start(bf16[272,512]{1,0:T(8,128)(2,1)S(1)} %get-tuple-element.25), channel_id=1, source_target_pairs={{0,4},{2,6},{4,0},{6,2},{1,5},{3,7},{5,1},{7,3},{8,12},{10,14},{12... | collective-permute-start | bytes 835592 | tf_op jit(solution)/shard_map/ppermute | solution.py:316
  25.9 10.4 %collective-permute-start.3 = (bf16[272,512]{1,0:T(8,128)(2,1)}, bf16[272,512]{1,0:T(8,128)(2,1)S(1)}, u32[]{:S(2)}, u32[]{:S(2)}) collective-permute-start(bf16[272,512]{1,0:T(8,128)(2,1)} %collective-permute-done.2), channel_id=1, source_target_pairs={{0,2},{2,0},{4,6},{6,4},{1,3},{3,1},{5,7},{7,5},{8,10},{10,8},{12,... | collective-permute-start | bytes 835592 | tf_op jit(solution)/shard_map/ppermute | solution.py:316
  26.2 13.2 %all-to-all-start.1 = ((bf16[8,2,128,128]{3,2,1,0:T(8,128)(2,1)}), bf16[8,2,128,128]{3,2,1,0:T(8,128)(2,1)S(1)}, u32[]{:S(2)}, u32[]{:S(2)}) async-start(bf16[8,2,128,128]{3,2,1,0:T(8,128)(2,1)} %copy-done.1), calls=%async_computation.1 | async-start | bytes 1048576 | tf_op jit(solution)/shard_map/all_to_all | solution.py:337
  31.6 14.6 %collective-permute-start.7 = (bf16[4,2,128,128]{3,2,1,0:T(8,128)(2,1)}, bf16[4,2,128,128]{3,2,1,0:T(8,128)(2,1)S(1)}, u32[]{:S(2)}, u32[]{:S(2)}) collective-permute-start(bf16[4,2,128,128]{3,2,1,0:T(8,128)(2,1)} %broadcast_select_fusion.1), channel_id=1, source_target_pairs={{16,24},{8,16},{17,25},{9,17},{18,26},{10,18},{19,27},{11,19},{20,... | collective-permute-start | bytes 786440 | tf_op jit(solution)/shard_map/ppermute | solution.py:342
  34.3 12.6 %collective-permute-start.8 = (bf16[4,2,128,128]{3,2,1,0:T(8,128)(2,1)}, bf16[4,2,128,128]{3,2,1,0:T(8,128)(2,1)S(1)}, u32[]{:S(2)}, u32[]{:S(2)}) collective-permute-start(bf16[4,2,128,128]{3,2,1,0:T(8,128)(2,1)} %broadcast_select_fusion), channel_id=1, source_target_pairs={{16,24},{8,16},{17,25},{9,17},{18,26},{10,18},{19,27},{11,19},{20,... | collective-permute-start | bytes 786440 | tf_op jit(solution)/shard_map/ppermute | solution.py:342
  49.3 15.0 %collective-permute-start.10 = (bf16[256,512]{1,0:T(8,128)(2,1)S(1)}, bf16[256,512]{1,0:T(8,128)(2,1)S(1)}, u32[]{:S(2)}, u32[]{:S(2)}) collective-permute-start(bf16[256,512]{1,0:T(8,128)(2,1)S(1)} %far_late.2), channel_id=1, source_target_pairs={{0,4},{2,6},{4,0},{6,2},{1,5},{3,7},{5,1},{7,3},{8,12},{10,14},{12... | collective-permute-start | bytes 786440 | tf_op jit(solution)/shard_map/ppermute | solution.py:316
  52.1 12.2 %collective-permute-start.11 = (bf16[256,512]{1,0:T(8,128)(2,1)S(1)}, bf16[256,512]{1,0:T(8,128)(2,1)S(1)}, u32[]{:S(2)}, u32[]{:S(2)}) collective-permute-start(bf16[256,512]{1,0:T(8,128)(2,1)S(1)} %far_late.3), channel_id=1, source_target_pairs={{0,6},{2,4},{4,2},{6,0},{1,7},{3,5},{5,3},{7,1},{8,14},{10,12},{12... | collective-permute-start | bytes 786440 | tf_op jit(solution)/shard_map/ppermute | solution.py:316
  64.3 1.6 %collective-permute-start.9 = (bf16[256,512]{1,0:T(8,128)(2,1)S(1)}, bf16[256,512]{1,0:T(8,128)(2,1)S(1)}, u32[]{:S(2)}, u32[]{:S(2)}) collective-permute-start(bf16[256,512]{1,0:T(8,128)(2,1)S(1)} %get-tuple-element.40), channel_id=1, source_target_pairs={{0,2},{2,0},{4,6},{6,4},{1,3},{3,1},{5,7},{7,5},{8,10},{10,8},{12,... | collective-permute-start | bytes 786440 | tf_op jit(solution)/shard_map/ppermute | solution.py:316

commit v9 on v8

--- a/solution.py
+++ b/solution.py
@@ -17,6 +17,7 @@
 PER = QH // KVH
 QW = PER * HD
 EXTRA = 16
+TOGETHER = 2
 
 FLOOR = -1e30
 SCALE = HD ** -0.5 * math.log2(math.e)
@@ -234,25 +235,33 @@
 
             def others(n):
                 at = [pl.ds(pl.multiple_of(w * BLK, BLK), BLK) for w in where[:n]]
-                for j in range(PER):
-                    here = slice(j * TILE, (j + 1) * TILE)
-                    old = m_old[at_old, here]
+
+                def scores(c):
+                    heads = range(c * TOGETHER, (c + 1) * TOGETHER)
+                    q = [q_buf[part, q_rows, j * HD : (j + 1) * HD] for j in heads]
+                    q = jnp.concatenate(q, axis=0)
+                    s = [dot_nt(q, k_buf[a]) for a in at]
+                    return jnp.concatenate(s, axis=1) if n > 1 else s[0]
+
+                chains = range(PER // TOGETHER)
+                ready = [scores(c) for c in chains] if n else None
+                for c in chains:
+                    here = slice(c * TOGETHER * TILE, (c + 1) * TOGETHER * TILE)
+                    m = m_old[at_old, here]
                     acc = acc_old[at_old, here]
                     if n:
-                        q = q_buf[part, q_rows, j * HD : (j + 1) * HD]
-                        s = [dot_nt(q, k_buf[a]) for a in at]
-                        s = jnp.concatenate(s, axis=1) if n > 1 else s[0]
+                        old, s = m, ready[c]
                         m = jnp.maximum(old, jnp.max(s, axis=1, keepdims=True))
                         p = jnp.exp2((s - jnp.tile(m, (1, n * BLK // HD))) * SCALE).astype(BF16)
-                        fade = jnp.exp2((old - m) * SCALE)
-                        acc = acc * jnp.tile(fade, (1, 2))
+                        acc = acc * jnp.tile(jnp.exp2((old - m) * SCALE), (1, 2))
                         for i, a in enumerate(at):
                             acc = acc + dot_nn(p[:, i * BLK : (i + 1) * BLK], v_buf[a])
-                        old = m
-                    if last:
-                        finish(j, acc)
-                    else:
-                        keep(j, old, acc)
+                    for i in range(TOGETHER):
+                        j, rows_of = c * TOGETHER + i, slice(i * TILE, (i + 1) * TILE)
+                        if last:
+                            finish(j, acc[rows_of])
+                        else:
+                            keep(j, m[rows_of], acc[rows_of])
 
             for n in range(most + 1):
                 pl.when(found == n)(functools.partial(others, n))
@@ -309,7 +318,7 @@
     rows = queries.shape[0]
     tiles_here = selected.shape[0]
     level_blocks = subs * rows // BLK
-    by_levels = levels == 4 and subs * rows % (2 * BLK) == 0
+    by_levels = levels == 4 and subs >= 4 and subs * rows % (2 * BLK) == 0
 
     def exchange(pieces, ks):
         return tuple(
@@ -379,8 +388,9 @@
         out_near = attention(
             "near", True, True, near, whole_range, q, sel, (own, *up, p2, *last_up), ()
         )
-        begun = unpack_output("unpack_far", subs, exchange(out_far, far), far, ())
-        return unpack_output("unpack_near", subs, exchange(out_near, near), near, (begun,))
+        out_near, out_far = exchange(out_near, near), exchange(out_far, far)
+        begun = unpack_output("unpack_most", subs, (*out_far, out_near[0]), (*far, 0), ())
+        return unpack_output("unpack_rest", subs, out_near[1:], near[1:], (begun,))
     sel = jnp.concatenate([piece[rows, : tiles_here * TOPK] for piece in q]).astype(jnp.int32)
     whole = lax.all_gather(own, "lev", axis=0, tiled=True)
     out = attention("all", True, True, everyone, lambda level: (0,), q, sel, (whole,), ())

time: 67.2 us -> 65.6 us (0.976)
  Pallas kernels: 26.2 us -> 24.5 us
    pallas_call x4, Pallas kernels: 21.2 us -> 19.4 us  [attention(): pl.pallas_call(kernel, in_specs=[SMEM] + [VMEM] * (n_q + n_src + len(stat...]
  transfers between devices with their start and end apart: 14 -> 14, of which waited for: 4 -> 4; matrix products, arithmetic and copies ran while one was open for 3% -> 3% of each run, Pallas kernels for 31% -> 30%
where the time goes in v9:
time: 65.6 us; the launch traced here: 65.3 us
  starting transfers between devices  28.6 us (44%)
  Pallas kernels  24.5 us (37%)
  waiting for transfers between devices  9.47 us (14%)
  other arithmetic  1.54 us (2%)
  local copies, waits for them, and re-layouts  0.9 us (1%)
    pallas_call x4, Pallas kernels, attention(): pl.pallas_call(kernel, in_specs=[SMEM] + [VMEM] * (n_q + n_src + len(stat...  19.4 us
    ppermute x2, starting transfers between devices, body(): up = [lax.ppermute(piece, 'lev', [(0, 2), (2, 3)]) for piece in halves]  8.58 us
    ppermute x7, starting transfers between devices, exchange(): lax.ppermute(piece, 'sub', [(i, i ^ k) for i in range(subs)])  6.22 us
    all_to_all x1, waiting for transfers between devices, body(): own = lax.all_to_all(packed, ('sub', 'head'), 0, 0, tiled=True)  5.31 us
    all_to_all x1, starting transfers between devices, body(): p2 = lax.all_to_all(raw, ('sub', 'head'), 0, 0, tiled=True)  4.66 us
    all_to_all x1, starting transfers between devices, body(): own = lax.all_to_all(packed, ('sub', 'head'), 0, 0, tiled=True)  4.52 us
    ppermute x2, starting transfers between devices, body(): lax.ppermute(jnp.where(forwards, a, b), 'lev', [(2, 3), (1, 2)])  3.89 us
    all_to_all x1, waiting for transfers between devices, body(): p2 = lax.all_to_all(raw, ('sub', 'head'), 0, 0, tiled=True)  3.05 us
  transfers between devices with their start and end apart: 14, of which 4 were waited for; matrix products, arithmetic and copies ran while one was open for 3% of the time, Pallas kernels for 30%

profile of v9, /device:TPU:23, one launch (start us, length us, event | category | flops | bytes accessed | tf_op | source)
XLA Modules:
  0.0 65.3 jit_solution(17093945033839236100)
XLA Ops:
  0.0 2.0 %pack_kv.1 = bf16[8,2,128,128]{3,2,1,0:T(8,128)(2,1)} custom-call(bf16[128,1024]{1,0:T(8,128)(2,1)} %k_ref.1, bf16[128,1024]{1,0:T(8,128)(2,1)} %v_ref.1), custom_call_target="tpu_custom_call" | custom-call | bytes 1048576 | tf_op jit(solution)/shard_map/pack_kv/pallas_call | solution.py:55
  2.0 0.7 %collective-permute-start.4 = (bf16[8,2,128,128]{3,2,1,0:T(8,128)(2,1)}, bf16[8,2,128,128]{3,2,1,0:T(8,128)(2,1)S(1)}, u32[]{:S(2)}, u32[]{:S(2)}) collective-permute-start(bf16[8,2,128,128]{3,2,1,0:T(8,128)(2,1)} %pack_kv.1), channel_id=1, source_target_pairs={{8,24},{0,8},{9,25},{1,9},{10,26},{2,10},{11,27},{3,11},{12,28},{4... | collective-permute-start | bytes 1572872 | tf_op jit(solution)/shard_map/ppermute | solution.py:332
  2.7 4.5 %all-to-all-start = ((bf16[8,2,128,128]{3,2,1,0:T(8,128)(2,1)}), bf16[8,2,128,128]{3,2,1,0:T(8,128)(2,1)S(1)}, u32[]{:S(2)}, u32[]{:S(2)}) async-start(bf16[8,2,128,128]{3,2,1,0:T(8,128)(2,1)} %pack_kv.1), calls=%async_computation | async-start | bytes 1048576 | tf_op jit(solution)/shard_map/all_to_all | solution.py:333
  7.2 0.1 copy.6.sel_ref
  7.3 1.4 %pack_q.1 = (bf16[272,512]{1,0:T(8,128)(2,1)S(1)}, bf16[272,512]{1,0:T(8,128)(2,1)}, bf16[272,512]{1,0:T(8,128)(2,1)S(1)}, bf16[272,512]{1,0:T(8,128)(2,1)S(1)}) custom-call(s32[2,4,3]{2,1,0:T(4,128)S(1)} %copy.6.sel_ref, bf16[256,2048]{1,0:T(8,128)(2,1)S(1)} %copy-done), custom_call_target="tpu_custom_call" | custom-call | bytes 2097152 | tf_op jit(solution)/shard_map/pack_q/pallas_call | solution.py:81
  8.7 0.3 collective-permute-start.2
  9.0 5.3 %all-to-all-done.refs_3_ = bf16[8,2,128,128]{3,2,1,0:T(8,128)(2,1)S(1)} async-done(((bf16[8,2,128,128]{3,2,1,0:T(8,128)(2,1)}), bf16[8,2,128,128]{3,2,1,0:T(8,128)(2,1)S(1)}, u32[]{:S(2)}, u32[]{:S(2)}) %all-to-all-start) | async-done | bytes 524320 | tf_op jit(solution)/shard_map/all_to_all | solution.py:333
  14.3 0.0 collective-permute-done.4
  14.4 0.7 %copy-done.1 = bf16[8,2,128,128]{3,2,1,0:T(8,128)(2,1)} copy-done((bf16[8,2,128,128]{3,2,1,0:T(8,128)(2,1)}, bf16[8,2,128,128]{3,2,1,0:T(8,128)(2,1)S(1)}, u32[]{:S(2)}) %copy-start.1) | copy-done | bytes 524312
  15.1 6.7 %collective-permute-start.5 = (bf16[4,2,128,128]{3,2,1,0:T(8,128)(2,1)S(1)}, bf16[4,2,128,128]{3,2,1,0:T(8,128)(2,1)S(1)}, u32[]{:S(2)}, u32[]{:S(2)}) collective-permute-start(bf16[4,2,128,128]{3,2,1,0:T(8,128)(2,1)S(1)} %get-tuple-element.28), channel_id=1, source_target_pairs={{0,16},{16,24},{1,17},{17,25},{2,18},{18,26},{3,19},{19,27},{4,20}... | collective-permute-start | bytes 786440 | tf_op jit(solution)/shard_map/ppermute | solution.py:345
  21.8 1.9 %collective-permute-start.6 = (bf16[4,2,128,128]{3,2,1,0:T(8,128)(2,1)S(1)}, bf16[4,2,128,128]{3,2,1,0:T(8,128)(2,1)S(1)}, u32[]{:S(2)}, u32[]{:S(2)}) collective-permute-start(bf16[4,2,128,128]{3,2,1,0:T(8,128)(2,1)S(1)} %get-tuple-element.29), channel_id=1, source_target_pairs={{0,16},{16,24},{1,17},{17,25},{2,18},{18,26},{3,19},{19,27},{4,20}... | collective-permute-start | bytes 786440 | tf_op jit(solution)/shard_map/ppermute | solution.py:345
  23.7 1.9 %collective-permute-start = (bf16[272,512]{1,0:T(8,128)(2,1)}, bf16[272,512]{1,0:T(8,128)(2,1)S(1)}, u32[]{:S(2)}, u32[]{:S(2)}) collective-permute-start(bf16[272,512]{1,0:T(8,128)(2,1)} %get-tuple-element.24), channel_id=1, source_target_pairs={{0,2},{2,0},{4,6},{6,4},{1,3},{3,1},{5,7},{7,5},{8,10},{10,8},{12,... | collective-permute-start | bytes 835592 | tf_op jit(solution)/shard_map/ppermute | solution.py:325
  25.6 0.3 collective-permute-start.1
  25.9 0.3 collective-permute-start.3
  26.2 4.7 %all-to-all-start.1 = ((bf16[8,2,128,128]{3,2,1,0:T(8,128)(2,1)}), bf16[8,2,128,128]{3,2,1,0:T(8,128)(2,1)S(1)}, u32[]{:S(2)}, u32[]{:S(2)}) async-start(bf16[8,2,128,128]{3,2,1,0:T(8,128)(2,1)} %copy-done.1), calls=%async_computation.1 | async-start | bytes 1048576 | tf_op jit(solution)/shard_map/all_to_all | solution.py:346
  30.9 0.7 %broadcast_select_fusion.1 = bf16[4,2,128,128]{3,2,1,0:T(8,128)(2,1)} fusion(bf16[4,2,128,128]{3,2,1,0:T(8,128)(2,1)S(1)} %collective-permute-done.5.refs_4_, bf16[4,2,128,128]{3,2,1,0:T(8,128)(2,1)S(1)} %get-tuple-element.28, pred[]{:T(512)S(6)} %eq.3), kind=kLoop, calls=%fused_computation.1 | loop fusion | flops 131072 | bytes 786433 | tf_op jit(solution)/shard_map/jit(_where)/select_n | solution.py:351
  31.6 1.9 %collective-permute-start.7 = (bf16[4,2,128,128]{3,2,1,0:T(8,128)(2,1)}, bf16[4,2,128,128]{3,2,1,0:T(8,128)(2,1)S(1)}, u32[]{:S(2)}, u32[]{:S(2)}) collective-permute-start(bf16[4,2,128,128]{3,2,1,0:T(8,128)(2,1)} %broadcast_select_fusion.1), channel_id=1, source_target_pairs={{16,24},{8,16},{17,25},{9,17},{18,26},{10,18},{19,27},{11,19},{20,... | collective-permute-start | bytes 786440 | tf_op jit(solution)/shard_map/ppermute | solution.py:351
  33.5 0.7 %broadcast_select_fusion = bf16[4,2,128,128]{3,2,1,0:T(8,128)(2,1)} fusion(bf16[4,2,128,128]{3,2,1,0:T(8,128)(2,1)S(1)} %collective-permute-done.6.refs_5_, bf16[4,2,128,128]{3,2,1,0:T(8,128)(2,1)S(1)} %get-tuple-element.29, pred[]{:T(512)S(6)} %eq.3), kind=kLoop, calls=%fused_computation | loop fusion | flops 131072 | bytes 786433 | tf_op jit(solution)/shard_map/jit(_where)/select_n | solution.py:351
  34.3 2.0 %collective-permute-start.8 = (bf16[4,2,128,128]{3,2,1,0:T(8,128)(2,1)}, bf16[4,2,128,128]{3,2,1,0:T(8,128)(2,1)S(1)}, u32[]{:S(2)}, u32[]{:S(2)}) collective-permute-start(bf16[4,2,128,128]{3,2,1,0:T(8,128)(2,1)} %broadcast_select_fusion), channel_id=1, source_target_pairs={{16,24},{8,16},{17,25},{9,17},{18,26},{10,18},{19,27},{11,19},{20,... | collective-permute-start | bytes 786440 | tf_op jit(solution)/shard_map/ppermute | solution.py:351
  36.3 0.1 maximum_convert_fusion.refs_0_
  36.4 3.0 %all-to-all-done.1.refs_6_ = bf16[8,2,128,128]{3,2,1,0:T(8,128)(2,1)S(1)} async-done(((bf16[8,2,128,128]{3,2,1,0:T(8,128)(2,1)}), bf16[8,2,128,128]{3,2,1,0:T(8,128)(2,1)S(1)}, u32[]{:S(2)}, u32[]{:S(2)}) %all-to-all-start.1) | async-done | bytes 524320 | tf_op jit(solution)/shard_map/all_to_all | solution.py:346
  39.5 6.9 %far_early.1 = (f32[4,512,128]{2,1,0:T(8,128)S(1)}, f32[4,512,256]{2,1,0:T(8,128)S(1)}) custom-call(s32[24]{0:T(128)S(1)} %maximum_convert_fusion.refs_0_, bf16[272,512]{1,0:T(8,128)(2,1)S(1)} %collective-permute-done.1.refs_1_, bf16[272,512]{1,0:T(8,128)(2,1)S(1)} %collective-permute-done.3.refs_2_.refs_1_, ...), custom_call_target="tpu_custom_call" | custom-call | flops 1610612736 | bytes 4194304 | tf_op jit(solution)/shard_map/far_early/pallas_call | solution.py:295
  46.3 0.5 collective-permute-done.8.refs_3_.refs_8_
  46.9 2.1 %far_late.2 = bf16[256,512]{1,0:T(8,128)(2,1)S(1)} custom-call(s32[24]{0:T(128)S(1)} %maximum_convert_fusion.refs_0_, bf16[272,512]{1,0:T(8,128)(2,1)S(1)} %collective-permute-done.1.refs_1_, bf16[4,2,128,128]{3,2,1,0:T(8,128)(2,1)S(1)} %collective-permute-done.7.refs_2_.refs_7_, bf16[4,2,128,128]{3,2,1,0:T(8,128)(2,1)S(1)} %collective-permute-done.8.refs_3_.refs_8_, ...), custom_call_target="tpu_custom_call" | custom-call | flops 805306368 | bytes 4194304 | tf_op jit(solution)/shard_map/far_late/pallas_call | solution.py:295
  49.0 0.5 collective-permute-start.10
  49.5 2.1 %far_late.3 = bf16[256,512]{1,0:T(8,128)(2,1)S(1)} custom-call(s32[24]{0:T(128)S(1)} %maximum_convert_fusion.refs_0_, bf16[272,512]{1,0:T(8,128)(2,1)S(1)} %collective-permute-done.3.refs_2_.refs_1_, bf16[4,2,128,128]{3,2,1,0:T(8,128)(2,1)S(1)} %collective-permute-done.7.refs_2_.refs_7_, bf16[4,2,128,128]{3,2,1,0:T(8,128)(2,1)S(1)} %collective-permute-done.8.refs_3_.refs_8_, ...), custom_call_target="tpu_custom_call" | custom-call | flops 805306368 | bytes 4194304 | tf_op jit(solution)/shard_map/far_late/pallas_call | solution.py:295
  51.6 2.8 %collective-permute-start.11 = (bf16[256,512]{1,0:T(8,128)(2,1)S(1)}, bf16[256,512]{1,0:T(8,128)(2,1)S(1)}, u32[]{:S(2)}, u32[]{:S(2)}) collective-permute-start(bf16[256,512]{1,0:T(8,128)(2,1)S(1)} %far_late.3), channel_id=1, source_target_pairs={{0,6},{2,4},{4,2},{6,0},{1,7},{3,5},{5,3},{7,1},{8,14},{10,12},{12... | collective-permute-start | bytes 786440 | tf_op jit(solution)/shard_map/ppermute | solution.py:325
  54.4 8.4 %near.1 = (bf16[256,512]{1,0:T(8,128)(2,1)S(1)}, bf16[256,512]{1,0:T(8,128)(2,1)S(1)}) custom-call(s32[24]{0:T(128)S(1)} %maximum_convert_fusion.refs_0_, bf16[272,512]{1,0:T(8,128)(2,1)S(1)} %get-tuple-element.37.refs_1_, bf16[272,512]{1,0:T(8,128)(2,1)S(1)} %collective-permute-done.refs_2_, bf16[8,2,128,128]{3,2,1,0:T(8,128)(2,1)S(1)} %all-to-all-done.refs_3_, ...), custom_call_target="tpu_custom_call" | custom-call | flops 1610612736 | bytes 4194304 | tf_op jit(solution)/shard_map/near/pallas_call | solution.py:295
  62.8 0.1 collective-permute-start.9
  62.9 0.9 %unpack_most.1.refs_1_ = bf16[256,2048]{1,0:T(8,128)(2,1)} custom-call(bf16[256,512]{1,0:T(8,128)(2,1)S(1)} %collective-permute-done.10.refs_0_, bf16[256,512]{1,0:T(8,128)(2,1)S(1)} %collective-permute-done.11.refs_1_, bf16[256,512]{1,0:T(8,128)(2,1)S(1)} %get-tuple-element.40.refs_2_), custom_call_target="tpu_custom_call" | custom-call | bytes 1572864 | tf_op jit(solution)/shard_map/unpack_most/pallas_call | solution.py:108
  63.8 0.6 collective-permute-done.9.refs_0_
  64.4 0.7 %unpack_rest.1 = bf16[256,2048]{1,0:T(8,128)(2,1)} custom-call(bf16[256,512]{1,0:T(8,128)(2,1)S(1)} %collective-permute-done.9.refs_0_, bf16[256,2048]{1,0:T(8,128)(2,1)} %unpack_most.1.refs_1_), custom_call_target="tpu_custom_call", output_to_operand_aliasing={{}: (1, {})} | custom-call | bytes 524288 | tf_op jit(solution)/shard_map/unpack_rest/pallas_call | solution.py:108
  (17 shorter events, 0.1 us)
Async XLA Ops:
  0.0 7.2 %copy-start.2 = (s32[2,4,3]{1,0,2:T(2,128)S(1)}, s32[2,4,3]{1,0,2:T(2,128)}, u32[]{:S(2)}) copy-start(s32[2,4,3]{1,0,2:T(2,128)} %param.7) | copy-start | bytes 292
  0.0 7.3 %copy-start = (bf16[256,2048]{1,0:T(8,128)(2,1)S(1)}, bf16[256,2048]{1,0:T(8,128)(2,1)}, u32[]{:S(2)}) copy-start(bf16[256,2048]{1,0:T(8,128)(2,1)} %q_ref.1) | copy-start | bytes 3145732
  2.0 12.3 %collective-permute-start.4 = (bf16[8,2,128,128]{3,2,1,0:T(8,128)(2,1)}, bf16[8,2,128,128]{3,2,1,0:T(8,128)(2,1)S(1)}, u32[]{:S(2)}, u32[]{:S(2)}) collective-permute-start(bf16[8,2,128,128]{3,2,1,0:T(8,128)(2,1)} %pack_kv.1), channel_id=1, source_target_pairs={{8,24},{0,8},{9,25},{1,9},{10,26},{2,10},{11,27},{3,11},{12,28},{4... | collective-permute-start | bytes 1572872 | tf_op jit(solution)/shard_map/ppermute | solution.py:332
  2.7 11.6 %all-to-all-start = ((bf16[8,2,128,128]{3,2,1,0:T(8,128)(2,1)}), bf16[8,2,128,128]{3,2,1,0:T(8,128)(2,1)S(1)}, u32[]{:S(2)}, u32[]{:S(2)}) async-start(bf16[8,2,128,128]{3,2,1,0:T(8,128)(2,1)} %pack_kv.1), calls=%async_computation | async-start | bytes 1048576 | tf_op jit(solution)/shard_map/all_to_all | solution.py:333
  8.7 17.1 %collective-permute-start.2 = (bf16[272,512]{1,0:T(8,128)(2,1)S(1)}, bf16[272,512]{1,0:T(8,128)(2,1)}, u32[]{:S(2)}, u32[]{:S(2)}) collective-permute-start(bf16[272,512]{1,0:T(8,128)(2,1)S(1)} %get-tuple-element.26), channel_id=1, source_target_pairs={{0,4},{2,6},{4,0},{6,2},{1,5},{3,7},{5,1},{7,3},{8,12},{10,14},{12... | collective-permute-start | bytes 835592 | tf_op jit(solution)/shard_map/ppermute | solution.py:325
  14.3 0.8 %copy-start.1 = (bf16[8,2,128,128]{3,2,1,0:T(8,128)(2,1)}, bf16[8,2,128,128]{3,2,1,0:T(8,128)(2,1)S(1)}, u32[]{:S(2)}) copy-start(bf16[8,2,128,128]{3,2,1,0:T(8,128)(2,1)S(1)} %collective-permute-done.4) | copy-start | bytes 1572868
  15.1 15.8 %collective-permute-start.5 = (bf16[4,2,128,128]{3,2,1,0:T(8,128)(2,1)S(1)}, bf16[4,2,128,128]{3,2,1,0:T(8,128)(2,1)S(1)}, u32[]{:S(2)}, u32[]{:S(2)}) collective-permute-start(bf16[4,2,128,128]{3,2,1,0:T(8,128)(2,1)S(1)} %get-tuple-element.28), channel_id=1, source_target_pairs={{0,16},{16,24},{1,17},{17,25},{2,18},{18,26},{3,19},{19,27},{4,20}... | collective-permute-start | bytes 786440 | tf_op jit(solution)/shard_map/ppermute | solution.py:345
  21.8 11.7 %collective-permute-start.6 = (bf16[4,2,128,128]{3,2,1,0:T(8,128)(2,1)S(1)}, bf16[4,2,128,128]{3,2,1,0:T(8,128)(2,1)S(1)}, u32[]{:S(2)}, u32[]{:S(2)}) collective-permute-start(bf16[4,2,128,128]{3,2,1,0:T(8,128)(2,1)S(1)} %get-tuple-element.29), channel_id=1, source_target_pairs={{0,16},{16,24},{1,17},{17,25},{2,18},{18,26},{3,19},{19,27},{4,20}... | collective-permute-start | bytes 786440 | tf_op jit(solution)/shard_map/ppermute | solution.py:345
  23.7 12.6 %collective-permute-start = (bf16[272,512]{1,0:T(8,128)(2,1)}, bf16[272,512]{1,0:T(8,128)(2,1)S(1)}, u32[]{:S(2)}, u32[]{:S(2)}) collective-permute-start(bf16[272,512]{1,0:T(8,128)(2,1)} %get-tuple-element.24), channel_id=1, source_target_pairs={{0,2},{2,0},{4,6},{6,4},{1,3},{3,1},{5,7},{7,5},{8,10},{10,8},{12,... | collective-permute-start | bytes 835592 | tf_op jit(solution)/shard_map/ppermute | solution.py:325
  25.6 10.7 %collective-permute-start.1 = (bf16[272,512]{1,0:T(8,128)(2,1)S(1)}, bf16[272,512]{1,0:T(8,128)(2,1)S(1)}, u32[]{:S(2)}, u32[]{:S(2)}) collective-permute-start(bf16[272,512]{1,0:T(8,128)(2,1)S(1)} %get-tuple-element.25), channel_id=1, source_target_pairs={{0,4},{2,6},{4,0},{6,2},{1,5},{3,7},{5,1},{7,3},{8,12},{10,14},{12... | collective-permute-start | bytes 835592 | tf_op jit(solution)/shard_map/ppermute | solution.py:325
  25.9 10.4 %collective-permute-start.3 = (bf16[272,512]{1,0:T(8,128)(2,1)}, bf16[272,512]{1,0:T(8,128)(2,1)S(1)}, u32[]{:S(2)}, u32[]{:S(2)}) collective-permute-start(bf16[272,512]{1,0:T(8,128)(2,1)} %collective-permute-done.2), channel_id=1, source_target_pairs={{0,2},{2,0},{4,6},{6,4},{1,3},{3,1},{5,7},{7,5},{8,10},{10,8},{12,... | collective-permute-start | bytes 835592 | tf_op jit(solution)/shard_map/ppermute | solution.py:325
  26.2 13.2 %all-to-all-start.1 = ((bf16[8,2,128,128]{3,2,1,0:T(8,128)(2,1)}), bf16[8,2,128,128]{3,2,1,0:T(8,128)(2,1)S(1)}, u32[]{:S(2)}, u32[]{:S(2)}) async-start(bf16[8,2,128,128]{3,2,1,0:T(8,128)(2,1)} %copy-done.1), calls=%async_computation.1 | async-start | bytes 1048576 | tf_op jit(solution)/shard_map/all_to_all | solution.py:346
  31.6 14.7 %collective-permute-start.7 = (bf16[4,2,128,128]{3,2,1,0:T(8,128)(2,1)}, bf16[4,2,128,128]{3,2,1,0:T(8,128)(2,1)S(1)}, u32[]{:S(2)}, u32[]{:S(2)}) collective-permute-start(bf16[4,2,128,128]{3,2,1,0:T(8,128)(2,1)} %broadcast_select_fusion.1), channel_id=1, source_target_pairs={{16,24},{8,16},{17,25},{9,17},{18,26},{10,18},{19,27},{11,19},{20,... | collective-permute-start | bytes 786440 | tf_op jit(solution)/shard_map/ppermute | solution.py:351
  34.3 12.6 %collective-permute-start.8 = (bf16[4,2,128,128]{3,2,1,0:T(8,128)(2,1)}, bf16[4,2,128,128]{3,2,1,0:T(8,128)(2,1)S(1)}, u32[]{:S(2)}, u32[]{:S(2)}) collective-permute-start(bf16[4,2,128,128]{3,2,1,0:T(8,128)(2,1)} %broadcast_select_fusion), channel_id=1, source_target_pairs={{16,24},{8,16},{17,25},{9,17},{18,26},{10,18},{19,27},{11,19},{20,... | collective-permute-start | bytes 786440 | tf_op jit(solution)/shard_map/ppermute | solution.py:351
  49.0 13.9 %collective-permute-start.10 = (bf16[256,512]{1,0:T(8,128)(2,1)S(1)}, bf16[256,512]{1,0:T(8,128)(2,1)S(1)}, u32[]{:S(2)}, u32[]{:S(2)}) collective-permute-start(bf16[256,512]{1,0:T(8,128)(2,1)S(1)} %far_late.2), channel_id=1, source_target_pairs={{0,4},{2,6},{4,0},{6,2},{1,5},{3,7},{5,1},{7,3},{8,12},{10,14},{12... | collective-permute-start | bytes 786440 | tf_op jit(solution)/shard_map/ppermute | solution.py:325
  51.6 11.3 %collective-permute-start.11 = (bf16[256,512]{1,0:T(8,128)(2,1)S(1)}, bf16[256,512]{1,0:T(8,128)(2,1)S(1)}, u32[]{:S(2)}, u32[]{:S(2)}) collective-permute-start(bf16[256,512]{1,0:T(8,128)(2,1)S(1)} %far_late.3), channel_id=1, source_target_pairs={{0,6},{2,4},{4,2},{6,0},{1,7},{3,5},{5,3},{7,1},{8,14},{10,12},{12... | collective-permute-start | bytes 786440 | tf_op jit(solution)/shard_map/ppermute | solution.py:325
  62.8 1.6 %collective-permute-start.9 = (bf16[256,512]{1,0:T(8,128)(2,1)S(1)}, bf16[256,512]{1,0:T(8,128)(2,1)S(1)}, u32[]{:S(2)}, u32[]{:S(2)}) collective-permute-start(bf16[256,512]{1,0:T(8,128)(2,1)S(1)} %get-tuple-element.39), channel_id=1, source_target_pairs={{0,2},{2,0},{4,6},{6,4},{1,3},{3,1},{5,7},{7,5},{8,10},{10,8},{12,... | collective-permute-start | bytes 786440 | tf_op jit(solution)/shard_map/ppermute | solution.py:325

commit v10 on v9

--- a/solution.py
+++ b/solution.py
@@ -339,7 +339,6 @@
     else:
         q = exchange(q, everyone)
     if by_levels:
-        own, raw = lax.optimization_barrier((own, raw))
         half = own.shape[0] // 2
         halves = lax.optimization_barrier((own[:half], own[half:]))
         up = [lax.ppermute(piece, "lev", [(0, 2), (2, 3)]) for piece in halves]

time: 65.6 us -> 74 us (1.13); the launches traced: 65.3 us -> 72.8 us
  starting transfers between devices: 28.6 us -> 38.3 us
  waiting for transfers between devices: 9.47 us -> 8.17 us
  local copies, waits for them, and re-layouts: 0.9 us -> 0.16 us
    ppermute x2, starting transfers between devices: 3.89 us -> 17 us  [body(): lax.ppermute(jnp.where(forwards, a, b), 'lev', [(2, 3), (1, 2)])]
    ppermute x2, starting transfers between devices: 8.58 us -> 5.23 us  [body(): up = [lax.ppermute(piece, 'lev', [(0, 2), (2, 3)]) for piece in halves]]
    all_to_all x1, waiting for transfers between devices: 3.05 us -> 0.01 us  [body(): p2 = lax.all_to_all(raw, ('sub', 'head'), 0, 0, tiled=True)]
    ppermute x2, waiting for transfers between devices: 0.51 us -> 2.37 us  [body(): lax.ppermute(jnp.where(forwards, a, b), 'lev', [(2, 3), (1, 2)])]
    all_to_all x1, waiting for transfers between devices: 5.31 us -> 3.86 us  [body(): own = lax.all_to_all(packed, ('sub', 'head'), 0, 0, tiled=True)]
    ppermute x2, waiting for transfers between devices: 0.01 us -> 1.33 us  [body(): up = [lax.ppermute(piece, 'lev', [(0, 2), (2, 3)]) for piece in halves]]
    ppermute x1, starting transfers between devices: 0.68 us -> 1.46 us  [body(): raw = lax.ppermute(packed, 'lev', [(1, 3), (0, 1)])]
    unnamed x7 -> x5, local copies, waits for them, and re-layouts: 0.85 us -> 0.11 us
  transfers between devices with their start and end apart: 14 -> 14, of which waited for: 4 -> 5; matrix products, arithmetic and copies ran while one was open for 3% -> 2% of each run, Pallas kernels for 30% -> 26%
where the time goes in v10:
time: 74 us; the launch traced here: 72.8 us
  starting transfers between devices  38.3 us (52%)
  Pallas kernels  24.3 us (33%)
  waiting for transfers between devices  8.17 us (11%)
  other arithmetic  1.54 us (2%)
    pallas_call x4, Pallas kernels, attention(): pl.pallas_call(kernel, in_specs=[SMEM] + [VMEM] * (n_q + n_src + len(stat...  19.3 us
    ppermute x2, starting transfers between devices, body(): lax.ppermute(jnp.where(forwards, a, b), 'lev', [(2, 3), (1, 2)])  17 us
    ppermute x7, starting transfers between devices, exchange(): lax.ppermute(piece, 'sub', [(i, i ^ k) for i in range(subs)])  6 us
    ppermute x2, starting transfers between devices, body(): up = [lax.ppermute(piece, 'lev', [(0, 2), (2, 3)]) for piece in halves]  5.23 us
    all_to_all x1, starting transfers between devices, body(): own = lax.all_to_all(packed, ('sub', 'head'), 0, 0, tiled=True)  4.51 us
    all_to_all x1, starting transfers between devices, body(): p2 = lax.all_to_all(raw, ('sub', 'head'), 0, 0, tiled=True)  4.14 us
    all_to_all x1, waiting for transfers between devices, body(): own = lax.all_to_all(packed, ('sub', 'head'), 0, 0, tiled=True)  3.86 us
    ppermute x2, waiting for transfers between devices, body(): lax.ppermute(jnp.where(forwards, a, b), 'lev', [(2, 3), (1, 2)])  2.37 us
  transfers between devices with their start and end apart: 14, of which 5 were waited for; matrix products, arithmetic and copies ran while one was open for 2% of the time, Pallas kernels for 26%

profile of v10, /device:TPU:23, one launch (start us, length us, event | category | flops | bytes accessed | tf_op | source)
XLA Modules:
  0.0 72.8 jit_solution(6744173930093707835)
XLA Ops:
  0.0 2.0 %pack_kv.1 = bf16[8,2,128,128]{3,2,1,0:T(8,128)(2,1)} custom-call(bf16[128,1024]{1,0:T(8,128)(2,1)} %k_ref.1, bf16[128,1024]{1,0:T(8,128)(2,1)} %v_ref.1), custom_call_target="tpu_custom_call" | custom-call | bytes 1048576 | tf_op jit(solution)/shard_map/pack_kv/pallas_call | solution.py:55
  2.0 4.5 %all-to-all-start = ((bf16[8,2,128,128]{3,2,1,0:T(8,128)(2,1)}), bf16[8,2,128,128]{3,2,1,0:T(8,128)(2,1)S(1)}, u32[]{:S(2)}, u32[]{:S(2)}) async-start(bf16[8,2,128,128]{3,2,1,0:T(8,128)(2,1)} %pack_kv.1), calls=%async_computation | async-start | bytes 1048576 | tf_op jit(solution)/shard_map/all_to_all | solution.py:333
  6.5 1.5 %collective-permute-start.8 = (bf16[8,2,128,128]{3,2,1,0:T(8,128)(2,1)}, bf16[8,2,128,128]{3,2,1,0:T(8,128)(2,1)}, u32[]{:S(2)}, u32[]{:S(2)}) collective-permute-start(bf16[8,2,128,128]{3,2,1,0:T(8,128)(2,1)} %pack_kv.1), channel_id=1, source_target_pairs={{8,24},{0,8},{9,25},{1,9},{10,26},{2,10},{11,27},{3,11},{12,28},{4... | collective-permute-start | bytes 1572872 | tf_op jit(solution)/shard_map/ppermute | solution.py:332
  8.0 0.1 copy.6.sel_ref
  8.1 1.4 %pack_q.1 = (bf16[272,512]{1,0:T(8,128)(2,1)S(1)}, bf16[272,512]{1,0:T(8,128)(2,1)}, bf16[272,512]{1,0:T(8,128)(2,1)S(1)}, bf16[272,512]{1,0:T(8,128)(2,1)S(1)}) custom-call(s32[2,4,3]{2,1,0:T(4,128)S(1)} %copy.6.sel_ref, bf16[256,2048]{1,0:T(8,128)(2,1)S(1)} %copy-done), custom_call_target="tpu_custom_call" | custom-call | bytes 2097152 | tf_op jit(solution)/shard_map/pack_q/pallas_call | solution.py:81
  9.5 0.3 collective-permute-start.2
  9.8 3.9 %all-to-all-done.refs_3_ = bf16[8,2,128,128]{3,2,1,0:T(8,128)(2,1)S(1)} async-done(((bf16[8,2,128,128]{3,2,1,0:T(8,128)(2,1)}), bf16[8,2,128,128]{3,2,1,0:T(8,128)(2,1)S(1)}, u32[]{:S(2)}, u32[]{:S(2)}) %all-to-all-start) | async-done | bytes 524320 | tf_op jit(solution)/shard_map/all_to_all | solution.py:333
  13.7 3.3 %collective-permute-start.4 = (bf16[4,2,128,128]{3,2,1,0:T(8,128)(2,1)S(1)}, bf16[4,2,128,128]{3,2,1,0:T(8,128)(2,1)S(1)}, u32[]{:S(2)}, u32[]{:S(2)}) collective-permute-start(bf16[4,2,128,128]{3,2,1,0:T(8,128)(2,1)S(1)} %get-tuple-element.25), channel_id=1, source_target_pairs={{0,16},{16,24},{1,17},{17,25},{2,18},{18,26},{3,19},{19,27},{4,20}... | collective-permute-start | bytes 786440 | tf_op jit(solution)/shard_map/ppermute | solution.py:344
  17.0 1.9 %collective-permute-start.5 = (bf16[4,2,128,128]{3,2,1,0:T(8,128)(2,1)S(1)}, bf16[4,2,128,128]{3,2,1,0:T(8,128)(2,1)S(1)}, u32[]{:S(2)}, u32[]{:S(2)}) collective-permute-start(bf16[4,2,128,128]{3,2,1,0:T(8,128)(2,1)S(1)} %get-tuple-element.26), channel_id=1, source_target_pairs={{0,16},{16,24},{1,17},{17,25},{2,18},{18,26},{3,19},{19,27},{4,20}... | collective-permute-start | bytes 786440 | tf_op jit(solution)/shard_map/ppermute | solution.py:344
  18.9 1.4 %collective-permute-start = (bf16[272,512]{1,0:T(8,128)(2,1)}, bf16[272,512]{1,0:T(8,128)(2,1)S(1)}, u32[]{:S(2)}, u32[]{:S(2)}) collective-permute-start(bf16[272,512]{1,0:T(8,128)(2,1)} %get-tuple-element.22), channel_id=1, source_target_pairs={{0,2},{2,0},{4,6},{6,4},{1,3},{3,1},{5,7},{7,5},{8,10},{10,8},{12,... | collective-permute-start | bytes 835592 | tf_op jit(solution)/shard_map/ppermute | solution.py:325
  20.3 1.2 %collective-permute-start.1 = (bf16[272,512]{1,0:T(8,128)(2,1)S(1)}, bf16[272,512]{1,0:T(8,128)(2,1)S(1)}, u32[]{:S(2)}, u32[]{:S(2)}) collective-permute-start(bf16[272,512]{1,0:T(8,128)(2,1)S(1)} %get-tuple-element.23), channel_id=1, source_target_pairs={{0,4},{2,6},{4,0},{6,2},{1,5},{3,7},{5,1},{7,3},{8,12},{10,14},{12... | collective-permute-start | bytes 835592 | tf_op jit(solution)/shard_map/ppermute | solution.py:325
  21.5 0.0 collective-permute-done.8
  21.5 0.4 collective-permute-start.3
  21.8 4.1 %all-to-all-start.1 = ((bf16[8,2,128,128]{3,2,1,0:T(8,128)(2,1)}), bf16[8,2,128,128]{3,2,1,0:T(8,128)(2,1)S(1)}, u32[]{:S(2)}, u32[]{:S(2)}) async-start(bf16[8,2,128,128]{3,2,1,0:T(8,128)(2,1)} %collective-permute-done.8), calls=%async_computation.1 | async-start | bytes 1048576 | tf_op jit(solution)/shard_map/all_to_all | solution.py:345
  26.0 1.3 %collective-permute-done.4.refs_4_ = bf16[4,2,128,128]{3,2,1,0:T(8,128)(2,1)S(1)} collective-permute-done((bf16[4,2,128,128]{3,2,1,0:T(8,128)(2,1)S(1)}, bf16[4,2,128,128]{3,2,1,0:T(8,128)(2,1)S(1)}, u32[]{:S(2)}, u32[]{:S(2)}) %collective-permute-start.4) | collective-permute-done | bytes 262176 | tf_op jit(solution)/shard_map/ppermute | solution.py:344
  27.3 0.7 %broadcast_select_fusion.1 = bf16[4,2,128,128]{3,2,1,0:T(8,128)(2,1)} fusion(bf16[4,2,128,128]{3,2,1,0:T(8,128)(2,1)S(1)} %collective-permute-done.4.refs_4_, bf16[4,2,128,128]{3,2,1,0:T(8,128)(2,1)S(1)} %get-tuple-element.25, pred[]{:T(512)S(6)} %eq.3), kind=kLoop, calls=%fused_computation.1 | loop fusion | flops 131072 | bytes 786433 | tf_op jit(solution)/shard_map/jit(_where)/select_n | solution.py:350
  28.0 15.1 %collective-permute-start.6 = (bf16[4,2,128,128]{3,2,1,0:T(8,128)(2,1)}, bf16[4,2,128,128]{3,2,1,0:T(8,128)(2,1)S(1)}, u32[]{:S(2)}, u32[]{:S(2)}) collective-permute-start(bf16[4,2,128,128]{3,2,1,0:T(8,128)(2,1)} %broadcast_select_fusion.1), channel_id=1, source_target_pairs={{16,24},{8,16},{17,25},{9,17},{18,26},{10,18},{19,27},{11,19},{20,... | collective-permute-start | bytes 786440 | tf_op jit(solution)/shard_map/ppermute | solution.py:350
  43.1 0.7 broadcast_select_fusion
  43.9 1.9 %collective-permute-start.7 = (bf16[4,2,128,128]{3,2,1,0:T(8,128)(2,1)}, bf16[4,2,128,128]{3,2,1,0:T(8,128)(2,1)S(1)}, u32[]{:S(2)}, u32[]{:S(2)}) collective-permute-start(bf16[4,2,128,128]{3,2,1,0:T(8,128)(2,1)} %broadcast_select_fusion), channel_id=1, source_target_pairs={{16,24},{8,16},{17,25},{9,17},{18,26},{10,18},{19,27},{11,19},{20,... | collective-permute-start | bytes 786440 | tf_op jit(solution)/shard_map/ppermute | solution.py:350
  45.8 0.1 maximum_convert_fusion.refs_0_
  45.9 6.1 %far_early.1 = (f32[4,512,128]{2,1,0:T(8,128)S(1)}, f32[4,512,256]{2,1,0:T(8,128)S(1)}) custom-call(s32[24]{0:T(128)S(1)} %maximum_convert_fusion.refs_0_, bf16[272,512]{1,0:T(8,128)(2,1)S(1)} %collective-permute-done.1.refs_1_, bf16[272,512]{1,0:T(8,128)(2,1)S(1)} %collective-permute-done.3.refs_2_.refs_1_, ...), custom_call_target="tpu_custom_call" | custom-call | flops 1610612736 | bytes 4194304 | tf_op jit(solution)/shard_map/far_early/pallas_call | solution.py:295
  52.0 2.4 %collective-permute-done.7.refs_3_.refs_8_ = bf16[4,2,128,128]{3,2,1,0:T(8,128)(2,1)S(1)} collective-permute-done((bf16[4,2,128,128]{3,2,1,0:T(8,128)(2,1)}, bf16[4,2,128,128]{3,2,1,0:T(8,128)(2,1)S(1)}, u32[]{:S(2)}, u32[]{:S(2)}) %collective-permute-start.7) | collective-permute-done | bytes 262176 | tf_op jit(solution)/shard_map/ppermute | solution.py:350
  54.4 2.5 %far_late.2 = bf16[256,512]{1,0:T(8,128)(2,1)S(1)} custom-call(s32[24]{0:T(128)S(1)} %maximum_convert_fusion.refs_0_, bf16[272,512]{1,0:T(8,128)(2,1)S(1)} %collective-permute-done.1.refs_1_, bf16[4,2,128,128]{3,2,1,0:T(8,128)(2,1)S(1)} %collective-permute-done.6.refs_2_.refs_7_, bf16[4,2,128,128]{3,2,1,0:T(8,128)(2,1)S(1)} %collective-permute-done.7.refs_3_.refs_8_, ...), custom_call_target="tpu_custom_call" | custom-call | flops 805306368 | bytes 4194304 | tf_op jit(solution)/shard_map/far_late/pallas_call | solution.py:295
  56.9 0.1 collective-permute-start.10
  57.0 2.3 %far_late.3 = bf16[256,512]{1,0:T(8,128)(2,1)S(1)} custom-call(s32[24]{0:T(128)S(1)} %maximum_convert_fusion.refs_0_, bf16[272,512]{1,0:T(8,128)(2,1)S(1)} %collective-permute-done.3.refs_2_.refs_1_, bf16[4,2,128,128]{3,2,1,0:T(8,128)(2,1)S(1)} %collective-permute-done.6.refs_2_.refs_7_, bf16[4,2,128,128]{3,2,1,0:T(8,128)(2,1)S(1)} %collective-permute-done.7.refs_3_.refs_8_, ...), custom_call_target="tpu_custom_call" | custom-call | flops 805306368 | bytes 4194304 | tf_op jit(solution)/shard_map/far_late/pallas_call | solution.py:295
  59.3 2.7 %collective-permute-start.11 = (bf16[256,512]{1,0:T(8,128)(2,1)S(1)}, bf16[256,512]{1,0:T(8,128)(2,1)S(1)}, u32[]{:S(2)}, u32[]{:S(2)}) collective-permute-start(bf16[256,512]{1,0:T(8,128)(2,1)S(1)} %far_late.3), channel_id=1, source_target_pairs={{0,6},{2,4},{4,2},{6,0},{1,7},{3,5},{5,3},{7,1},{8,14},{10,12},{12... | collective-permute-start | bytes 786440 | tf_op jit(solution)/shard_map/ppermute | solution.py:325
  61.9 8.4 %near.1 = (bf16[256,512]{1,0:T(8,128)(2,1)S(1)}, bf16[256,512]{1,0:T(8,128)(2,1)S(1)}) custom-call(s32[24]{0:T(128)S(1)} %maximum_convert_fusion.refs_0_, bf16[272,512]{1,0:T(8,128)(2,1)S(1)} %get-tuple-element.33.refs_1_, bf16[272,512]{1,0:T(8,128)(2,1)S(1)} %collective-permute-done.refs_2_, bf16[8,2,128,128]{3,2,1,0:T(8,128)(2,1)S(1)} %all-to-all-done.refs_3_, ...), custom_call_target="tpu_custom_call" | custom-call | flops 1610612736 | bytes 4194304 | tf_op jit(solution)/shard_map/near/pallas_call | solution.py:295
  70.3 0.1 collective-permute-start.9
  70.4 0.2 collective-permute-done.11.refs_1_
  70.6 0.9 %unpack_most.1.refs_1_ = bf16[256,2048]{1,0:T(8,128)(2,1)} custom-call(bf16[256,512]{1,0:T(8,128)(2,1)S(1)} %collective-permute-done.10.refs_0_, bf16[256,512]{1,0:T(8,128)(2,1)S(1)} %collective-permute-done.11.refs_1_, bf16[256,512]{1,0:T(8,128)(2,1)S(1)} %get-tuple-element.36.refs_2_), custom_call_target="tpu_custom_call" | custom-call | bytes 1572864 | tf_op jit(solution)/shard_map/unpack_most/pallas_call | solution.py:108
  71.5 0.4 collective-permute-done.9.refs_0_
  71.9 0.7 unpack_rest.1
  (15 shorter events, 0.1 us)
Async XLA Ops:
  0.0 8.0 %copy-start.1 = (s32[2,4,3]{1,0,2:T(2,128)S(1)}, s32[2,4,3]{1,0,2:T(2,128)}, u32[]{:S(2)}) copy-start(s32[2,4,3]{1,0,2:T(2,128)} %param.7) | copy-start | bytes 292
  0.0 8.1 %copy-start = (bf16[256,2048]{1,0:T(8,128)(2,1)S(1)}, bf16[256,2048]{1,0:T(8,128)(2,1)}, u32[]{:S(2)}) copy-start(bf16[256,2048]{1,0:T(8,128)(2,1)} %q_ref.1) | copy-start | bytes 3145732
  2.0 11.6 %all-to-all-start = ((bf16[8,2,128,128]{3,2,1,0:T(8,128)(2,1)}), bf16[8,2,128,128]{3,2,1,0:T(8,128)(2,1)S(1)}, u32[]{:S(2)}, u32[]{:S(2)}) async-start(bf16[8,2,128,128]{3,2,1,0:T(8,128)(2,1)} %pack_kv.1), calls=%async_computation | async-start | bytes 1048576 | tf_op jit(solution)/shard_map/all_to_all | solution.py:333
  6.5 15.0 %collective-permute-start.8 = (bf16[8,2,128,128]{3,2,1,0:T(8,128)(2,1)}, bf16[8,2,128,128]{3,2,1,0:T(8,128)(2,1)}, u32[]{:S(2)}, u32[]{:S(2)}) collective-permute-start(bf16[8,2,128,128]{3,2,1,0:T(8,128)(2,1)} %pack_kv.1), channel_id=1, source_target_pairs={{8,24},{0,8},{9,25},{1,9},{10,26},{2,10},{11,27},{3,11},{12,28},{4... | collective-permute-start | bytes 1572872 | tf_op jit(solution)/shard_map/ppermute | solution.py:332
  9.5 10.8 %collective-permute-start.2 = (bf16[272,512]{1,0:T(8,128)(2,1)S(1)}, bf16[272,512]{1,0:T(8,128)(2,1)}, u32[]{:S(2)}, u32[]{:S(2)}) collective-permute-start(bf16[272,512]{1,0:T(8,128)(2,1)S(1)} %get-tuple-element.24), channel_id=1, source_target_pairs={{0,4},{2,6},{4,0},{6,2},{1,5},{3,7},{5,1},{7,3},{8,12},{10,14},{12... | collective-permute-start | bytes 835592 | tf_op jit(solution)/shard_map/ppermute | solution.py:325
  13.7 13.6 %collective-permute-start.4 = (bf16[4,2,128,128]{3,2,1,0:T(8,128)(2,1)S(1)}, bf16[4,2,128,128]{3,2,1,0:T(8,128)(2,1)S(1)}, u32[]{:S(2)}, u32[]{:S(2)}) collective-permute-start(bf16[4,2,128,128]{3,2,1,0:T(8,128)(2,1)S(1)} %get-tuple-element.25), channel_id=1, source_target_pairs={{0,16},{16,24},{1,17},{17,25},{2,18},{18,26},{3,19},{19,27},{4,20}... | collective-permute-start | bytes 786440 | tf_op jit(solution)/shard_map/ppermute | solution.py:344
  17.0 26.1 %collective-permute-start.5 = (bf16[4,2,128,128]{3,2,1,0:T(8,128)(2,1)S(1)}, bf16[4,2,128,128]{3,2,1,0:T(8,128)(2,1)S(1)}, u32[]{:S(2)}, u32[]{:S(2)}) collective-permute-start(bf16[4,2,128,128]{3,2,1,0:T(8,128)(2,1)S(1)} %get-tuple-element.26), channel_id=1, source_target_pairs={{0,16},{16,24},{1,17},{17,25},{2,18},{18,26},{3,19},{19,27},{4,20}... | collective-permute-start | bytes 786440 | tf_op jit(solution)/shard_map/ppermute | solution.py:344
  18.9 26.9 %collective-permute-start = (bf16[272,512]{1,0:T(8,128)(2,1)}, bf16[272,512]{1,0:T(8,128)(2,1)S(1)}, u32[]{:S(2)}, u32[]{:S(2)}) collective-permute-start(bf16[272,512]{1,0:T(8,128)(2,1)} %get-tuple-element.22), channel_id=1, source_target_pairs={{0,2},{2,0},{4,6},{6,4},{1,3},{3,1},{5,7},{7,5},{8,10},{10,8},{12,... | collective-permute-start | bytes 835592 | tf_op jit(solution)/shard_map/ppermute | solution.py:325
  20.3 25.5 %collective-permute-start.1 = (bf16[272,512]{1,0:T(8,128)(2,1)S(1)}, bf16[272,512]{1,0:T(8,128)(2,1)S(1)}, u32[]{:S(2)}, u32[]{:S(2)}) collective-permute-start(bf16[272,512]{1,0:T(8,128)(2,1)S(1)} %get-tuple-element.23), channel_id=1, source_target_pairs={{0,4},{2,6},{4,0},{6,2},{1,5},{3,7},{5,1},{7,3},{8,12},{10,14},{12... | collective-permute-start | bytes 835592 | tf_op jit(solution)/shard_map/ppermute | solution.py:325
  21.5 24.3 %collective-permute-start.3 = (bf16[272,512]{1,0:T(8,128)(2,1)}, bf16[272,512]{1,0:T(8,128)(2,1)S(1)}, u32[]{:S(2)}, u32[]{:S(2)}) collective-permute-start(bf16[272,512]{1,0:T(8,128)(2,1)} %collective-permute-done.2), channel_id=1, source_target_pairs={{0,2},{2,0},{4,6},{6,4},{1,3},{3,1},{5,7},{7,5},{8,10},{10,8},{12,... | collective-permute-start | bytes 835592 | tf_op jit(solution)/shard_map/ppermute | solution.py:325
  21.8 24.1 %all-to-all-start.1 = ((bf16[8,2,128,128]{3,2,1,0:T(8,128)(2,1)}), bf16[8,2,128,128]{3,2,1,0:T(8,128)(2,1)S(1)}, u32[]{:S(2)}, u32[]{:S(2)}) async-start(bf16[8,2,128,128]{3,2,1,0:T(8,128)(2,1)} %collective-permute-done.8), calls=%async_computation.1 | async-start | bytes 1048576 | tf_op jit(solution)/shard_map/all_to_all | solution.py:345
  28.0 23.9 %collective-permute-start.6 = (bf16[4,2,128,128]{3,2,1,0:T(8,128)(2,1)}, bf16[4,2,128,128]{3,2,1,0:T(8,128)(2,1)S(1)}, u32[]{:S(2)}, u32[]{:S(2)}) collective-permute-start(bf16[4,2,128,128]{3,2,1,0:T(8,128)(2,1)} %broadcast_select_fusion.1), channel_id=1, source_target_pairs={{16,24},{8,16},{17,25},{9,17},{18,26},{10,18},{19,27},{11,19},{20,... | collective-permute-start | bytes 786440 | tf_op jit(solution)/shard_map/ppermute | solution.py:350
  43.9 10.5 %collective-permute-start.7 = (bf16[4,2,128,128]{3,2,1,0:T(8,128)(2,1)}, bf16[4,2,128,128]{3,2,1,0:T(8,128)(2,1)S(1)}, u32[]{:S(2)}, u32[]{:S(2)}) collective-permute-start(bf16[4,2,128,128]{3,2,1,0:T(8,128)(2,1)} %broadcast_select_fusion), channel_id=1, source_target_pairs={{16,24},{8,16},{17,25},{9,17},{18,26},{10,18},{19,27},{11,19},{20,... | collective-permute-start | bytes 786440 | tf_op jit(solution)/shard_map/ppermute | solution.py:350
  56.9 13.5 %collective-permute-start.10 = (bf16[256,512]{1,0:T(8,128)(2,1)S(1)}, bf16[256,512]{1,0:T(8,128)(2,1)S(1)}, u32[]{:S(2)}, u32[]{:S(2)}) collective-permute-start(bf16[256,512]{1,0:T(8,128)(2,1)S(1)} %far_late.2), channel_id=1, source_target_pairs={{0,4},{2,6},{4,0},{6,2},{1,5},{3,7},{5,1},{7,3},{8,12},{10,14},{12... | collective-permute-start | bytes 786440 | tf_op jit(solution)/shard_map/ppermute | solution.py:325
  59.3 11.3 %collective-permute-start.11 = (bf16[256,512]{1,0:T(8,128)(2,1)S(1)}, bf16[256,512]{1,0:T(8,128)(2,1)S(1)}, u32[]{:S(2)}, u32[]{:S(2)}) collective-permute-start(bf16[256,512]{1,0:T(8,128)(2,1)S(1)} %far_late.3), channel_id=1, source_target_pairs={{0,6},{2,4},{4,2},{6,0},{1,7},{3,5},{5,3},{7,1},{8,14},{10,12},{12... | collective-permute-start | bytes 786440 | tf_op jit(solution)/shard_map/ppermute | solution.py:325
  70.3 1.6 %collective-permute-start.9 = (bf16[256,512]{1,0:T(8,128)(2,1)S(1)}, bf16[256,512]{1,0:T(8,128)(2,1)S(1)}, u32[]{:S(2)}, u32[]{:S(2)}) collective-permute-start(bf16[256,512]{1,0:T(8,128)(2,1)S(1)} %get-tuple-element.35), channel_id=1, source_target_pairs={{0,2},{2,0},{4,6},{6,4},{1,3},{3,1},{5,7},{7,5},{8,10},{10,8},{12,... | collective-permute-start | bytes 786440 | tf_op jit(solution)/shard_map/ppermute | solution.py:325

commit v11 on v9

--- a/solution.py
+++ b/solution.py
@@ -175,16 +175,26 @@
             count = pieces * TILE
             keys_at = pl.ds(pl.multiple_of((own - bases[0]) * BLK, BLK), count)
             q_rows = pl.ds(pl.multiple_of(at, TILE), TILE)
-            key_at = lax.broadcasted_iota(jnp.int32, (TILE, TILE), 1)
-            query_at = lax.broadcasted_iota(jnp.int32, (TILE, TILE), 0)
-            for j in range(PER):
-                here = slice(j * TILE, (j + 1) * TILE)
-                s = dot_nt(q_buf[part, q_rows, j * HD : (j + 1) * HD], k_buf[keys_at])
+            together = PER if pieces <= 2 else TOGETHER
+            edge_shape = (together * TILE, TILE)
+            key_at = lax.broadcasted_iota(jnp.int32, edge_shape, 1)
+            query_at = lax.broadcasted_iota(jnp.int32, edge_shape, 0) & (TILE - 1)
+
+            def scores(c):
+                heads = range(c * together, (c + 1) * together)
+                q = [q_buf[part, q_rows, j * HD : (j + 1) * HD] for j in heads]
+                s = dot_nt(jnp.concatenate(q, axis=0), k_buf[keys_at])
                 edge = jnp.where(key_at <= query_at, s[:, count - TILE :], FLOOR)
-                s = jnp.concatenate([s[:, : count - TILE], edge], axis=1) if pieces > 1 else edge
+                if pieces == 1:
+                    return edge
+                return jnp.concatenate([s[:, : count - TILE], edge], axis=1)
+
+            ready = [scores(c) for c in range(PER // together)]
+            for c, s in enumerate(ready):
+                here = slice(c * together * TILE, (c + 1) * together * TILE)
                 m = jnp.max(s, axis=1, keepdims=True)
                 p = jnp.exp2((s - m) * SCALE).astype(BF16)
-                m_tmp[slot, here] = jnp.broadcast_to(m, (TILE, HD))
+                m_tmp[slot, here] = jnp.broadcast_to(m, (together * TILE, HD))
                 acc_tmp[slot, here] = dot_nn(p, v_buf[keys_at])
 
         if first and one_block:

time: 65.6 us -> 65.3 us (level)
  waiting for transfers between devices: 9.47 us -> 11.3 us
  Pallas kernels: 24.5 us -> 22.8 us
  starting transfers between devices: 28.6 us -> 27.9 us
    pallas_call x4, Pallas kernels: 19.4 us -> 17.8 us  [attention(): pl.pallas_call(kernel, in_specs=[SMEM] + [VMEM] * (n_q + n_src + len(stat...]
    ppermute x2, waiting for transfers between devices: 0.51 us -> 2.04 us  [body(): lax.ppermute(jnp.where(forwards, a, b), 'lev', [(2, 3), (1, 2)])]
  transfers between devices with their start and end apart: 14 -> 14, of which waited for: 4 -> 4; matrix products, arithmetic and copies ran while one was open for 3% -> 3% of each run, Pallas kernels for 30% -> 27%
where the time goes in v11:
time: 65.3 us; the launch traced here: 64.9 us
  starting transfers between devices  27.9 us (43%)
  Pallas kernels  22.8 us (35%)
  waiting for transfers between devices  11.3 us (17%)
  other arithmetic  1.54 us (2%)
  local copies, waits for them, and re-layouts  0.9 us (1%)
    pallas_call x4, Pallas kernels, attention(): pl.pallas_call(kernel, in_specs=[SMEM] + [VMEM] * (n_q + n_src + len(stat...  17.8 us
    ppermute x2, starting transfers between devices, body(): up = [lax.ppermute(piece, 'lev', [(0, 2), (2, 3)]) for piece in halves]  8.58 us
    ppermute x7, starting transfers between devices, exchange(): lax.ppermute(piece, 'sub', [(i, i ^ k) for i in range(subs)])  5.6 us
    all_to_all x1, waiting for transfers between devices, body(): own = lax.all_to_all(packed, ('sub', 'head'), 0, 0, tiled=True)  5.31 us
    all_to_all x1, starting transfers between devices, body(): p2 = lax.all_to_all(raw, ('sub', 'head'), 0, 0, tiled=True)  4.66 us
    all_to_all x1, starting transfers between devices, body(): own = lax.all_to_all(packed, ('sub', 'head'), 0, 0, tiled=True)  4.52 us
    ppermute x2, starting transfers between devices, body(): lax.ppermute(jnp.where(forwards, a, b), 'lev', [(2, 3), (1, 2)])  3.89 us
    all_to_all x1, waiting for transfers between devices, body(): p2 = lax.all_to_all(raw, ('sub', 'head'), 0, 0, tiled=True)  3.05 us
  transfers between devices with their start and end apart: 14, of which 4 were waited for; matrix products, arithmetic and copies ran while one was open for 3% of the time, Pallas kernels for 27%

profile of v11, /device:TPU:23, one launch (start us, length us, event | category | flops | bytes accessed | tf_op | source)
XLA Modules:
  0.0 64.9 jit_solution(9923798228790841251)
XLA Ops:
  0.0 2.0 %pack_kv.1 = bf16[8,2,128,128]{3,2,1,0:T(8,128)(2,1)} custom-call(bf16[128,1024]{1,0:T(8,128)(2,1)} %k_ref.1, bf16[128,1024]{1,0:T(8,128)(2,1)} %v_ref.1), custom_call_target="tpu_custom_call" | custom-call | bytes 1048576 | tf_op jit(solution)/shard_map/pack_kv/pallas_call | solution.py:55
  2.0 0.7 %collective-permute-start.4 = (bf16[8,2,128,128]{3,2,1,0:T(8,128)(2,1)}, bf16[8,2,128,128]{3,2,1,0:T(8,128)(2,1)S(1)}, u32[]{:S(2)}, u32[]{:S(2)}) collective-permute-start(bf16[8,2,128,128]{3,2,1,0:T(8,128)(2,1)} %pack_kv.1), channel_id=1, source_target_pairs={{8,24},{0,8},{9,25},{1,9},{10,26},{2,10},{11,27},{3,11},{12,28},{4... | collective-permute-start | bytes 1572872 | tf_op jit(solution)/shard_map/ppermute | solution.py:342
  2.7 4.5 %all-to-all-start = ((bf16[8,2,128,128]{3,2,1,0:T(8,128)(2,1)}), bf16[8,2,128,128]{3,2,1,0:T(8,128)(2,1)S(1)}, u32[]{:S(2)}, u32[]{:S(2)}) async-start(bf16[8,2,128,128]{3,2,1,0:T(8,128)(2,1)} %pack_kv.1), calls=%async_computation | async-start | bytes 1048576 | tf_op jit(solution)/shard_map/all_to_all | solution.py:343
  7.2 0.1 copy.6.sel_ref
  7.3 1.4 %pack_q.1 = (bf16[272,512]{1,0:T(8,128)(2,1)S(1)}, bf16[272,512]{1,0:T(8,128)(2,1)}, bf16[272,512]{1,0:T(8,128)(2,1)S(1)}, bf16[272,512]{1,0:T(8,128)(2,1)S(1)}) custom-call(s32[2,4,3]{2,1,0:T(4,128)S(1)} %copy.6.sel_ref, bf16[256,2048]{1,0:T(8,128)(2,1)S(1)} %copy-done), custom_call_target="tpu_custom_call" | custom-call | bytes 2097152 | tf_op jit(solution)/shard_map/pack_q/pallas_call | solution.py:81
  8.7 0.3 collective-permute-start.2
  9.0 5.3 %all-to-all-done.refs_3_ = bf16[8,2,128,128]{3,2,1,0:T(8,128)(2,1)S(1)} async-done(((bf16[8,2,128,128]{3,2,1,0:T(8,128)(2,1)}), bf16[8,2,128,128]{3,2,1,0:T(8,128)(2,1)S(1)}, u32[]{:S(2)}, u32[]{:S(2)}) %all-to-all-start) | async-done | bytes 524320 | tf_op jit(solution)/shard_map/all_to_all | solution.py:343
  14.3 0.0 collective-permute-done.4
  14.4 0.7 %copy-done.1 = bf16[8,2,128,128]{3,2,1,0:T(8,128)(2,1)} copy-done((bf16[8,2,128,128]{3,2,1,0:T(8,128)(2,1)}, bf16[8,2,128,128]{3,2,1,0:T(8,128)(2,1)S(1)}, u32[]{:S(2)}) %copy-start.1) | copy-done | bytes 524312
  15.1 6.7 %collective-permute-start.5 = (bf16[4,2,128,128]{3,2,1,0:T(8,128)(2,1)S(1)}, bf16[4,2,128,128]{3,2,1,0:T(8,128)(2,1)S(1)}, u32[]{:S(2)}, u32[]{:S(2)}) collective-permute-start(bf16[4,2,128,128]{3,2,1,0:T(8,128)(2,1)S(1)} %get-tuple-element.28), channel_id=1, source_target_pairs={{0,16},{16,24},{1,17},{17,25},{2,18},{18,26},{3,19},{19,27},{4,20}... | collective-permute-start | bytes 786440 | tf_op jit(solution)/shard_map/ppermute | solution.py:355
  21.8 1.9 %collective-permute-start.6 = (bf16[4,2,128,128]{3,2,1,0:T(8,128)(2,1)S(1)}, bf16[4,2,128,128]{3,2,1,0:T(8,128)(2,1)S(1)}, u32[]{:S(2)}, u32[]{:S(2)}) collective-permute-start(bf16[4,2,128,128]{3,2,1,0:T(8,128)(2,1)S(1)} %get-tuple-element.29), channel_id=1, source_target_pairs={{0,16},{16,24},{1,17},{17,25},{2,18},{18,26},{3,19},{19,27},{4,20}... | collective-permute-start | bytes 786440 | tf_op jit(solution)/shard_map/ppermute | solution.py:355
  23.7 1.9 %collective-permute-start = (bf16[272,512]{1,0:T(8,128)(2,1)}, bf16[272,512]{1,0:T(8,128)(2,1)S(1)}, u32[]{:S(2)}, u32[]{:S(2)}) collective-permute-start(bf16[272,512]{1,0:T(8,128)(2,1)} %get-tuple-element.24), channel_id=1, source_target_pairs={{0,2},{2,0},{4,6},{6,4},{1,3},{3,1},{5,7},{7,5},{8,10},{10,8},{12,... | collective-permute-start | bytes 835592 | tf_op jit(solution)/shard_map/ppermute | solution.py:335
  25.6 0.3 collective-permute-start.1
  25.9 0.3 collective-permute-start.3
  26.2 4.7 %all-to-all-start.1 = ((bf16[8,2,128,128]{3,2,1,0:T(8,128)(2,1)}), bf16[8,2,128,128]{3,2,1,0:T(8,128)(2,1)S(1)}, u32[]{:S(2)}, u32[]{:S(2)}) async-start(bf16[8,2,128,128]{3,2,1,0:T(8,128)(2,1)} %copy-done.1), calls=%async_computation.1 | async-start | bytes 1048576 | tf_op jit(solution)/shard_map/all_to_all | solution.py:356
  30.9 0.7 %broadcast_select_fusion.1 = bf16[4,2,128,128]{3,2,1,0:T(8,128)(2,1)} fusion(bf16[4,2,128,128]{3,2,1,0:T(8,128)(2,1)S(1)} %collective-permute-done.5.refs_4_, bf16[4,2,128,128]{3,2,1,0:T(8,128)(2,1)S(1)} %get-tuple-element.28, pred[]{:T(512)S(6)} %eq.3), kind=kLoop, calls=%fused_computation.1 | loop fusion | flops 131072 | bytes 786433 | tf_op jit(solution)/shard_map/jit(_where)/select_n | solution.py:361
  31.6 1.9 %collective-permute-start.7 = (bf16[4,2,128,128]{3,2,1,0:T(8,128)(2,1)}, bf16[4,2,128,128]{3,2,1,0:T(8,128)(2,1)S(1)}, u32[]{:S(2)}, u32[]{:S(2)}) collective-permute-start(bf16[4,2,128,128]{3,2,1,0:T(8,128)(2,1)} %broadcast_select_fusion.1), channel_id=1, source_target_pairs={{16,24},{8,16},{17,25},{9,17},{18,26},{10,18},{19,27},{11,19},{20,... | collective-permute-start | bytes 786440 | tf_op jit(solution)/shard_map/ppermute | solution.py:361
  33.5 0.7 %broadcast_select_fusion = bf16[4,2,128,128]{3,2,1,0:T(8,128)(2,1)} fusion(bf16[4,2,128,128]{3,2,1,0:T(8,128)(2,1)S(1)} %collective-permute-done.6.refs_5_, bf16[4,2,128,128]{3,2,1,0:T(8,128)(2,1)S(1)} %get-tuple-element.29, pred[]{:T(512)S(6)} %eq.3), kind=kLoop, calls=%fused_computation | loop fusion | flops 131072 | bytes 786433 | tf_op jit(solution)/shard_map/jit(_where)/select_n | solution.py:361
  34.3 2.0 %collective-permute-start.8 = (bf16[4,2,128,128]{3,2,1,0:T(8,128)(2,1)}, bf16[4,2,128,128]{3,2,1,0:T(8,128)(2,1)S(1)}, u32[]{:S(2)}, u32[]{:S(2)}) collective-permute-start(bf16[4,2,128,128]{3,2,1,0:T(8,128)(2,1)} %broadcast_select_fusion), channel_id=1, source_target_pairs={{16,24},{8,16},{17,25},{9,17},{18,26},{10,18},{19,27},{11,19},{20,... | collective-permute-start | bytes 786440 | tf_op jit(solution)/shard_map/ppermute | solution.py:361
  36.3 0.1 maximum_convert_fusion.refs_0_
  36.4 3.0 %all-to-all-done.1.refs_6_ = bf16[8,2,128,128]{3,2,1,0:T(8,128)(2,1)S(1)} async-done(((bf16[8,2,128,128]{3,2,1,0:T(8,128)(2,1)}), bf16[8,2,128,128]{3,2,1,0:T(8,128)(2,1)S(1)}, u32[]{:S(2)}, u32[]{:S(2)}) %all-to-all-start.1) | async-done | bytes 524320 | tf_op jit(solution)/shard_map/all_to_all | solution.py:356
  39.5 5.3 %far_early.1 = (f32[4,512,128]{2,1,0:T(8,128)S(1)}, f32[4,512,256]{2,1,0:T(8,128)S(1)}) custom-call(s32[24]{0:T(128)S(1)} %maximum_convert_fusion.refs_0_, bf16[272,512]{1,0:T(8,128)(2,1)S(1)} %collective-permute-done.1.refs_1_, bf16[272,512]{1,0:T(8,128)(2,1)S(1)} %collective-permute-done.3.refs_2_.refs_1_, ...), custom_call_target="tpu_custom_call" | custom-call | flops 1610612736 | bytes 4194304 | tf_op jit(solution)/shard_map/far_early/pallas_call | solution.py:305
  44.8 2.0 %collective-permute-done.8.refs_3_.refs_8_ = bf16[4,2,128,128]{3,2,1,0:T(8,128)(2,1)S(1)} collective-permute-done((bf16[4,2,128,128]{3,2,1,0:T(8,128)(2,1)}, bf16[4,2,128,128]{3,2,1,0:T(8,128)(2,1)S(1)}, u32[]{:S(2)}, u32[]{:S(2)}) %collective-permute-start.8) | collective-permute-done | bytes 262176 | tf_op jit(solution)/shard_map/ppermute | solution.py:361
  46.9 2.5 %far_late.2 = bf16[256,512]{1,0:T(8,128)(2,1)S(1)} custom-call(s32[24]{0:T(128)S(1)} %maximum_convert_fusion.refs_0_, bf16[272,512]{1,0:T(8,128)(2,1)S(1)} %collective-permute-done.1.refs_1_, bf16[4,2,128,128]{3,2,1,0:T(8,128)(2,1)S(1)} %collective-permute-done.7.refs_2_.refs_7_, bf16[4,2,128,128]{3,2,1,0:T(8,128)(2,1)S(1)} %collective-permute-done.8.refs_3_.refs_8_, ...), custom_call_target="tpu_custom_call" | custom-call | flops 805306368 | bytes 4194304 | tf_op jit(solution)/shard_map/far_late/pallas_call | solution.py:305
  49.4 0.1 collective-permute-start.10
  49.5 2.3 %far_late.3 = bf16[256,512]{1,0:T(8,128)(2,1)S(1)} custom-call(s32[24]{0:T(128)S(1)} %maximum_convert_fusion.refs_0_, bf16[272,512]{1,0:T(8,128)(2,1)S(1)} %collective-permute-done.3.refs_2_.refs_1_, bf16[4,2,128,128]{3,2,1,0:T(8,128)(2,1)S(1)} %collective-permute-done.7.refs_2_.refs_7_, bf16[4,2,128,128]{3,2,1,0:T(8,128)(2,1)S(1)} %collective-permute-done.8.refs_3_.refs_8_, ...), custom_call_target="tpu_custom_call" | custom-call | flops 805306368 | bytes 4194304 | tf_op jit(solution)/shard_map/far_late/pallas_call | solution.py:305
  51.8 2.7 %collective-permute-start.11 = (bf16[256,512]{1,0:T(8,128)(2,1)S(1)}, bf16[256,512]{1,0:T(8,128)(2,1)S(1)}, u32[]{:S(2)}, u32[]{:S(2)}) collective-permute-start(bf16[256,512]{1,0:T(8,128)(2,1)S(1)} %far_late.3), channel_id=1, source_target_pairs={{0,6},{2,4},{4,2},{6,0},{1,7},{3,5},{5,3},{7,1},{8,14},{10,12},{12... | collective-permute-start | bytes 786440 | tf_op jit(solution)/shard_map/ppermute | solution.py:335
  54.4 7.7 %near.1 = (bf16[256,512]{1,0:T(8,128)(2,1)S(1)}, bf16[256,512]{1,0:T(8,128)(2,1)S(1)}) custom-call(s32[24]{0:T(128)S(1)} %maximum_convert_fusion.refs_0_, bf16[272,512]{1,0:T(8,128)(2,1)S(1)} %get-tuple-element.37.refs_1_, bf16[272,512]{1,0:T(8,128)(2,1)S(1)} %collective-permute-done.refs_2_, bf16[8,2,128,128]{3,2,1,0:T(8,128)(2,1)S(1)} %all-to-all-done.refs_3_, ...), custom_call_target="tpu_custom_call" | custom-call | flops 1610612736 | bytes 4194304 | tf_op jit(solution)/shard_map/near/pallas_call | solution.py:305
  62.1 0.1 collective-permute-start.9
  62.2 0.9 %collective-permute-done.11.refs_1_ = bf16[256,512]{1,0:T(8,128)(2,1)S(1)} collective-permute-done((bf16[256,512]{1,0:T(8,128)(2,1)S(1)}, bf16[256,512]{1,0:T(8,128)(2,1)S(1)}, u32[]{:S(2)}, u32[]{:S(2)}) %collective-permute-start.11) | collective-permute-done | bytes 262176 | tf_op jit(solution)/shard_map/ppermute | solution.py:335
  63.1 0.9 %unpack_most.1.refs_1_ = bf16[256,2048]{1,0:T(8,128)(2,1)} custom-call(bf16[256,512]{1,0:T(8,128)(2,1)S(1)} %collective-permute-done.10.refs_0_, bf16[256,512]{1,0:T(8,128)(2,1)S(1)} %collective-permute-done.11.refs_1_, bf16[256,512]{1,0:T(8,128)(2,1)S(1)} %get-tuple-element.40.refs_2_), custom_call_target="tpu_custom_call" | custom-call | bytes 1572864 | tf_op jit(solution)/shard_map/unpack_most/pallas_call | solution.py:108
  64.0 0.7 %unpack_rest.1 = bf16[256,2048]{1,0:T(8,128)(2,1)} custom-call(bf16[256,512]{1,0:T(8,128)(2,1)S(1)} %collective-permute-done.9.refs_0_, bf16[256,2048]{1,0:T(8,128)(2,1)} %unpack_most.1.refs_1_), custom_call_target="tpu_custom_call", output_to_operand_aliasing={{}: (1, {})} | custom-call | bytes 524288 | tf_op jit(solution)/shard_map/unpack_rest/pallas_call | solution.py:108
  (17 shorter events, 0.1 us)
Async XLA Ops:
  0.0 7.2 %copy-start.2 = (s32[2,4,3]{1,0,2:T(2,128)S(1)}, s32[2,4,3]{1,0,2:T(2,128)}, u32[]{:S(2)}) copy-start(s32[2,4,3]{1,0,2:T(2,128)} %param.7) | copy-start | bytes 292
  0.0 7.3 %copy-start = (bf16[256,2048]{1,0:T(8,128)(2,1)S(1)}, bf16[256,2048]{1,0:T(8,128)(2,1)}, u32[]{:S(2)}) copy-start(bf16[256,2048]{1,0:T(8,128)(2,1)} %q_ref.1) | copy-start | bytes 3145732
  2.0 12.3 %collective-permute-start.4 = (bf16[8,2,128,128]{3,2,1,0:T(8,128)(2,1)}, bf16[8,2,128,128]{3,2,1,0:T(8,128)(2,1)S(1)}, u32[]{:S(2)}, u32[]{:S(2)}) collective-permute-start(bf16[8,2,128,128]{3,2,1,0:T(8,128)(2,1)} %pack_kv.1), channel_id=1, source_target_pairs={{8,24},{0,8},{9,25},{1,9},{10,26},{2,10},{11,27},{3,11},{12,28},{4... | collective-permute-start | bytes 1572872 | tf_op jit(solution)/shard_map/ppermute | solution.py:342
  2.7 11.6 %all-to-all-start = ((bf16[8,2,128,128]{3,2,1,0:T(8,128)(2,1)}), bf16[8,2,128,128]{3,2,1,0:T(8,128)(2,1)S(1)}, u32[]{:S(2)}, u32[]{:S(2)}) async-start(bf16[8,2,128,128]{3,2,1,0:T(8,128)(2,1)} %pack_kv.1), calls=%async_computation | async-start | bytes 1048576 | tf_op jit(solution)/shard_map/all_to_all | solution.py:343
  8.7 17.1 %collective-permute-start.2 = (bf16[272,512]{1,0:T(8,128)(2,1)S(1)}, bf16[272,512]{1,0:T(8,128)(2,1)}, u32[]{:S(2)}, u32[]{:S(2)}) collective-permute-start(bf16[272,512]{1,0:T(8,128)(2,1)S(1)} %get-tuple-element.26), channel_id=1, source_target_pairs={{0,4},{2,6},{4,0},{6,2},{1,5},{3,7},{5,1},{7,3},{8,12},{10,14},{12... | collective-permute-start | bytes 835592 | tf_op jit(solution)/shard_map/ppermute | solution.py:335
  14.3 0.8 %copy-start.1 = (bf16[8,2,128,128]{3,2,1,0:T(8,128)(2,1)}, bf16[8,2,128,128]{3,2,1,0:T(8,128)(2,1)S(1)}, u32[]{:S(2)}) copy-start(bf16[8,2,128,128]{3,2,1,0:T(8,128)(2,1)S(1)} %collective-permute-done.4) | copy-start | bytes 1572868
  15.1 15.8 %collective-permute-start.5 = (bf16[4,2,128,128]{3,2,1,0:T(8,128)(2,1)S(1)}, bf16[4,2,128,128]{3,2,1,0:T(8,128)(2,1)S(1)}, u32[]{:S(2)}, u32[]{:S(2)}) collective-permute-start(bf16[4,2,128,128]{3,2,1,0:T(8,128)(2,1)S(1)} %get-tuple-element.28), channel_id=1, source_target_pairs={{0,16},{16,24},{1,17},{17,25},{2,18},{18,26},{3,19},{19,27},{4,20}... | collective-permute-start | bytes 786440 | tf_op jit(solution)/shard_map/ppermute | solution.py:355
  21.8 11.7 %collective-permute-start.6 = (bf16[4,2,128,128]{3,2,1,0:T(8,128)(2,1)S(1)}, bf16[4,2,128,128]{3,2,1,0:T(8,128)(2,1)S(1)}, u32[]{:S(2)}, u32[]{:S(2)}) collective-permute-start(bf16[4,2,128,128]{3,2,1,0:T(8,128)(2,1)S(1)} %get-tuple-element.29), channel_id=1, source_target_pairs={{0,16},{16,24},{1,17},{17,25},{2,18},{18,26},{3,19},{19,27},{4,20}... | collective-permute-start | bytes 786440 | tf_op jit(solution)/shard_map/ppermute | solution.py:355
  23.7 12.6 %collective-permute-start = (bf16[272,512]{1,0:T(8,128)(2,1)}, bf16[272,512]{1,0:T(8,128)(2,1)S(1)}, u32[]{:S(2)}, u32[]{:S(2)}) collective-permute-start(bf16[272,512]{1,0:T(8,128)(2,1)} %get-tuple-element.24), channel_id=1, source_target_pairs={{0,2},{2,0},{4,6},{6,4},{1,3},{3,1},{5,7},{7,5},{8,10},{10,8},{12,... | collective-permute-start | bytes 835592 | tf_op jit(solution)/shard_map/ppermute | solution.py:335
  25.6 10.7 %collective-permute-start.1 = (bf16[272,512]{1,0:T(8,128)(2,1)S(1)}, bf16[272,512]{1,0:T(8,128)(2,1)S(1)}, u32[]{:S(2)}, u32[]{:S(2)}) collective-permute-start(bf16[272,512]{1,0:T(8,128)(2,1)S(1)} %get-tuple-element.25), channel_id=1, source_target_pairs={{0,4},{2,6},{4,0},{6,2},{1,5},{3,7},{5,1},{7,3},{8,12},{10,14},{12... | collective-permute-start | bytes 835592 | tf_op jit(solution)/shard_map/ppermute | solution.py:335
  25.9 10.4 %collective-permute-start.3 = (bf16[272,512]{1,0:T(8,128)(2,1)}, bf16[272,512]{1,0:T(8,128)(2,1)S(1)}, u32[]{:S(2)}, u32[]{:S(2)}) collective-permute-start(bf16[272,512]{1,0:T(8,128)(2,1)} %collective-permute-done.2), channel_id=1, source_target_pairs={{0,2},{2,0},{4,6},{6,4},{1,3},{3,1},{5,7},{7,5},{8,10},{10,8},{12,... | collective-permute-start | bytes 835592 | tf_op jit(solution)/shard_map/ppermute | solution.py:335
  26.2 13.2 %all-to-all-start.1 = ((bf16[8,2,128,128]{3,2,1,0:T(8,128)(2,1)}), bf16[8,2,128,128]{3,2,1,0:T(8,128)(2,1)S(1)}, u32[]{:S(2)}, u32[]{:S(2)}) async-start(bf16[8,2,128,128]{3,2,1,0:T(8,128)(2,1)} %copy-done.1), calls=%async_computation.1 | async-start | bytes 1048576 | tf_op jit(solution)/shard_map/all_to_all | solution.py:356
  31.6 13.2 %collective-permute-start.7 = (bf16[4,2,128,128]{3,2,1,0:T(8,128)(2,1)}, bf16[4,2,128,128]{3,2,1,0:T(8,128)(2,1)S(1)}, u32[]{:S(2)}, u32[]{:S(2)}) collective-permute-start(bf16[4,2,128,128]{3,2,1,0:T(8,128)(2,1)} %broadcast_select_fusion.1), channel_id=1, source_target_pairs={{16,24},{8,16},{17,25},{9,17},{18,26},{10,18},{19,27},{11,19},{20,... | collective-permute-start | bytes 786440 | tf_op jit(solution)/shard_map/ppermute | solution.py:361
  34.3 12.6 %collective-permute-start.8 = (bf16[4,2,128,128]{3,2,1,0:T(8,128)(2,1)}, bf16[4,2,128,128]{3,2,1,0:T(8,128)(2,1)S(1)}, u32[]{:S(2)}, u32[]{:S(2)}) collective-permute-start(bf16[4,2,128,128]{3,2,1,0:T(8,128)(2,1)} %broadcast_select_fusion), channel_id=1, source_target_pairs={{16,24},{8,16},{17,25},{9,17},{18,26},{10,18},{19,27},{11,19},{20,... | collective-permute-start | bytes 786440 | tf_op jit(solution)/shard_map/ppermute | solution.py:361
  49.4 12.8 %collective-permute-start.10 = (bf16[256,512]{1,0:T(8,128)(2,1)S(1)}, bf16[256,512]{1,0:T(8,128)(2,1)S(1)}, u32[]{:S(2)}, u32[]{:S(2)}) collective-permute-start(bf16[256,512]{1,0:T(8,128)(2,1)S(1)} %far_late.2), channel_id=1, source_target_pairs={{0,4},{2,6},{4,0},{6,2},{1,5},{3,7},{5,1},{7,3},{8,12},{10,14},{12... | collective-permute-start | bytes 786440 | tf_op jit(solution)/shard_map/ppermute | solution.py:335
  51.8 11.3 %collective-permute-start.11 = (bf16[256,512]{1,0:T(8,128)(2,1)S(1)}, bf16[256,512]{1,0:T(8,128)(2,1)S(1)}, u32[]{:S(2)}, u32[]{:S(2)}) collective-permute-start(bf16[256,512]{1,0:T(8,128)(2,1)S(1)} %far_late.3), channel_id=1, source_target_pairs={{0,6},{2,4},{4,2},{6,0},{1,7},{3,5},{5,3},{7,1},{8,14},{10,12},{12... | collective-permute-start | bytes 786440 | tf_op jit(solution)/shard_map/ppermute | solution.py:335
  62.1 1.9 %collective-permute-start.9 = (bf16[256,512]{1,0:T(8,128)(2,1)S(1)}, bf16[256,512]{1,0:T(8,128)(2,1)S(1)}, u32[]{:S(2)}, u32[]{:S(2)}) collective-permute-start(bf16[256,512]{1,0:T(8,128)(2,1)S(1)} %get-tuple-element.39), channel_id=1, source_target_pairs={{0,2},{2,0},{4,6},{6,4},{1,3},{3,1},{5,7},{7,5},{8,10},{10,8},{12,... | collective-permute-start | bytes 786440 | tf_op jit(solution)/shard_map/ppermute | solution.py:335

commit v12 on v11

--- a/solution.py
+++ b/solution.py
@@ -116,6 +116,24 @@
         compiler_params=pltpu.CompilerParams(vmem_limit_bytes=8 * MIB),
         name=name,
     )(*pieces, *begun)
+
+
+def in_place(*pieces):
+    n = len(pieces)
+
+    def kernel(*refs):
+        pass
+
+    return pl.pallas_call(
+        kernel,
+        in_specs=[ANY] * n,
+        out_specs=(ANY,) * n,
+        out_shape=tuple(jax.ShapeDtypeStruct(piece.shape, piece.dtype) for piece in pieces),
+        input_output_aliases={i: i for i in range(n)},
+        cost_estimate=copy_cost(4 * n * pieces[0].size),
+        compiler_params=pltpu.CompilerParams(vmem_limit_bytes=8 * MIB),
+        name="landed",
+    )(*pieces)
 
 
 def attention(
@@ -399,8 +417,8 @@
             "near", True, True, near, whole_range, q, sel, (own, *up, p2, *last_up), ()
         )
         out_near, out_far = exchange(out_near, near), exchange(out_far, far)
-        begun = unpack_output("unpack_most", subs, (*out_far, out_near[0]), (*far, 0), ())
-        return unpack_output("unpack_rest", subs, out_near[1:], near[1:], (begun,))
+        landed = in_place(*out_far)
+        return unpack_output("unpack", subs, (*landed, *out_near), (*far, *near), ())
     sel = jnp.concatenate([piece[rows, : tiles_here * TOPK] for piece in q]).astype(jnp.int32)
     whole = lax.all_gather(own, "lev", axis=0, tiled=True)
     out = attention("all", True, True, everyone, lambda level: (0,), q, sel, (whole,), ())

time: 65.3 us -> 65.3 us (level)
    pallas_call x2 -> x1, Pallas kernels: 1.63 us -> 0.99 us  [unpack_output(): pl.pallas_call(kernel, in_specs=[VMEM] * n + [ANY] * len(begun), out_spec...]
  transfers between devices with their start and end apart: 14 -> 14, of which waited for: 4 -> 5; matrix products, arithmetic and copies ran while one was open for 3% -> 3% of each run, Pallas kernels for 27% -> 27%
where the time goes in v12:
time: 65.3 us; the launch traced here: 64.7 us
  starting transfers between devices  27.9 us (43%)
  Pallas kernels  22.3 us (34%)
  waiting for transfers between devices  11.7 us (18%)
  other arithmetic  1.55 us (2%)
  local copies, waits for them, and re-layouts  0.9 us (1%)
    pallas_call x4, Pallas kernels, attention(): pl.pallas_call(kernel, in_specs=[SMEM] + [VMEM] * (n_q + n_src + len(stat...  17.9 us
    ppermute x2, starting transfers between devices, body(): up = [lax.ppermute(piece, 'lev', [(0, 2), (2, 3)]) for piece in halves]  8.58 us
    ppermute x7, starting transfers between devices, exchange(): lax.ppermute(piece, 'sub', [(i, i ^ k) for i in range(subs)])  5.61 us
    all_to_all x1, waiting for transfers between devices, body(): own = lax.all_to_all(packed, ('sub', 'head'), 0, 0, tiled=True)  5.31 us
    all_to_all x1, starting transfers between devices, body(): p2 = lax.all_to_all(raw, ('sub', 'head'), 0, 0, tiled=True)  4.66 us
    all_to_all x1, starting transfers between devices, body(): own = lax.all_to_all(packed, ('sub', 'head'), 0, 0, tiled=True)  4.52 us
    ppermute x2, starting transfers between devices, body(): lax.ppermute(jnp.where(forwards, a, b), 'lev', [(2, 3), (1, 2)])  3.89 us
    all_to_all x1, waiting for transfers between devices, body(): p2 = lax.all_to_all(raw, ('sub', 'head'), 0, 0, tiled=True)  3.05 us
  transfers between devices with their start and end apart: 14, of which 5 were waited for; matrix products, arithmetic and copies ran while one was open for 3% of the time, Pallas kernels for 27%

profile of v12, /device:TPU:23, one launch (start us, length us, event | category | flops | bytes accessed | tf_op | source)
XLA Modules:
  0.0 64.7 jit_solution(18251091933989321624)
XLA Ops:
  0.0 2.0 %pack_kv.1 = bf16[8,2,128,128]{3,2,1,0:T(8,128)(2,1)} custom-call(bf16[128,1024]{1,0:T(8,128)(2,1)} %k_ref.1, bf16[128,1024]{1,0:T(8,128)(2,1)} %v_ref.1), custom_call_target="tpu_custom_call" | custom-call | bytes 1048576 | tf_op jit(solution)/shard_map/pack_kv/pallas_call | solution.py:55
  2.0 0.7 %collective-permute-start.4 = (bf16[8,2,128,128]{3,2,1,0:T(8,128)(2,1)}, bf16[8,2,128,128]{3,2,1,0:T(8,128)(2,1)S(1)}, u32[]{:S(2)}, u32[]{:S(2)}) collective-permute-start(bf16[8,2,128,128]{3,2,1,0:T(8,128)(2,1)} %pack_kv.1), channel_id=1, source_target_pairs={{8,24},{0,8},{9,25},{1,9},{10,26},{2,10},{11,27},{3,11},{12,28},{4... | collective-permute-start | bytes 1572872 | tf_op jit(solution)/shard_map/ppermute | solution.py:360
  2.7 4.5 %all-to-all-start = ((bf16[8,2,128,128]{3,2,1,0:T(8,128)(2,1)}), bf16[8,2,128,128]{3,2,1,0:T(8,128)(2,1)S(1)}, u32[]{:S(2)}, u32[]{:S(2)}) async-start(bf16[8,2,128,128]{3,2,1,0:T(8,128)(2,1)} %pack_kv.1), calls=%async_computation | async-start | bytes 1048576 | tf_op jit(solution)/shard_map/all_to_all | solution.py:361
  7.2 0.1 copy.7.sel_ref
  7.3 1.4 %pack_q.1 = (bf16[272,512]{1,0:T(8,128)(2,1)S(1)}, bf16[272,512]{1,0:T(8,128)(2,1)}, bf16[272,512]{1,0:T(8,128)(2,1)S(1)}, bf16[272,512]{1,0:T(8,128)(2,1)S(1)}) custom-call(s32[2,4,3]{2,1,0:T(4,128)S(1)} %copy.7.sel_ref, bf16[256,2048]{1,0:T(8,128)(2,1)S(1)} %copy-done), custom_call_target="tpu_custom_call" | custom-call | bytes 2097152 | tf_op jit(solution)/shard_map/pack_q/pallas_call | solution.py:81
  8.7 0.3 collective-permute-start.2
  9.0 5.3 %all-to-all-done.refs_3_ = bf16[8,2,128,128]{3,2,1,0:T(8,128)(2,1)S(1)} async-done(((bf16[8,2,128,128]{3,2,1,0:T(8,128)(2,1)}), bf16[8,2,128,128]{3,2,1,0:T(8,128)(2,1)S(1)}, u32[]{:S(2)}, u32[]{:S(2)}) %all-to-all-start) | async-done | bytes 524320 | tf_op jit(solution)/shard_map/all_to_all | solution.py:361
  14.3 0.0 collective-permute-done.4
  14.4 0.7 %copy-done.1 = bf16[8,2,128,128]{3,2,1,0:T(8,128)(2,1)} copy-done((bf16[8,2,128,128]{3,2,1,0:T(8,128)(2,1)}, bf16[8,2,128,128]{3,2,1,0:T(8,128)(2,1)S(1)}, u32[]{:S(2)}) %copy-start.1) | copy-done | bytes 524312
  15.1 6.7 %collective-permute-start.5 = (bf16[4,2,128,128]{3,2,1,0:T(8,128)(2,1)S(1)}, bf16[4,2,128,128]{3,2,1,0:T(8,128)(2,1)S(1)}, u32[]{:S(2)}, u32[]{:S(2)}) collective-permute-start(bf16[4,2,128,128]{3,2,1,0:T(8,128)(2,1)S(1)} %get-tuple-element.30), channel_id=1, source_target_pairs={{0,16},{16,24},{1,17},{17,25},{2,18},{18,26},{3,19},{19,27},{4,20}... | collective-permute-start | bytes 786440 | tf_op jit(solution)/shard_map/ppermute | solution.py:373
  21.8 1.9 %collective-permute-start.6 = (bf16[4,2,128,128]{3,2,1,0:T(8,128)(2,1)S(1)}, bf16[4,2,128,128]{3,2,1,0:T(8,128)(2,1)S(1)}, u32[]{:S(2)}, u32[]{:S(2)}) collective-permute-start(bf16[4,2,128,128]{3,2,1,0:T(8,128)(2,1)S(1)} %get-tuple-element.31), channel_id=1, source_target_pairs={{0,16},{16,24},{1,17},{17,25},{2,18},{18,26},{3,19},{19,27},{4,20}... | collective-permute-start | bytes 786440 | tf_op jit(solution)/shard_map/ppermute | solution.py:373
  23.7 1.9 %collective-permute-start = (bf16[272,512]{1,0:T(8,128)(2,1)}, bf16[272,512]{1,0:T(8,128)(2,1)S(1)}, u32[]{:S(2)}, u32[]{:S(2)}) collective-permute-start(bf16[272,512]{1,0:T(8,128)(2,1)} %get-tuple-element.26), channel_id=1, source_target_pairs={{0,2},{2,0},{4,6},{6,4},{1,3},{3,1},{5,7},{7,5},{8,10},{10,8},{12,... | collective-permute-start | bytes 835592 | tf_op jit(solution)/shard_map/ppermute | solution.py:353
  25.6 0.3 collective-permute-start.1
  25.9 0.3 collective-permute-start.3
  26.2 4.7 %all-to-all-start.1 = ((bf16[8,2,128,128]{3,2,1,0:T(8,128)(2,1)}), bf16[8,2,128,128]{3,2,1,0:T(8,128)(2,1)S(1)}, u32[]{:S(2)}, u32[]{:S(2)}) async-start(bf16[8,2,128,128]{3,2,1,0:T(8,128)(2,1)} %copy-done.1), calls=%async_computation.1 | async-start | bytes 1048576 | tf_op jit(solution)/shard_map/all_to_all | solution.py:374
  30.9 0.7 %broadcast_select_fusion.1 = bf16[4,2,128,128]{3,2,1,0:T(8,128)(2,1)} fusion(bf16[4,2,128,128]{3,2,1,0:T(8,128)(2,1)S(1)} %collective-permute-done.5.refs_4_, bf16[4,2,128,128]{3,2,1,0:T(8,128)(2,1)S(1)} %get-tuple-element.30, pred[]{:T(512)S(6)} %eq.3), kind=kLoop, calls=%fused_computation.1 | loop fusion | flops 131072 | bytes 786433 | tf_op jit(solution)/shard_map/jit(_where)/select_n | solution.py:379
  31.6 1.9 %collective-permute-start.7 = (bf16[4,2,128,128]{3,2,1,0:T(8,128)(2,1)}, bf16[4,2,128,128]{3,2,1,0:T(8,128)(2,1)S(1)}, u32[]{:S(2)}, u32[]{:S(2)}) collective-permute-start(bf16[4,2,128,128]{3,2,1,0:T(8,128)(2,1)} %broadcast_select_fusion.1), channel_id=1, source_target_pairs={{16,24},{8,16},{17,25},{9,17},{18,26},{10,18},{19,27},{11,19},{20,... | collective-permute-start | bytes 786440 | tf_op jit(solution)/shard_map/ppermute | solution.py:379
  33.5 0.7 %broadcast_select_fusion = bf16[4,2,128,128]{3,2,1,0:T(8,128)(2,1)} fusion(bf16[4,2,128,128]{3,2,1,0:T(8,128)(2,1)S(1)} %collective-permute-done.6.refs_5_, bf16[4,2,128,128]{3,2,1,0:T(8,128)(2,1)S(1)} %get-tuple-element.31, pred[]{:T(512)S(6)} %eq.3), kind=kLoop, calls=%fused_computation | loop fusion | flops 131072 | bytes 786433 | tf_op jit(solution)/shard_map/jit(_where)/select_n | solution.py:379
  34.3 2.0 %collective-permute-start.8 = (bf16[4,2,128,128]{3,2,1,0:T(8,128)(2,1)}, bf16[4,2,128,128]{3,2,1,0:T(8,128)(2,1)S(1)}, u32[]{:S(2)}, u32[]{:S(2)}) collective-permute-start(bf16[4,2,128,128]{3,2,1,0:T(8,128)(2,1)} %broadcast_select_fusion), channel_id=1, source_target_pairs={{16,24},{8,16},{17,25},{9,17},{18,26},{10,18},{19,27},{11,19},{20,... | collective-permute-start | bytes 786440 | tf_op jit(solution)/shard_map/ppermute | solution.py:379
  36.3 0.1 maximum_convert_fusion.refs_0_
  36.4 3.0 %all-to-all-done.1.refs_6_ = bf16[8,2,128,128]{3,2,1,0:T(8,128)(2,1)S(1)} async-done(((bf16[8,2,128,128]{3,2,1,0:T(8,128)(2,1)}), bf16[8,2,128,128]{3,2,1,0:T(8,128)(2,1)S(1)}, u32[]{:S(2)}, u32[]{:S(2)}) %all-to-all-start.1) | async-done | bytes 524320 | tf_op jit(solution)/shard_map/all_to_all | solution.py:374
  39.5 5.6 %far_early.1 = (f32[4,512,128]{2,1,0:T(8,128)S(1)}, f32[4,512,256]{2,1,0:T(8,128)S(1)}) custom-call(s32[24]{0:T(128)S(1)} %maximum_convert_fusion.refs_0_, bf16[272,512]{1,0:T(8,128)(2,1)S(1)} %collective-permute-done.1.refs_1_, bf16[272,512]{1,0:T(8,128)(2,1)S(1)} %collective-permute-done.3.refs_2_.refs_1_, ...), custom_call_target="tpu_custom_call" | custom-call | flops 1610612736 | bytes 4194304 | tf_op jit(solution)/shard_map/far_early/pallas_call | solution.py:323
  45.1 1.8 %collective-permute-done.8.refs_3_.refs_8_ = bf16[4,2,128,128]{3,2,1,0:T(8,128)(2,1)S(1)} collective-permute-done((bf16[4,2,128,128]{3,2,1,0:T(8,128)(2,1)}, bf16[4,2,128,128]{3,2,1,0:T(8,128)(2,1)S(1)}, u32[]{:S(2)}, u32[]{:S(2)}) %collective-permute-start.8) | collective-permute-done | bytes 262176 | tf_op jit(solution)/shard_map/ppermute | solution.py:379
  46.9 2.1 %far_late.2 = bf16[256,512]{1,0:T(8,128)(2,1)S(1)} custom-call(s32[24]{0:T(128)S(1)} %maximum_convert_fusion.refs_0_, bf16[272,512]{1,0:T(8,128)(2,1)S(1)} %collective-permute-done.1.refs_1_, bf16[4,2,128,128]{3,2,1,0:T(8,128)(2,1)S(1)} %collective-permute-done.7.refs_2_.refs_7_, bf16[4,2,128,128]{3,2,1,0:T(8,128)(2,1)S(1)} %collective-permute-done.8.refs_3_.refs_8_, ...), custom_call_target="tpu_custom_call" | custom-call | flops 805306368 | bytes 4194304 | tf_op jit(solution)/shard_map/far_late/pallas_call | solution.py:323
  49.0 0.3 collective-permute-start.9
  49.3 2.5 %far_late.3 = bf16[256,512]{1,0:T(8,128)(2,1)S(1)} custom-call(s32[24]{0:T(128)S(1)} %maximum_convert_fusion.refs_0_, bf16[272,512]{1,0:T(8,128)(2,1)S(1)} %collective-permute-done.3.refs_2_.refs_1_, bf16[4,2,128,128]{3,2,1,0:T(8,128)(2,1)S(1)} %collective-permute-done.7.refs_2_.refs_7_, bf16[4,2,128,128]{3,2,1,0:T(8,128)(2,1)S(1)} %collective-permute-done.8.refs_3_.refs_8_, ...), custom_call_target="tpu_custom_call" | custom-call | flops 805306368 | bytes 4194304 | tf_op jit(solution)/shard_map/far_late/pallas_call | solution.py:323
  51.8 2.4 %collective-permute-start.10 = (bf16[256,512]{1,0:T(8,128)(2,1)S(1)}, bf16[256,512]{1,0:T(8,128)(2,1)S(1)}, u32[]{:S(2)}, u32[]{:S(2)}) collective-permute-start(bf16[256,512]{1,0:T(8,128)(2,1)S(1)} %far_late.3), channel_id=1, source_target_pairs={{0,6},{2,4},{4,2},{6,0},{1,7},{3,5},{5,3},{7,1},{8,14},{10,12},{12... | collective-permute-start | bytes 786440 | tf_op jit(solution)/shard_map/ppermute | solution.py:353
  54.2 7.7 %near.1 = (bf16[256,512]{1,0:T(8,128)(2,1)S(1)}, bf16[256,512]{1,0:T(8,128)(2,1)S(1)}) custom-call(s32[24]{0:T(128)S(1)} %maximum_convert_fusion.refs_0_, bf16[272,512]{1,0:T(8,128)(2,1)S(1)} %get-tuple-element.41.refs_1_, bf16[272,512]{1,0:T(8,128)(2,1)S(1)} %collective-permute-done.refs_2_, bf16[8,2,128,128]{3,2,1,0:T(8,128)(2,1)S(1)} %all-to-all-done.refs_3_, ...), custom_call_target="tpu_custom_call" | custom-call | flops 1610612736 | bytes 4194304 | tf_op jit(solution)/shard_map/near/pallas_call | solution.py:323
  61.9 0.1 collective-permute-start.11
  62.0 0.7 %collective-permute-done.10.refs_1_ = bf16[256,512]{1,0:T(8,128)(2,1)S(1)} collective-permute-done((bf16[256,512]{1,0:T(8,128)(2,1)S(1)}, bf16[256,512]{1,0:T(8,128)(2,1)S(1)}, u32[]{:S(2)}, u32[]{:S(2)}) %collective-permute-start.10) | collective-permute-done | bytes 262176 | tf_op jit(solution)/shard_map/ppermute | solution.py:353
  62.7 0.8 %collective-permute-done.11.refs_3_ = bf16[256,512]{1,0:T(8,128)(2,1)S(1)} collective-permute-done((bf16[256,512]{1,0:T(8,128)(2,1)S(1)}, bf16[256,512]{1,0:T(8,128)(2,1)S(1)}, u32[]{:S(2)}, u32[]{:S(2)}) %collective-permute-start.11) | collective-permute-done | bytes 262176 | tf_op jit(solution)/shard_map/ppermute | solution.py:353
  63.5 1.0 %unpack.1 = bf16[256,2048]{1,0:T(8,128)(2,1)} custom-call(bf16[256,512]{1,0:T(8,128)(2,1)S(1)} %get-tuple-element.39.refs_0_, bf16[256,512]{1,0:T(8,128)(2,1)S(1)} %get-tuple-element.40.refs_1_, bf16[256,512]{1,0:T(8,128)(2,1)S(1)} %get-tuple-element.43.refs_2_, bf16[256,512]{1,0:T(8,128)(2,1)S(1)} %collective-permute-done.11.refs_3_), custom_call_target="tpu_custom_call" | custom-call | bytes 2097152 | tf_op jit(solution)/shard_map/unpack/pallas_call | solution.py:108
  (17 shorter events, 0.1 us)
Async XLA Ops:
  0.0 7.2 %copy-start.2 = (s32[2,4,3]{1,0,2:T(2,128)S(1)}, s32[2,4,3]{1,0,2:T(2,128)}, u32[]{:S(2)}) copy-start(s32[2,4,3]{1,0,2:T(2,128)} %param.7) | copy-start | bytes 292
  0.0 7.3 %copy-start = (bf16[256,2048]{1,0:T(8,128)(2,1)S(1)}, bf16[256,2048]{1,0:T(8,128)(2,1)}, u32[]{:S(2)}) copy-start(bf16[256,2048]{1,0:T(8,128)(2,1)} %q_ref.1) | copy-start | bytes 3145732
  2.0 12.3 %collective-permute-start.4 = (bf16[8,2,128,128]{3,2,1,0:T(8,128)(2,1)}, bf16[8,2,128,128]{3,2,1,0:T(8,128)(2,1)S(1)}, u32[]{:S(2)}, u32[]{:S(2)}) collective-permute-start(bf16[8,2,128,128]{3,2,1,0:T(8,128)(2,1)} %pack_kv.1), channel_id=1, source_target_pairs={{8,24},{0,8},{9,25},{1,9},{10,26},{2,10},{11,27},{3,11},{12,28},{4... | collective-permute-start | bytes 1572872 | tf_op jit(solution)/shard_map/ppermute | solution.py:360
  2.7 11.6 %all-to-all-start = ((bf16[8,2,128,128]{3,2,1,0:T(8,128)(2,1)}), bf16[8,2,128,128]{3,2,1,0:T(8,128)(2,1)S(1)}, u32[]{:S(2)}, u32[]{:S(2)}) async-start(bf16[8,2,128,128]{3,2,1,0:T(8,128)(2,1)} %pack_kv.1), calls=%async_computation | async-start | bytes 1048576 | tf_op jit(solution)/shard_map/all_to_all | solution.py:361
  8.7 17.2 %collective-permute-start.2 = (bf16[272,512]{1,0:T(8,128)(2,1)S(1)}, bf16[272,512]{1,0:T(8,128)(2,1)}, u32[]{:S(2)}, u32[]{:S(2)}) collective-permute-start(bf16[272,512]{1,0:T(8,128)(2,1)S(1)} %get-tuple-element.28), channel_id=1, source_target_pairs={{0,4},{2,6},{4,0},{6,2},{1,5},{3,7},{5,1},{7,3},{8,12},{10,14},{12... | collective-permute-start | bytes 835592 | tf_op jit(solution)/shard_map/ppermute | solution.py:353
  14.3 0.8 %copy-start.1 = (bf16[8,2,128,128]{3,2,1,0:T(8,128)(2,1)}, bf16[8,2,128,128]{3,2,1,0:T(8,128)(2,1)S(1)}, u32[]{:S(2)}) copy-start(bf16[8,2,128,128]{3,2,1,0:T(8,128)(2,1)S(1)} %collective-permute-done.4) | copy-start | bytes 1572868
  15.1 15.8 %collective-permute-start.5 = (bf16[4,2,128,128]{3,2,1,0:T(8,128)(2,1)S(1)}, bf16[4,2,128,128]{3,2,1,0:T(8,128)(2,1)S(1)}, u32[]{:S(2)}, u32[]{:S(2)}) collective-permute-start(bf16[4,2,128,128]{3,2,1,0:T(8,128)(2,1)S(1)} %get-tuple-element.30), channel_id=1, source_target_pairs={{0,16},{16,24},{1,17},{17,25},{2,18},{18,26},{3,19},{19,27},{4,20}... | collective-permute-start | bytes 786440 | tf_op jit(solution)/shard_map/ppermute | solution.py:373
  21.8 11.8 %collective-permute-start.6 = (bf16[4,2,128,128]{3,2,1,0:T(8,128)(2,1)S(1)}, bf16[4,2,128,128]{3,2,1,0:T(8,128)(2,1)S(1)}, u32[]{:S(2)}, u32[]{:S(2)}) collective-permute-start(bf16[4,2,128,128]{3,2,1,0:T(8,128)(2,1)S(1)} %get-tuple-element.31), channel_id=1, source_target_pairs={{0,16},{16,24},{1,17},{17,25},{2,18},{18,26},{3,19},{19,27},{4,20}... | collective-permute-start | bytes 786440 | tf_op jit(solution)/shard_map/ppermute | solution.py:373
  23.7 12.6 %collective-permute-start = (bf16[272,512]{1,0:T(8,128)(2,1)}, bf16[272,512]{1,0:T(8,128)(2,1)S(1)}, u32[]{:S(2)}, u32[]{:S(2)}) collective-permute-start(bf16[272,512]{1,0:T(8,128)(2,1)} %get-tuple-element.26), channel_id=1, source_target_pairs={{0,2},{2,0},{4,6},{6,4},{1,3},{3,1},{5,7},{7,5},{8,10},{10,8},{12,... | collective-permute-start | bytes 835592 | tf_op jit(solution)/shard_map/ppermute | solution.py:353
  25.6 10.7 %collective-permute-start.1 = (bf16[272,512]{1,0:T(8,128)(2,1)S(1)}, bf16[272,512]{1,0:T(8,128)(2,1)S(1)}, u32[]{:S(2)}, u32[]{:S(2)}) collective-permute-start(bf16[272,512]{1,0:T(8,128)(2,1)S(1)} %get-tuple-element.27), channel_id=1, source_target_pairs={{0,4},{2,6},{4,0},{6,2},{1,5},{3,7},{5,1},{7,3},{8,12},{10,14},{12... | collective-permute-start | bytes 835592 | tf_op jit(solution)/shard_map/ppermute | solution.py:353
  25.9 10.4 %collective-permute-start.3 = (bf16[272,512]{1,0:T(8,128)(2,1)}, bf16[272,512]{1,0:T(8,128)(2,1)S(1)}, u32[]{:S(2)}, u32[]{:S(2)}) collective-permute-start(bf16[272,512]{1,0:T(8,128)(2,1)} %collective-permute-done.2), channel_id=1, source_target_pairs={{0,2},{2,0},{4,6},{6,4},{1,3},{3,1},{5,7},{7,5},{8,10},{10,8},{12,... | collective-permute-start | bytes 835592 | tf_op jit(solution)/shard_map/ppermute | solution.py:353
  26.2 13.2 %all-to-all-start.1 = ((bf16[8,2,128,128]{3,2,1,0:T(8,128)(2,1)}), bf16[8,2,128,128]{3,2,1,0:T(8,128)(2,1)S(1)}, u32[]{:S(2)}, u32[]{:S(2)}) async-start(bf16[8,2,128,128]{3,2,1,0:T(8,128)(2,1)} %copy-done.1), calls=%async_computation.1 | async-start | bytes 1048576 | tf_op jit(solution)/shard_map/all_to_all | solution.py:374
  31.6 13.5 %collective-permute-start.7 = (bf16[4,2,128,128]{3,2,1,0:T(8,128)(2,1)}, bf16[4,2,128,128]{3,2,1,0:T(8,128)(2,1)S(1)}, u32[]{:S(2)}, u32[]{:S(2)}) collective-permute-start(bf16[4,2,128,128]{3,2,1,0:T(8,128)(2,1)} %broadcast_select_fusion.1), channel_id=1, source_target_pairs={{16,24},{8,16},{17,25},{9,17},{18,26},{10,18},{19,27},{11,19},{20,... | collective-permute-start | bytes 786440 | tf_op jit(solution)/shard_map/ppermute | solution.py:379
  34.3 12.6 %collective-permute-start.8 = (bf16[4,2,128,128]{3,2,1,0:T(8,128)(2,1)}, bf16[4,2,128,128]{3,2,1,0:T(8,128)(2,1)S(1)}, u32[]{:S(2)}, u32[]{:S(2)}) collective-permute-start(bf16[4,2,128,128]{3,2,1,0:T(8,128)(2,1)} %broadcast_select_fusion), channel_id=1, source_target_pairs={{16,24},{8,16},{17,25},{9,17},{18,26},{10,18},{19,27},{11,19},{20,... | collective-permute-start | bytes 786440 | tf_op jit(solution)/shard_map/ppermute | solution.py:379
  49.0 13.0 %collective-permute-start.9 = (bf16[256,512]{1,0:T(8,128)(2,1)S(1)}, bf16[256,512]{1,0:T(8,128)(2,1)S(1)}, u32[]{:S(2)}, u32[]{:S(2)}) collective-permute-start(bf16[256,512]{1,0:T(8,128)(2,1)S(1)} %far_late.2), channel_id=1, source_target_pairs={{0,4},{2,6},{4,0},{6,2},{1,5},{3,7},{5,1},{7,3},{8,12},{10,14},{12... | collective-permute-start | bytes 786440 | tf_op jit(solution)/shard_map/ppermute | solution.py:353
  51.8 10.9 %collective-permute-start.10 = (bf16[256,512]{1,0:T(8,128)(2,1)S(1)}, bf16[256,512]{1,0:T(8,128)(2,1)S(1)}, u32[]{:S(2)}, u32[]{:S(2)}) collective-permute-start(bf16[256,512]{1,0:T(8,128)(2,1)S(1)} %far_late.3), channel_id=1, source_target_pairs={{0,6},{2,4},{4,2},{6,0},{1,7},{3,5},{5,3},{7,1},{8,14},{10,12},{12... | collective-permute-start | bytes 786440 | tf_op jit(solution)/shard_map/ppermute | solution.py:353
  61.9 1.6 %collective-permute-start.11 = (bf16[256,512]{1,0:T(8,128)(2,1)S(1)}, bf16[256,512]{1,0:T(8,128)(2,1)S(1)}, u32[]{:S(2)}, u32[]{:S(2)}) collective-permute-start(bf16[256,512]{1,0:T(8,128)(2,1)S(1)} %get-tuple-element.44), channel_id=1, source_target_pairs={{0,2},{2,0},{4,6},{6,4},{1,3},{3,1},{5,7},{7,5},{8,10},{10,8},{12,... | collective-permute-start | bytes 786440 | tf_op jit(solution)/shard_map/ppermute | solution.py:353

commit v13 on v12

--- a/solution.py
+++ b/solution.py
@@ -262,19 +262,20 @@
                     start += n
 
             def others(n):
+                together = PER if n <= 1 else TOGETHER
                 at = [pl.ds(pl.multiple_of(w * BLK, BLK), BLK) for w in where[:n]]
 
                 def scores(c):
-                    heads = range(c * TOGETHER, (c + 1) * TOGETHER)
+                    heads = range(c * together, (c + 1) * together)
                     q = [q_buf[part, q_rows, j * HD : (j + 1) * HD] for j in heads]
                     q = jnp.concatenate(q, axis=0)
                     s = [dot_nt(q, k_buf[a]) for a in at]
                     return jnp.concatenate(s, axis=1) if n > 1 else s[0]
 
-                chains = range(PER // TOGETHER)
+                chains = range(PER // together)
                 ready = [scores(c) for c in chains] if n else None
                 for c in chains:
-                    here = slice(c * TOGETHER * TILE, (c + 1) * TOGETHER * TILE)
+                    here = slice(c * together * TILE, (c + 1) * together * TILE)
                     m = m_old[at_old, here]
                     acc = acc_old[at_old, here]
                     if n:
@@ -284,8 +285,8 @@
                         acc = acc * jnp.tile(jnp.exp2((old - m) * SCALE), (1, 2))
                         for i, a in enumerate(at):
                             acc = acc + dot_nn(p[:, i * BLK : (i + 1) * BLK], v_buf[a])
-                    for i in range(TOGETHER):
-                        j, rows_of = c * TOGETHER + i, slice(i * TILE, (i + 1) * TILE)
+                    for i in range(together):
+                        j, rows_of = c * together + i, slice(i * TILE, (i + 1) * TILE)
                         if last:
                             finish(j, acc[rows_of])
                         else:

time: 65.3 us -> 65.4 us (level)
  no operation moved by 1% of the time
where the time goes in v13:
time: 65.4 us; the launch traced here: 65.1 us
  starting transfers between devices  28.2 us (43%)
  Pallas kernels  22.9 us (35%)
  waiting for transfers between devices  11.2 us (17%)
  other arithmetic  1.55 us (2%)
  local copies, waits for them, and re-layouts  0.9 us (1%)
    pallas_call x4, Pallas kernels, attention(): pl.pallas_call(kernel, in_specs=[SMEM] + [VMEM] * (n_q + n_src + len(stat...  18.5 us
    ppermute x2, starting transfers between devices, body(): up = [lax.ppermute(piece, 'lev', [(0, 2), (2, 3)]) for piece in halves]  8.58 us
    ppermute x7, starting transfers between devices, exchange(): lax.ppermute(piece, 'sub', [(i, i ^ k) for i in range(subs)])  5.9 us
    all_to_all x1, waiting for transfers between devices, body(): own = lax.all_to_all(packed, ('sub', 'head'), 0, 0, tiled=True)  5.31 us
    all_to_all x1, starting transfers between devices, body(): p2 = lax.all_to_all(raw, ('sub', 'head'), 0, 0, tiled=True)  4.66 us
    all_to_all x1, starting transfers between devices, body(): own = lax.all_to_all(packed, ('sub', 'head'), 0, 0, tiled=True)  4.52 us
    ppermute x2, starting transfers between devices, body(): lax.ppermute(jnp.where(forwards, a, b), 'lev', [(2, 3), (1, 2)])  3.89 us
    all_to_all x1, waiting for transfers between devices, body(): p2 = lax.all_to_all(raw, ('sub', 'head'), 0, 0, tiled=True)  3.05 us
  transfers between devices with their start and end apart: 14, of which 5 were waited for; matrix products, arithmetic and copies ran while one was open for 3% of the time, Pallas kernels for 27%

profile of v13, /device:TPU:23, one launch (start us, length us, event | category | flops | bytes accessed | tf_op | source)
XLA Modules:
  0.0 65.1 jit_solution(1826765685287791163)
XLA Ops:
  0.0 2.0 %pack_kv.1 = bf16[8,2,128,128]{3,2,1,0:T(8,128)(2,1)} custom-call(bf16[128,1024]{1,0:T(8,128)(2,1)} %k_ref.1, bf16[128,1024]{1,0:T(8,128)(2,1)} %v_ref.1), custom_call_target="tpu_custom_call" | custom-call | bytes 1048576 | tf_op jit(solution)/shard_map/pack_kv/pallas_call | solution.py:55
  2.0 0.7 %collective-permute-start.4 = (bf16[8,2,128,128]{3,2,1,0:T(8,128)(2,1)}, bf16[8,2,128,128]{3,2,1,0:T(8,128)(2,1)S(1)}, u32[]{:S(2)}, u32[]{:S(2)}) collective-permute-start(bf16[8,2,128,128]{3,2,1,0:T(8,128)(2,1)} %pack_kv.1), channel_id=1, source_target_pairs={{8,24},{0,8},{9,25},{1,9},{10,26},{2,10},{11,27},{3,11},{12,28},{4... | collective-permute-start | bytes 1572872 | tf_op jit(solution)/shard_map/ppermute | solution.py:361
  2.7 4.5 %all-to-all-start = ((bf16[8,2,128,128]{3,2,1,0:T(8,128)(2,1)}), bf16[8,2,128,128]{3,2,1,0:T(8,128)(2,1)S(1)}, u32[]{:S(2)}, u32[]{:S(2)}) async-start(bf16[8,2,128,128]{3,2,1,0:T(8,128)(2,1)} %pack_kv.1), calls=%async_computation | async-start | bytes 1048576 | tf_op jit(solution)/shard_map/all_to_all | solution.py:362
  7.2 0.1 copy.7.sel_ref
  7.3 1.4 %pack_q.1 = (bf16[272,512]{1,0:T(8,128)(2,1)S(1)}, bf16[272,512]{1,0:T(8,128)(2,1)}, bf16[272,512]{1,0:T(8,128)(2,1)S(1)}, bf16[272,512]{1,0:T(8,128)(2,1)S(1)}) custom-call(s32[2,4,3]{2,1,0:T(4,128)S(1)} %copy.7.sel_ref, bf16[256,2048]{1,0:T(8,128)(2,1)S(1)} %copy-done), custom_call_target="tpu_custom_call" | custom-call | bytes 2097152 | tf_op jit(solution)/shard_map/pack_q/pallas_call | solution.py:81
  8.7 0.3 collective-permute-start.2
  9.0 5.3 %all-to-all-done.refs_3_ = bf16[8,2,128,128]{3,2,1,0:T(8,128)(2,1)S(1)} async-done(((bf16[8,2,128,128]{3,2,1,0:T(8,128)(2,1)}), bf16[8,2,128,128]{3,2,1,0:T(8,128)(2,1)S(1)}, u32[]{:S(2)}, u32[]{:S(2)}) %all-to-all-start) | async-done | bytes 524320 | tf_op jit(solution)/shard_map/all_to_all | solution.py:362
  14.3 0.0 collective-permute-done.4
  14.4 0.7 %copy-done.1 = bf16[8,2,128,128]{3,2,1,0:T(8,128)(2,1)} copy-done((bf16[8,2,128,128]{3,2,1,0:T(8,128)(2,1)}, bf16[8,2,128,128]{3,2,1,0:T(8,128)(2,1)S(1)}, u32[]{:S(2)}) %copy-start.1) | copy-done | bytes 524312
  15.1 6.7 %collective-permute-start.5 = (bf16[4,2,128,128]{3,2,1,0:T(8,128)(2,1)S(1)}, bf16[4,2,128,128]{3,2,1,0:T(8,128)(2,1)S(1)}, u32[]{:S(2)}, u32[]{:S(2)}) collective-permute-start(bf16[4,2,128,128]{3,2,1,0:T(8,128)(2,1)S(1)} %get-tuple-element.30), channel_id=1, source_target_pairs={{0,16},{16,24},{1,17},{17,25},{2,18},{18,26},{3,19},{19,27},{4,20}... | collective-permute-start | bytes 786440 | tf_op jit(solution)/shard_map/ppermute | solution.py:374
  21.8 1.9 %collective-permute-start.6 = (bf16[4,2,128,128]{3,2,1,0:T(8,128)(2,1)S(1)}, bf16[4,2,128,128]{3,2,1,0:T(8,128)(2,1)S(1)}, u32[]{:S(2)}, u32[]{:S(2)}) collective-permute-start(bf16[4,2,128,128]{3,2,1,0:T(8,128)(2,1)S(1)} %get-tuple-element.31), channel_id=1, source_target_pairs={{0,16},{16,24},{1,17},{17,25},{2,18},{18,26},{3,19},{19,27},{4,20}... | collective-permute-start | bytes 786440 | tf_op jit(solution)/shard_map/ppermute | solution.py:374
  23.7 1.9 %collective-permute-start = (bf16[272,512]{1,0:T(8,128)(2,1)}, bf16[272,512]{1,0:T(8,128)(2,1)S(1)}, u32[]{:S(2)}, u32[]{:S(2)}) collective-permute-start(bf16[272,512]{1,0:T(8,128)(2,1)} %get-tuple-element.26), channel_id=1, source_target_pairs={{0,2},{2,0},{4,6},{6,4},{1,3},{3,1},{5,7},{7,5},{8,10},{10,8},{12,... | collective-permute-start | bytes 835592 | tf_op jit(solution)/shard_map/ppermute | solution.py:354
  25.6 0.3 collective-permute-start.1
  25.9 0.3 collective-permute-start.3
  26.2 4.7 %all-to-all-start.1 = ((bf16[8,2,128,128]{3,2,1,0:T(8,128)(2,1)}), bf16[8,2,128,128]{3,2,1,0:T(8,128)(2,1)S(1)}, u32[]{:S(2)}, u32[]{:S(2)}) async-start(bf16[8,2,128,128]{3,2,1,0:T(8,128)(2,1)} %copy-done.1), calls=%async_computation.1 | async-start | bytes 1048576 | tf_op jit(solution)/shard_map/all_to_all | solution.py:375
  30.9 0.7 %broadcast_select_fusion.1 = bf16[4,2,128,128]{3,2,1,0:T(8,128)(2,1)} fusion(bf16[4,2,128,128]{3,2,1,0:T(8,128)(2,1)S(1)} %collective-permute-done.5.refs_4_, bf16[4,2,128,128]{3,2,1,0:T(8,128)(2,1)S(1)} %get-tuple-element.30, pred[]{:T(512)S(6)} %eq.3), kind=kLoop, calls=%fused_computation.1 | loop fusion | flops 131072 | bytes 786433 | tf_op jit(solution)/shard_map/jit(_where)/select_n | solution.py:380
  31.6 1.9 %collective-permute-start.7 = (bf16[4,2,128,128]{3,2,1,0:T(8,128)(2,1)}, bf16[4,2,128,128]{3,2,1,0:T(8,128)(2,1)S(1)}, u32[]{:S(2)}, u32[]{:S(2)}) collective-permute-start(bf16[4,2,128,128]{3,2,1,0:T(8,128)(2,1)} %broadcast_select_fusion.1), channel_id=1, source_target_pairs={{16,24},{8,16},{17,25},{9,17},{18,26},{10,18},{19,27},{11,19},{20,... | collective-permute-start | bytes 786440 | tf_op jit(solution)/shard_map/ppermute | solution.py:380
  33.5 0.7 %broadcast_select_fusion = bf16[4,2,128,128]{3,2,1,0:T(8,128)(2,1)} fusion(bf16[4,2,128,128]{3,2,1,0:T(8,128)(2,1)S(1)} %collective-permute-done.6.refs_5_, bf16[4,2,128,128]{3,2,1,0:T(8,128)(2,1)S(1)} %get-tuple-element.31, pred[]{:T(512)S(6)} %eq.3), kind=kLoop, calls=%fused_computation | loop fusion | flops 131072 | bytes 786433 | tf_op jit(solution)/shard_map/jit(_where)/select_n | solution.py:380
  34.3 2.0 %collective-permute-start.8 = (bf16[4,2,128,128]{3,2,1,0:T(8,128)(2,1)}, bf16[4,2,128,128]{3,2,1,0:T(8,128)(2,1)S(1)}, u32[]{:S(2)}, u32[]{:S(2)}) collective-permute-start(bf16[4,2,128,128]{3,2,1,0:T(8,128)(2,1)} %broadcast_select_fusion), channel_id=1, source_target_pairs={{16,24},{8,16},{17,25},{9,17},{18,26},{10,18},{19,27},{11,19},{20,... | collective-permute-start | bytes 786440 | tf_op jit(solution)/shard_map/ppermute | solution.py:380
  36.3 0.1 maximum_convert_fusion.refs_0_
  36.4 3.0 %all-to-all-done.1.refs_6_ = bf16[8,2,128,128]{3,2,1,0:T(8,128)(2,1)S(1)} async-done(((bf16[8,2,128,128]{3,2,1,0:T(8,128)(2,1)}), bf16[8,2,128,128]{3,2,1,0:T(8,128)(2,1)S(1)}, u32[]{:S(2)}, u32[]{:S(2)}) %all-to-all-start.1) | async-done | bytes 524320 | tf_op jit(solution)/shard_map/all_to_all | solution.py:375
  39.5 6.0 %far_early.1 = (f32[4,512,128]{2,1,0:T(8,128)S(1)}, f32[4,512,256]{2,1,0:T(8,128)S(1)}) custom-call(s32[24]{0:T(128)S(1)} %maximum_convert_fusion.refs_0_, bf16[272,512]{1,0:T(8,128)(2,1)S(1)} %collective-permute-done.1.refs_1_, bf16[272,512]{1,0:T(8,128)(2,1)S(1)} %collective-permute-done.3.refs_2_.refs_1_, ...), custom_call_target="tpu_custom_call" | custom-call | flops 1610612736 | bytes 4194304 | tf_op jit(solution)/shard_map/far_early/pallas_call | solution.py:324
  45.5 1.3 %collective-permute-done.8.refs_3_.refs_8_ = bf16[4,2,128,128]{3,2,1,0:T(8,128)(2,1)S(1)} collective-permute-done((bf16[4,2,128,128]{3,2,1,0:T(8,128)(2,1)}, bf16[4,2,128,128]{3,2,1,0:T(8,128)(2,1)S(1)}, u32[]{:S(2)}, u32[]{:S(2)}) %collective-permute-start.8) | collective-permute-done | bytes 262176 | tf_op jit(solution)/shard_map/ppermute | solution.py:380
  46.9 2.3 %far_late.2 = bf16[256,512]{1,0:T(8,128)(2,1)S(1)} custom-call(s32[24]{0:T(128)S(1)} %maximum_convert_fusion.refs_0_, bf16[272,512]{1,0:T(8,128)(2,1)S(1)} %collective-permute-done.1.refs_1_, bf16[4,2,128,128]{3,2,1,0:T(8,128)(2,1)S(1)} %collective-permute-done.7.refs_2_.refs_7_, bf16[4,2,128,128]{3,2,1,0:T(8,128)(2,1)S(1)} %collective-permute-done.8.refs_3_.refs_8_, ...), custom_call_target="tpu_custom_call" | custom-call | flops 805306368 | bytes 4194304 | tf_op jit(solution)/shard_map/far_late/pallas_call | solution.py:324
  49.2 0.3 collective-permute-start.9
  49.5 2.4 %far_late.3 = bf16[256,512]{1,0:T(8,128)(2,1)S(1)} custom-call(s32[24]{0:T(128)S(1)} %maximum_convert_fusion.refs_0_, bf16[272,512]{1,0:T(8,128)(2,1)S(1)} %collective-permute-done.3.refs_2_.refs_1_, bf16[4,2,128,128]{3,2,1,0:T(8,128)(2,1)S(1)} %collective-permute-done.7.refs_2_.refs_7_, bf16[4,2,128,128]{3,2,1,0:T(8,128)(2,1)S(1)} %collective-permute-done.8.refs_3_.refs_8_, ...), custom_call_target="tpu_custom_call" | custom-call | flops 805306368 | bytes 4194304 | tf_op jit(solution)/shard_map/far_late/pallas_call | solution.py:324
  52.0 2.7 %collective-permute-start.10 = (bf16[256,512]{1,0:T(8,128)(2,1)S(1)}, bf16[256,512]{1,0:T(8,128)(2,1)S(1)}, u32[]{:S(2)}, u32[]{:S(2)}) collective-permute-start(bf16[256,512]{1,0:T(8,128)(2,1)S(1)} %far_late.3), channel_id=1, source_target_pairs={{0,6},{2,4},{4,2},{6,0},{1,7},{3,5},{5,3},{7,1},{8,14},{10,12},{12... | collective-permute-start | bytes 786440 | tf_op jit(solution)/shard_map/ppermute | solution.py:354
  54.7 7.7 %near.1 = (bf16[256,512]{1,0:T(8,128)(2,1)S(1)}, bf16[256,512]{1,0:T(8,128)(2,1)S(1)}) custom-call(s32[24]{0:T(128)S(1)} %maximum_convert_fusion.refs_0_, bf16[272,512]{1,0:T(8,128)(2,1)S(1)} %get-tuple-element.41.refs_1_, bf16[272,512]{1,0:T(8,128)(2,1)S(1)} %collective-permute-done.refs_2_, bf16[8,2,128,128]{3,2,1,0:T(8,128)(2,1)S(1)} %all-to-all-done.refs_3_, ...), custom_call_target="tpu_custom_call" | custom-call | flops 1610612736 | bytes 4194304 | tf_op jit(solution)/shard_map/near/pallas_call | solution.py:324
  62.3 0.1 collective-permute-start.11
  62.4 0.5 collective-permute-done.10.refs_1_
  62.9 1.0 %collective-permute-done.11.refs_3_ = bf16[256,512]{1,0:T(8,128)(2,1)S(1)} collective-permute-done((bf16[256,512]{1,0:T(8,128)(2,1)S(1)}, bf16[256,512]{1,0:T(8,128)(2,1)S(1)}, u32[]{:S(2)}, u32[]{:S(2)}) %collective-permute-start.11) | collective-permute-done | bytes 262176 | tf_op jit(solution)/shard_map/ppermute | solution.py:354
  63.9 1.0 %unpack.1 = bf16[256,2048]{1,0:T(8,128)(2,1)} custom-call(bf16[256,512]{1,0:T(8,128)(2,1)S(1)} %get-tuple-element.39.refs_0_, bf16[256,512]{1,0:T(8,128)(2,1)S(1)} %get-tuple-element.40.refs_1_, bf16[256,512]{1,0:T(8,128)(2,1)S(1)} %get-tuple-element.43.refs_2_, bf16[256,512]{1,0:T(8,128)(2,1)S(1)} %collective-permute-done.11.refs_3_), custom_call_target="tpu_custom_call" | custom-call | bytes 2097152 | tf_op jit(solution)/shard_map/unpack/pallas_call | solution.py:108
  (17 shorter events, 0.1 us)
Async XLA Ops:
  0.0 7.2 %copy-start.2 = (s32[2,4,3]{1,0,2:T(2,128)S(1)}, s32[2,4,3]{1,0,2:T(2,128)}, u32[]{:S(2)}) copy-start(s32[2,4,3]{1,0,2:T(2,128)} %param.7) | copy-start | bytes 292
  0.0 7.3 %copy-start = (bf16[256,2048]{1,0:T(8,128)(2,1)S(1)}, bf16[256,2048]{1,0:T(8,128)(2,1)}, u32[]{:S(2)}) copy-start(bf16[256,2048]{1,0:T(8,128)(2,1)} %q_ref.1) | copy-start | bytes 3145732
  2.0 12.3 %collective-permute-start.4 = (bf16[8,2,128,128]{3,2,1,0:T(8,128)(2,1)}, bf16[8,2,128,128]{3,2,1,0:T(8,128)(2,1)S(1)}, u32[]{:S(2)}, u32[]{:S(2)}) collective-permute-start(bf16[8,2,128,128]{3,2,1,0:T(8,128)(2,1)} %pack_kv.1), channel_id=1, source_target_pairs={{8,24},{0,8},{9,25},{1,9},{10,26},{2,10},{11,27},{3,11},{12,28},{4... | collective-permute-start | bytes 1572872 | tf_op jit(solution)/shard_map/ppermute | solution.py:361
  2.7 11.6 %all-to-all-start = ((bf16[8,2,128,128]{3,2,1,0:T(8,128)(2,1)}), bf16[8,2,128,128]{3,2,1,0:T(8,128)(2,1)S(1)}, u32[]{:S(2)}, u32[]{:S(2)}) async-start(bf16[8,2,128,128]{3,2,1,0:T(8,128)(2,1)} %pack_kv.1), calls=%async_computation | async-start | bytes 1048576 | tf_op jit(solution)/shard_map/all_to_all | solution.py:362
  8.7 17.2 %collective-permute-start.2 = (bf16[272,512]{1,0:T(8,128)(2,1)S(1)}, bf16[272,512]{1,0:T(8,128)(2,1)}, u32[]{:S(2)}, u32[]{:S(2)}) collective-permute-start(bf16[272,512]{1,0:T(8,128)(2,1)S(1)} %get-tuple-element.28), channel_id=1, source_target_pairs={{0,4},{2,6},{4,0},{6,2},{1,5},{3,7},{5,1},{7,3},{8,12},{10,14},{12... | collective-permute-start | bytes 835592 | tf_op jit(solution)/shard_map/ppermute | solution.py:354
  14.3 0.8 %copy-start.1 = (bf16[8,2,128,128]{3,2,1,0:T(8,128)(2,1)}, bf16[8,2,128,128]{3,2,1,0:T(8,128)(2,1)S(1)}, u32[]{:S(2)}) copy-start(bf16[8,2,128,128]{3,2,1,0:T(8,128)(2,1)S(1)} %collective-permute-done.4) | copy-start | bytes 1572868
  15.1 15.8 %collective-permute-start.5 = (bf16[4,2,128,128]{3,2,1,0:T(8,128)(2,1)S(1)}, bf16[4,2,128,128]{3,2,1,0:T(8,128)(2,1)S(1)}, u32[]{:S(2)}, u32[]{:S(2)}) collective-permute-start(bf16[4,2,128,128]{3,2,1,0:T(8,128)(2,1)S(1)} %get-tuple-element.30), channel_id=1, source_target_pairs={{0,16},{16,24},{1,17},{17,25},{2,18},{18,26},{3,19},{19,27},{4,20}... | collective-permute-start | bytes 786440 | tf_op jit(solution)/shard_map/ppermute | solution.py:374
  21.8 11.8 %collective-permute-start.6 = (bf16[4,2,128,128]{3,2,1,0:T(8,128)(2,1)S(1)}, bf16[4,2,128,128]{3,2,1,0:T(8,128)(2,1)S(1)}, u32[]{:S(2)}, u32[]{:S(2)}) collective-permute-start(bf16[4,2,128,128]{3,2,1,0:T(8,128)(2,1)S(1)} %get-tuple-element.31), channel_id=1, source_target_pairs={{0,16},{16,24},{1,17},{17,25},{2,18},{18,26},{3,19},{19,27},{4,20}... | collective-permute-start | bytes 786440 | tf_op jit(solution)/shard_map/ppermute | solution.py:374
  23.7 12.6 %collective-permute-start = (bf16[272,512]{1,0:T(8,128)(2,1)}, bf16[272,512]{1,0:T(8,128)(2,1)S(1)}, u32[]{:S(2)}, u32[]{:S(2)}) collective-permute-start(bf16[272,512]{1,0:T(8,128)(2,1)} %get-tuple-element.26), channel_id=1, source_target_pairs={{0,2},{2,0},{4,6},{6,4},{1,3},{3,1},{5,7},{7,5},{8,10},{10,8},{12,... | collective-permute-start | bytes 835592 | tf_op jit(solution)/shard_map/ppermute | solution.py:354
  25.6 10.7 %collective-permute-start.1 = (bf16[272,512]{1,0:T(8,128)(2,1)S(1)}, bf16[272,512]{1,0:T(8,128)(2,1)S(1)}, u32[]{:S(2)}, u32[]{:S(2)}) collective-permute-start(bf16[272,512]{1,0:T(8,128)(2,1)S(1)} %get-tuple-element.27), channel_id=1, source_target_pairs={{0,4},{2,6},{4,0},{6,2},{1,5},{3,7},{5,1},{7,3},{8,12},{10,14},{12... | collective-permute-start | bytes 835592 | tf_op jit(solution)/shard_map/ppermute | solution.py:354
  25.9 10.4 %collective-permute-start.3 = (bf16[272,512]{1,0:T(8,128)(2,1)}, bf16[272,512]{1,0:T(8,128)(2,1)S(1)}, u32[]{:S(2)}, u32[]{:S(2)}) collective-permute-start(bf16[272,512]{1,0:T(8,128)(2,1)} %collective-permute-done.2), channel_id=1, source_target_pairs={{0,2},{2,0},{4,6},{6,4},{1,3},{3,1},{5,7},{7,5},{8,10},{10,8},{12,... | collective-permute-start | bytes 835592 | tf_op jit(solution)/shard_map/ppermute | solution.py:354
  26.2 13.2 %all-to-all-start.1 = ((bf16[8,2,128,128]{3,2,1,0:T(8,128)(2,1)}), bf16[8,2,128,128]{3,2,1,0:T(8,128)(2,1)S(1)}, u32[]{:S(2)}, u32[]{:S(2)}) async-start(bf16[8,2,128,128]{3,2,1,0:T(8,128)(2,1)} %copy-done.1), calls=%async_computation.1 | async-start | bytes 1048576 | tf_op jit(solution)/shard_map/all_to_all | solution.py:375
  31.6 13.9 %collective-permute-start.7 = (bf16[4,2,128,128]{3,2,1,0:T(8,128)(2,1)}, bf16[4,2,128,128]{3,2,1,0:T(8,128)(2,1)S(1)}, u32[]{:S(2)}, u32[]{:S(2)}) collective-permute-start(bf16[4,2,128,128]{3,2,1,0:T(8,128)(2,1)} %broadcast_select_fusion.1), channel_id=1, source_target_pairs={{16,24},{8,16},{17,25},{9,17},{18,26},{10,18},{19,27},{11,19},{20,... | collective-permute-start | bytes 786440 | tf_op jit(solution)/shard_map/ppermute | solution.py:380
  34.3 12.6 %collective-permute-start.8 = (bf16[4,2,128,128]{3,2,1,0:T(8,128)(2,1)}, bf16[4,2,128,128]{3,2,1,0:T(8,128)(2,1)S(1)}, u32[]{:S(2)}, u32[]{:S(2)}) collective-permute-start(bf16[4,2,128,128]{3,2,1,0:T(8,128)(2,1)} %broadcast_select_fusion), channel_id=1, source_target_pairs={{16,24},{8,16},{17,25},{9,17},{18,26},{10,18},{19,27},{11,19},{20,... | collective-permute-start | bytes 786440 | tf_op jit(solution)/shard_map/ppermute | solution.py:380
  49.2 13.2 %collective-permute-start.9 = (bf16[256,512]{1,0:T(8,128)(2,1)S(1)}, bf16[256,512]{1,0:T(8,128)(2,1)S(1)}, u32[]{:S(2)}, u32[]{:S(2)}) collective-permute-start(bf16[256,512]{1,0:T(8,128)(2,1)S(1)} %far_late.2), channel_id=1, source_target_pairs={{0,4},{2,6},{4,0},{6,2},{1,5},{3,7},{5,1},{7,3},{8,12},{10,14},{12... | collective-permute-start | bytes 786440 | tf_op jit(solution)/shard_map/ppermute | solution.py:354
  52.0 11.0 %collective-permute-start.10 = (bf16[256,512]{1,0:T(8,128)(2,1)S(1)}, bf16[256,512]{1,0:T(8,128)(2,1)S(1)}, u32[]{:S(2)}, u32[]{:S(2)}) collective-permute-start(bf16[256,512]{1,0:T(8,128)(2,1)S(1)} %far_late.3), channel_id=1, source_target_pairs={{0,6},{2,4},{4,2},{6,0},{1,7},{3,5},{5,3},{7,1},{8,14},{10,12},{12... | collective-permute-start | bytes 786440 | tf_op jit(solution)/shard_map/ppermute | solution.py:354
  62.3 1.6 %collective-permute-start.11 = (bf16[256,512]{1,0:T(8,128)(2,1)S(1)}, bf16[256,512]{1,0:T(8,128)(2,1)S(1)}, u32[]{:S(2)}, u32[]{:S(2)}) collective-permute-start(bf16[256,512]{1,0:T(8,128)(2,1)S(1)} %get-tuple-element.44), channel_id=1, source_target_pairs={{0,2},{2,0},{4,6},{6,4},{1,3},{3,1},{5,7},{7,5},{8,10},{10,8},{12,... | collective-permute-start | bytes 786440 | tf_op jit(solution)/shard_map/ppermute | solution.py:354

commit v14 on v12

--- a/solution.py
+++ b/solution.py
@@ -235,7 +235,7 @@
                 m_old, acc_old, at_old = m_in, acc_in, t + (partners[0] - state_from) * tiles_in_part
 
             def finish(j, acc):
-                out_ref[out_at, j * HD : (j + 1) * HD] = (acc[:, :HD] / acc[:, HD:]).astype(BF16)
+                out_ref[out_at, j * HD : (j + 1) * HD] = (acc[:, :HD] * pl.reciprocal(acc[:, HD:])).astype(BF16)
 
             def keep(j, m, acc):
                 outs[0][t, j * TILE : (j + 1) * TILE] = m

time: 65.3 us -> 65.2 us (level)
  no operation moved by 1% of the time
where the time goes in v14:
time: 65.2 us; the launch traced here: 64.7 us
  starting transfers between devices  28.4 us (44%)
  Pallas kernels  22.4 us (34%)
  waiting for transfers between devices  11.1 us (17%)
  other arithmetic  1.55 us (2%)
  local copies, waits for them, and re-layouts  0.9 us (1%)
    pallas_call x4, Pallas kernels, attention(): pl.pallas_call(kernel, in_specs=[SMEM] + [VMEM] * (n_q + n_src + len(stat...  18 us
    ppermute x2, starting transfers between devices, body(): up = [lax.ppermute(piece, 'lev', [(0, 2), (2, 3)]) for piece in halves]  8.58 us
    ppermute x7, starting transfers between devices, exchange(): lax.ppermute(piece, 'sub', [(i, i ^ k) for i in range(subs)])  6.02 us
    all_to_all x1, waiting for transfers between devices, body(): own = lax.all_to_all(packed, ('sub', 'head'), 0, 0, tiled=True)  5.31 us
    all_to_all x1, starting transfers between devices, body(): p2 = lax.all_to_all(raw, ('sub', 'head'), 0, 0, tiled=True)  4.66 us
    all_to_all x1, starting transfers between devices, body(): own = lax.all_to_all(packed, ('sub', 'head'), 0, 0, tiled=True)  4.52 us
    ppermute x2, starting transfers between devices, body(): lax.ppermute(jnp.where(forwards, a, b), 'lev', [(2, 3), (1, 2)])  3.89 us
    all_to_all x1, waiting for transfers between devices, body(): p2 = lax.all_to_all(raw, ('sub', 'head'), 0, 0, tiled=True)  3.05 us
  transfers between devices with their start and end apart: 14, of which 5 were waited for; matrix products, arithmetic and copies ran while one was open for 3% of the time, Pallas kernels for 27%

profile of v14, /device:TPU:23, one launch (start us, length us, event | category | flops | bytes accessed | tf_op | source)
XLA Modules:
  0.0 64.7 jit_solution(18251091933989321624)
XLA Ops:
  0.0 2.0 %pack_kv.1 = bf16[8,2,128,128]{3,2,1,0:T(8,128)(2,1)} custom-call(bf16[128,1024]{1,0:T(8,128)(2,1)} %k_ref.1, bf16[128,1024]{1,0:T(8,128)(2,1)} %v_ref.1), custom_call_target="tpu_custom_call" | custom-call | bytes 1048576 | tf_op jit(solution)/shard_map/pack_kv/pallas_call | solution.py:55
  2.0 0.7 %collective-permute-start.4 = (bf16[8,2,128,128]{3,2,1,0:T(8,128)(2,1)}, bf16[8,2,128,128]{3,2,1,0:T(8,128)(2,1)S(1)}, u32[]{:S(2)}, u32[]{:S(2)}) collective-permute-start(bf16[8,2,128,128]{3,2,1,0:T(8,128)(2,1)} %pack_kv.1), channel_id=1, source_target_pairs={{8,24},{0,8},{9,25},{1,9},{10,26},{2,10},{11,27},{3,11},{12,28},{4... | collective-permute-start | bytes 1572872 | tf_op jit(solution)/shard_map/ppermute | solution.py:360
  2.7 4.5 %all-to-all-start = ((bf16[8,2,128,128]{3,2,1,0:T(8,128)(2,1)}), bf16[8,2,128,128]{3,2,1,0:T(8,128)(2,1)S(1)}, u32[]{:S(2)}, u32[]{:S(2)}) async-start(bf16[8,2,128,128]{3,2,1,0:T(8,128)(2,1)} %pack_kv.1), calls=%async_computation | async-start | bytes 1048576 | tf_op jit(solution)/shard_map/all_to_all | solution.py:361
  7.2 0.1 copy.7.sel_ref
  7.3 1.4 %pack_q.1 = (bf16[272,512]{1,0:T(8,128)(2,1)S(1)}, bf16[272,512]{1,0:T(8,128)(2,1)}, bf16[272,512]{1,0:T(8,128)(2,1)S(1)}, bf16[272,512]{1,0:T(8,128)(2,1)S(1)}) custom-call(s32[2,4,3]{2,1,0:T(4,128)S(1)} %copy.7.sel_ref, bf16[256,2048]{1,0:T(8,128)(2,1)S(1)} %copy-done), custom_call_target="tpu_custom_call" | custom-call | bytes 2097152 | tf_op jit(solution)/shard_map/pack_q/pallas_call | solution.py:81
  8.7 0.3 collective-permute-start.2
  9.0 5.3 %all-to-all-done.refs_3_ = bf16[8,2,128,128]{3,2,1,0:T(8,128)(2,1)S(1)} async-done(((bf16[8,2,128,128]{3,2,1,0:T(8,128)(2,1)}), bf16[8,2,128,128]{3,2,1,0:T(8,128)(2,1)S(1)}, u32[]{:S(2)}, u32[]{:S(2)}) %all-to-all-start) | async-done | bytes 524320 | tf_op jit(solution)/shard_map/all_to_all | solution.py:361
  14.3 0.0 collective-permute-done.4
  14.4 0.7 %copy-done.1 = bf16[8,2,128,128]{3,2,1,0:T(8,128)(2,1)} copy-done((bf16[8,2,128,128]{3,2,1,0:T(8,128)(2,1)}, bf16[8,2,128,128]{3,2,1,0:T(8,128)(2,1)S(1)}, u32[]{:S(2)}) %copy-start.1) | copy-done | bytes 524312
  15.1 6.7 %collective-permute-start.5 = (bf16[4,2,128,128]{3,2,1,0:T(8,128)(2,1)S(1)}, bf16[4,2,128,128]{3,2,1,0:T(8,128)(2,1)S(1)}, u32[]{:S(2)}, u32[]{:S(2)}) collective-permute-start(bf16[4,2,128,128]{3,2,1,0:T(8,128)(2,1)S(1)} %get-tuple-element.30), channel_id=1, source_target_pairs={{0,16},{16,24},{1,17},{17,25},{2,18},{18,26},{3,19},{19,27},{4,20}... | collective-permute-start | bytes 786440 | tf_op jit(solution)/shard_map/ppermute | solution.py:373
  21.8 1.9 %collective-permute-start.6 = (bf16[4,2,128,128]{3,2,1,0:T(8,128)(2,1)S(1)}, bf16[4,2,128,128]{3,2,1,0:T(8,128)(2,1)S(1)}, u32[]{:S(2)}, u32[]{:S(2)}) collective-permute-start(bf16[4,2,128,128]{3,2,1,0:T(8,128)(2,1)S(1)} %get-tuple-element.31), channel_id=1, source_target_pairs={{0,16},{16,24},{1,17},{17,25},{2,18},{18,26},{3,19},{19,27},{4,20}... | collective-permute-start | bytes 786440 | tf_op jit(solution)/shard_map/ppermute | solution.py:373
  23.7 1.9 %collective-permute-start = (bf16[272,512]{1,0:T(8,128)(2,1)}, bf16[272,512]{1,0:T(8,128)(2,1)S(1)}, u32[]{:S(2)}, u32[]{:S(2)}) collective-permute-start(bf16[272,512]{1,0:T(8,128)(2,1)} %get-tuple-element.26), channel_id=1, source_target_pairs={{0,2},{2,0},{4,6},{6,4},{1,3},{3,1},{5,7},{7,5},{8,10},{10,8},{12,... | collective-permute-start | bytes 835592 | tf_op jit(solution)/shard_map/ppermute | solution.py:353
  25.6 0.3 collective-permute-start.1
  25.9 0.3 collective-permute-start.3
  26.2 4.7 %all-to-all-start.1 = ((bf16[8,2,128,128]{3,2,1,0:T(8,128)(2,1)}), bf16[8,2,128,128]{3,2,1,0:T(8,128)(2,1)S(1)}, u32[]{:S(2)}, u32[]{:S(2)}) async-start(bf16[8,2,128,128]{3,2,1,0:T(8,128)(2,1)} %copy-done.1), calls=%async_computation.1 | async-start | bytes 1048576 | tf_op jit(solution)/shard_map/all_to_all | solution.py:374
  30.9 0.7 %broadcast_select_fusion.1 = bf16[4,2,128,128]{3,2,1,0:T(8,128)(2,1)} fusion(bf16[4,2,128,128]{3,2,1,0:T(8,128)(2,1)S(1)} %collective-permute-done.5.refs_4_, bf16[4,2,128,128]{3,2,1,0:T(8,128)(2,1)S(1)} %get-tuple-element.30, pred[]{:T(512)S(6)} %eq.3), kind=kLoop, calls=%fused_computation.1 | loop fusion | flops 131072 | bytes 786433 | tf_op jit(solution)/shard_map/jit(_where)/select_n | solution.py:379
  31.6 1.9 %collective-permute-start.7 = (bf16[4,2,128,128]{3,2,1,0:T(8,128)(2,1)}, bf16[4,2,128,128]{3,2,1,0:T(8,128)(2,1)S(1)}, u32[]{:S(2)}, u32[]{:S(2)}) collective-permute-start(bf16[4,2,128,128]{3,2,1,0:T(8,128)(2,1)} %broadcast_select_fusion.1), channel_id=1, source_target_pairs={{16,24},{8,16},{17,25},{9,17},{18,26},{10,18},{19,27},{11,19},{20,... | collective-permute-start | bytes 786440 | tf_op jit(solution)/shard_map/ppermute | solution.py:379
  33.5 0.7 %broadcast_select_fusion = bf16[4,2,128,128]{3,2,1,0:T(8,128)(2,1)} fusion(bf16[4,2,128,128]{3,2,1,0:T(8,128)(2,1)S(1)} %collective-permute-done.6.refs_5_, bf16[4,2,128,128]{3,2,1,0:T(8,128)(2,1)S(1)} %get-tuple-element.31, pred[]{:T(512)S(6)} %eq.3), kind=kLoop, calls=%fused_computation | loop fusion | flops 131072 | bytes 786433 | tf_op jit(solution)/shard_map/jit(_where)/select_n | solution.py:379
  34.3 2.0 %collective-permute-start.8 = (bf16[4,2,128,128]{3,2,1,0:T(8,128)(2,1)}, bf16[4,2,128,128]{3,2,1,0:T(8,128)(2,1)S(1)}, u32[]{:S(2)}, u32[]{:S(2)}) collective-permute-start(bf16[4,2,128,128]{3,2,1,0:T(8,128)(2,1)} %broadcast_select_fusion), channel_id=1, source_target_pairs={{16,24},{8,16},{17,25},{9,17},{18,26},{10,18},{19,27},{11,19},{20,... | collective-permute-start | bytes 786440 | tf_op jit(solution)/shard_map/ppermute | solution.py:379
  36.3 0.1 maximum_convert_fusion.refs_0_
  36.4 3.0 %all-to-all-done.1.refs_6_ = bf16[8,2,128,128]{3,2,1,0:T(8,128)(2,1)S(1)} async-done(((bf16[8,2,128,128]{3,2,1,0:T(8,128)(2,1)}), bf16[8,2,128,128]{3,2,1,0:T(8,128)(2,1)S(1)}, u32[]{:S(2)}, u32[]{:S(2)}) %all-to-all-start.1) | async-done | bytes 524320 | tf_op jit(solution)/shard_map/all_to_all | solution.py:374
  39.5 6.1 %far_early.1 = (f32[4,512,128]{2,1,0:T(8,128)S(1)}, f32[4,512,256]{2,1,0:T(8,128)S(1)}) custom-call(s32[24]{0:T(128)S(1)} %maximum_convert_fusion.refs_0_, bf16[272,512]{1,0:T(8,128)(2,1)S(1)} %collective-permute-done.1.refs_1_, bf16[272,512]{1,0:T(8,128)(2,1)S(1)} %collective-permute-done.3.refs_2_.refs_1_, ...), custom_call_target="tpu_custom_call" | custom-call | flops 1610612736 | bytes 4194304 | tf_op jit(solution)/shard_map/far_early/pallas_call | solution.py:323
  45.6 1.2 %collective-permute-done.8.refs_3_.refs_8_ = bf16[4,2,128,128]{3,2,1,0:T(8,128)(2,1)S(1)} collective-permute-done((bf16[4,2,128,128]{3,2,1,0:T(8,128)(2,1)}, bf16[4,2,128,128]{3,2,1,0:T(8,128)(2,1)S(1)}, u32[]{:S(2)}, u32[]{:S(2)}) %collective-permute-start.8) | collective-permute-done | bytes 262176 | tf_op jit(solution)/shard_map/ppermute | solution.py:379
  46.9 2.1 %far_late.2 = bf16[256,512]{1,0:T(8,128)(2,1)S(1)} custom-call(s32[24]{0:T(128)S(1)} %maximum_convert_fusion.refs_0_, bf16[272,512]{1,0:T(8,128)(2,1)S(1)} %collective-permute-done.1.refs_1_, bf16[4,2,128,128]{3,2,1,0:T(8,128)(2,1)S(1)} %collective-permute-done.7.refs_2_.refs_7_, bf16[4,2,128,128]{3,2,1,0:T(8,128)(2,1)S(1)} %collective-permute-done.8.refs_3_.refs_8_, ...), custom_call_target="tpu_custom_call" | custom-call | flops 805306368 | bytes 4194304 | tf_op jit(solution)/shard_map/far_late/pallas_call | solution.py:323
  49.0 0.5 collective-permute-start.9
  49.5 2.1 %far_late.3 = bf16[256,512]{1,0:T(8,128)(2,1)S(1)} custom-call(s32[24]{0:T(128)S(1)} %maximum_convert_fusion.refs_0_, bf16[272,512]{1,0:T(8,128)(2,1)S(1)} %collective-permute-done.3.refs_2_.refs_1_, bf16[4,2,128,128]{3,2,1,0:T(8,128)(2,1)S(1)} %collective-permute-done.7.refs_2_.refs_7_, bf16[4,2,128,128]{3,2,1,0:T(8,128)(2,1)S(1)} %collective-permute-done.8.refs_3_.refs_8_, ...), custom_call_target="tpu_custom_call" | custom-call | flops 805306368 | bytes 4194304 | tf_op jit(solution)/shard_map/far_late/pallas_call | solution.py:323
  51.6 2.6 %collective-permute-start.10 = (bf16[256,512]{1,0:T(8,128)(2,1)S(1)}, bf16[256,512]{1,0:T(8,128)(2,1)S(1)}, u32[]{:S(2)}, u32[]{:S(2)}) collective-permute-start(bf16[256,512]{1,0:T(8,128)(2,1)S(1)} %far_late.3), channel_id=1, source_target_pairs={{0,6},{2,4},{4,2},{6,0},{1,7},{3,5},{5,3},{7,1},{8,14},{10,12},{12... | collective-permute-start | bytes 786440 | tf_op jit(solution)/shard_map/ppermute | solution.py:353
  54.2 7.7 %near.1 = (bf16[256,512]{1,0:T(8,128)(2,1)S(1)}, bf16[256,512]{1,0:T(8,128)(2,1)S(1)}) custom-call(s32[24]{0:T(128)S(1)} %maximum_convert_fusion.refs_0_, bf16[272,512]{1,0:T(8,128)(2,1)S(1)} %get-tuple-element.41.refs_1_, bf16[272,512]{1,0:T(8,128)(2,1)S(1)} %collective-permute-done.refs_2_, bf16[8,2,128,128]{3,2,1,0:T(8,128)(2,1)S(1)} %all-to-all-done.refs_3_, ...), custom_call_target="tpu_custom_call" | custom-call | flops 1610612736 | bytes 4194304 | tf_op jit(solution)/shard_map/near/pallas_call | solution.py:323
  61.9 0.1 collective-permute-start.11
  62.0 0.7 %collective-permute-done.10.refs_1_ = bf16[256,512]{1,0:T(8,128)(2,1)S(1)} collective-permute-done((bf16[256,512]{1,0:T(8,128)(2,1)S(1)}, bf16[256,512]{1,0:T(8,128)(2,1)S(1)}, u32[]{:S(2)}, u32[]{:S(2)}) %collective-permute-start.10) | collective-permute-done | bytes 262176 | tf_op jit(solution)/shard_map/ppermute | solution.py:353
  62.7 0.8 %collective-permute-done.11.refs_3_ = bf16[256,512]{1,0:T(8,128)(2,1)S(1)} collective-permute-done((bf16[256,512]{1,0:T(8,128)(2,1)S(1)}, bf16[256,512]{1,0:T(8,128)(2,1)S(1)}, u32[]{:S(2)}, u32[]{:S(2)}) %collective-permute-start.11) | collective-permute-done | bytes 262176 | tf_op jit(solution)/shard_map/ppermute | solution.py:353
  63.5 1.0 %unpack.1 = bf16[256,2048]{1,0:T(8,128)(2,1)} custom-call(bf16[256,512]{1,0:T(8,128)(2,1)S(1)} %get-tuple-element.39.refs_0_, bf16[256,512]{1,0:T(8,128)(2,1)S(1)} %get-tuple-element.40.refs_1_, bf16[256,512]{1,0:T(8,128)(2,1)S(1)} %get-tuple-element.43.refs_2_, bf16[256,512]{1,0:T(8,128)(2,1)S(1)} %collective-permute-done.11.refs_3_), custom_call_target="tpu_custom_call" | custom-call | bytes 2097152 | tf_op jit(solution)/shard_map/unpack/pallas_call | solution.py:108
  (17 shorter events, 0.1 us)
Async XLA Ops:
  0.0 7.2 %copy-start.2 = (s32[2,4,3]{1,0,2:T(2,128)S(1)}, s32[2,4,3]{1,0,2:T(2,128)}, u32[]{:S(2)}) copy-start(s32[2,4,3]{1,0,2:T(2,128)} %param.7) | copy-start | bytes 292
  0.0 7.3 %copy-start = (bf16[256,2048]{1,0:T(8,128)(2,1)S(1)}, bf16[256,2048]{1,0:T(8,128)(2,1)}, u32[]{:S(2)}) copy-start(bf16[256,2048]{1,0:T(8,128)(2,1)} %q_ref.1) | copy-start | bytes 3145732
  2.0 12.3 %collective-permute-start.4 = (bf16[8,2,128,128]{3,2,1,0:T(8,128)(2,1)}, bf16[8,2,128,128]{3,2,1,0:T(8,128)(2,1)S(1)}, u32[]{:S(2)}, u32[]{:S(2)}) collective-permute-start(bf16[8,2,128,128]{3,2,1,0:T(8,128)(2,1)} %pack_kv.1), channel_id=1, source_target_pairs={{8,24},{0,8},{9,25},{1,9},{10,26},{2,10},{11,27},{3,11},{12,28},{4... | collective-permute-start | bytes 1572872 | tf_op jit(solution)/shard_map/ppermute | solution.py:360
  2.7 11.6 %all-to-all-start = ((bf16[8,2,128,128]{3,2,1,0:T(8,128)(2,1)}), bf16[8,2,128,128]{3,2,1,0:T(8,128)(2,1)S(1)}, u32[]{:S(2)}, u32[]{:S(2)}) async-start(bf16[8,2,128,128]{3,2,1,0:T(8,128)(2,1)} %pack_kv.1), calls=%async_computation | async-start | bytes 1048576 | tf_op jit(solution)/shard_map/all_to_all | solution.py:361
  8.7 17.2 %collective-permute-start.2 = (bf16[272,512]{1,0:T(8,128)(2,1)S(1)}, bf16[272,512]{1,0:T(8,128)(2,1)}, u32[]{:S(2)}, u32[]{:S(2)}) collective-permute-start(bf16[272,512]{1,0:T(8,128)(2,1)S(1)} %get-tuple-element.28), channel_id=1, source_target_pairs={{0,4},{2,6},{4,0},{6,2},{1,5},{3,7},{5,1},{7,3},{8,12},{10,14},{12... | collective-permute-start | bytes 835592 | tf_op jit(solution)/shard_map/ppermute | solution.py:353
  14.3 0.8 %copy-start.1 = (bf16[8,2,128,128]{3,2,1,0:T(8,128)(2,1)}, bf16[8,2,128,128]{3,2,1,0:T(8,128)(2,1)S(1)}, u32[]{:S(2)}) copy-start(bf16[8,2,128,128]{3,2,1,0:T(8,128)(2,1)S(1)} %collective-permute-done.4) | copy-start | bytes 1572868
  15.1 15.8 %collective-permute-start.5 = (bf16[4,2,128,128]{3,2,1,0:T(8,128)(2,1)S(1)}, bf16[4,2,128,128]{3,2,1,0:T(8,128)(2,1)S(1)}, u32[]{:S(2)}, u32[]{:S(2)}) collective-permute-start(bf16[4,2,128,128]{3,2,1,0:T(8,128)(2,1)S(1)} %get-tuple-element.30), channel_id=1, source_target_pairs={{0,16},{16,24},{1,17},{17,25},{2,18},{18,26},{3,19},{19,27},{4,20}... | collective-permute-start | bytes 786440 | tf_op jit(solution)/shard_map/ppermute | solution.py:373
  21.8 11.8 %collective-permute-start.6 = (bf16[4,2,128,128]{3,2,1,0:T(8,128)(2,1)S(1)}, bf16[4,2,128,128]{3,2,1,0:T(8,128)(2,1)S(1)}, u32[]{:S(2)}, u32[]{:S(2)}) collective-permute-start(bf16[4,2,128,128]{3,2,1,0:T(8,128)(2,1)S(1)} %get-tuple-element.31), channel_id=1, source_target_pairs={{0,16},{16,24},{1,17},{17,25},{2,18},{18,26},{3,19},{19,27},{4,20}... | collective-permute-start | bytes 786440 | tf_op jit(solution)/shard_map/ppermute | solution.py:373
  23.7 12.6 %collective-permute-start = (bf16[272,512]{1,0:T(8,128)(2,1)}, bf16[272,512]{1,0:T(8,128)(2,1)S(1)}, u32[]{:S(2)}, u32[]{:S(2)}) collective-permute-start(bf16[272,512]{1,0:T(8,128)(2,1)} %get-tuple-element.26), channel_id=1, source_target_pairs={{0,2},{2,0},{4,6},{6,4},{1,3},{3,1},{5,7},{7,5},{8,10},{10,8},{12,... | collective-permute-start | bytes 835592 | tf_op jit(solution)/shard_map/ppermute | solution.py:353
  25.6 10.7 %collective-permute-start.1 = (bf16[272,512]{1,0:T(8,128)(2,1)S(1)}, bf16[272,512]{1,0:T(8,128)(2,1)S(1)}, u32[]{:S(2)}, u32[]{:S(2)}) collective-permute-start(bf16[272,512]{1,0:T(8,128)(2,1)S(1)} %get-tuple-element.27), channel_id=1, source_target_pairs={{0,4},{2,6},{4,0},{6,2},{1,5},{3,7},{5,1},{7,3},{8,12},{10,14},{12... | collective-permute-start | bytes 835592 | tf_op jit(solution)/shard_map/ppermute | solution.py:353
  25.9 10.4 %collective-permute-start.3 = (bf16[272,512]{1,0:T(8,128)(2,1)}, bf16[272,512]{1,0:T(8,128)(2,1)S(1)}, u32[]{:S(2)}, u32[]{:S(2)}) collective-permute-start(bf16[272,512]{1,0:T(8,128)(2,1)} %collective-permute-done.2), channel_id=1, source_target_pairs={{0,2},{2,0},{4,6},{6,4},{1,3},{3,1},{5,7},{7,5},{8,10},{10,8},{12,... | collective-permute-start | bytes 835592 | tf_op jit(solution)/shard_map/ppermute | solution.py:353
  26.2 13.2 %all-to-all-start.1 = ((bf16[8,2,128,128]{3,2,1,0:T(8,128)(2,1)}), bf16[8,2,128,128]{3,2,1,0:T(8,128)(2,1)S(1)}, u32[]{:S(2)}, u32[]{:S(2)}) async-start(bf16[8,2,128,128]{3,2,1,0:T(8,128)(2,1)} %copy-done.1), calls=%async_computation.1 | async-start | bytes 1048576 | tf_op jit(solution)/shard_map/all_to_all | solution.py:374
  31.6 14.0 %collective-permute-start.7 = (bf16[4,2,128,128]{3,2,1,0:T(8,128)(2,1)}, bf16[4,2,128,128]{3,2,1,0:T(8,128)(2,1)S(1)}, u32[]{:S(2)}, u32[]{:S(2)}) collective-permute-start(bf16[4,2,128,128]{3,2,1,0:T(8,128)(2,1)} %broadcast_select_fusion.1), channel_id=1, source_target_pairs={{16,24},{8,16},{17,25},{9,17},{18,26},{10,18},{19,27},{11,19},{20,... | collective-permute-start | bytes 786440 | tf_op jit(solution)/shard_map/ppermute | solution.py:379
  34.3 12.6 %collective-permute-start.8 = (bf16[4,2,128,128]{3,2,1,0:T(8,128)(2,1)}, bf16[4,2,128,128]{3,2,1,0:T(8,128)(2,1)S(1)}, u32[]{:S(2)}, u32[]{:S(2)}) collective-permute-start(bf16[4,2,128,128]{3,2,1,0:T(8,128)(2,1)} %broadcast_select_fusion), channel_id=1, source_target_pairs={{16,24},{8,16},{17,25},{9,17},{18,26},{10,18},{19,27},{11,19},{20,... | collective-permute-start | bytes 786440 | tf_op jit(solution)/shard_map/ppermute | solution.py:379
  49.0 13.0 %collective-permute-start.9 = (bf16[256,512]{1,0:T(8,128)(2,1)S(1)}, bf16[256,512]{1,0:T(8,128)(2,1)S(1)}, u32[]{:S(2)}, u32[]{:S(2)}) collective-permute-start(bf16[256,512]{1,0:T(8,128)(2,1)S(1)} %far_late.2), channel_id=1, source_target_pairs={{0,4},{2,6},{4,0},{6,2},{1,5},{3,7},{5,1},{7,3},{8,12},{10,14},{12... | collective-permute-start | bytes 786440 | tf_op jit(solution)/shard_map/ppermute | solution.py:353
  51.6 11.1 %collective-permute-start.10 = (bf16[256,512]{1,0:T(8,128)(2,1)S(1)}, bf16[256,512]{1,0:T(8,128)(2,1)S(1)}, u32[]{:S(2)}, u32[]{:S(2)}) collective-permute-start(bf16[256,512]{1,0:T(8,128)(2,1)S(1)} %far_late.3), channel_id=1, source_target_pairs={{0,6},{2,4},{4,2},{6,0},{1,7},{3,5},{5,3},{7,1},{8,14},{10,12},{12... | collective-permute-start | bytes 786440 | tf_op jit(solution)/shard_map/ppermute | solution.py:353
  61.9 1.6 %collective-permute-start.11 = (bf16[256,512]{1,0:T(8,128)(2,1)S(1)}, bf16[256,512]{1,0:T(8,128)(2,1)S(1)}, u32[]{:S(2)}, u32[]{:S(2)}) collective-permute-start(bf16[256,512]{1,0:T(8,128)(2,1)S(1)} %get-tuple-element.44), channel_id=1, source_target_pairs={{0,2},{2,0},{4,6},{6,4},{1,3},{3,1},{5,7},{7,5},{8,10},{10,8},{12,... | collective-permute-start | bytes 786440 | tf_op jit(solution)/shard_map/ppermute | solution.py:353
